TPU v7x, 256 devices: a whole 4x4x8 slice. The times are simulated.
256 devices in a mesh: cfg: 2 (over z_hi), seq: 16 (over z_lo, y), dp: 8 (over x, core).
Axes of the slice: x: 4, y: 4, z: 8 (z_hi: 2, z_lo: 4; z = z_hi * 4 + z_lo), core: 2. Of those that a mesh axis runs over, the one named last changes fastest.
Arguments:
- teacher_query: bfloat16 [2, 2, 8, 2048, 2048], P('cfg', None, 'dp', 'seq'), may hold values from -6 to 6
- teacher_key: bfloat16 [2, 2, 8, 2048, 2048], P('cfg', None, 'dp', 'seq'), may hold values from -6 to 6
- teacher_value: bfloat16 [2, 2, 8, 2048, 2048], P('cfg', None, 'dp', 'seq'), may hold values from -6 to 6
- hidden: bfloat16 [2, 8, 2048, 3072], P('cfg', 'dp', 'seq'), may hold values from -6 to 6
- adapter_down_weight: bfloat16 [3, 3072, 128], replicated, may hold values from -0.109375 to 0.109375
- adapter_up_weight: bfloat16 [3, 128, 2048], replicated, may hold values from -0.5 to 0.5
- guidance_index: int32 [2, 8], P(None, 'dp'), may hold values from 0 to 7
- timestep_index: int32 [2, 8], P(None, 'dp'), may hold values from 0 to 999
Outputs:
- student_out: bfloat16 [2, 8, 2048, 2048], P('cfg', 'dp', 'seq')
- grad_down: float32 [3, 3072, 128], P(None, ('cfg', 'seq', 'dp'))
- grad_up: float32 [3, 128, 2048], P(None, ('cfg', 'dp'), 'seq')
All inputs are finite; a program needn't handle non-finite values.
Results may differ from a plain program's by a relative error of at most 0.02.
The roundings to bfloat16 on the way count: a program that leaves them out, or rounds other values in their place, can miss the bound.
Values may be sent and summed in bfloat16 or wider, within the bound.
No kernel may reach another device: no remote copies, remote signals or barrier semaphores. Data moves between devices by JAX's collectives and lax.ppermute only.
A program may use at most 128 MiB of HBM per device.

v0:
```python
import math

import jax
import jax.numpy as jnp
from jax import lax
from jax.sharding import PartitionSpec as P

HDIM = 128
ADAPTER_RANK = 128
TSTEPS = 1000


def side_by_side(arrays, axis, split_dim, concat_dim, along):
    both = jnp.concatenate(arrays, axis=along)
    whole, at, done = (
        lax.all_to_all(both, axis, split_axis=split_dim, concat_axis=concat_dim, tiled=True),
        0,
        [],
    )
    for a in arrays:
        done.append(lax.slice_in_dim(whole, at, at + a.shape[along], axis=along))
        at += a.shape[along]
    return tuple(done)


def swapped(value, axis, distance):
    mask = 2**distance
    pairs = [(source, source ^ mask) for source in range(lax.axis_size(axis))]
    return lax.ppermute(value, axis, pairs)


def passed_along(value, axis, steps):
    count = lax.axis_size(axis)
    leading, last = (max(0, -steps), min(count, count - steps))
    return lax.ppermute(value, axis, [(source, source + steps) for source in range(leading, last)])


def laid_out(parts, dim):
    parts = jnp.moveaxis(parts, 0, dim)
    dims = parts.shape
    return parts.reshape(*dims[:dim], dims[dim] * dims[dim + 1], *dims[dim + 2 :])


def from_everyone(array, axis):
    peers = lax.axis_size(axis)
    return lax.all_to_all(
        jnp.broadcast_to(array[None], (peers, *array.shape)), axis, 0, 0, tiled=True
    )


def gathered_copies(array, axis, dim):
    return laid_out(from_everyone(array, axis), dim)


def split_up(array, dim, peers):
    dims = array.shape
    parts = array.reshape(*dims[:dim], peers, dims[dim] // peers, *dims[dim + 1 :])
    return jnp.moveaxis(parts, dim, 0)


def sent_and_summed(array, axis, dim):
    parts = split_up(array, dim, lax.axis_size(axis))
    arrived = lax.all_to_all(parts, axis, split_axis=0, concat_axis=0, tiled=True)
    return arrived.astype(jnp.float32).sum(axis=0)


def head_probs(query_block, key_heads, factor):
    scores = (
        jnp.einsum("qhd,khd->hqk", query_block, key_heads, preferred_element_type=jnp.float32)
        * factor
    )
    highest = jnp.max(scores, axis=-1, keepdims=True)
    raised = jnp.exp(scores - highest)
    return raised / jnp.sum(raised, axis=-1, keepdims=True)


def attention_forward(queries, keys, values):
    length, columns_all = queries.shape
    heads_here = columns_all // HDIM
    factor = HDIM ** (-0.5)
    step_rows = min(512, length)
    key_heads = keys.reshape(length, heads_here, HDIM)
    value_heads = values.reshape(length, heads_here, HDIM)
    query_blocks = queries.reshape(length // step_rows, step_rows, heads_here, HDIM)

    def one_block(query_block):
        weights = head_probs(query_block, key_heads, factor).astype(jnp.bfloat16)
        return jnp.einsum("hqk,khd->qhd", weights, value_heads, preferred_element_type=jnp.float32)

    return lax.map(one_block, query_blocks).reshape(length, columns_all)


def attention_backward(queries, keys, values, upstream):
    length, columns_all = queries.shape
    heads_here = columns_all // HDIM
    factor = HDIM ** (-0.5)
    step_rows = min(512, length)
    key_heads = keys.reshape(length, heads_here, HDIM)
    value_heads = values.reshape(length, heads_here, HDIM)
    query_blocks = queries.reshape(length // step_rows, step_rows, heads_here, HDIM)
    upstream_blocks = upstream.reshape(length // step_rows, step_rows, heads_here, HDIM)

    def one_block(running, block_pair):
        key_grad, value_grad = running
        query_block, upstream_block = block_pair
        probability = head_probs(query_block, key_heads, factor)
        weights = probability.astype(jnp.bfloat16)
        value_grad = value_grad + jnp.einsum(
            "hqk,qhd->khd", weights, upstream_block, preferred_element_type=jnp.float32
        )
        prob_grad = jnp.einsum(
            "qhd,khd->hqk", upstream_block, value_heads, preferred_element_type=jnp.float32
        )
        center = jnp.sum(probability * prob_grad, axis=-1, keepdims=True)
        score_grad = (probability * (prob_grad - center)).astype(jnp.bfloat16)
        query_grad = (
            jnp.einsum("hqk,khd->qhd", score_grad, key_heads, preferred_element_type=jnp.float32)
            * factor
        )
        key_grad = (
            key_grad
            + jnp.einsum(
                "hqk,qhd->khd", score_grad, query_block, preferred_element_type=jnp.float32
            )
            * factor
        )
        return ((key_grad, value_grad), query_grad)

    empty_grad = jnp.zeros((length, heads_here, HDIM), jnp.float32)
    (key_grad, value_grad), query_grad = lax.scan(
        one_block, (empty_grad, empty_grad), (query_blocks, upstream_blocks)
    )
    return (
        query_grad.reshape(length, columns_all).astype(jnp.bfloat16),
        key_grad.reshape(length, columns_all).astype(jnp.bfloat16),
        value_grad.reshape(length, columns_all).astype(jnp.bfloat16),
    )


def body(
    teacher_query,
    teacher_key,
    teacher_value,
    hidden,
    adapter_down_weight,
    adapter_up_weight,
    guidance_index,
    timestep_index,
):
    cfg_index = lax.axis_index("cfg")
    seq_index = lax.axis_index("seq")
    seq_count = lax.axis_size("seq")
    tok_here = hidden.shape[2]
    head_cols = teacher_query.shape[-1] // seq_count
    total_rows = 2 * lax.axis_size("dp") * tok_here * seq_count
    input_features = hidden[0, 0]
    half_cols = input_features.shape[1] // (2 * seq_count)
    split_view = input_features.reshape(tok_here, 2, seq_count, half_cols)
    column_block = lax.all_to_all(split_view, "seq", split_axis=2, concat_axis=0, tiled=True)
    column_block = column_block.reshape(tok_here * seq_count, 2 * half_cols)
    own_pass = (teacher_query[0, :, 0], teacher_key[0, :, 0], teacher_value[0, :, 0])
    teacher_heads = side_by_side((own_pass[0], own_pass[1], own_pass[2]), "seq", 2, 1, 0)
    teacher_local = jnp.stack(
        [
            attention_forward(
                teacher_heads[0][half_index],
                teacher_heads[1][half_index],
                teacher_heads[2][half_index],
            )
            for half_index in range(2)
        ]
    )
    teacher_tokens = lax.all_to_all(
        teacher_local.astype(jnp.bfloat16), "seq", split_axis=1, concat_axis=2, tiled=True
    )
    guide_scale = 1.0 + 0.5 * guidance_index[:, 0].astype(jnp.float32)
    time_frac = (timestep_index[:, 0].astype(jnp.float32) + 0.5) / TSTEPS
    own_scale = lax.dynamic_index_in_dim(guide_scale, cfg_index, 0, keepdims=False)
    own_time = lax.dynamic_index_in_dim(time_frac, cfg_index, 0, keepdims=False)
    outgoing = lax.dynamic_index_in_dim(teacher_tokens, 1 - cfg_index, 0, keepdims=False)
    incoming = swapped(outgoing, "cfg", 0)
    own_output = lax.dynamic_index_in_dim(teacher_tokens, cfg_index, 0, keepdims=False)
    conditional = jnp.where(cfg_index == 0, own_output, incoming).astype(jnp.float32)
    unconditional = jnp.where(cfg_index == 0, incoming, own_output).astype(jnp.float32)
    target = unconditional + own_scale * (conditional - unconditional)
    rank_index = jnp.arange(1, ADAPTER_RANK + 1).astype(jnp.float32)
    feature_modulation = 1.0 + 0.5 * jnp.cos(
        math.pi * rank_index * own_time + 0.25 * rank_index * own_scale
    )
    rank_projected = (
        jnp.einsum(
            "cl,elj->ecj", input_features, adapter_down_weight, preferred_element_type=jnp.float32
        )
        * feature_modulation
    ).astype(jnp.bfloat16)
    partner = passed_along(
        (teacher_heads[0][1], teacher_heads[1][1], teacher_heads[2][1]), "cfg", 1
    )
    low_all = gathered_copies(rank_projected, "seq", 1)
    up_cols = lax.dynamic_slice_in_dim(adapter_up_weight, seq_index * head_cols, head_cols, 2)
    projected = []
    for stack_member in range(3):
        frozen = jnp.where(cfg_index == 0, teacher_heads[stack_member][0], partner[stack_member])
        adapted_output = jnp.dot(
            low_all[stack_member], up_cols[stack_member], preferred_element_type=jnp.float32
        )
        projected.append((frozen.astype(jnp.float32) + adapted_output).astype(jnp.bfloat16))
    student = tuple(projected)
    student_local = attention_forward(student[0], student[1], student[2]).astype(jnp.bfloat16)
    student_tokens = lax.all_to_all(student_local, "seq", split_axis=0, concat_axis=1, tiled=True)
    upstream = (
        (student_tokens.astype(jnp.float32) - target) * (1.0 / math.sqrt(total_rows))
    ).astype(jnp.bfloat16)
    upstream_heads = lax.all_to_all(upstream, "seq", split_axis=1, concat_axis=0, tiled=True)
    grads_heads = attention_backward(student[0], student[1], student[2], upstream_heads)
    gradient_stack = jnp.stack(grads_heads)
    rank_backward = sent_and_summed(
        jnp.einsum(
            "ktc,krc->tkr", gradient_stack, up_cols, preferred_element_type=jnp.float32
        ).astype(jnp.bfloat16),
        "seq",
        0,
    )
    up_partial = jnp.einsum(
        "ktr,ktc->krc", low_all, gradient_stack, preferred_element_type=jnp.float32
    )
    grad_up = sent_and_summed(up_partial.astype(jnp.bfloat16), ("cfg", "dp"), 1)
    low_grad = jnp.transpose((rank_backward * feature_modulation).astype(jnp.bfloat16), (1, 0, 2))
    grad_rows = gathered_copies(low_grad, "seq", 1)
    column_partial = jnp.einsum(
        "tc,ktr->kcr", column_block, grad_rows, preferred_element_type=jnp.float32
    )
    grad_down = sent_and_summed(column_partial.astype(jnp.bfloat16), ("cfg", "dp"), 1)
    return (student_tokens[None, None], grad_down, grad_up)


def solution(mesh):
    placed = (
        P("cfg", None, "dp", "seq", None),
        P("cfg", None, "dp", "seq", None),
        P("cfg", None, "dp", "seq", None),
        P("cfg", "dp", "seq", None),
        P(),
        P(),
        P(None, "dp"),
        P(None, "dp"),
    )
    return jax.shard_map(
        body,
        mesh=mesh,
        in_specs=placed,
        out_specs=(
            P("cfg", "dp", "seq", None),
            P(None, ("cfg", "seq", "dp"), None),
            P(None, ("cfg", "dp"), "seq"),
        ),
        check_vma=False,
    )
```

profile of v0, /device:TPU:6, one launch (start us, length us, event | category | flops | bytes accessed | tf_op | source)
XLA Modules:
  0.0 525.3 jit_solution(5186441463782181478)
XLA Ops:
  8.2 8.6 %all-to-all-start.1 = ((bf16[16,3,128,128]{2,3,1,0:T(8,128)(2,1)}), bf16[16,3,128,128]{2,3,1,0:T(8,128)(2,1)S(1)}, u32[]{:S(2)}, u32[]{:S(2)}) async-start(bf16[16,3,128,128]{2,3,1,0:T(8,128)(2,1)} %broadcast_in_dim.30), calls=%async_computation.1 | async-start | bytes 3145728 | tf_op jit(solution)/shard_map/all_to_all | solution.py:46
  16.9 2.4 copy.104
  19.3 3.7 copy.105
  23.0 3.7 copy.106
  26.7 6.0 %pad_maximum_fusion = bf16[6,128,2048]{1,0,2:T(8,128)(2,1)} fusion(bf16[2,128,2048]{1,0,2:T(2,128)(2,1)} %bitcast.331, bf16[2,128,2048]{1,0,2:T(2,128)(2,1)} %bitcast.330, bf16[2,128,2048]{1,0,2:T(2,128)(2,1)S(1)} %bitcast.329), kind=kLoop, calls=%fused_computation.74 | loop fusion | flops 9437184 | bytes 6291456 | tf_op jit(solution)/shard_map/concatenate | solution.py:14
  32.7 18.0 %all-to-all-done.1 = bf16[16,3,128,128]{2,3,1,0:T(8,128)(2,1)S(1)} async-done(((bf16[16,3,128,128]{2,3,1,0:T(8,128)(2,1)}), bf16[16,3,128,128]{2,3,1,0:T(8,128)(2,1)S(1)}, u32[]{:S(2)}, u32[]{:S(2)}) %all-to-all-start.1) | async-done | bytes 1572896 | tf_op jit(solution)/shard_map/all_to_all | solution.py:46
  50.7 8.3 %all-to-all-start = ((bf16[6,128,2048]{1,0,2:T(8,128)(2,1)}), bf16[6,128,2048]{1,0,2:T(8,128)(2,1)}, u32[]{:S(2)}, u32[]{:S(2)}) async-start(bf16[6,128,2048]{1,0,2:T(8,128)(2,1)} %pad_maximum_fusion), calls=%async_computation | async-start | bytes 8388608 | tf_op jit(solution)/shard_map/all_to_all | solution.py:16
  60.7 2.7 fusion.93
  63.4 74.6 %all-to-all-done = bf16[6,128,2048]{1,0,2:T(8,128)(2,1)} async-done(((bf16[6,128,2048]{1,0,2:T(8,128)(2,1)}), bf16[6,128,2048]{1,0,2:T(8,128)(2,1)}, u32[]{:S(2)}, u32[]{:S(2)}) %all-to-all-start) | async-done | bytes 3145760 | tf_op jit(solution)/shard_map/all_to_all | solution.py:16
  138.0 2.6 copy.107
  141.9 7.1 %collective-permute-start.2 = (bf16[2048,128]{1,0:T(8,128)(2,1)}, bf16[2048,128]{1,0:T(8,128)(2,1)}, u32[]{:S(2)}, u32[]{:S(2)}) collective-permute-start(bf16[2048,128]{1,0:T(8,128)(2,1)} %bitcast.353), channel_id=1, source_target_pairs={{0,128},{1,129},{2,130},{3,131},{4,132},{5,133},{6,134},{7,135},{8... | collective-permute-start | bytes 1572872 | tf_op jit(solution)/shard_map/ppermute | solution.py:35
  150.3 2.1 collective-permute-start.1
  153.7 2.1 collective-permute-start
  156.2 10.7 %while.46 = (s32[]{:T(128)}, bf16[4,512,1,128]{3,1,2,0:T(8,128)(2,1)S(1)}, bf16[4,512,1,128]{3,1,2,0:T(8,128)(2,1)S(1)}, bf16[2048,1,128]{2,0,1:T(8,128)(2,1)S(1)}, bf16[2048,1,128]{2,0,1:T(8,128)(2,1)S(1)}, /*index=5*/s32[]{:T(128)}) while((s32[]{:T(128)}, bf16[4,512,1,128]{3,1,2,0:T(8,128)(2,1)S(1)}, bf16[4,512,1,128]{3,1,2,0:T(8,128)(2,1)S(1)}, ...), condition=%wide.region_7.8_spmd, body=%wide.region_4.7_spmd.sunk | while | flops 546307072 | bytes 14035021 | solution.py:90
  167.7 15.2 %while.47 = (s32[]{:T(128)}, bf16[4,512,1,128]{3,1,2,0:T(8,128)(2,1)S(1)}, bf16[4,512,1,128]{3,1,2,0:T(8,128)(2,1)}, bf16[2048,1,128]{2,0,1:T(8,128)(2,1)}, bf16[2048,1,128]{2,0,1:T(8,128)(2,1)S(1)}, /*index=5*/s32[]{:T(128)}) while((s32[]{:T(128)}, bf16[4,512,1,128]{3,1,2,0:T(8,128)(2,1)S(1)}, bf16[4,512,1,128]{3,1,2,0:T(8,128)(2,1)}, ...), condition=%wide.region_11.12_spmd, body=%wide.region_8.11_spmd.sunk | while | flops 546307072 | bytes 14035529 | solution.py:90
  183.0 9.5 %copy.129 = bf16[2,2048,128]{2,0,1:T(2,128)(2,1)} copy(bf16[2,2048,128]{2,1,0:T(8,128)(2,1)S(1)} %pad_maximum_fusion.2) | data formatting | bytes 2097152 | tf_op jit(solution)/shard_map/stack | solution.py:163
  192.4 47.4 %all-to-all-start.3 = ((bf16[2,2048,128]{2,0,1:T(2,128)(2,1)}), bf16[2,2048,128]{2,0,1:T(2,128)(2,1)S(1)}, u32[]{:S(2)}, u32[]{:S(2)}) async-start(bf16[2,2048,128]{2,0,1:T(2,128)(2,1)} %copy.129), calls=%async_computation.3 | async-start | bytes 2097152 | tf_op jit(solution)/shard_map/all_to_all | solution.py:173
  239.8 2.1 fusion.78
  244.4 10.8 %while.45 = (s32[]{:T(128)}, bf16[4,512,1,128]{3,1,2,0:T(8,128)(2,1)S(1)}, bf16[4,512,1,128]{3,1,2,0:T(8,128)(2,1)S(1)}, bf16[2048,1,128]{2,0,1:T(8,128)(2,1)S(1)}, bf16[2048,1,128]{2,0,1:T(8,128)(2,1)}, /*index=5*/s32[]{:T(128)}) while((s32[]{:T(128)}, bf16[4,512,1,128]{3,1,2,0:T(8,128)(2,1)S(1)}, bf16[4,512,1,128]{3,1,2,0:T(8,128)(2,1)S(1)}, ...), condition=%wide.region_3.4_spmd, body=%wide.region_0.3_spmd.sunk | while | flops 546307072 | bytes 16132201 | solution.py:90
  256.2 6.4 %all-to-all-done.3 = bf16[2,2048,128]{2,0,1:T(2,128)(2,1)S(1)} async-done(((bf16[2,2048,128]{2,0,1:T(2,128)(2,1)}), bf16[2,2048,128]{2,0,1:T(2,128)(2,1)S(1)}, u32[]{:S(2)}, u32[]{:S(2)}) %all-to-all-start.3) | async-done | bytes 1048608 | tf_op jit(solution)/shard_map/all_to_all | solution.py:173
  263.7 5.8 %all-to-all-start.2 = ((bf16[16,128,128]{1,2,0:T(8,128)(2,1)}), bf16[16,128,128]{1,2,0:T(8,128)(2,1)S(1)}, u32[]{:S(2)}, u32[]{:S(2)}) async-start(bf16[16,128,128]{1,2,0:T(8,128)(2,1)} %copy.117), calls=%async_computation.2 | async-start | bytes 1048576 | tf_op jit(solution)/shard_map/all_to_all | solution.py:210
  273.3 32.5 %all-to-all-done.2 = bf16[16,128,128]{1,2,0:T(8,128)(2,1)S(1)} async-done(((bf16[16,128,128]{1,2,0:T(8,128)(2,1)}), bf16[16,128,128]{1,2,0:T(8,128)(2,1)S(1)}, u32[]{:S(2)}, u32[]{:S(2)}) %all-to-all-start.2) | async-done | bytes 524320 | tf_op jit(solution)/shard_map/all_to_all | solution.py:210
  305.8 2.9 fusion.75
  308.7 4.4 all-to-all-start.4
  313.2 14.1 %all-to-all-done.4 = bf16[128,16,128]{0,2,1:T(8,128)(2,1)S(1)} async-done(((bf16[128,16,128]{0,2,1:T(8,128)(2,1)}), bf16[128,16,128]{0,2,1:T(8,128)(2,1)S(1)}, u32[]{:S(2)}, u32[]{:S(2)}) %all-to-all-start.4) | async-done | bytes 524320 | tf_op jit(solution)/shard_map/all_to_all | solution.py:214
  328.3 57.0 %while.48 = (s32[]{:T(128)}, f32[2048,1,128]{0,2,1:T(8,128)}, f32[2048,1,128]{0,2,1:T(8,128)}, bf16[4,512,1,128]{3,1,2,0:T(8,128)(2,1)S(1)}, bf16[4,512,1,128]{3...) while((s32[]{:T(128)}, f32[2048,1,128]{0,2,1:T(8,128)}, ...), condition=%wide.region_16.17_spmd.clone, body=%wide.region_12.16_spmd.clone.sunk | while | flops 1364523520 | bytes 86269192 | solution.py:130
  331.9 3.6 fusion.140
  335.6 2.4 multiply_reduce_fusion.14
  345.3 3.6 fusion.140
  349.0 2.4 multiply_reduce_fusion.14
  352.8 2.7 fusion.139
  359.8 3.6 fusion.140
  363.5 2.4 multiply_reduce_fusion.14
  367.3 2.7 fusion.139
  374.4 3.6 fusion.140
  378.1 2.4 multiply_reduce_fusion.14
  381.9 2.7 fusion.139
  392.7 4.4 all-to-all-start.5
  399.6 30.0 %all-to-all-done.5 = bf16[16,128,3,128]{1,3,2,0:T(8,128)(2,1)S(1)} async-done(((bf16[16,128,3,128]{1,3,2,0:T(8,128)(2,1)}), bf16[16,128,3,128]{1,3,2,0:T(8,128)(2,1)S(1)}, u32[]{:S(2)}, u32[]{:S(2)}) %all-to-all-start.5) | async-done | bytes 1572896 | tf_op jit(solution)/shard_map/all_to_all | solution.py:63
  429.6 8.2 %all-to-all-start.7 = ((bf16[128,2,16,96]{0,3,1,2:T(8,128)(2,1)}), bf16[128,2,16,96]{0,3,1,2:T(8,128)(2,1)S(1)}, u32[]{:S(2)}, u32[]{:S(2)}) async-start(bf16[128,2,16,96]{0,3,1,2:T(8,128)(2,1)} %copy.142), calls=%async_computation.7 | async-start | bytes 1572864 | tf_op jit(solution)/shard_map/all_to_all | solution.py:159
  439.8 17.1 %all-to-all-done.7 = bf16[128,2,16,96]{0,3,1,2:T(8,128)(2,1)S(1)} async-done(((bf16[128,2,16,96]{0,3,1,2:T(8,128)(2,1)}), bf16[128,2,16,96]{0,3,1,2:T(8,128)(2,1)S(1)}, u32[]{:S(2)}, u32[]{:S(2)}) %all-to-all-start.7) | async-done | bytes 786464 | tf_op jit(solution)/shard_map/all_to_all | solution.py:159
  458.5 5.3 %all-to-all-start.6 = ((bf16[16,3,128,128]{3,2,1,0:T(8,128)(2,1)}), bf16[16,3,128,128]{3,2,1,0:T(8,128)(2,1)}, u32[]{:S(2)}, u32[]{:S(2)}) async-start(bf16[16,3,128,128]{3,2,1,0:T(8,128)(2,1)} %broadcast_in_dim.45), calls=%async_computation.6 | async-start | bytes 3145728 | tf_op jit(solution)/shard_map/all_to_all | solution.py:46
  465.2 2.2 reshape.308
  469.9 26.7 %all-to-all-done.6 = bf16[16,3,128,128]{3,2,1,0:T(8,128)(2,1)} async-done(((bf16[16,3,128,128]{3,2,1,0:T(8,128)(2,1)}), bf16[16,3,128,128]{3,2,1,0:T(8,128)(2,1)}, u32[]{:S(2)}, u32[]{:S(2)}) %all-to-all-start.6) | async-done | bytes 1572896 | tf_op jit(solution)/shard_map/all_to_all | solution.py:46
  496.6 5.3 %all-to-all-start.9 = ((bf16[16,3,8,128]{3,2,1,0:T(8,128)(2,1)}), bf16[16,3,8,128]{3,2,1,0:T(8,128)(2,1)S(1)}, u32[]{:S(2)}, u32[]{:S(2)}) async-start(bf16[16,3,8,128]{3,2,1,0:T(8,128)(2,1)} %bitcast.270), calls=%async_computation.9 | async-start | bytes 196608 | tf_op jit(solution)/shard_map/all_to_all | solution.py:63
  505.9 4.3 all-to-all-done.9
  510.2 5.4 %all-to-all-start.8 = ((bf16[16,3,12,128]{3,2,1,0:T(8,128)(2,1)}), bf16[16,3,12,128]{3,2,1,0:T(8,128)(2,1)S(1)}, u32[]{:S(2)}, u32[]{:S(2)}) async-start(bf16[16,3,12,128]{3,2,1,0:T(8,128)(2,1)} %copy.144), calls=%async_computation.8 | async-start | bytes 393216 | tf_op jit(solution)/shard_map/all_to_all | solution.py:63
  517.2 7.5 %all-to-all-done.8 = bf16[16,3,12,128]{3,2,1,0:T(8,128)(2,1)S(1)} async-done(((bf16[16,3,12,128]{3,2,1,0:T(8,128)(2,1)}), bf16[16,3,12,128]{3,2,1,0:T(8,128)(2,1)S(1)}, u32[]{:S(2)}, u32[]{:S(2)}) %all-to-all-start.8) | async-done | bytes 147488 | tf_op jit(solution)/shard_map/all_to_all | solution.py:63
  (180 shorter events, 106.6 us)
Async XLA Ops:
  0.6 4.1 copy-start
  8.2 42.5 %all-to-all-start.1 = ((bf16[16,3,128,128]{2,3,1,0:T(8,128)(2,1)}), bf16[16,3,128,128]{2,3,1,0:T(8,128)(2,1)S(1)}, u32[]{:S(2)}, u32[]{:S(2)}) async-start(bf16[16,3,128,128]{2,3,1,0:T(8,128)(2,1)} %broadcast_in_dim.30), calls=%async_computation.1 | async-start | bytes 3145728 | tf_op jit(solution)/shard_map/all_to_all | solution.py:46
  50.7 8.4 %copy-start.4 = (bf16[16,3,128,128]{2,3,1,0:T(8,128)(2,1)}, bf16[16,3,128,128]{2,3,1,0:T(8,128)(2,1)S(1)}, u32[]{:S(2)}) copy-start(bf16[16,3,128,128]{2,3,1,0:T(8,128)(2,1)S(1)} %all-to-all-done.1) | copy-start | bytes 4718596
  50.7 87.2 %all-to-all-start = ((bf16[6,128,2048]{1,0,2:T(8,128)(2,1)}), bf16[6,128,2048]{1,0,2:T(8,128)(2,1)}, u32[]{:S(2)}, u32[]{:S(2)}) async-start(bf16[6,128,2048]{1,0,2:T(8,128)(2,1)} %pad_maximum_fusion), calls=%async_computation | async-start | bytes 8388608 | tf_op jit(solution)/shard_map/all_to_all | solution.py:16
  141.9 97.9 %collective-permute-start.2 = (bf16[2048,128]{1,0:T(8,128)(2,1)}, bf16[2048,128]{1,0:T(8,128)(2,1)}, u32[]{:S(2)}, u32[]{:S(2)}) collective-permute-start(bf16[2048,128]{1,0:T(8,128)(2,1)} %bitcast.353), channel_id=1, source_target_pairs={{0,128},{1,129},{2,130},{3,131},{4,132},{5,133},{6,134},{7,135},{8... | collective-permute-start | bytes 1572872 | tf_op jit(solution)/shard_map/ppermute | solution.py:35
  150.3 93.0 %collective-permute-start.1 = (bf16[2048,128]{1,0:T(8,128)(2,1)}, bf16[2048,128]{1,0:T(8,128)(2,1)}, u32[]{:S(2)}, u32[]{:S(2)}) collective-permute-start(bf16[2048,128]{1,0:T(8,128)(2,1)} %bitcast.40), channel_id=1, source_target_pairs={{0,128},{1,129},{2,130},{3,131},{4,132},{5,133},{6,134},{7,135},{8... | collective-permute-start | bytes 1572872 | tf_op jit(solution)/shard_map/ppermute | solution.py:35
  153.7 88.3 %collective-permute-start = (bf16[2048,128]{1,0:T(8,128)(2,1)}, bf16[2048,128]{1,0:T(8,128)(2,1)}, u32[]{:S(2)}, u32[]{:S(2)}) collective-permute-start(bf16[2048,128]{1,0:T(8,128)(2,1)} %bitcast.28), channel_id=1, source_target_pairs={{0,128},{1,129},{2,130},{3,131},{4,132},{5,133},{6,134},{7,135},{8... | collective-permute-start | bytes 1572872 | tf_op jit(solution)/shard_map/ppermute | solution.py:35
  156.2 10.8 %copy-start.14 = (bf16[1,16,128,128]{3,2,1,0:T(8,128)(2,1)S(1)}, bf16[1,16,128,128]{3,2,1,0:T(8,128)(2,1)}, u32[]{:S(2)}) copy-start(bf16[1,16,128,128]{3,2,1,0:T(8,128)(2,1)} %copy.115) | copy-start | bytes 1572868
  182.8 57.0 %copy-start.8 = (bf16[2048,1,128]{2,0,1:T(8,128)(2,1)S(1)}, bf16[2048,1,128]{2,0,1:T(8,128)(2,1)}, u32[]{:S(2)}) copy-start(bf16[2048,1,128]{2,0,1:T(8,128)(2,1)} %copy-done.7) | copy-start | bytes 1572868
  182.9 60.3 %copy-start.9 = (bf16[1,16,128,128]{3,2,1,0:T(8,128)(2,1)S(1)}, bf16[1,16,128,128]{3,2,1,0:T(8,128)(2,1)}, u32[]{:S(2)}) copy-start(bf16[1,16,128,128]{3,2,1,0:T(8,128)(2,1)} %get-tuple-element.329) | copy-start | bytes 1572868
  192.4 70.3 %all-to-all-start.3 = ((bf16[2,2048,128]{2,0,1:T(2,128)(2,1)}), bf16[2,2048,128]{2,0,1:T(2,128)(2,1)S(1)}, u32[]{:S(2)}, u32[]{:S(2)}) async-start(bf16[2,2048,128]{2,0,1:T(2,128)(2,1)} %copy.129), calls=%async_computation.3 | async-start | bytes 2097152 | tf_op jit(solution)/shard_map/all_to_all | solution.py:173
  244.5 1.6 copy-start.15
  247.1 1.6 copy-start.15
  249.8 1.6 copy-start.15
  252.5 1.6 copy-start.15
  262.7 1.0 copy-start.6
  263.7 42.1 %all-to-all-start.2 = ((bf16[16,128,128]{1,2,0:T(8,128)(2,1)}), bf16[16,128,128]{1,2,0:T(8,128)(2,1)S(1)}, u32[]{:S(2)}, u32[]{:S(2)}) async-start(bf16[16,128,128]{1,2,0:T(8,128)(2,1)} %copy.117), calls=%async_computation.2 | async-start | bytes 1048576 | tf_op jit(solution)/shard_map/all_to_all | solution.py:210
  273.2 32.6 %collective-permute-start.3 = (bf16[128,2048]{0,1:T(8,128)(2,1)S(1)}, bf16[128,2048]{0,1:T(8,128)(2,1)S(1)}, u32[]{:S(2)}, u32[]{:S(2)}) collective-permute-start(bf16[128,2048]{0,1:T(8,128)(2,1)S(1)} %dynamic-slice_bitcast_fusion), channel_id=1, source_target_pairs={{0,128},{128,0},{1,129},{129,1},{2,130},{130,2},{3,131},{131,3},{4... | collective-permute-start | bytes 1572872 | tf_op jit(solution)/shard_map/ppermute | solution.py:29
  308.7 18.5 %all-to-all-start.4 = ((bf16[128,16,128]{0,2,1:T(8,128)(2,1)}), bf16[128,16,128]{0,2,1:T(8,128)(2,1)S(1)}, u32[]{:S(2)}, u32[]{:S(2)}) async-start(bf16[128,16,128]{0,2,1:T(8,128)(2,1)} %bitcast.71), calls=%async_computation.4 | async-start | bytes 1048576 | tf_op jit(solution)/shard_map/all_to_all | solution.py:214
  328.3 3.6 copy-start.10
  329.1 2.0 copy-start.2
  331.9 3.7 copy-start.3
  331.9 3.7 copy-start.16
  335.6 2.4 copy-start.11
  341.7 3.6 copy-start.10
  342.5 2.0 copy-start.2
  345.3 3.7 copy-start.3
  345.3 3.7 copy-start.16
  348.9 2.4 copy-start.11
  356.2 3.6 copy-start.10
  357.0 2.0 copy-start.2
  359.8 3.7 copy-start.3
  359.8 3.7 copy-start.16
  363.5 2.4 copy-start.11
  370.8 3.6 copy-start.10
  371.6 2.0 copy-start.2
  374.4 3.7 copy-start.3
  374.4 3.7 copy-start.16
  378.1 2.4 copy-start.11
  389.2 3.5 copy-start.12
  392.7 45.4 %copy-start.18 = (f32[128]{0:T(128)S(1)}, f32[128]{0:T(128)}, u32[]{:S(2)}) copy-start(f32[128]{0:T(128)} %copy-done.17) | copy-start | bytes 1540
  392.7 36.9 %all-to-all-start.5 = ((bf16[16,128,3,128]{1,3,2,0:T(8,128)(2,1)}), bf16[16,128,3,128]{1,3,2,0:T(8,128)(2,1)S(1)}, u32[]{:S(2)}, u32[]{:S(2)}) async-start(bf16[16,128,3,128]{1,3,2,0:T(8,128)(2,1)} %bitcast.323), calls=%async_computation.5 | async-start | bytes 3145728 | tf_op jit(solution)/shard_map/all_to_all | solution.py:63
  429.6 27.4 %all-to-all-start.7 = ((bf16[128,2,16,96]{0,3,1,2:T(8,128)(2,1)}), bf16[128,2,16,96]{0,3,1,2:T(8,128)(2,1)S(1)}, u32[]{:S(2)}, u32[]{:S(2)}) async-start(bf16[128,2,16,96]{0,3,1,2:T(8,128)(2,1)} %copy.142), calls=%async_computation.7 | async-start | bytes 1572864 | tf_op jit(solution)/shard_map/all_to_all | solution.py:159
  438.1 29.3 %copy-start.5 = (bf16[16,3,128,128]{2,3,1,0:T(8,128)(2,1)S(1)}, bf16[16,3,128,128]{2,3,1,0:T(8,128)(2,1)}, u32[]{:S(2)}) copy-start(bf16[16,3,128,128]{2,3,1,0:T(8,128)(2,1)} %copy-done.4) | copy-start | bytes 4718596
  458.5 38.1 %all-to-all-start.6 = ((bf16[16,3,128,128]{3,2,1,0:T(8,128)(2,1)}), bf16[16,3,128,128]{3,2,1,0:T(8,128)(2,1)}, u32[]{:S(2)}, u32[]{:S(2)}) async-start(bf16[16,3,128,128]{3,2,1,0:T(8,128)(2,1)} %broadcast_in_dim.45), calls=%async_computation.6 | async-start | bytes 3145728 | tf_op jit(solution)/shard_map/all_to_all | solution.py:46
  469.2 56.1 %copy-start.1 = (bf16[3,3072,128]{2,1,0:T(8,128)(2,1)S(1)}, bf16[3,3072,128]{2,1,0:T(8,128)(2,1)}, u32[]{:S(2)}) copy-start(bf16[3,3072,128]{2,1,0:T(8,128)(2,1)} %param.20) | copy-start | bytes 7077892
  496.6 13.6 %all-to-all-start.9 = ((bf16[16,3,8,128]{3,2,1,0:T(8,128)(2,1)}), bf16[16,3,8,128]{3,2,1,0:T(8,128)(2,1)S(1)}, u32[]{:S(2)}, u32[]{:S(2)}) async-start(bf16[16,3,8,128]{3,2,1,0:T(8,128)(2,1)} %bitcast.270), calls=%async_computation.9 | async-start | bytes 196608 | tf_op jit(solution)/shard_map/all_to_all | solution.py:63
  510.2 14.5 %all-to-all-start.8 = ((bf16[16,3,12,128]{3,2,1,0:T(8,128)(2,1)}), bf16[16,3,12,128]{3,2,1,0:T(8,128)(2,1)S(1)}, u32[]{:S(2)}, u32[]{:S(2)}) async-start(bf16[16,3,12,128]{3,2,1,0:T(8,128)(2,1)} %copy.144), calls=%async_computation.8 | async-start | bytes 393216 | tf_op jit(solution)/shard_map/all_to_all | solution.py:63
  (3 other events, 2.1 us)
where the time goes:
time: 534 us; the launch traced here: 525 us
  waiting for transfers between devices  231 us (43%)
  starting transfers between devices  115 us (22%)
  matrix products  78.2 us (15%)
  local copies, waits for them, and re-layouts  65.9 us (12%)
  other arithmetic  32.3 us (6%)
    all_to_all x1, waiting for transfers between devices, side_by_side(): lax.all_to_all(both, axis, split_axis=split_dim, concat_axis=concat_dim,...  74.6 us
    all_to_all x1, starting transfers between devices, body(): lax.all_to_all(teacher_local.astype(jnp.bfloat16), 'seq', split_axis=1, c...  47.4 us
    all_to_all x2, waiting for transfers between devices, from_everyone(): lax.all_to_all(jnp.broadcast_to(array[None], (peers, *array.shape)), axis...  44.7 us
    all_to_all x3, waiting for transfers between devices, sent_and_summed(): lax.all_to_all(parts, axis, split_axis=0, concat_axis=0, tiled=True)  41.8 us
    all_to_all x1, waiting for transfers between devices, body(): lax.all_to_all(student_local, 'seq', split_axis=0, concat_axis=1, tiled=T...  32.5 us
    all_to_all x1, waiting for transfers between devices, body(): lax.all_to_all(split_view, 'seq', split_axis=2, concat_axis=0, tiled=True)  17.1 us
    dot_general x16, matrix products, head_probs(): jnp.einsum('qhd,khd->hqk', query_block, key_heads, preferred_element_type...  17.1 us
    all_to_all x3, starting transfers between devices, sent_and_summed(): lax.all_to_all(parts, axis, split_axis=0, concat_axis=0, tiled=True)  15.1 us
  transfers between devices with their start and end apart: 14, of which 10 were waited for; matrix products, arithmetic and copies ran while one was open for 18% of the time, Pallas kernels for 0%

commit v1 on v0

v1 whole, which is shorter than its diff:
```python
import functools
import math

import jax
import jax.numpy as jnp
from jax import lax
from jax.experimental import pallas as pl
from jax.experimental.pallas import tpu as pltpu
from jax.sharding import Mesh
from jax.sharding import PartitionSpec as P

HDIM = 128
RANK = 128
TSTEPS = 1000
FACTOR = HDIM ** (-0.5)
LOG2E = math.log2(math.e)
SCALE2 = FACTOR * LOG2E
BF = jnp.bfloat16
F32 = jnp.float32
NT = (((1,), (1,)), ((), ()))
TN = (((0,), (0,)), ((), ()))
MIB = 1 << 20


def dot(a, b, dims=(((1,), (0,)), ((), ()))):
    return lax.dot_general(a, b, dims, preferred_element_type=F32)


def exchange(value, axes):
    return lax.all_to_all(value, axes, split_axis=0, concat_axis=0, tiled=True)


def copies_from_all(value, axis):
    peers = lax.axis_size(axis)
    return exchange(jnp.broadcast_to(value[None], (peers, *value.shape)), axis)


def summed_blocks(value, axes):
    return exchange(value, axes).astype(F32).sum(axis=0)


def pack_kernel(q_ref, k_ref, v_ref, out_ref):
    heads = out_ref.shape[0]
    for part, ref in enumerate((q_ref, k_ref, v_ref)):
        for head in range(heads):
            out_ref[head, part] = ref[0, :, head * HDIM : (head + 1) * HDIM]


def packed_by_head(q, k, v):
    halves, rows, columns = q.shape
    heads = columns // HDIM
    spec = pl.BlockSpec((1, rows, columns), lambda i: (i, 0, 0))
    return pl.pallas_call(
        pack_kernel,
        grid=(halves,),
        in_specs=[spec] * 3,
        out_specs=pl.BlockSpec((heads, 3, rows, HDIM), lambda i: (i, 0, 0, 0)),
        out_shape=jax.ShapeDtypeStruct((halves * heads, 3, rows, HDIM), q.dtype),
        cost_estimate=pl.CostEstimate(flops=0, transcendentals=0, bytes_accessed=12 * q.size),
        name="pack_heads",
    )(q, k, v)


def softmax_rows(query, key):
    scores = dot(query, key, NT)
    highest = jnp.max(scores, axis=-1, keepdims=True)
    raised = jnp.exp2((scores - highest) * SCALE2)
    total = jnp.sum(raised, axis=-1, keepdims=True)
    return raised.astype(BF), highest, total


def forward_kernel(
    scale_ref, heads_ref, low_ref, up_ref, inv_ref, out_ref, upstream_ref, student_ref, stats_ref, keys_ref
):
    pass_tok, rows = heads_ref.shape[1], heads_ref.shape[3]
    tokens = pass_tok * rows
    n_slow, n_fast = low_ref.shape[1], low_ref.shape[0]
    scale = scale_ref[0]
    inverse = inv_ref[0]

    for part in range(3):
        up = up_ref[part]
        for block in range(pass_tok):
            slow, fast = block // n_fast, block % n_fast
            adapted = dot(low_ref[fast, slow, :, part * RANK : (part + 1) * RANK], up)
            frozen = heads_ref[0, block, part].astype(F32)
            student_ref[part, block * rows : (block + 1) * rows] = (frozen + adapted).astype(BF)
            for one in range(2):
                keys_ref[one, part, block * rows : (block + 1) * rows] = heads_ref[one, block, part]

    step_rows = 256

    def one_block(step, carry):
        here = pl.ds(pl.multiple_of(step * step_rows, step_rows), step_rows)
        outs = []
        for one in range(2):
            raised, _, total = softmax_rows(keys_ref[one, 0, here], keys_ref[one, 1])
            attended = dot(raised, keys_ref[one, 2]) / total
            outs.append(attended.astype(BF).astype(F32))
        raised, highest, total = softmax_rows(student_ref[0, here], student_ref[1])
        attended = dot(raised, student_ref[2]) / total
        rounded = attended.astype(BF)
        out_ref[here] = rounded
        target = outs[1] + scale * (outs[0] - outs[1])
        upstream = ((rounded.astype(F32) - target) * inverse).astype(BF)
        upstream_ref[here] = upstream
        level = highest * SCALE2 + jnp.log2(total)
        center = jnp.sum(attended * upstream.astype(F32), axis=-1, keepdims=True)
        stats_ref[0:1, here] = jnp.transpose(jnp.broadcast_to(level, (step_rows, HDIM)))[0:1]
        stats_ref[1:2, here] = jnp.transpose(jnp.broadcast_to(center, (step_rows, HDIM)))[0:1]
        return carry

    stats_ref[...] = jnp.zeros_like(stats_ref)
    lax.fori_loop(0, tokens // step_rows, one_block, 0)


def forward(scale, heads, low, up, inverse):
    tokens = heads.shape[1] * heads.shape[3]
    vmem = pl.BlockSpec(memory_space=pltpu.VMEM)
    smem = pl.BlockSpec(memory_space=pltpu.SMEM)
    return pl.pallas_call(
        forward_kernel,
        in_specs=[smem, vmem, vmem, vmem, smem],
        out_specs=[vmem] * 4,
        out_shape=[
            jax.ShapeDtypeStruct((tokens, HDIM), BF),
            jax.ShapeDtypeStruct((tokens, HDIM), BF),
            jax.ShapeDtypeStruct((3, tokens, HDIM), BF),
            jax.ShapeDtypeStruct((8, tokens), F32),
        ],
        scratch_shapes=[pltpu.VMEM((2, 3, tokens, HDIM), BF)],
        cost_estimate=pl.CostEstimate(
            flops=12 * tokens * tokens * HDIM,
            transcendentals=3 * tokens * tokens,
            bytes_accessed=8 * MIB,
        ),
        compiler_params=pltpu.CompilerParams(vmem_limit_bytes=56 * MIB),
        name="attention_forward",
    )(scale, heads, low, up, inverse)


def backward_kernel(
    student_ref, upstream_ref, stats_ref, low_ref, up_ref, back_ref, grad_up_ref, dq_ref, dk_ref, dv_ref
):
    tokens = student_ref.shape[1]
    n_fast, n_slow, rows, _ = low_ref.shape
    step_rows = 256
    dk_ref[...] = jnp.zeros_like(dk_ref)
    dv_ref[...] = jnp.zeros_like(dv_ref)

    def one_block(step, carry):
        here = pl.ds(pl.multiple_of(step * step_rows, step_rows), step_rows)
        query = student_ref[0, here]
        upstream = upstream_ref[here]
        key = student_ref[1]
        level = stats_ref[0:1, here]
        center = stats_ref[1:2, here]
        prob = jnp.exp2(dot(key, query, NT) * SCALE2 - level)
        dv_ref[...] += dot(prob.astype(BF), upstream)
        dprob = dot(student_ref[2], upstream, NT)
        dscore = (prob * (dprob - center)).astype(BF)
        dk_ref[...] += dot(dscore, query)
        dq_ref[here] = dot(dscore, key, TN)
        return carry

    lax.fori_loop(0, tokens // step_rows, one_block, 0)
    for part, (ref, factor) in enumerate(((dq_ref, FACTOR), (dk_ref, FACTOR), (dv_ref, 1.0))):
        up = up_ref[part]
        total = jnp.zeros((RANK, HDIM), F32)
        for slow in range(n_slow):
            for fast in range(n_fast):
                first = (slow * n_fast + fast) * rows
                grad = (ref[first : first + rows] * factor).astype(BF)
                columns = slice(part * RANK, (part + 1) * RANK)
                back_ref[fast, slow, :, columns] = dot(grad, up, NT).astype(BF)
                total += dot(low_ref[fast, slow, :, columns], grad, TN)
        grad_up_ref[part] = total.astype(BF)


def backward(student, upstream, stats, low, up):
    tokens = student.shape[1]
    vmem = pl.BlockSpec(memory_space=pltpu.VMEM)
    return pl.pallas_call(
        backward_kernel,
        in_specs=[vmem] * 5,
        out_specs=[vmem] * 2,
        out_shape=[
            jax.ShapeDtypeStruct(low.shape, BF),
            jax.ShapeDtypeStruct((3, RANK, HDIM), BF),
        ],
        scratch_shapes=[pltpu.VMEM((tokens, HDIM), F32)] * 3,
        cost_estimate=pl.CostEstimate(
            flops=10 * tokens * tokens * HDIM,
            transcendentals=tokens * tokens,
            bytes_accessed=6 * MIB,
        ),
        compiler_params=pltpu.CompilerParams(vmem_limit_bytes=56 * MIB),
        name="attention_backward",
    )(student, upstream, stats, low, up)


def body(
    teacher_query,
    teacher_key,
    teacher_value,
    hidden,
    adapter_down_weight,
    adapter_up_weight,
    guidance_index,
    timestep_index,
):
    n_cfg, n_slow, n_fast = (lax.axis_size(a) for a in ("cfg", "z", "y"))
    n_x, n_core = (lax.axis_size(a) for a in ("x", "core"))
    cfg_index = lax.axis_index("cfg")
    seq_index = lax.axis_index(("z", "y"))
    features = hidden[0, 0]
    rows, width = features.shape
    tokens = rows * n_slow * n_fast
    total_rows = n_cfg * n_x * n_core * tokens

    packed = packed_by_head(teacher_query[0, :, 0], teacher_key[0, :, 0], teacher_value[0, :, 0])
    heads = exchange(packed, ("cfg", "z", "y"))
    heads = heads.reshape(n_cfg, n_slow * n_fast, 3, rows, HDIM)

    scale = 1.0 + 0.5 * lax.dynamic_slice(guidance_index[:, 0], (cfg_index,), (1,)).astype(F32)
    time = (lax.dynamic_slice(timestep_index[:, 0], (cfg_index,), (1,)).astype(F32) + 0.5) / TSTEPS
    rank_index = jnp.arange(1, RANK + 1).astype(F32)
    modulation = 1.0 + 0.5 * jnp.cos(math.pi * rank_index * time + 0.25 * rank_index * scale)

    low = jnp.einsum("cl,elj->cej", features, adapter_down_weight, preferred_element_type=F32)
    low = (low * modulation).astype(BF).reshape(rows, 3 * RANK)
    low_all = copies_from_all(copies_from_all(low, "z"), "y")

    groups = n_cfg * n_slow
    part_cols = width // (groups * n_fast)
    spread = jnp.moveaxis(features.reshape(rows, groups, n_fast, part_cols), 2, 0)
    columns = exchange(spread.reshape(n_fast, rows, groups * part_cols), "y")
    columns = columns.reshape(n_fast * rows, groups * part_cols)

    up = lax.dynamic_slice_in_dim(adapter_up_weight, seq_index * HDIM, HDIM, 2)
    inverse = jnp.full((1,), 1.0 / math.sqrt(total_rows), F32)
    out, upstream, student, stats = forward(scale, heads, low_all, up, inverse)
    tokens_out = exchange(out.reshape(n_slow * n_fast, rows, HDIM), ("z", "y"))
    student_out = jnp.moveaxis(tokens_out, 0, 1).reshape(rows, -1)

    back, up_partial = backward(student, upstream, stats, low_all, up)
    back = summed_blocks(back, "y").astype(BF)
    back = summed_blocks(back, "z")
    low_grad = (back.reshape(rows, 3, RANK) * modulation).astype(BF).reshape(rows, 3 * RANK)
    low_grads = copies_from_all(low_grad, "y").reshape(n_fast * rows, 3 * RANK)
    down = dot(columns, low_grads, TN).astype(BF)
    peers = groups * n_x * n_core
    down = summed_blocks(down.reshape(peers, -1, 3 * RANK), ("cfg", "z", "x", "core"))
    grad_down = jnp.moveaxis(down.reshape(-1, 3, RANK), 1, 0)

    owners = n_cfg * n_x * n_core
    up_blocks = jnp.moveaxis(up_partial.reshape(3, owners, RANK // owners, HDIM), 1, 0)
    grad_up = summed_blocks(up_blocks, ("cfg", "x", "core"))
    return student_out[None, None], grad_down, grad_up


def solution(mesh):
    sizes = {"cfg": 2, "z": 4, "y": 4, "x": 4, "core": 2}
    mesh = Mesh(mesh.devices.reshape(tuple(sizes.values())), tuple(sizes))
    seq, dp = ("z", "y"), ("x", "core")
    teacher = P("cfg", None, dp, seq, None)
    return jax.shard_map(
        body,
        mesh=mesh,
        in_specs=(
            teacher,
            teacher,
            teacher,
            P("cfg", dp, seq, None),
            P(),
            P(),
            P(None, dp),
            P(None, dp),
        ),
        out_specs=(
            P("cfg", dp, seq, None),
            P(None, ("cfg", *seq, *dp), None),
            P(None, ("cfg", *dp), seq),
        ),
        check_vma=False,
    )
```

time: 534 us -> 300 us (0.56); the launches traced: 525 us -> 299 us
  waiting for transfers between devices: 231 us -> 143 us
  starting transfers between devices: 115 us -> 33.1 us
  matrix products: 78.2 us -> 3.9 us
  blocking collectives: 0 us -> 51.3 us
  local copies, waits for them, and re-layouts: 65.9 us -> 14.7 us
  Pallas kernels: 0 us -> 47.6 us
  other arithmetic: 32.3 us -> 2.65 us
    all_to_all x10 -> x7, waiting for transfers between devices: 231 us -> 143 us  [exchange(): return lax.all_to_all(value, axes, split_axis=0, concat_axis=0, tiled=True)]
    dot_general x51 -> x1, matrix products: 78.2 us -> 1.46 us  [dot(): return lax.dot_general(a, b, dims, preferred_element_type=F32)]
    all_to_all x10 -> x7, starting transfers between devices: 103 us -> 33.1 us  [exchange(): return lax.all_to_all(value, axes, split_axis=0, concat_axis=0, tiled=True)]
    all_to_all x0 -> x3, blocking collectives: none -> 51.3 us  [exchange(): return lax.all_to_all(value, axes, split_axis=0, concat_axis=0, tiled=True)]
    pallas_call x0 -> x3, Pallas kernels: none -> 47.6 us  [the longest x1 26.2 us: forward(): pl.pallas_call(forward_kernel, in_specs=[smem, vmem, vmem, vmem, smem], o...]
    reduce_sum x19 -> x4, other arithmetic: 14.7 us -> 1.92 us  [summed_blocks(): return exchange(value, axes).astype(F32).sum(axis=0)]
    ppermute x4 -> x0, starting transfers between devices: 11.4 us -> none  [the longest x3 11.3 us: passed_along(): lax.ppermute(value, axis, [(source, source + steps) for source in range(l...]
    while x50 -> x0, local copies, waits for them, and re-layouts: 10.9 us -> none
  transfers between devices with their start and end apart: 14 -> 7, of which waited for: 10 -> 7; matrix products, arithmetic and copies ran while one was open for 18% -> 3% of each run, Pallas kernels for 0% -> 1%
where the time goes in v1:
time: 300 us; the launch traced here: 299 us
  waiting for transfers between devices  143 us (48%)
  blocking collectives  51.3 us (17%)
  Pallas kernels  47.6 us (16%)
  starting transfers between devices  33.1 us (11%)
  local copies, waits for them, and re-layouts  14.7 us (5%)
  matrix products  3.9 us (1%)
    all_to_all x7, waiting for transfers between devices, exchange(): return lax.all_to_all(value, axes, split_axis=0, concat_axis=0, tiled=True)  143 us
    all_to_all x3, blocking collectives, exchange(): return lax.all_to_all(value, axes, split_axis=0, concat_axis=0, tiled=True)  51.3 us
    all_to_all x7, starting transfers between devices, exchange(): return lax.all_to_all(value, axes, split_axis=0, concat_axis=0, tiled=True)  33.1 us
    pallas_call x1, Pallas kernels, forward(): pl.pallas_call(forward_kernel, in_specs=[smem, vmem, vmem, vmem, smem], o...  26.2 us
    pallas_call x1, Pallas kernels, backward(): pl.pallas_call(backward_kernel, in_specs=[vmem] * 5, out_specs=[vmem] * 2...  18.1 us
    unnamed x19, local copies, waits for them, and re-layouts  7.72 us
  transfers between devices with their start and end apart: 7, of which 7 were waited for; matrix products, arithmetic and copies ran while one was open for 3% of the time, Pallas kernels for 1%

profile of v1, /device:TPU:6, one launch (start us, length us, event | category | flops | bytes accessed | tf_op | source)
XLA Modules:
  0.0 298.7 jit_solution(8428419586806397707)
XLA Ops:
  0.6 0.0 copy-start
  0.7 0.0 copy-start.6
  0.7 0.0 copy-start.1
  0.7 4.4 %copy.32 = bf16[3,3072,128]{1,2,0:T(8,128)(2,1)} copy(bf16[3,3072,128]{2,1,0:T(8,128)(2,1)} %param.12) | data formatting | bytes 4718592 | tf_op args[4]
  5.1 0.6 fusion.6
  7.0 0.0 copy-done.1
  7.1 2.4 fusion.2
  9.5 0.1 multiply_convert_fusion.1
  9.6 0.1 copy.33
  9.8 17.4 %all_to_all.50 = bf16[4,128,384]{2,1,0:T(8,128)(2,1)S(1)} all-to-all(bf16[4,128,384]{2,1,0:T(8,128)(2,1)S(1)} %broadcast_in_dim.9), channel_id=1, replica_groups=mesh['cfg'=2,'z'=4,'y'=4,'x'=4,'core'=2] {'z'}, dimensions={0} | all-to-all | bytes 786432 | tf_op jit(solution)/shard_map/all_to_all | solution.py:30
  27.1 1.4 broadcast_in_dim.10
  28.5 4.5 %all-to-all-start.2 = ((bf16[4,4,128,384]{3,2,1,0:T(8,128)(2,1)}), bf16[4,4,128,384]{3,2,1,0:T(8,128)(2,1)S(1)}, u32[]{:S(2)}, u32[]{:S(2)}) async-start(bf16[4,4,128,384]{3,2,1,0:T(8,128)(2,1)} %broadcast_in_dim.10), calls=%async_computation.2 | async-start | bytes 3145728 | tf_op jit(solution)/shard_map/all_to_all | solution.py:30
  33.0 3.3 %pack_heads.1 = bf16[32,3,128,128]{3,2,1,0:T(8,128)(2,1)} custom-call(bf16[2,128,2048]{2,1,0:T(8,128)(2,1)} %bitcast.44, bf16[2,128,2048]{2,1,0:T(8,128)(2,1)} %bitcast.45, bf16[2,128,2048]{2,1,0:T(8,128)(2,1)} %bitcast.46), custom_call_target="tpu_custom_call" | custom-call | bytes 6291456 | tf_op jit(solution)/shard_map/pack_heads/pallas_call | solution.py:53
  36.3 16.3 %all-to-all-done.2.low_ref = bf16[4,4,128,384]{3,2,1,0:T(8,128)(2,1)S(1)} async-done(((bf16[4,4,128,384]{3,2,1,0:T(8,128)(2,1)}), bf16[4,4,128,384]{3,2,1,0:T(8,128)(2,1)S(1)}, u32[]{:S(2)}, u32[]{:S(2)}) %all-to-all-start.2) | async-done | bytes 1572896 | tf_op jit(solution)/shard_map/all_to_all | solution.py:30
  52.6 1.1 copy-done.2
  53.7 6.9 %all-to-all-start = ((bf16[32,3,128,128]{3,2,1,0:T(8,128)(2,1)}), bf16[32,3,128,128]{3,2,1,0:T(8,128)(2,1)}, u32[]{:S(2)}, u32[]{:S(2)}) async-start(bf16[32,3,128,128]{3,2,1,0:T(8,128)(2,1)} %pack_heads.1), calls=%async_computation | async-start | bytes 6291456 | tf_op jit(solution)/shard_map/all_to_all | solution.py:30
  60.6 0.7 constant_dynamic-slice_fusion.up_ref
  61.3 70.3 %all-to-all-done = bf16[32,3,128,128]{3,2,1,0:T(8,128)(2,1)} async-done(((bf16[32,3,128,128]{3,2,1,0:T(8,128)(2,1)}), bf16[32,3,128,128]{3,2,1,0:T(8,128)(2,1)}, u32[]{:S(2)}, u32[]{:S(2)}) %all-to-all-start) | async-done | bytes 3145760 | tf_op jit(solution)/shard_map/all_to_all | solution.py:30
  131.6 26.2 %attention_forward.1 = (bf16[2048,128]{1,0:T(8,128)(2,1)}, bf16[2048,128]{1,0:T(8,128)(2,1)}, bf16[3,2048,128]{2,1,0:T(8,128)(2,1)}, f32[8,2048]{1,0:T(8,128)}) custom-call(f32[1]{0:T(128)} %bitcast.scale_ref, bf16[2,16,3,128,128]{4,3,2,1,0:T(8,128)(2,1)} %bitcast.4.heads_ref, bf16[4,4,128,384]{3,2,1,0:T(8,128)(2,1)} %copy-done.2, ...), custom_call_target="tpu_custom_call" | custom-call | flops 6442450944 | bytes 8388608 | tf_op jit(solution)/shard_map/attention_forward/pallas_call | solution.py:121
  157.8 18.1 %attention_backward.1 = (bf16[4,4,128,384]{3,2,1,0:T(8,128)(2,1)}, bf16[3,128,128]{2,1,0:T(8,128)(2,1)}) custom-call(bf16[3,2048,128]{2,1,0:T(8,128)(2,1)} %get-tuple-element.10.student_ref, bf16[2048,128]{1,0:T(8,128)(2,1)} %get-tuple-element.11.upstream_ref, f32[8,2048]{1,0:T(8,128)} %get-tuple-element.12.stats_ref, bf16[4,4,128,384]{3,2,1,0:T(8,128)(2,1)} %copy-done.2, ...), custom_call_target="tpu_custom_call" | custom-call | flops 5368709120 | bytes 6291456 | tf_op jit(solution)/shard_map/attention_backward/pallas_call | solution.py:183
  175.9 22.2 %all_to_all.51 = bf16[4,4,128,384]{3,2,1,0:T(8,128)(2,1)S(1)} all-to-all(bf16[4,4,128,384]{3,2,1,0:T(8,128)(2,1)} %get-tuple-element.13), channel_id=1, replica_groups=mesh['cfg'=2,'z'=4,'y'=4,'x'=4,'core'=2] {'y'}, dimensions={0} | all-to-all | bytes 3145728 | tf_op jit(solution)/shard_map/all_to_all | solution.py:30
  198.1 1.1 reduce_sum.39
  199.2 3.5 %all-to-all-start.5 = ((bf16[4,128,384]{2,1,0:T(8,128)(2,1)}), bf16[4,128,384]{2,1,0:T(8,128)(2,1)S(1)}, u32[]{:S(2)}, u32[]{:S(2)}) async-start(bf16[4,128,384]{2,1,0:T(8,128)(2,1)} %reduce_sum.39), calls=%async_computation.5 | async-start | bytes 786432 | tf_op jit(solution)/shard_map/all_to_all | solution.py:30
  202.7 1.5 copy.36
  204.2 0.1 copy.37
  204.3 0.0 copy-start.5
  204.3 1.2 copy.38
  205.5 6.1 %all-to-all-done.5 = bf16[4,128,384]{2,1,0:T(8,128)(2,1)S(1)} async-done(((bf16[4,128,384]{2,1,0:T(8,128)(2,1)}), bf16[4,128,384]{2,1,0:T(8,128)(2,1)S(1)}, u32[]{:S(2)}, u32[]{:S(2)}) %all-to-all-start.5) | async-done | bytes 393248 | tf_op jit(solution)/shard_map/all_to_all | solution.py:30
  211.5 3.5 %all-to-all-start.7 = ((bf16[4,128,768]{2,1,0:T(8,128)(2,1)}), bf16[4,128,768]{2,1,0:T(8,128)(2,1)S(1)}, u32[]{:S(2)}, u32[]{:S(2)}) async-start(bf16[4,128,768]{2,1,0:T(8,128)(2,1)} %copy.38), calls=%async_computation.7 | async-start | bytes 1572864 | tf_op jit(solution)/shard_map/all_to_all | solution.py:30
  215.1 0.6 copy_bitcast_fusion
  215.8 8.7 %all-to-all-done.7 = bf16[4,128,768]{2,1,0:T(8,128)(2,1)S(1)} async-done(((bf16[4,128,768]{2,1,0:T(8,128)(2,1)}), bf16[4,128,768]{2,1,0:T(8,128)(2,1)S(1)}, u32[]{:S(2)}, u32[]{:S(2)}) %all-to-all-start.7) | async-done | bytes 786464 | tf_op jit(solution)/shard_map/all_to_all | solution.py:30
  224.5 4.8 %all-to-all-start.9 = ((bf16[16,3,8,128]{3,2,1,0:T(8,128)(2,1)}), bf16[16,3,8,128]{3,2,1,0:T(8,128)(2,1)S(1)}, u32[]{:S(2)}, u32[]{:S(2)}) async-start(bf16[16,3,8,128]{3,2,1,0:T(8,128)(2,1)} %copy_bitcast_fusion), calls=%async_computation.9 | async-start | bytes 196608 | tf_op jit(solution)/shard_map/all_to_all | solution.py:30
  229.3 0.1 copy.35
  229.4 8.1 %all-to-all-done.9 = bf16[16,3,8,128]{3,2,1,0:T(8,128)(2,1)S(1)} async-done(((bf16[16,3,8,128]{3,2,1,0:T(8,128)(2,1)}), bf16[16,3,8,128]{3,2,1,0:T(8,128)(2,1)S(1)}, u32[]{:S(2)}, u32[]{:S(2)}) %all-to-all-start.9) | async-done | bytes 98336 | tf_op jit(solution)/shard_map/all_to_all | solution.py:30
  237.6 0.1 broadcast_in_dim.11
  237.6 11.7 %all_to_all.52 = bf16[4,128,384]{1,2,0:T(8,128)(2,1)} all-to-all(bf16[4,128,384]{1,2,0:T(8,128)(2,1)S(1)} %broadcast_in_dim.11), channel_id=1, replica_groups=mesh['cfg'=2,'z'=4,'y'=4,'x'=4,'core'=2] {'y'}, dimensions={0} | all-to-all | bytes 786432 | tf_op jit(solution)/shard_map/all_to_all | solution.py:30
  249.3 3.6 %all-to-all-start.3 = ((bf16[16,128,128]{2,1,0:T(8,128)(2,1)}), bf16[16,128,128]{2,1,0:T(8,128)(2,1)S(1)}, u32[]{:S(2)}, u32[]{:S(2)}) async-start(bf16[16,128,128]{2,1,0:T(8,128)(2,1)} %bitcast.48), calls=%async_computation.3 | async-start | bytes 1048576 | tf_op jit(solution)/shard_map/all_to_all | solution.py:30
  252.9 1.5 fusion.1
  254.4 0.3 copy.39
  254.7 1.0 reshape.76
  255.7 12.6 %all-to-all-done.3 = bf16[16,128,128]{2,1,0:T(8,128)(2,1)S(1)} async-done(((bf16[16,128,128]{2,1,0:T(8,128)(2,1)}), bf16[16,128,128]{2,1,0:T(8,128)(2,1)S(1)}, u32[]{:S(2)}, u32[]{:S(2)}) %all-to-all-start.3) | async-done | bytes 524320 | tf_op jit(solution)/shard_map/all_to_all | solution.py:30
  268.3 6.4 %all-to-all-start.8 = ((bf16[64,12,384]{2,1,0:T(8,128)(2,1)}), bf16[64,12,384]{2,1,0:T(8,128)(2,1)S(1)}, u32[]{:S(2)}, u32[]{:S(2)}) async-start(bf16[64,12,384]{2,1,0:T(8,128)(2,1)} %reshape.76), calls=%async_computation.8 | async-start | bytes 1572864 | tf_op jit(solution)/shard_map/all_to_all | solution.py:30
  274.7 0.6 convert_reduce_fusion.2
  275.3 0.3 copy.34
  275.7 1.0 broadcast_in_dim_reshape.2
  276.7 21.2 %all-to-all-done.8 = bf16[64,12,384]{2,1,0:T(8,128)(2,1)S(1)} async-done(((bf16[64,12,384]{2,1,0:T(8,128)(2,1)}), bf16[64,12,384]{2,1,0:T(8,128)(2,1)S(1)}, u32[]{:S(2)}, u32[]{:S(2)}) %all-to-all-start.8) | async-done | bytes 589856 | tf_op jit(solution)/shard_map/all_to_all | solution.py:30
  297.9 0.2 convert_reduce_fusion
  298.1 0.6 copy.41
  (16 shorter events, 0.2 us)
Async XLA Ops:
  0.6 60.0 %copy-start = (bf16[3,128,2048]{2,1,0:T(8,128)(2,1)S(1)}, bf16[3,128,2048]{2,1,0:T(8,128)(2,1)}, u32[]{:S(2)}) copy-start(bf16[3,128,2048]{2,1,0:T(8,128)(2,1)} %param.13) | copy-start | bytes 4718596
  0.7 4.5 %copy-start.6 = (s32[2,1]{0,1:T(1,128)S(1)}, s32[2,1]{0,1:T(1,128)}, u32[]{:S(2)}) copy-start(s32[2,1]{0,1:T(1,128)} %param.14) | copy-start | bytes 28
  0.7 4.4 %copy-start.7 = (s32[2,1]{0,1:T(1,128)S(1)}, s32[2,1]{0,1:T(1,128)}, u32[]{:S(2)}) copy-start(s32[2,1]{0,1:T(1,128)} %param.15) | copy-start | bytes 28
  0.7 6.4 %copy-start.1 = (bf16[1,1,128,3072]{3,2,1,0:T(8,128)(2,1)S(1)}, bf16[1,1,128,3072]{3,2,1,0:T(8,128)(2,1)}, u32[]{:S(2)}) copy-start(bf16[1,1,128,3072]{3,2,1,0:T(8,128)(2,1)} %param.11) | copy-start | bytes 2359300
  28.5 24.0 %all-to-all-start.2 = ((bf16[4,4,128,384]{3,2,1,0:T(8,128)(2,1)}), bf16[4,4,128,384]{3,2,1,0:T(8,128)(2,1)S(1)}, u32[]{:S(2)}, u32[]{:S(2)}) async-start(bf16[4,4,128,384]{3,2,1,0:T(8,128)(2,1)} %broadcast_in_dim.10), calls=%async_computation.2 | async-start | bytes 3145728 | tf_op jit(solution)/shard_map/all_to_all | solution.py:30
  52.6 1.1 copy-start.2
  53.7 77.9 %all-to-all-start = ((bf16[32,3,128,128]{3,2,1,0:T(8,128)(2,1)}), bf16[32,3,128,128]{3,2,1,0:T(8,128)(2,1)}, u32[]{:S(2)}, u32[]{:S(2)}) async-start(bf16[32,3,128,128]{3,2,1,0:T(8,128)(2,1)} %pack_heads.1), calls=%async_computation | async-start | bytes 6291456 | tf_op jit(solution)/shard_map/all_to_all | solution.py:30
  199.2 12.3 %all-to-all-start.5 = ((bf16[4,128,384]{2,1,0:T(8,128)(2,1)}), bf16[4,128,384]{2,1,0:T(8,128)(2,1)S(1)}, u32[]{:S(2)}, u32[]{:S(2)}) async-start(bf16[4,128,384]{2,1,0:T(8,128)(2,1)} %reduce_sum.39), calls=%async_computation.5 | async-start | bytes 786432 | tf_op jit(solution)/shard_map/all_to_all | solution.py:30
  204.3 10.8 %copy-start.5 = (bf16[3,128,128]{2,1,0:T(8,128)(2,1)S(1)}, bf16[3,128,128]{2,1,0:T(8,128)(2,1)}, u32[]{:S(2)}) copy-start(bf16[3,128,128]{2,1,0:T(8,128)(2,1)} %get-tuple-element.14) | copy-start | bytes 294916
  211.5 13.0 %all-to-all-start.7 = ((bf16[4,128,768]{2,1,0:T(8,128)(2,1)}), bf16[4,128,768]{2,1,0:T(8,128)(2,1)S(1)}, u32[]{:S(2)}, u32[]{:S(2)}) async-start(bf16[4,128,768]{2,1,0:T(8,128)(2,1)} %copy.38), calls=%async_computation.7 | async-start | bytes 1572864 | tf_op jit(solution)/shard_map/all_to_all | solution.py:30
  224.5 13.1 %all-to-all-start.9 = ((bf16[16,3,8,128]{3,2,1,0:T(8,128)(2,1)}), bf16[16,3,8,128]{3,2,1,0:T(8,128)(2,1)S(1)}, u32[]{:S(2)}, u32[]{:S(2)}) async-start(bf16[16,3,8,128]{3,2,1,0:T(8,128)(2,1)} %copy_bitcast_fusion), calls=%async_computation.9 | async-start | bytes 196608 | tf_op jit(solution)/shard_map/all_to_all | solution.py:30
  237.6 11.8 %copy-start.3 = (bf16[16,3,8,128]{3,2,1,0:T(8,128)(2,1)}, bf16[16,3,8,128]{3,2,1,0:T(8,128)(2,1)S(1)}, u32[]{:S(2)}) copy-start(bf16[16,3,8,128]{3,2,1,0:T(8,128)(2,1)S(1)} %all-to-all-done.9) | copy-start | bytes 294916
  249.3 19.0 %all-to-all-start.3 = ((bf16[16,128,128]{2,1,0:T(8,128)(2,1)}), bf16[16,128,128]{2,1,0:T(8,128)(2,1)S(1)}, u32[]{:S(2)}, u32[]{:S(2)}) async-start(bf16[16,128,128]{2,1,0:T(8,128)(2,1)} %bitcast.48), calls=%async_computation.3 | async-start | bytes 1048576 | tf_op jit(solution)/shard_map/all_to_all | solution.py:30
  254.7 20.0 %copy-start.4 = (bf16[16,3,8,128]{3,2,1,0:T(8,128)(2,1)S(1)}, bf16[16,3,8,128]{3,2,1,0:T(8,128)(2,1)}, u32[]{:S(2)}) copy-start(bf16[16,3,8,128]{3,2,1,0:T(8,128)(2,1)} %copy-done.3) | copy-start | bytes 294916
  268.3 29.6 %all-to-all-start.8 = ((bf16[64,12,384]{2,1,0:T(8,128)(2,1)}), bf16[64,12,384]{2,1,0:T(8,128)(2,1)S(1)}, u32[]{:S(2)}, u32[]{:S(2)}) async-start(bf16[64,12,384]{2,1,0:T(8,128)(2,1)} %reshape.76), calls=%async_computation.8 | async-start | bytes 1572864 | tf_op jit(solution)/shard_map/all_to_all | solution.py:30

commit v2 on v1

--- a/solution.py
+++ b/solution.py
@@ -30,13 +30,34 @@
     return lax.all_to_all(value, axes, split_axis=0, concat_axis=0, tiled=True)
 
 
-def copies_from_all(value, axis):
-    peers = lax.axis_size(axis)
-    return exchange(jnp.broadcast_to(value[None], (peers, *value.shape)), axis)
-
-
-def summed_blocks(value, axes):
-    return exchange(value, axes).astype(F32).sum(axis=0)
+def shifted(value, axis, distance):
+    size = lax.axis_size(axis)
+    return lax.ppermute(value, axis, [(i, (i + distance) % size) for i in range(size)])
+
+
+def from_each(value, axis):
+    return [value] + [shifted(value, axis, d) for d in range(1, lax.axis_size(axis))]
+
+
+def summed_parts(parts, axis):
+    total = parts[0].astype(F32)
+    for d in range(1, lax.axis_size(axis)):
+        total = total + shifted(parts[d].astype(BF), axis, d).astype(F32)
+    return total
+
+
+def parts_ahead(value, axis, dim):
+    size, here = lax.axis_size(axis), lax.axis_index(axis)
+    return [
+        lax.dynamic_index_in_dim(value, (here + d) % size, dim, keepdims=False)
+        for d in range(size)
+    ]
+
+
+def reduced(value, axes):
+    for axis in axes:
+        value = summed_parts(parts_ahead(value, axis, 0), axis)
+    return value
 
 
 def pack_kernel(q_ref, k_ref, v_ref, out_ref):
@@ -70,23 +91,31 @@
 
 
 def forward_kernel(
-    scale_ref, heads_ref, low_ref, up_ref, inv_ref, out_ref, upstream_ref, student_ref, stats_ref, keys_ref
+    place_ref, scale_ref, inv_ref, heads_ref, up_ref, *refs
 ):
+    low_refs, (out_ref, upstream_ref, student_ref, stats_ref, keys_ref) = refs[:-5], refs[-5:]
     pass_tok, rows = heads_ref.shape[1], heads_ref.shape[3]
     tokens = pass_tok * rows
-    n_slow, n_fast = low_ref.shape[1], low_ref.shape[0]
+    n_fast, n_slow = len(low_refs), low_refs[0].shape[0]
+    here_slow, here_fast = place_ref[0], place_ref[1]
     scale = scale_ref[0]
     inverse = inv_ref[0]
 
     for part in range(3):
         up = up_ref[part]
         for block in range(pass_tok):
-            slow, fast = block // n_fast, block % n_fast
-            adapted = dot(low_ref[fast, slow, :, part * RANK : (part + 1) * RANK], up)
-            frozen = heads_ref[0, block, part].astype(F32)
-            student_ref[part, block * rows : (block + 1) * rows] = (frozen + adapted).astype(BF)
             for one in range(2):
                 keys_ref[one, part, block * rows : (block + 1) * rows] = heads_ref[one, block, part]
+        for fast in range(n_fast):
+            for slow in range(n_slow):
+                block = lax.rem(here_slow - slow + n_slow, n_slow) * n_fast + lax.rem(
+                    here_fast - fast + n_fast, n_fast
+                )
+                columns = slice(part * RANK, (part + 1) * RANK)
+                adapted = dot(low_refs[fast][slow, :, columns], up)
+                frozen = heads_ref[0, block, part].astype(F32)
+                where = pl.ds(pl.multiple_of(block * rows, rows), rows)
+                student_ref[part, where] = (frozen + adapted).astype(BF)
 
     step_rows = 256
 
@@ -114,13 +143,13 @@
     lax.fori_loop(0, tokens // step_rows, one_block, 0)
 
 
-def forward(scale, heads, low, up, inverse):
+def forward(place, scale, inverse, heads, up, low):
     tokens = heads.shape[1] * heads.shape[3]
     vmem = pl.BlockSpec(memory_space=pltpu.VMEM)
     smem = pl.BlockSpec(memory_space=pltpu.SMEM)
     return pl.pallas_call(
         forward_kernel,
-        in_specs=[smem, vmem, vmem, vmem, smem],
+        in_specs=[smem] * 3 + [vmem] * (2 + len(low)),
         out_specs=[vmem] * 4,
         out_shape=[
             jax.ShapeDtypeStruct((tokens, HDIM), BF),
@@ -136,14 +165,17 @@
         ),
         compiler_params=pltpu.CompilerParams(vmem_limit_bytes=56 * MIB),
         name="attention_forward",
-    )(scale, heads, low, up, inverse)
+    )(place, scale, inverse, heads, up, *low)
 
 
 def backward_kernel(
-    student_ref, upstream_ref, stats_ref, low_ref, up_ref, back_ref, grad_up_ref, dq_ref, dk_ref, dv_ref
+    n_fast, place_ref, student_ref, upstream_ref, stats_ref, up_ref, *refs
 ):
+    low_refs, back_refs = refs[:n_fast], refs[n_fast : 2 * n_fast]
+    grad_up_ref, dq_ref, dk_ref, dv_ref = refs[2 * n_fast :]
     tokens = student_ref.shape[1]
-    n_fast, n_slow, rows, _ = low_ref.shape
+    n_slow, rows, _ = low_refs[0].shape
+    here_slow, here_fast = place_ref[0], place_ref[1]
     step_rows = 256
     dk_ref[...] = jnp.zeros_like(dk_ref)
     dv_ref[...] = jnp.zeros_like(dv_ref)
@@ -167,25 +199,31 @@
     for part, (ref, factor) in enumerate(((dq_ref, FACTOR), (dk_ref, FACTOR), (dv_ref, 1.0))):
         up = up_ref[part]
         total = jnp.zeros((RANK, HDIM), F32)
-        for slow in range(n_slow):
-            for fast in range(n_fast):
-                first = (slow * n_fast + fast) * rows
-                grad = (ref[first : first + rows] * factor).astype(BF)
-                columns = slice(part * RANK, (part + 1) * RANK)
-                back_ref[fast, slow, :, columns] = dot(grad, up, NT).astype(BF)
-                total += dot(low_ref[fast, slow, :, columns], grad, TN)
+        columns = slice(part * RANK, (part + 1) * RANK)
+        for fast in range(n_fast):
+            for slow in range(n_slow):
+                ahead = lax.rem(here_slow + slow, n_slow) * n_fast + lax.rem(
+                    here_fast + fast, n_fast
+                )
+                behind = lax.rem(here_slow - slow + n_slow, n_slow) * n_fast + lax.rem(
+                    here_fast - fast + n_fast, n_fast
+                )
+                grad = ref[pl.ds(pl.multiple_of(ahead * rows, rows), rows)] * factor
+                back_refs[fast][slow, :, columns] = dot(grad.astype(BF), up, NT).astype(BF)
+                grad = ref[pl.ds(pl.multiple_of(behind * rows, rows), rows)] * factor
+                total += dot(low_refs[fast][slow, :, columns], grad.astype(BF), TN)
         grad_up_ref[part] = total.astype(BF)
 
 
-def backward(student, upstream, stats, low, up):
-    tokens = student.shape[1]
+def backward(place, student, upstream, stats, up, low):
+    tokens, n_fast = student.shape[1], len(low)
     vmem = pl.BlockSpec(memory_space=pltpu.VMEM)
     return pl.pallas_call(
-        backward_kernel,
-        in_specs=[vmem] * 5,
-        out_specs=[vmem] * 2,
-        out_shape=[
-            jax.ShapeDtypeStruct(low.shape, BF),
+        functools.partial(backward_kernel, n_fast),
+        in_specs=[pl.BlockSpec(memory_space=pltpu.SMEM)] + [vmem] * (4 + n_fast),
+        out_specs=[vmem] * (n_fast + 1),
+        out_shape=[jax.ShapeDtypeStruct(low[0].shape, BF)] * n_fast
+        + [
             jax.ShapeDtypeStruct((3, RANK, HDIM), BF),
         ],
         scratch_shapes=[pltpu.VMEM((tokens, HDIM), F32)] * 3,
@@ -196,7 +234,7 @@
         ),
         compiler_params=pltpu.CompilerParams(vmem_limit_bytes=56 * MIB),
         name="attention_backward",
-    )(student, upstream, stats, low, up)
+    )(place, student, upstream, stats, up, *low)
 
 
 def body(
@@ -229,33 +267,35 @@
 
     low = jnp.einsum("cl,elj->cej", features, adapter_down_weight, preferred_element_type=F32)
     low = (low * modulation).astype(BF).reshape(rows, 3 * RANK)
-    low_all = copies_from_all(copies_from_all(low, "z"), "y")
+    low_all = from_each(jnp.stack(from_each(low, "z")), "y")
 
     groups = n_cfg * n_slow
     part_cols = width // (groups * n_fast)
-    spread = jnp.moveaxis(features.reshape(rows, groups, n_fast, part_cols), 2, 0)
-    columns = exchange(spread.reshape(n_fast, rows, groups * part_cols), "y")
-    columns = columns.reshape(n_fast * rows, groups * part_cols)
-
+    spread = parts_ahead(features.reshape(rows, groups, n_fast, part_cols), "y", 2)
+    spread = [part.reshape(rows, groups * part_cols) for part in spread]
+    columns = jnp.concatenate(
+        [spread[0]] + [shifted(spread[d], "y", d) for d in range(1, n_fast)]
+    )
+
+    place = jnp.stack([lax.axis_index("z"), lax.axis_index("y")]).astype(jnp.int32)
     up = lax.dynamic_slice_in_dim(adapter_up_weight, seq_index * HDIM, HDIM, 2)
     inverse = jnp.full((1,), 1.0 / math.sqrt(total_rows), F32)
-    out, upstream, student, stats = forward(scale, heads, low_all, up, inverse)
+    out, upstream, student, stats = forward(place, scale, inverse, heads, up, low_all)
     tokens_out = exchange(out.reshape(n_slow * n_fast, rows, HDIM), ("z", "y"))
     student_out = jnp.moveaxis(tokens_out, 0, 1).reshape(rows, -1)
 
-    back, up_partial = backward(student, upstream, stats, low_all, up)
-    back = summed_blocks(back, "y").astype(BF)
-    back = summed_blocks(back, "z")
+    *back, up_partial = backward(place, student, upstream, stats, up, low_all)
+    back = summed_parts(back, "y").astype(BF)
+    back = summed_parts([back[d] for d in range(n_slow)], "z")
     low_grad = (back.reshape(rows, 3, RANK) * modulation).astype(BF).reshape(rows, 3 * RANK)
-    low_grads = copies_from_all(low_grad, "y").reshape(n_fast * rows, 3 * RANK)
+    low_grads = jnp.concatenate(from_each(low_grad, "y"))
     down = dot(columns, low_grads, TN).astype(BF)
-    peers = groups * n_x * n_core
-    down = summed_blocks(down.reshape(peers, -1, 3 * RANK), ("cfg", "z", "x", "core"))
+    down = down.reshape(n_cfg, n_slow, n_x, n_core, -1, 3 * RANK).transpose(3, 2, 0, 1, 4, 5)
+    down = reduced(down, ("core", "x", "cfg", "z"))
     grad_down = jnp.moveaxis(down.reshape(-1, 3, RANK), 1, 0)
 
-    owners = n_cfg * n_x * n_core
-    up_blocks = jnp.moveaxis(up_partial.reshape(3, owners, RANK // owners, HDIM), 1, 0)
-    grad_up = summed_blocks(up_blocks, ("cfg", "x", "core"))
+    up_blocks = up_partial.reshape(3, n_cfg, n_x, n_core, -1, HDIM).transpose(3, 2, 1, 0, 4, 5)
+    grad_up = reduced(up_blocks, ("core", "x", "cfg"))
     return student_out[None, None], grad_down, grad_up
 
 

time: 300 us -> 244 us (0.81)
  blocking collectives: 51.3 us -> 0 us
  waiting for transfers between devices: 143 us -> 110 us
  starting transfers between devices: 33.1 us -> 63.6 us
  local copies, waits for them, and re-layouts: 14.7 us -> 10.2 us
    all_to_all x7 -> x2, waiting for transfers between devices: 143 us -> 0.01 us  [exchange(): return lax.all_to_all(value, axes, split_axis=0, concat_axis=0, tiled=True)]
    ppermute x0 -> x31, waiting for transfers between devices: none -> 110 us  [shifted(): lax.ppermute(value, axis, [(i, (i + distance) % size) for i in range(size)])]
    all_to_all x3 -> x0, blocking collectives: 51.3 us -> none  [exchange(): return lax.all_to_all(value, axes, split_axis=0, concat_axis=0, tiled=True)]
    ppermute x0 -> x31, starting transfers between devices: none -> 47.5 us  [shifted(): lax.ppermute(value, axis, [(i, (i + distance) % size) for i in range(size)])]
    all_to_all x7 -> x2, starting transfers between devices: 33.1 us -> 16.1 us  [exchange(): return lax.all_to_all(value, axes, split_axis=0, concat_axis=0, tiled=True)]
    unnamed x19 -> x22, local copies, waits for them, and re-layouts: 7.72 us -> 6.81 us
  transfers between devices with their start and end apart: 7 -> 33, of which waited for: 7 -> 14; matrix products, arithmetic and copies ran while one was open for 3% -> 8% of each run, Pallas kernels for 1% -> 0%
where the time goes in v2:
time: 244 us; the launch traced here: 243 us
  waiting for transfers between devices  110 us (45%)
  starting transfers between devices  63.6 us (26%)
  Pallas kernels  47.3 us (19%)
  local copies, waits for them, and re-layouts  10.2 us (4%)
  other arithmetic  5.41 us (2%)
  matrix products  4.03 us (2%)
    ppermute x31, waiting for transfers between devices, shifted(): lax.ppermute(value, axis, [(i, (i + distance) % size) for i in range(size)])  110 us
    ppermute x31, starting transfers between devices, shifted(): lax.ppermute(value, axis, [(i, (i + distance) % size) for i in range(size)])  47.5 us
    pallas_call x1, Pallas kernels, forward(): pl.pallas_call(forward_kernel, in_specs=[smem] * 3 + [vmem] * (2 + len(lo...  26.1 us
    pallas_call x1, Pallas kernels, backward(): pl.pallas_call(functools.partial(backward_kernel, n_fast), in_specs=[pl.B...  17.7 us
    all_to_all x2, starting transfers between devices, exchange(): return lax.all_to_all(value, axes, split_axis=0, concat_axis=0, tiled=True)  16.1 us
    unnamed x22, local copies, waits for them, and re-layouts  6.81 us
  transfers between devices with their start and end apart: 33, of which 14 were waited for; matrix products, arithmetic and copies ran while one was open for 8% of the time, Pallas kernels for 0%

profile of v2, /device:TPU:6, one launch (start us, length us, event | category | flops | bytes accessed | tf_op | source)
XLA Modules:
  0.0 242.6 jit_solution(13497054883874949702)
XLA Ops:
  0.6 3.4 %pack_heads.1 = bf16[32,3,128,128]{3,2,1,0:T(8,128)(2,1)} custom-call(bf16[2,128,2048]{2,1,0:T(8,128)(2,1)} %bitcast.118, bf16[2,128,2048]{2,1,0:T(8,128)(2,1)} %bitcast.119, bf16[2,128,2048]{2,1,0:T(8,128)(2,1)} %bitcast.120), custom_call_target="tpu_custom_call" | custom-call | bytes 6291456 | tf_op jit(solution)/shard_map/pack_heads/pallas_call | solution.py:74
  4.1 11.6 %all-to-all-start = ((bf16[32,3,128,128]{3,2,1,0:T(8,128)(2,1)}), bf16[32,3,128,128]{3,2,1,0:T(8,128)(2,1)}, u32[]{:S(2)}, u32[]{:S(2)}) async-start(bf16[32,3,128,128]{3,2,1,0:T(8,128)(2,1)} %pack_heads.1), calls=%async_computation | async-start | bytes 6291456 | tf_op jit(solution)/shard_map/all_to_all | solution.py:30
  15.7 4.4 %copy.20 = bf16[3,3072,128]{1,2,0:T(8,128)(2,1)} copy(bf16[3,3072,128]{2,1,0:T(8,128)(2,1)} %param.12) | data formatting | bytes 4718592 | tf_op args[4]
  22.1 2.4 %fusion.7 = f32[128,384]{0,1:S(1)} fusion(bf16[3072,384]{0,1:T(8,128)(2,1)} %bitcast.115, bf16[1,1,128,3072]{3,2,1,0:T(8,128)(2,1)S(1)} %copy-done.1), kind=kOutput, calls=%fused_computation.9 | convolution fusion | flops 301989888 | bytes 3342336
  24.8 3.6 %collective-permute-start.2 = (bf16[128,384]{1,0:T(8,128)(2,1)S(1)}, bf16[128,384]{1,0:T(8,128)(2,1)S(1)}, u32[]{:S(2)}, u32[]{:S(2)}) collective-permute-start(bf16[128,384]{1,0:T(8,128)(2,1)S(1)} %copy.21), channel_id=1, source_target_pairs={{0,96},{32,0},{64,32},{96,64},{1,97},{33,1},{65,33},{97,65},{2,98}... | collective-permute-start | bytes 294920 | tf_op jit(solution)/shard_map/ppermute | solution.py:35
  28.4 1.1 collective-permute-start
  29.6 58.1 %collective-permute-done.2 = bf16[128,384]{1,0:T(8,128)(2,1)S(1)} collective-permute-done((bf16[128,384]{1,0:T(8,128)(2,1)S(1)}, bf16[128,384]{1,0:T(8,128)(2,1)S(1)}, u32[]{:S(2)}, u32[]{:S(2)}) %collective-permute-start.2) | collective-permute-done | bytes 98336 | tf_op jit(solution)/shard_map/ppermute | solution.py:35
  87.7 6.8 %collective-permute-done.1 = bf16[128,384]{1,0:T(8,128)(2,1)S(1)} collective-permute-done((bf16[128,384]{1,0:T(8,128)(2,1)S(1)}, bf16[128,384]{1,0:T(8,128)(2,1)S(1)}, u32[]{:S(2)}, u32[]{:S(2)}) %collective-permute-start.1) | collective-permute-done | bytes 98336 | tf_op jit(solution)/shard_map/ppermute | solution.py:35
  94.5 1.5 collective-permute-start.3
  96.0 2.6 %collective-permute-start.4 = (bf16[4,128,384]{2,1,0:T(8,128)(2,1)S(1)}, bf16[4,128,384]{2,1,0:T(8,128)(2,1)S(1)}, u32[]{:S(2)}, u32[]{:S(2)}) collective-permute-start(bf16[4,128,384]{2,1,0:T(8,128)(2,1)S(1)} %pad_maximum_fusion.refs_0_), channel_id=1, source_target_pairs={{0,16},{8,24},{16,0},{24,8},{1,17},{9,25},{17,1},{25,9},{2,18},{10... | collective-permute-start | bytes 1179656 | tf_op jit(solution)/shard_map/ppermute | solution.py:35
  98.6 1.5 collective-permute-start.5
  101.5 4.8 %collective-permute-done.3.refs_1_ = bf16[4,128,384]{2,1,0:T(8,128)(2,1)S(1)} collective-permute-done((bf16[4,128,384]{2,1,0:T(8,128)(2,1)S(1)}, bf16[4,128,384]{2,1,0:T(8,128)(2,1)S(1)}, u32[]{:S(2)}, u32[]{:S(2)}) %collective-permute-start.3) | collective-permute-done | bytes 393248 | tf_op jit(solution)/shard_map/ppermute | solution.py:35
  106.3 8.7 %collective-permute-done.4.refs_2_ = bf16[4,128,384]{2,1,0:T(8,128)(2,1)S(1)} collective-permute-done((bf16[4,128,384]{2,1,0:T(8,128)(2,1)S(1)}, bf16[4,128,384]{2,1,0:T(8,128)(2,1)S(1)}, u32[]{:S(2)}, u32[]{:S(2)}) %collective-permute-start.4) | collective-permute-done | bytes 393248 | tf_op jit(solution)/shard_map/ppermute | solution.py:35
  115.0 0.7 copy-done.8
  115.8 26.1 %attention_forward.1 = (bf16[2048,128]{1,0:T(8,128)(2,1)}, bf16[2048,128]{1,0:T(8,128)(2,1)}, bf16[3,2048,128]{2,1,0:T(8,128)(2,1)}, f32[8,2048]{1,0:T(8,128)}) custom-call(s32[2]{0:T(128)} %pad_add_fusion.place_ref, f32[1]{0:T(128)} %bitcast.2.scale_ref, f32[1]{0:T(128)} %constant.201.clone.1.inv_ref, bf16[2,16,3,128,128]{4,3,2,1,0:T(8,128)(2,1)} %bitcast.6.heads_ref, ...), custom_call_target="tpu_custom_call" | custom-call | flops 6442450944 | bytes 8388608 | tf_op jit(solution)/shard_map/attention_forward/pallas_call | solution.py:150
  141.9 17.7 %attention_backward.1 = (bf16[4,128,384]{2,1,0:T(8,128)(2,1)}, bf16[4,128,384]{2,1,0:T(8,128)(2,1)}, bf16[4,128,384]{2,1,0:T(8,128)(2,1)}, bf16[4,128,384]{2,1,0:T(8,128)(2,1)}, bf16[3,128,128]{2,1,0:T(8,128)(2,1)}) custom-call(s32[2]{0:T(128)} %pad_add_fusion.place_ref, bf16[3,2048,128]{2,1,0:T(8,128)(2,1)} %get-tuple-element.13.student_ref, ...), custom_call_target="tpu_custom_call" | custom-call | flops 5368709120 | bytes 6291456 | tf_op jit(solution)/shard_map/attention_backward/pallas_call | solution.py:221
  159.6 1.6 collective-permute-start.11
  162.5 0.8 constant_dynamic-slice_fusion.5
  163.3 2.6 %collective-permute-start.8 = (bf16[128,768]{0,1:T(8,128)(2,1)}, bf16[128,768]{0,1:T(8,128)(2,1)}, u32[]{:S(2)}, u32[]{:S(2)}) collective-permute-start(bf16[128,768]{0,1:T(8,128)(2,1)} %bitcast.24), channel_id=1, source_target_pairs={{0,24},{8,0},{16,8},{24,16},{1,25},{9,1},{17,9},{25,17},{2,26},{10... | collective-permute-start | bytes 589832 | tf_op jit(solution)/shard_map/ppermute | solution.py:35
  165.9 2.1 collective-permute-start.7
  168.0 12.7 %collective-permute-done.11 = bf16[4,128,384]{2,1,0:T(8,128)(2,1)} collective-permute-done((bf16[4,128,384]{2,1,0:T(8,128)(2,1)}, bf16[4,128,384]{2,1,0:T(8,128)(2,1)}, u32[]{:S(2)}, u32[]{:S(2)}) %collective-permute-start.11) | collective-permute-done | bytes 393248 | tf_op jit(solution)/shard_map/ppermute | solution.py:35
  180.6 2.1 collective-permute-done.9
  182.7 1.4 add_convert_fusion
  184.5 1.6 collective-permute-start.13
  186.1 1.9 collective-permute-start.12
  188.0 4.5 %all-to-all-start.1 = ((bf16[16,128,128]{2,1,0:T(8,128)(2,1)}), bf16[16,128,128]{2,1,0:T(8,128)(2,1)S(1)}, u32[]{:S(2)}, u32[]{:S(2)}) async-start(bf16[16,128,128]{2,1,0:T(8,128)(2,1)} %bitcast.18), calls=%async_computation.1 | async-start | bytes 1048576 | tf_op jit(solution)/shard_map/all_to_all | solution.py:30
  192.5 2.0 collective-permute-start.6
  194.5 1.0 fusion.19
  195.5 1.4 collective-permute-start.17
  196.9 2.2 collective-permute-start.16
  200.3 7.7 %collective-permute-done.6 = bf16[128,768]{0,1:T(8,128)(2,1)S(1)} collective-permute-done((bf16[128,768]{0,1:T(8,128)(2,1)S(1)}, bf16[128,768]{0,1:T(8,128)(2,1)S(1)}, u32[]{:S(2)}, u32[]{:S(2)}) %collective-permute-start.6) | collective-permute-done | bytes 196640 | tf_op jit(solution)/shard_map/ppermute | solution.py:35
  208.0 0.9 collective-permute-done.16
  209.5 1.6 convolution_convert_fusion
  211.4 0.8 bitcast_add_fusion.2
  212.3 0.9 collective-permute-start.29
  213.2 1.1 collective-permute-start.28
  214.3 2.1 collective-permute-start.27
  216.7 2.3 collective-permute-start.20
  219.0 2.4 collective-permute-start.19
  221.4 2.9 %collective-permute-done.21 = bf16[2,4,12,384]{3,2,1,0:T(8,128)(2,1)S(1)} collective-permute-done((bf16[2,4,12,384]{3,2,1,0:T(8,128)(2,1)S(1)}, bf16[2,4,12,384]{3,2,1,0:T(8,128)(2,1)S(1)}, u32[]{:S(2)}, u32[]{:S(2)}) %collective-permute-start.21) | collective-permute-done | bytes 73760 | tf_op jit(solution)/shard_map/ppermute | solution.py:35
  225.0 3.8 %collective-permute-start.22 = (bf16[4,12,384]{2,1,0:T(8,128)(2,1)S(1)}, bf16[4,12,384]{2,1,0:T(8,128)(2,1)S(1)}, u32[]{:S(2)}, u32[]{:S(2)}) collective-permute-start(bf16[4,12,384]{2,1,0:T(8,128)(2,1)S(1)} %fusion.25), channel_id=1, source_target_pairs={{0,128},{128,0},{1,129},{129,1},{2,130},{130,2},{3,131},{131,3},{4... | collective-permute-start | bytes 110600 | tf_op jit(solution)/shard_map/ppermute | solution.py:35
  228.7 2.2 collective-permute-start.30
  231.0 2.1 collective-permute-done.22
  233.1 3.3 %collective-permute-start.25 = (bf16[12,384]{1,0:T(8,128)(2,1)S(1)}, bf16[12,384]{1,0:T(8,128)(2,1)S(1)}, u32[]{:S(2)}, u32[]{:S(2)}) collective-permute-start(bf16[12,384]{1,0:T(8,128)(2,1)S(1)} %get-tuple-element.40), channel_id=1, source_target_pairs={{0,96},{32,0},{64,32},{96,64},{1,97},{33,1},{65,33},{97,65},{2,98}... | collective-permute-start | bytes 27656 | tf_op jit(solution)/shard_map/ppermute | solution.py:35
  236.4 1.8 collective-permute-start.23
  239.2 1.0 broadcast_in_dim_reshape.3
  240.2 0.8 collective-permute-done.24
  241.0 0.9 collective-permute-done.23
  (76 shorter events, 8.7 us)
Async XLA Ops:
  0.6 100.2 %copy-start = (bf16[3,128,2048]{2,1,0:T(8,128)(2,1)S(1)}, bf16[3,128,2048]{2,1,0:T(8,128)(2,1)}, u32[]{:S(2)}) copy-start(bf16[3,128,2048]{2,1,0:T(8,128)(2,1)} %param.13) | copy-start | bytes 4718596
  4.1 110.9 %all-to-all-start = ((bf16[32,3,128,128]{3,2,1,0:T(8,128)(2,1)}), bf16[32,3,128,128]{3,2,1,0:T(8,128)(2,1)}, u32[]{:S(2)}, u32[]{:S(2)}) async-start(bf16[32,3,128,128]{3,2,1,0:T(8,128)(2,1)} %pack_heads.1), calls=%async_computation | async-start | bytes 6291456 | tf_op jit(solution)/shard_map/all_to_all | solution.py:30
  15.7 4.5 %copy-start.5 = (s32[2,1]{0,1:T(1,128)S(1)}, s32[2,1]{0,1:T(1,128)}, u32[]{:S(2)}) copy-start(s32[2,1]{0,1:T(1,128)} %param.14) | copy-start | bytes 28
  15.7 4.5 %copy-start.6 = (s32[2,1]{0,1:T(1,128)S(1)}, s32[2,1]{0,1:T(1,128)}, u32[]{:S(2)}) copy-start(s32[2,1]{0,1:T(1,128)} %param.15) | copy-start | bytes 28
  15.7 6.4 %copy-start.1 = (bf16[1,1,128,3072]{3,2,1,0:T(8,128)(2,1)S(1)}, bf16[1,1,128,3072]{3,2,1,0:T(8,128)(2,1)}, u32[]{:S(2)}) copy-start(bf16[1,1,128,3072]{3,2,1,0:T(8,128)(2,1)} %param.11) | copy-start | bytes 2359300
  24.8 62.9 %collective-permute-start.2 = (bf16[128,384]{1,0:T(8,128)(2,1)S(1)}, bf16[128,384]{1,0:T(8,128)(2,1)S(1)}, u32[]{:S(2)}, u32[]{:S(2)}) collective-permute-start(bf16[128,384]{1,0:T(8,128)(2,1)S(1)} %copy.21), channel_id=1, source_target_pairs={{0,96},{32,0},{64,32},{96,64},{1,97},{33,1},{65,33},{97,65},{2,98}... | collective-permute-start | bytes 294920 | tf_op jit(solution)/shard_map/ppermute | solution.py:35
  28.4 66.1 %collective-permute-start.1 = (bf16[128,384]{1,0:T(8,128)(2,1)S(1)}, bf16[128,384]{1,0:T(8,128)(2,1)S(1)}, u32[]{:S(2)}, u32[]{:S(2)}) collective-permute-start(bf16[128,384]{1,0:T(8,128)(2,1)S(1)} %copy.21), channel_id=1, source_target_pairs={{0,64},{32,96},{64,0},{96,32},{1,65},{33,97},{65,1},{97,33},{2,66}... | collective-permute-start | bytes 294920 | tf_op jit(solution)/shard_map/ppermute | solution.py:35
  28.4 66.1 %collective-permute-start = (bf16[128,384]{1,0:T(8,128)(2,1)S(1)}, bf16[128,384]{1,0:T(8,128)(2,1)S(1)}, u32[]{:S(2)}, u32[]{:S(2)}) collective-permute-start(bf16[128,384]{1,0:T(8,128)(2,1)S(1)} %copy.21), channel_id=1, source_target_pairs={{0,32},{32,64},{64,96},{96,0},{1,33},{33,65},{65,97},{97,1},{2,34}... | collective-permute-start | bytes 294920 | tf_op jit(solution)/shard_map/ppermute | solution.py:35
  94.5 20.5 %copy-start.2 = (bf16[4,128,384]{2,1,0:T(8,128)(2,1)}, bf16[4,128,384]{2,1,0:T(8,128)(2,1)S(1)}, u32[]{:S(2)}) copy-start(bf16[4,128,384]{2,1,0:T(8,128)(2,1)S(1)} %pad_maximum_fusion.refs_0_) | copy-start | bytes 1179652
  94.5 11.7 %collective-permute-start.3 = (bf16[4,128,384]{2,1,0:T(8,128)(2,1)S(1)}, bf16[4,128,384]{2,1,0:T(8,128)(2,1)S(1)}, u32[]{:S(2)}, u32[]{:S(2)}) collective-permute-start(bf16[4,128,384]{2,1,0:T(8,128)(2,1)S(1)} %pad_maximum_fusion.refs_0_), channel_id=1, source_target_pairs={{0,8},{8,16},{16,24},{24,0},{1,9},{9,17},{17,25},{25,1},{2,10},{10... | collective-permute-start | bytes 1179656 | tf_op jit(solution)/shard_map/ppermute | solution.py:35
  96.0 19.0 %collective-permute-start.4 = (bf16[4,128,384]{2,1,0:T(8,128)(2,1)S(1)}, bf16[4,128,384]{2,1,0:T(8,128)(2,1)S(1)}, u32[]{:S(2)}, u32[]{:S(2)}) collective-permute-start(bf16[4,128,384]{2,1,0:T(8,128)(2,1)S(1)} %pad_maximum_fusion.refs_0_), channel_id=1, source_target_pairs={{0,16},{8,24},{16,0},{24,8},{1,17},{9,25},{17,1},{25,9},{2,18},{10... | collective-permute-start | bytes 1179656 | tf_op jit(solution)/shard_map/ppermute | solution.py:35
  98.6 16.4 %collective-permute-start.5 = (bf16[4,128,384]{2,1,0:T(8,128)(2,1)S(1)}, bf16[4,128,384]{2,1,0:T(8,128)(2,1)}, u32[]{:S(2)}, u32[]{:S(2)}) collective-permute-start(bf16[4,128,384]{2,1,0:T(8,128)(2,1)S(1)} %pad_maximum_fusion.refs_0_), channel_id=1, source_target_pairs={{0,24},{8,0},{16,8},{24,16},{1,25},{9,1},{17,9},{25,17},{2,26},{10... | collective-permute-start | bytes 1179656 | tf_op jit(solution)/shard_map/ppermute | solution.py:35
  106.3 8.7 %copy-start.7 = (bf16[4,128,384]{2,1,0:T(8,128)(2,1)}, bf16[4,128,384]{2,1,0:T(8,128)(2,1)S(1)}, u32[]{:S(2)}) copy-start(bf16[4,128,384]{2,1,0:T(8,128)(2,1)S(1)} %collective-permute-done.3.refs_1_) | copy-start | bytes 1179652
  115.0 0.8 copy-start.8
  159.6 21.0 %collective-permute-start.11 = (bf16[4,128,384]{2,1,0:T(8,128)(2,1)}, bf16[4,128,384]{2,1,0:T(8,128)(2,1)}, u32[]{:S(2)}, u32[]{:S(2)}) collective-permute-start(bf16[4,128,384]{2,1,0:T(8,128)(2,1)} %get-tuple-element.19), channel_id=1, source_target_pairs={{0,24},{8,0},{16,8},{24,16},{1,25},{9,1},{17,9},{25,17},{2,26},{10... | collective-permute-start | bytes 1179656 | tf_op jit(solution)/shard_map/ppermute | solution.py:35
  161.1 19.5 %collective-permute-start.10 = (bf16[4,128,384]{2,1,0:T(8,128)(2,1)}, bf16[4,128,384]{2,1,0:T(8,128)(2,1)}, u32[]{:S(2)}, u32[]{:S(2)}) collective-permute-start(bf16[4,128,384]{2,1,0:T(8,128)(2,1)} %get-tuple-element.18), channel_id=1, source_target_pairs={{0,16},{8,24},{16,0},{24,8},{1,17},{9,25},{17,1},{25,9},{2,18},{10... | collective-permute-start | bytes 1179656 | tf_op jit(solution)/shard_map/ppermute | solution.py:35
  161.4 21.3 %copy-start.3 = (bf16[4,128,384]{2,1,0:T(8,128)(2,1)S(1)}, bf16[4,128,384]{2,1,0:T(8,128)(2,1)}, u32[]{:S(2)}) copy-start(bf16[4,128,384]{2,1,0:T(8,128)(2,1)} %get-tuple-element.16) | copy-start | bytes 1179652
  161.4 21.3 %collective-permute-start.9 = (bf16[4,128,384]{2,1,0:T(8,128)(2,1)}, bf16[4,128,384]{2,1,0:T(8,128)(2,1)}, u32[]{:S(2)}, u32[]{:S(2)}) collective-permute-start(bf16[4,128,384]{2,1,0:T(8,128)(2,1)} %get-tuple-element.17), channel_id=1, source_target_pairs={{0,8},{8,16},{16,24},{24,0},{1,9},{9,17},{17,25},{25,1},{2,10},{10... | collective-permute-start | bytes 1179656 | tf_op jit(solution)/shard_map/ppermute | solution.py:35
  163.3 35.8 %collective-permute-start.8 = (bf16[128,768]{0,1:T(8,128)(2,1)}, bf16[128,768]{0,1:T(8,128)(2,1)}, u32[]{:S(2)}, u32[]{:S(2)}) collective-permute-start(bf16[128,768]{0,1:T(8,128)(2,1)} %bitcast.24), channel_id=1, source_target_pairs={{0,24},{8,0},{16,8},{24,16},{1,25},{9,1},{17,9},{25,17},{2,26},{10... | collective-permute-start | bytes 589832 | tf_op jit(solution)/shard_map/ppermute | solution.py:35
  165.9 34.4 %collective-permute-start.7 = (bf16[128,768]{0,1:T(8,128)(2,1)}, bf16[128,768]{0,1:T(8,128)(2,1)}, u32[]{:S(2)}, u32[]{:S(2)}) collective-permute-start(bf16[128,768]{0,1:T(8,128)(2,1)} %bitcast.23), channel_id=1, source_target_pairs={{0,16},{8,24},{16,0},{24,8},{1,17},{9,25},{17,1},{25,9},{2,18},{10... | collective-permute-start | bytes 589832 | tf_op jit(solution)/shard_map/ppermute | solution.py:35
  184.2 15.5 %copy-start.4 = (bf16[3,128,128]{2,1,0:T(8,128)(2,1)S(1)}, bf16[3,128,128]{2,1,0:T(8,128)(2,1)}, u32[]{:S(2)}) copy-start(bf16[3,128,128]{2,1,0:T(8,128)(2,1)} %get-tuple-element.20) | copy-start | bytes 294916
  184.2 8.3 %collective-permute-start.14 = (bf16[128,384]{1,0:T(8,128)(2,1)S(1)}, bf16[128,384]{1,0:T(8,128)(2,1)S(1)}, u32[]{:S(2)}, u32[]{:S(2)}) collective-permute-start(bf16[128,384]{1,0:T(8,128)(2,1)S(1)} %get-tuple-element.32), channel_id=1, source_target_pairs={{0,96},{32,0},{64,32},{96,64},{1,97},{33,1},{65,33},{97,65},{2,98}... | collective-permute-start | bytes 294920 | tf_op jit(solution)/shard_map/ppermute | solution.py:35
  184.5 10.1 %collective-permute-start.13 = (bf16[128,384]{1,0:T(8,128)(2,1)S(1)}, bf16[128,384]{1,0:T(8,128)(2,1)S(1)}, u32[]{:S(2)}, u32[]{:S(2)}) collective-permute-start(bf16[128,384]{1,0:T(8,128)(2,1)S(1)} %get-tuple-element.33), channel_id=1, source_target_pairs={{0,64},{32,96},{64,0},{96,32},{1,65},{33,97},{65,1},{97,33},{2,66}... | collective-permute-start | bytes 294920 | tf_op jit(solution)/shard_map/ppermute | solution.py:35
  186.1 8.5 %collective-permute-start.12 = (bf16[128,384]{1,0:T(8,128)(2,1)S(1)}, bf16[128,384]{1,0:T(8,128)(2,1)}, u32[]{:S(2)}, u32[]{:S(2)}) collective-permute-start(bf16[128,384]{1,0:T(8,128)(2,1)S(1)} %get-tuple-element.31), channel_id=1, source_target_pairs={{0,32},{32,64},{64,96},{96,0},{1,33},{33,65},{65,97},{97,1},{2,34}... | collective-permute-start | bytes 294920 | tf_op jit(solution)/shard_map/ppermute | solution.py:35
  188.0 50.8 %all-to-all-start.1 = ((bf16[16,128,128]{2,1,0:T(8,128)(2,1)}), bf16[16,128,128]{2,1,0:T(8,128)(2,1)S(1)}, u32[]{:S(2)}, u32[]{:S(2)}) async-start(bf16[16,128,128]{2,1,0:T(8,128)(2,1)} %bitcast.18), calls=%async_computation.1 | async-start | bytes 1048576 | tf_op jit(solution)/shard_map/all_to_all | solution.py:30
  192.5 15.4 %collective-permute-start.6 = (bf16[128,768]{0,1:T(8,128)(2,1)S(1)}, bf16[128,768]{0,1:T(8,128)(2,1)S(1)}, u32[]{:S(2)}, u32[]{:S(2)}) collective-permute-start(bf16[128,768]{0,1:T(8,128)(2,1)S(1)} %bitcast.125), channel_id=1, source_target_pairs={{0,8},{8,16},{16,24},{24,0},{1,9},{9,17},{17,25},{25,1},{2,10},{10... | collective-permute-start | bytes 589832 | tf_op jit(solution)/shard_map/ppermute | solution.py:35
  195.5 12.5 %collective-permute-start.17 = (bf16[128,384]{1,0:T(8,128)(2,1)S(1)}, bf16[128,384]{1,0:T(8,128)(2,1)S(1)}, u32[]{:S(2)}, u32[]{:S(2)}) collective-permute-start(bf16[128,384]{1,0:T(8,128)(2,1)S(1)} %fusion.19), channel_id=1, source_target_pairs={{0,24},{8,0},{16,8},{24,16},{1,25},{9,1},{17,9},{25,17},{2,26},{10... | collective-permute-start | bytes 294920 | tf_op jit(solution)/shard_map/ppermute | solution.py:35
  196.9 12.0 %collective-permute-start.16 = (bf16[128,384]{1,0:T(8,128)(2,1)S(1)}, bf16[128,384]{1,0:T(8,128)(2,1)S(1)}, u32[]{:S(2)}, u32[]{:S(2)}) collective-permute-start(bf16[128,384]{1,0:T(8,128)(2,1)S(1)} %fusion.19), channel_id=1, source_target_pairs={{0,16},{8,24},{16,0},{24,8},{1,17},{9,25},{17,1},{25,9},{2,18},{10... | collective-permute-start | bytes 294920 | tf_op jit(solution)/shard_map/ppermute | solution.py:35
  199.1 10.5 %collective-permute-start.15 = (bf16[128,384]{1,0:T(8,128)(2,1)S(1)}, bf16[128,384]{1,0:T(8,128)(2,1)S(1)}, u32[]{:S(2)}, u32[]{:S(2)}) collective-permute-start(bf16[128,384]{1,0:T(8,128)(2,1)S(1)} %fusion.19), channel_id=1, source_target_pairs={{0,8},{8,16},{16,24},{24,0},{1,9},{9,17},{17,25},{25,1},{2,10},{10... | collective-permute-start | bytes 294920 | tf_op jit(solution)/shard_map/ppermute | solution.py:35
  200.3 11.1 %collective-permute-start.26 = (bf16[4,2,3,8,128]{4,3,2,1,0:T(8,128)(2,1)}, bf16[4,2,3,8,128]{4,3,2,1,0:T(8,128)(2,1)}, u32[]{:S(2)}, u32[]{:S(2)}) collective-permute-start(bf16[4,2,3,8,128]{4,3,2,1,0:T(8,128)(2,1)} %bitcast.114), channel_id=1, source_target_pairs={{0,1},{1,0},{2,3},{3,2},{4,5},{5,4},{6,7},{7,6},{8,9},{9,8},{10,11... | collective-permute-start | bytes 147464 | tf_op jit(solution)/shard_map/ppermute | solution.py:35
  211.3 5.1 %collective-permute-start.18 = (bf16[4,2,4,12,384]{4,3,0,2,1:T(8,128)(2,1)S(1)}, bf16[4,2,4,12,384]{4,3,0,2,1:T(8,128)(2,1)S(1)}, u32[]{:S(2)}, u32[]{:S(2)}) collective-permute-start(bf16[4,2,4,12,384]{4,3,0,2,1:T(8,128)(2,1)S(1)} %dynamic-slice_bitcast_fusion), channel_id=1, source_target_pairs={{0,1},{1,0},{2,3},{3,2},{4,5},{5,4},{6,7},{7,6},{8,9},{9,8},{10,11... | collective-permute-start | bytes 884744 | tf_op jit(solution)/shard_map/ppermute | solution.py:35
  212.3 6.7 %collective-permute-start.29 = (bf16[2,3,8,128]{3,2,1,0:T(8,128)(2,1)S(1)}, bf16[2,3,8,128]{3,2,1,0:T(8,128)(2,1)S(1)}, u32[]{:S(2)}, u32[]{:S(2)}) collective-permute-start(bf16[2,3,8,128]{3,2,1,0:T(8,128)(2,1)S(1)} %get-tuple-element.35), channel_id=1, source_target_pairs={{0,6},{2,0},{4,2},{6,4},{1,7},{3,1},{5,3},{7,5},{8,14},{10,8},{12,... | collective-permute-start | bytes 36872 | tf_op jit(solution)/shard_map/ppermute | solution.py:35
  213.2 8.2 %collective-permute-start.28 = (bf16[2,3,8,128]{3,2,1,0:T(8,128)(2,1)S(1)}, bf16[2,3,8,128]{3,2,1,0:T(8,128)(2,1)S(1)}, u32[]{:S(2)}, u32[]{:S(2)}) collective-permute-start(bf16[2,3,8,128]{3,2,1,0:T(8,128)(2,1)S(1)} %get-tuple-element.36), channel_id=1, source_target_pairs={{0,4},{2,6},{4,0},{6,2},{1,5},{3,7},{5,1},{7,3},{8,12},{10,14},{12... | collective-permute-start | bytes 36872 | tf_op jit(solution)/shard_map/ppermute | solution.py:35
  214.3 7.1 %collective-permute-start.27 = (bf16[2,3,8,128]{3,2,1,0:T(8,128)(2,1)S(1)}, bf16[2,3,8,128]{3,2,1,0:T(8,128)(2,1)S(1)}, u32[]{:S(2)}, u32[]{:S(2)}) collective-permute-start(bf16[2,3,8,128]{3,2,1,0:T(8,128)(2,1)S(1)} %get-tuple-element.34), channel_id=1, source_target_pairs={{0,2},{2,4},{4,6},{6,0},{1,3},{3,5},{5,7},{7,1},{8,10},{10,12},{12... | collective-permute-start | bytes 36872 | tf_op jit(solution)/shard_map/ppermute | solution.py:35
  216.6 7.7 %collective-permute-start.21 = (bf16[2,4,12,384]{3,2,1,0:T(8,128)(2,1)S(1)}, bf16[2,4,12,384]{3,2,1,0:T(8,128)(2,1)S(1)}, u32[]{:S(2)}, u32[]{:S(2)}) collective-permute-start(bf16[2,4,12,384]{3,2,1,0:T(8,128)(2,1)S(1)} %get-tuple-element.25), channel_id=1, source_target_pairs={{0,6},{2,0},{4,2},{6,4},{1,7},{3,1},{5,3},{7,5},{8,14},{10,8},{12,... | collective-permute-start | bytes 221192 | tf_op jit(solution)/shard_map/ppermute | solution.py:35
  216.7 7.6 %collective-permute-start.20 = (bf16[2,4,12,384]{3,2,1,0:T(8,128)(2,1)S(1)}, bf16[2,4,12,384]{3,2,1,0:T(8,128)(2,1)S(1)}, u32[]{:S(2)}, u32[]{:S(2)}) collective-permute-start(bf16[2,4,12,384]{3,2,1,0:T(8,128)(2,1)S(1)} %get-tuple-element.26), channel_id=1, source_target_pairs={{0,4},{2,6},{4,0},{6,2},{1,5},{3,7},{5,1},{7,3},{8,12},{10,14},{12... | collective-permute-start | bytes 221192 | tf_op jit(solution)/shard_map/ppermute | solution.py:35
  219.0 5.9 %collective-permute-start.19 = (bf16[2,4,12,384]{3,2,1,0:T(8,128)(2,1)S(1)}, bf16[2,4,12,384]{3,2,1,0:T(8,128)(2,1)S(1)}, u32[]{:S(2)}, u32[]{:S(2)}) collective-permute-start(bf16[2,4,12,384]{3,2,1,0:T(8,128)(2,1)S(1)} %get-tuple-element.24), channel_id=1, source_target_pairs={{0,2},{2,4},{4,6},{6,0},{1,3},{3,5},{5,7},{7,1},{8,10},{10,12},{12... | collective-permute-start | bytes 221192 | tf_op jit(solution)/shard_map/ppermute | solution.py:35
  225.0 8.1 %collective-permute-start.22 = (bf16[4,12,384]{2,1,0:T(8,128)(2,1)S(1)}, bf16[4,12,384]{2,1,0:T(8,128)(2,1)S(1)}, u32[]{:S(2)}, u32[]{:S(2)}) collective-permute-start(bf16[4,12,384]{2,1,0:T(8,128)(2,1)S(1)} %fusion.25), channel_id=1, source_target_pairs={{0,128},{128,0},{1,129},{129,1},{2,130},{130,2},{3,131},{131,3},{4... | collective-permute-start | bytes 110600 | tf_op jit(solution)/shard_map/ppermute | solution.py:35
  228.7 9.5 %collective-permute-start.30 = (bf16[3,8,128]{2,1,0:T(8,128)(2,1)S(1)}, bf16[3,8,128]{2,1,0:T(8,128)(2,1)S(1)}, u32[]{:S(2)}, u32[]{:S(2)}) collective-permute-start(bf16[3,8,128]{2,1,0:T(8,128)(2,1)S(1)} %fusion.36), channel_id=1, source_target_pairs={{0,128},{128,0},{1,129},{129,1},{2,130},{130,2},{3,131},{131,3},{4... | collective-permute-start | bytes 18440 | tf_op jit(solution)/shard_map/ppermute | solution.py:35
  233.1 7.0 %collective-permute-start.25 = (bf16[12,384]{1,0:T(8,128)(2,1)S(1)}, bf16[12,384]{1,0:T(8,128)(2,1)S(1)}, u32[]{:S(2)}, u32[]{:S(2)}) collective-permute-start(bf16[12,384]{1,0:T(8,128)(2,1)S(1)} %get-tuple-element.40), channel_id=1, source_target_pairs={{0,96},{32,0},{64,32},{96,64},{1,97},{33,1},{65,33},{97,65},{2,98}... | collective-permute-start | bytes 27656 | tf_op jit(solution)/shard_map/ppermute | solution.py:35
  236.4 4.6 %collective-permute-start.24 = (bf16[12,384]{1,0:T(8,128)(2,1)S(1)}, bf16[12,384]{1,0:T(8,128)(2,1)S(1)}, u32[]{:S(2)}, u32[]{:S(2)}) collective-permute-start(bf16[12,384]{1,0:T(8,128)(2,1)S(1)} %get-tuple-element.41), channel_id=1, source_target_pairs={{0,64},{32,96},{64,0},{96,32},{1,65},{33,97},{65,1},{97,33},{2,66}... | collective-permute-start | bytes 27656 | tf_op jit(solution)/shard_map/ppermute | solution.py:35
  236.4 5.5 %collective-permute-start.23 = (bf16[12,384]{1,0:T(8,128)(2,1)S(1)}, bf16[12,384]{1,0:T(8,128)(2,1)S(1)}, u32[]{:S(2)}, u32[]{:S(2)}) collective-permute-start(bf16[12,384]{1,0:T(8,128)(2,1)S(1)} %get-tuple-element.39), channel_id=1, source_target_pairs={{0,32},{32,64},{64,96},{96,0},{1,33},{33,65},{65,97},{97,1},{2,34}... | collective-permute-start | bytes 27656 | tf_op jit(solution)/shard_map/ppermute | solution.py:35

commit v3 on v2

--- a/solution.py
+++ b/solution.py
@@ -54,10 +54,20 @@
     ]
 
 
-def reduced(value, axes):
-    for axis in axes:
-        value = summed_parts(parts_ahead(value, axis, 0), axis)
-    return value
+def summed_over_pair(value, slow, fast):
+    n_slow, n_fast = lax.axis_size(slow), lax.axis_size(fast)
+    total = None
+    for ds, across in enumerate(parts_ahead(value, slow, 0)):
+        for df, part in enumerate(parts_ahead(across, fast, 0)):
+            if ds or df:
+                pairs = [
+                    (i * n_fast + j, (i + ds) % n_slow * n_fast + (j + df) % n_fast)
+                    for i in range(n_slow)
+                    for j in range(n_fast)
+                ]
+                part = lax.ppermute(part.astype(BF), (slow, fast), pairs)
+            total = part.astype(F32) if total is None else total + part.astype(F32)
+    return total
 
 
 def pack_kernel(q_ref, k_ref, v_ref, out_ref):
@@ -90,22 +100,59 @@
     return raised.astype(BF), highest, total
 
 
-def forward_kernel(
-    place_ref, scale_ref, inv_ref, heads_ref, up_ref, *refs
-):
-    low_refs, (out_ref, upstream_ref, student_ref, stats_ref, keys_ref) = refs[:-5], refs[-5:]
-    pass_tok, rows = heads_ref.shape[1], heads_ref.shape[3]
-    tokens = pass_tok * rows
-    n_fast, n_slow = len(low_refs), low_refs[0].shape[0]
+def teacher_kernel(scale_ref, heads_ref, target_ref, keys_ref):
+    blocks, rows = heads_ref.shape[1], heads_ref.shape[3]
+    tokens = blocks * rows
+    scale = scale_ref[0]
+    for one in range(2):
+        for part in range(3):
+            for block in range(blocks):
+                keys_ref[one, part, block * rows : (block + 1) * rows] = heads_ref[one, block, part]
+    step_rows = 256
+
+    def one_block(step, carry):
+        here = pl.ds(pl.multiple_of(step * step_rows, step_rows), step_rows)
+        outs = []
+        for one in range(2):
+            raised, _, total = softmax_rows(keys_ref[one, 0, here], keys_ref[one, 1])
+            attended = dot(raised, keys_ref[one, 2]) / total
+            outs.append(attended.astype(BF).astype(F32))
+        target_ref[here] = outs[1] + scale * (outs[0] - outs[1])
+        return carry
+
+    lax.fori_loop(0, tokens // step_rows, one_block, 0)
+
+
+def teacher(scale, heads):
+    tokens = heads.shape[1] * heads.shape[3]
+    vmem = pl.BlockSpec(memory_space=pltpu.VMEM)
+    return pl.pallas_call(
+        teacher_kernel,
+        in_specs=[pl.BlockSpec(memory_space=pltpu.SMEM), vmem],
+        out_specs=vmem,
+        out_shape=jax.ShapeDtypeStruct((tokens, HDIM), F32),
+        scratch_shapes=[pltpu.VMEM((2, 3, tokens, HDIM), BF)],
+        cost_estimate=pl.CostEstimate(
+            flops=8 * tokens * tokens * HDIM,
+            transcendentals=2 * tokens * tokens,
+            bytes_accessed=4 * MIB,
+        ),
+        compiler_params=pltpu.CompilerParams(vmem_limit_bytes=48 * MIB),
+        name="teacher_forward",
+    )(scale, heads)
+
+
+def student_kernel(n_fast, place_ref, inv_ref, heads_ref, target_ref, up_ref, *refs):
+    low_refs = refs[:n_fast]
+    out_ref, upstream_ref, student_ref, stats_ref = refs[n_fast:]
+    rows = heads_ref.shape[3]
+    tokens = out_ref.shape[0]
+    n_slow = low_refs[0].shape[0]
     here_slow, here_fast = place_ref[0], place_ref[1]
-    scale = scale_ref[0]
     inverse = inv_ref[0]
 
     for part in range(3):
         up = up_ref[part]
-        for block in range(pass_tok):
-            for one in range(2):
-                keys_ref[one, part, block * rows : (block + 1) * rows] = heads_ref[one, block, part]
         for fast in range(n_fast):
             for slow in range(n_slow):
                 block = lax.rem(here_slow - slow + n_slow, n_slow) * n_fast + lax.rem(
@@ -116,22 +163,15 @@
                 frozen = heads_ref[0, block, part].astype(F32)
                 where = pl.ds(pl.multiple_of(block * rows, rows), rows)
                 student_ref[part, where] = (frozen + adapted).astype(BF)
-
     step_rows = 256
 
     def one_block(step, carry):
         here = pl.ds(pl.multiple_of(step * step_rows, step_rows), step_rows)
-        outs = []
-        for one in range(2):
-            raised, _, total = softmax_rows(keys_ref[one, 0, here], keys_ref[one, 1])
-            attended = dot(raised, keys_ref[one, 2]) / total
-            outs.append(attended.astype(BF).astype(F32))
         raised, highest, total = softmax_rows(student_ref[0, here], student_ref[1])
         attended = dot(raised, student_ref[2]) / total
         rounded = attended.astype(BF)
         out_ref[here] = rounded
-        target = outs[1] + scale * (outs[0] - outs[1])
-        upstream = ((rounded.astype(F32) - target) * inverse).astype(BF)
+        upstream = ((rounded.astype(F32) - target_ref[here]) * inverse).astype(BF)
         upstream_ref[here] = upstream
         level = highest * SCALE2 + jnp.log2(total)
         center = jnp.sum(attended * upstream.astype(F32), axis=-1, keepdims=True)
@@ -143,13 +183,16 @@
     lax.fori_loop(0, tokens // step_rows, one_block, 0)
 
 
-def forward(place, scale, inverse, heads, up, low):
-    tokens = heads.shape[1] * heads.shape[3]
+def student_forward(place, inverse, heads, target, up, low):
+    tokens = target.shape[0]
+    one_pass = (1, *heads.shape[1:])
     vmem = pl.BlockSpec(memory_space=pltpu.VMEM)
     smem = pl.BlockSpec(memory_space=pltpu.SMEM)
     return pl.pallas_call(
-        forward_kernel,
-        in_specs=[smem] * 3 + [vmem] * (2 + len(low)),
+        functools.partial(student_kernel, len(low)),
+        grid=(1,),
+        in_specs=[smem, smem, pl.BlockSpec(one_pass, lambda i: (0, 0, 0, 0, 0))]
+        + [vmem] * (2 + len(low)),
         out_specs=[vmem] * 4,
         out_shape=[
             jax.ShapeDtypeStruct((tokens, HDIM), BF),
@@ -157,15 +200,14 @@
             jax.ShapeDtypeStruct((3, tokens, HDIM), BF),
             jax.ShapeDtypeStruct((8, tokens), F32),
         ],
-        scratch_shapes=[pltpu.VMEM((2, 3, tokens, HDIM), BF)],
         cost_estimate=pl.CostEstimate(
-            flops=12 * tokens * tokens * HDIM,
-            transcendentals=3 * tokens * tokens,
-            bytes_accessed=8 * MIB,
-        ),
-        compiler_params=pltpu.CompilerParams(vmem_limit_bytes=56 * MIB),
-        name="attention_forward",
-    )(place, scale, inverse, heads, up, *low)
+            flops=4 * tokens * tokens * HDIM,
+            transcendentals=tokens * tokens,
+            bytes_accessed=6 * MIB,
+        ),
+        compiler_params=pltpu.CompilerParams(vmem_limit_bytes=48 * MIB),
+        name="student_forward",
+    )(place, inverse, heads, target, up, *low)
 
 
 def backward_kernel(
@@ -267,35 +309,46 @@
 
     low = jnp.einsum("cl,elj->cej", features, adapter_down_weight, preferred_element_type=F32)
     low = (low * modulation).astype(BF).reshape(rows, 3 * RANK)
-    low_all = from_each(jnp.stack(from_each(low, "z")), "y")
+    low_slow = jnp.stack(from_each(low, "z"))
 
     groups = n_cfg * n_slow
     part_cols = width // (groups * n_fast)
     spread = parts_ahead(features.reshape(rows, groups, n_fast, part_cols), "y", 2)
     spread = [part.reshape(rows, groups * part_cols) for part in spread]
-    columns = jnp.concatenate(
-        [spread[0]] + [shifted(spread[d], "y", d) for d in range(1, n_fast)]
-    )
+    columns = [spread[0]] + [shifted(spread[d], "y", d) for d in range(1, n_fast)]
 
     place = jnp.stack([lax.axis_index("z"), lax.axis_index("y")]).astype(jnp.int32)
     up = lax.dynamic_slice_in_dim(adapter_up_weight, seq_index * HDIM, HDIM, 2)
     inverse = jnp.full((1,), 1.0 / math.sqrt(total_rows), F32)
-    out, upstream, student, stats = forward(place, scale, inverse, heads, up, low_all)
+
+    heads, low_slow, up, place, *columns = lax.optimization_barrier(
+        (heads, low_slow, up, place, *columns)
+    )
+    low_all = from_each(low_slow, "y")
+    target = teacher(scale, heads)
+    target, *low_all = lax.optimization_barrier((target, *low_all))
+    out, upstream, student, stats = student_forward(place, inverse, heads, target, up, low_all)
     tokens_out = exchange(out.reshape(n_slow * n_fast, rows, HDIM), ("z", "y"))
+
+    *back, up_partial = backward(place, student, upstream, stats, up, low_all)
+    tokens_out, up_partial, *back = lax.optimization_barrier((tokens_out, up_partial, *back))
     student_out = jnp.moveaxis(tokens_out, 0, 1).reshape(rows, -1)
 
-    *back, up_partial = backward(place, student, upstream, stats, up, low_all)
+    owners = n_cfg * n_x * n_core
+    up_blocks = jnp.moveaxis(up_partial.reshape(3, owners, RANK // owners, HDIM), 1, 0)
+    grad_up = exchange(up_blocks, ("cfg", "x", "core"))
+
     back = summed_parts(back, "y").astype(BF)
     back = summed_parts([back[d] for d in range(n_slow)], "z")
     low_grad = (back.reshape(rows, 3, RANK) * modulation).astype(BF).reshape(rows, 3 * RANK)
+    low_grad, grad_up = lax.optimization_barrier((low_grad, grad_up))
+    grad_up = grad_up.astype(F32).sum(axis=0)
     low_grads = jnp.concatenate(from_each(low_grad, "y"))
-    down = dot(columns, low_grads, TN).astype(BF)
-    down = down.reshape(n_cfg, n_slow, n_x, n_core, -1, 3 * RANK).transpose(3, 2, 0, 1, 4, 5)
-    down = reduced(down, ("core", "x", "cfg", "z"))
+    down = dot(jnp.concatenate(columns), low_grads, TN).astype(BF)
+    down = down.reshape(n_cfg, n_slow, n_x, n_core, -1, 3 * RANK).transpose(2, 3, 0, 1, 4, 5)
+    down = summed_over_pair(down, "x", "core")
+    down = summed_over_pair(down, "cfg", "z")
     grad_down = jnp.moveaxis(down.reshape(-1, 3, RANK), 1, 0)
-
-    up_blocks = up_partial.reshape(3, n_cfg, n_x, n_core, -1, HDIM).transpose(3, 2, 1, 0, 4, 5)
-    grad_up = reduced(up_blocks, ("core", "x", "cfg"))
     return student_out[None, None], grad_down, grad_up
 
 

time: 244 us -> 249 us (1.020)
  waiting for transfers between devices: 110 us -> 90.4 us
  starting transfers between devices: 63.6 us -> 83.1 us
  Pallas kernels: 47.3 us -> 50.3 us
  local copies, waits for them, and re-layouts: 10.2 us -> 12.8 us
    ppermute x31 -> x18, waiting for transfers between devices: 110 us -> 72 us  [shifted(): lax.ppermute(value, axis, [(i, (i + distance) % size) for i in range(size)])]
    ppermute x0 -> x14, starting transfers between devices: none -> 20.7 us  [summed_over_pair(): part = lax.ppermute(part.astype(BF), (slow, fast), pairs)]
    ppermute x31 -> x18, starting transfers between devices: 47.5 us -> 34.2 us  [shifted(): lax.ppermute(value, axis, [(i, (i + distance) % size) for i in range(size)])]
    all_to_all x2 -> x3, starting transfers between devices: 16.1 us -> 28.2 us  [exchange(): return lax.all_to_all(value, axes, split_axis=0, concat_axis=0, tiled=True)]
    ppermute x0 -> x14, waiting for transfers between devices: none -> 10.2 us  [summed_over_pair(): part = lax.ppermute(part.astype(BF), (slow, fast), pairs)]
    all_to_all x2 -> x3, waiting for transfers between devices: 0.01 us -> 8.19 us  [exchange(): return lax.all_to_all(value, axes, split_axis=0, concat_axis=0, tiled=True)]
    pallas_call x1 -> x2, Pallas kernels: 26.1 us -> 29.2 us  [the longest x1 16.6 us: teacher(): pl.pallas_call(teacher_kernel, in_specs=[pl.BlockSpec(memory_space=pltpu....]
    unnamed x22 -> x41, local copies, waits for them, and re-layouts: 6.81 us -> 8.09 us
  transfers between devices with their start and end apart: 33 -> 35, of which waited for: 14 -> 13; matrix products, arithmetic and copies ran while one was open for 8% -> 5% of each run, Pallas kernels for 0% -> 14%
where the time goes in v3:
time: 249 us; the launch traced here: 248 us
  waiting for transfers between devices  90.4 us (36%)
  starting transfers between devices  83.1 us (33%)
  Pallas kernels  50.3 us (20%)
  local copies, waits for them, and re-layouts  12.8 us (5%)
  other arithmetic  4.88 us (2%)
  matrix products  4.22 us (2%)
    ppermute x18, waiting for transfers between devices, shifted(): lax.ppermute(value, axis, [(i, (i + distance) % size) for i in range(size)])  72 us
    ppermute x18, starting transfers between devices, shifted(): lax.ppermute(value, axis, [(i, (i + distance) % size) for i in range(size)])  34.2 us
    all_to_all x3, starting transfers between devices, exchange(): return lax.all_to_all(value, axes, split_axis=0, concat_axis=0, tiled=True)  28.2 us
    ppermute x14, starting transfers between devices, summed_over_pair(): part = lax.ppermute(part.astype(BF), (slow, fast), pairs)  20.7 us
    pallas_call x1, Pallas kernels, backward(): pl.pallas_call(functools.partial(backward_kernel, n_fast), in_specs=[pl.B...  17.8 us
    pallas_call x1, Pallas kernels, teacher(): pl.pallas_call(teacher_kernel, in_specs=[pl.BlockSpec(memory_space=pltpu....  16.6 us
    pallas_call x1, Pallas kernels, student_forward(): pl.pallas_call(functools.partial(student_kernel, len(low)), grid=(1,), in...  12.5 us
    ppermute x14, waiting for transfers between devices, summed_over_pair(): part = lax.ppermute(part.astype(BF), (slow, fast), pairs)  10.2 us
  transfers between devices with their start and end apart: 35, of which 13 were waited for; matrix products, arithmetic and copies ran while one was open for 5% of the time, Pallas kernels for 14%

profile of v3, /device:TPU:6, one launch (start us, length us, event | category | flops | bytes accessed | tf_op | source)
XLA Modules:
  0.0 248.1 jit_solution(4171009252688316989)
XLA Ops:
  0.6 3.4 %pack_heads.1 = bf16[32,3,128,128]{3,2,1,0:T(8,128)(2,1)} custom-call(bf16[2,128,2048]{2,1,0:T(8,128)(2,1)} %bitcast.96, bf16[2,128,2048]{2,1,0:T(8,128)(2,1)} %bitcast.97, bf16[2,128,2048]{2,1,0:T(8,128)(2,1)} %bitcast.98), custom_call_target="tpu_custom_call" | custom-call | bytes 6291456 | tf_op jit(solution)/shard_map/pack_heads/pallas_call | solution.py:84
  4.1 11.7 %all-to-all-start = ((bf16[32,3,128,128]{3,2,1,0:T(8,128)(2,1)}), bf16[32,3,128,128]{3,2,1,0:T(8,128)(2,1)}, u32[]{:S(2)}, u32[]{:S(2)}) async-start(bf16[32,3,128,128]{3,2,1,0:T(8,128)(2,1)} %pack_heads.1), calls=%async_computation | async-start | bytes 6291456 | tf_op jit(solution)/shard_map/all_to_all | solution.py:30
  17.7 4.4 %copy.23 = bf16[3,3072,128]{1,2,0:T(8,128)(2,1)} copy(bf16[3,3072,128]{2,1,0:T(8,128)(2,1)} %param.12) | data formatting | bytes 4718592 | tf_op args[4]
  22.2 2.4 fusion.7
  25.5 1.7 collective-permute-start
  27.3 2.4 collective-permute-start.1
  29.6 1.5 collective-permute-start.2
  32.3 1.5 collective-permute-start.3
  33.8 2.7 %collective-permute-start.4 = (bf16[128,768]{0,1:T(8,128)(2,1)}, bf16[128,768]{0,1:T(8,128)(2,1)S(1)}, u32[]{:S(2)}, u32[]{:S(2)}) collective-permute-start(bf16[128,768]{0,1:T(8,128)(2,1)} %bitcast.21), channel_id=1, source_target_pairs={{0,16},{8,24},{16,0},{24,8},{1,17},{9,25},{17,1},{25,9},{2,18},{10... | collective-permute-start | bytes 589832 | tf_op jit(solution)/shard_map/ppermute | solution.py:35
  36.6 52.9 %collective-permute-done = bf16[128,384]{1,0:T(8,128)(2,1)S(1)} collective-permute-done((bf16[128,384]{1,0:T(8,128)(2,1)}, bf16[128,384]{1,0:T(8,128)(2,1)S(1)}, u32[]{:S(2)}, u32[]{:S(2)}) %collective-permute-start) | collective-permute-done | bytes 98336 | tf_op jit(solution)/shard_map/ppermute | solution.py:35
  89.5 2.7 %collective-permute-start.5 = (bf16[128,768]{0,1:T(8,128)(2,1)S(1)}, bf16[128,768]{0,1:T(8,128)(2,1)S(1)}, u32[]{:S(2)}, u32[]{:S(2)}) collective-permute-start(bf16[128,768]{0,1:T(8,128)(2,1)S(1)} %bitcast.103), channel_id=1, source_target_pairs={{0,24},{8,0},{16,8},{24,16},{1,25},{9,1},{17,9},{25,17},{2,26},{10... | collective-permute-start | bytes 589832 | tf_op jit(solution)/shard_map/ppermute | solution.py:35
  92.3 1.4 collective-permute-done.1
  95.4 1.3 collective-permute-start.6
  96.6 3.9 %collective-permute-start.7 = (bf16[4,128,384]{2,1,0:T(8,128)(2,1)S(1)}, bf16[4,128,384]{2,1,0:T(8,128)(2,1)S(1)}, u32[]{:S(2)}, u32[]{:S(2)}) collective-permute-start(bf16[4,128,384]{2,1,0:T(8,128)(2,1)S(1)} %pad_maximum_fusion.refs_0_), channel_id=1, source_target_pairs={{0,16},{8,24},{16,0},{24,8},{1,17},{9,25},{17,1},{25,9},{2,18},{10... | collective-permute-start | bytes 1179656 | tf_op jit(solution)/shard_map/ppermute | solution.py:35
  100.8 16.6 %teacher_forward.1.target_ref = f32[2048,128]{1,0:T(8,128)S(1)} custom-call(f32[1]{0:T(128)} %bitcast.9.scale_ref, bf16[2,16,3,128,128]{4,3,2,1,0:T(8,128)(2,1)} %bitcast.3.heads_ref), custom_call_target="tpu_custom_call" | custom-call | flops 4294967296 | bytes 4194304 | tf_op jit(solution)/shard_map/teacher_forward/pallas_call | solution.py:129
  117.6 12.5 %student_forward.1 = (bf16[2048,128]{1,0:T(8,128)(2,1)}, bf16[2048,128]{1,0:T(8,128)(2,1)S(1)}, bf16[3,2048,128]{2,1,0:T(8,128)(2,1)S(1)}, f32[8,2048]{1,0:T(8,128)S(1)}) custom-call(s32[2]{0:T(128)S(1)} %pad_add_fusion.place_ref, f32[1]{0:T(128)} %constant.597.clone.1.inv_ref, bf16[2,16,3,128,128]{4,3,2,1,0:T(8,128)(2,1)} %bitcast.3.heads_ref, ...), custom_call_target="tpu_custom_call" | custom-call | flops 2147483648 | bytes 6291456 | tf_op jit(solution)/shard_map/student_forward/pallas_call | solution.py:191
  130.1 1.2 copy-done.7
  132.7 6.1 %all-to-all-start.1 = ((bf16[16,128,128]{2,1,0:T(8,128)(2,1)}), bf16[16,128,128]{2,1,0:T(8,128)(2,1)S(1)}, u32[]{:S(2)}, u32[]{:S(2)}) async-start(bf16[16,128,128]{2,1,0:T(8,128)(2,1)} %bitcast.23), calls=%async_computation.1 | async-start | bytes 1048576 | tf_op jit(solution)/shard_map/all_to_all | solution.py:30
  138.8 17.8 %attention_backward.1 = (bf16[4,128,384]{2,1,0:T(8,128)(2,1)}, bf16[4,128,384]{2,1,0:T(8,128)(2,1)}, bf16[4,128,384]{2,1,0:T(8,128)(2,1)}, bf16[4,128,384]{2,1,0:T(8,128)(2,1)}, bf16[3,128,128]{2,1,0:T(8,128)(2,1)}) custom-call(s32[2]{0:T(128)} %copy-done.6, bf16[3,2048,128]{2,1,0:T(8,128)(2,1)} %copy-done.7, bf16[2048,128]{1,0:T(8,128)(2,1)} %copy-done.8, ...), custom_call_target="tpu_custom_call" | custom-call | flops 5368709120 | bytes 6291456 | tf_op jit(solution)/shard_map/attention_backward/pallas_call | solution.py:263
  156.6 3.5 %collective-permute-start.10 = (bf16[4,128,384]{2,1,0:T(8,128)(2,1)}, bf16[4,128,384]{2,1,0:T(8,128)(2,1)S(1)}, u32[]{:S(2)}, u32[]{:S(2)}) collective-permute-start(bf16[4,128,384]{2,1,0:T(8,128)(2,1)} %get-tuple-element.58), channel_id=1, source_target_pairs={{0,16},{8,24},{16,0},{24,8},{1,17},{9,25},{17,1},{25,9},{2,18},{10... | collective-permute-start | bytes 1179656 | tf_op jit(solution)/shard_map/ppermute | solution.py:35
  160.1 1.2 collective-permute-start.11
  162.1 8.3 %collective-permute-done.10 = bf16[4,128,384]{2,1,0:T(8,128)(2,1)S(1)} collective-permute-done((bf16[4,128,384]{2,1,0:T(8,128)(2,1)}, bf16[4,128,384]{2,1,0:T(8,128)(2,1)S(1)}, u32[]{:S(2)}, u32[]{:S(2)}) %collective-permute-start.10) | collective-permute-done | bytes 393248 | tf_op jit(solution)/shard_map/ppermute | solution.py:35
  170.5 5.2 %collective-permute-done.11 = bf16[4,128,384]{2,1,0:T(8,128)(2,1)S(1)} collective-permute-done((bf16[4,128,384]{2,1,0:T(8,128)(2,1)}, bf16[4,128,384]{2,1,0:T(8,128)(2,1)S(1)}, u32[]{:S(2)}, u32[]{:S(2)}) %collective-permute-start.11) | collective-permute-done | bytes 393248 | tf_op jit(solution)/shard_map/ppermute | solution.py:35
  175.7 1.2 add_convert_fusion
  176.9 1.5 collective-permute-start.12
  178.5 2.4 collective-permute-start.13
  180.9 1.5 collective-permute-start.14
  183.0 10.3 %all-to-all-start.2 = ((bf16[16,3,8,128]{3,2,1,0:T(8,128)(2,1)}), bf16[16,3,8,128]{3,2,1,0:T(8,128)(2,1)S(1)}, u32[]{:S(2)}, u32[]{:S(2)}) async-start(bf16[16,3,8,128]{3,2,1,0:T(8,128)(2,1)} %copy_bitcast_fusion), calls=%async_computation.2 | async-start | bytes 196608 | tf_op jit(solution)/shard_map/all_to_all | solution.py:30
  193.4 8.2 %all-to-all-done.2 = bf16[16,3,8,128]{3,2,1,0:T(8,128)(2,1)S(1)} async-done(((bf16[16,3,8,128]{3,2,1,0:T(8,128)(2,1)}), bf16[16,3,8,128]{3,2,1,0:T(8,128)(2,1)S(1)}, u32[]{:S(2)}, u32[]{:S(2)}) %all-to-all-start.2) | async-done | bytes 98336 | tf_op jit(solution)/shard_map/all_to_all | solution.py:30
  201.6 1.5 collective-permute-start.15
  203.0 2.6 %collective-permute-start.16 = (bf16[128,384]{1,0:T(8,128)(2,1)S(1)}, bf16[128,384]{1,0:T(8,128)(2,1)S(1)}, u32[]{:S(2)}, u32[]{:S(2)}) collective-permute-start(bf16[128,384]{1,0:T(8,128)(2,1)S(1)} %fusion.25), channel_id=1, source_target_pairs={{0,16},{8,24},{16,0},{24,8},{1,17},{9,25},{17,1},{25,9},{2,18},{10... | collective-permute-start | bytes 294920 | tf_op jit(solution)/shard_map/ppermute | solution.py:35
  205.7 1.5 collective-permute-start.17
  207.6 3.0 %collective-permute-done.16 = bf16[128,384]{1,0:T(8,128)(2,1)S(1)} collective-permute-done((bf16[128,384]{1,0:T(8,128)(2,1)S(1)}, bf16[128,384]{1,0:T(8,128)(2,1)S(1)}, u32[]{:S(2)}, u32[]{:S(2)}) %collective-permute-start.16) | collective-permute-done | bytes 98336 | tf_op jit(solution)/shard_map/ppermute | solution.py:35
  210.6 1.8 convolution_convert_fusion
  213.3 1.9 collective-permute-start.19
  215.6 1.7 collective-permute-start.21
  217.2 1.5 collective-permute-start.22
  218.7 1.5 collective-permute-start.23
  220.4 4.0 %collective-permute-done.20 = bf16[2,4,12,384]{3,2,1,0:T(8,128)(2,1)} collective-permute-done((bf16[2,4,12,384]{3,2,1,0:T(8,128)(2,1)}, bf16[2,4,12,384]{3,2,1,0:T(8,128)(2,1)}, u32[]{:S(2)}, u32[]{:S(2)}) %collective-permute-start.20) | collective-permute-done | bytes 73760 | tf_op jit(solution)/shard_map/ppermute | solution.py:68
  224.3 2.3 collective-permute-done.23
  226.6 2.0 collective-permute-done.24
  228.6 1.2 fusion.21
  229.9 1.7 collective-permute-start.25
  231.9 1.0 broadcast_in_dim_reshape.3
  232.9 2.5 collective-permute-start.27
  235.9 4.2 %collective-permute-start.29 = (bf16[12,384]{1,0:T(8,128)(2,1)S(1)}, bf16[12,384]{1,0:T(8,128)(2,1)S(1)}, u32[]{:S(2)}, u32[]{:S(2)}) collective-permute-start(bf16[12,384]{1,0:T(8,128)(2,1)S(1)} %get-tuple-element.86), channel_id=1, source_target_pairs={{0,160},{32,192},{64,224},{96,128},{128,32},{160,64},{192,96},{224... | collective-permute-start | bytes 27656 | tf_op jit(solution)/shard_map/ppermute | solution.py:68
  240.7 4.1 %collective-permute-start.31 = (bf16[12,384]{1,0:T(8,128)(2,1)S(1)}, bf16[12,384]{1,0:T(8,128)(2,1)S(1)}, u32[]{:S(2)}, u32[]{:S(2)}) collective-permute-start(bf16[12,384]{1,0:T(8,128)(2,1)S(1)} %get-tuple-element.84), channel_id=1, source_target_pairs={{0,224},{32,128},{64,160},{96,192},{128,96},{160,0},{192,32},{224,... | collective-permute-start | bytes 27656 | tf_op jit(solution)/shard_map/ppermute | solution.py:68
  246.0 1.5 collective-permute-done.31
  (92 shorter events, 13.2 us)
Async XLA Ops:
  0.6 36.0 %copy-start = (bf16[3,128,2048]{2,1,0:T(8,128)(2,1)S(1)}, bf16[3,128,2048]{2,1,0:T(8,128)(2,1)}, u32[]{:S(2)}) copy-start(bf16[3,128,2048]{2,1,0:T(8,128)(2,1)} %param.13) | copy-start | bytes 4718596
  4.1 11.8 %copy-start.15 = (s32[2,1]{0,1:T(1,128)S(1)}, s32[2,1]{0,1:T(1,128)}, u32[]{:S(2)}) copy-start(s32[2,1]{0,1:T(1,128)} %param.14) | copy-start | bytes 28
  4.1 91.3 %all-to-all-start = ((bf16[32,3,128,128]{3,2,1,0:T(8,128)(2,1)}), bf16[32,3,128,128]{3,2,1,0:T(8,128)(2,1)}, u32[]{:S(2)}, u32[]{:S(2)}) async-start(bf16[32,3,128,128]{3,2,1,0:T(8,128)(2,1)} %pack_heads.1), calls=%async_computation | async-start | bytes 6291456 | tf_op jit(solution)/shard_map/all_to_all | solution.py:30
  25.5 64.0 %collective-permute-start = (bf16[128,384]{1,0:T(8,128)(2,1)}, bf16[128,384]{1,0:T(8,128)(2,1)S(1)}, u32[]{:S(2)}, u32[]{:S(2)}) collective-permute-start(bf16[128,384]{1,0:T(8,128)(2,1)} %copy.24), channel_id=1, source_target_pairs={{0,32},{32,64},{64,96},{96,0},{1,33},{33,65},{65,97},{97,1},{2,34}... | collective-permute-start | bytes 294920 | tf_op jit(solution)/shard_map/ppermute | solution.py:35
  27.3 66.4 %collective-permute-start.1 = (bf16[128,384]{1,0:T(8,128)(2,1)}, bf16[128,384]{1,0:T(8,128)(2,1)}, u32[]{:S(2)}, u32[]{:S(2)}) collective-permute-start(bf16[128,384]{1,0:T(8,128)(2,1)} %copy.24), channel_id=1, source_target_pairs={{0,64},{32,96},{64,0},{96,32},{1,65},{33,97},{65,1},{97,33},{2,66}... | collective-permute-start | bytes 294920 | tf_op jit(solution)/shard_map/ppermute | solution.py:35
  29.6 64.0 %collective-permute-start.2 = (bf16[128,384]{1,0:T(8,128)(2,1)}, bf16[128,384]{1,0:T(8,128)(2,1)}, u32[]{:S(2)}, u32[]{:S(2)}) collective-permute-start(bf16[128,384]{1,0:T(8,128)(2,1)} %copy.24), channel_id=1, source_target_pairs={{0,96},{32,0},{64,32},{96,64},{1,97},{33,1},{65,33},{97,65},{2,98}... | collective-permute-start | bytes 294920 | tf_op jit(solution)/shard_map/ppermute | solution.py:35
  32.3 62.4 %collective-permute-start.3 = (bf16[128,768]{0,1:T(8,128)(2,1)}, bf16[128,768]{0,1:T(8,128)(2,1)S(1)}, u32[]{:S(2)}, u32[]{:S(2)}) collective-permute-start(bf16[128,768]{0,1:T(8,128)(2,1)} %bitcast.20), channel_id=1, source_target_pairs={{0,8},{8,16},{16,24},{24,0},{1,9},{9,17},{17,25},{25,1},{2,10},{10... | collective-permute-start | bytes 589832 | tf_op jit(solution)/shard_map/ppermute | solution.py:35
  33.8 60.9 %collective-permute-start.4 = (bf16[128,768]{0,1:T(8,128)(2,1)}, bf16[128,768]{0,1:T(8,128)(2,1)S(1)}, u32[]{:S(2)}, u32[]{:S(2)}) collective-permute-start(bf16[128,768]{0,1:T(8,128)(2,1)} %bitcast.21), channel_id=1, source_target_pairs={{0,16},{8,24},{16,0},{24,8},{1,17},{9,25},{17,1},{25,9},{2,18},{10... | collective-permute-start | bytes 589832 | tf_op jit(solution)/shard_map/ppermute | solution.py:35
  36.6 80.9 %copy-start.2 = (bf16[3,128,128]{2,1,0:T(8,128)(2,1)}, bf16[3,128,128]{2,1,0:T(8,128)(2,1)S(1)}, u32[]{:S(2)}) copy-start(bf16[3,128,128]{2,1,0:T(8,128)(2,1)S(1)} %constant_dynamic-slice_fusion.4.up_ref) | copy-start | bytes 294916
  89.5 5.9 %collective-permute-start.5 = (bf16[128,768]{0,1:T(8,128)(2,1)S(1)}, bf16[128,768]{0,1:T(8,128)(2,1)S(1)}, u32[]{:S(2)}, u32[]{:S(2)}) collective-permute-start(bf16[128,768]{0,1:T(8,128)(2,1)S(1)} %bitcast.103), channel_id=1, source_target_pairs={{0,24},{8,0},{16,8},{24,16},{1,25},{9,1},{17,9},{25,17},{2,26},{10... | collective-permute-start | bytes 589832 | tf_op jit(solution)/shard_map/ppermute | solution.py:35
  92.3 25.3 %copy-start.6 = (s32[2]{0:T(128)}, s32[2]{0:T(128)S(1)}, u32[]{:S(2)}) copy-start(s32[2]{0:T(128)S(1)} %pad_add_fusion.place_ref) | copy-start | bytes 28
  94.7 22.9 %copy-start.1 = (bf16[4,128,384]{2,1,0:T(8,128)(2,1)}, bf16[4,128,384]{2,1,0:T(8,128)(2,1)S(1)}, u32[]{:S(2)}) copy-start(bf16[4,128,384]{2,1,0:T(8,128)(2,1)S(1)} %pad_maximum_fusion.refs_0_) | copy-start | bytes 1179652
  94.7 22.8 %copy-start.16 = (bf16[128,768]{0,1:T(8,128)(2,1)}, bf16[128,768]{0,1:T(8,128)(2,1)S(1)}, u32[]{:S(2)}) copy-start(bf16[128,768]{0,1:T(8,128)(2,1)S(1)} %collective-permute-done.3) | copy-start | bytes 589828
  94.7 22.8 %copy-start.17 = (bf16[128,768]{0,1:T(8,128)(2,1)}, bf16[128,768]{0,1:T(8,128)(2,1)S(1)}, u32[]{:S(2)}) copy-start(bf16[128,768]{0,1:T(8,128)(2,1)S(1)} %collective-permute-done.4) | copy-start | bytes 589828
  95.4 22.1 %copy-start.18 = (bf16[128,768]{0,1:T(8,128)(2,1)}, bf16[128,768]{0,1:T(8,128)(2,1)S(1)}, u32[]{:S(2)}) copy-start(bf16[128,768]{0,1:T(8,128)(2,1)S(1)} %collective-permute-done.5) | copy-start | bytes 589828
  95.4 22.1 %collective-permute-start.6 = (bf16[4,128,384]{2,1,0:T(8,128)(2,1)S(1)}, bf16[4,128,384]{2,1,0:T(8,128)(2,1)S(1)}, u32[]{:S(2)}, u32[]{:S(2)}) collective-permute-start(bf16[4,128,384]{2,1,0:T(8,128)(2,1)S(1)} %pad_maximum_fusion.refs_0_), channel_id=1, source_target_pairs={{0,8},{8,16},{16,24},{24,0},{1,9},{9,17},{17,25},{25,1},{2,10},{10... | collective-permute-start | bytes 1179656 | tf_op jit(solution)/shard_map/ppermute | solution.py:35
  96.6 20.9 %collective-permute-start.7 = (bf16[4,128,384]{2,1,0:T(8,128)(2,1)S(1)}, bf16[4,128,384]{2,1,0:T(8,128)(2,1)S(1)}, u32[]{:S(2)}, u32[]{:S(2)}) collective-permute-start(bf16[4,128,384]{2,1,0:T(8,128)(2,1)S(1)} %pad_maximum_fusion.refs_0_), channel_id=1, source_target_pairs={{0,16},{8,24},{16,0},{24,8},{1,17},{9,25},{17,1},{25,9},{2,18},{10... | collective-permute-start | bytes 1179656 | tf_op jit(solution)/shard_map/ppermute | solution.py:35
  100.5 17.0 %collective-permute-start.8 = (bf16[4,128,384]{2,1,0:T(8,128)(2,1)S(1)}, bf16[4,128,384]{2,1,0:T(8,128)(2,1)S(1)}, u32[]{:S(2)}, u32[]{:S(2)}) collective-permute-start(bf16[4,128,384]{2,1,0:T(8,128)(2,1)S(1)} %pad_maximum_fusion.refs_0_), channel_id=1, source_target_pairs={{0,24},{8,0},{16,8},{24,16},{1,25},{9,1},{17,9},{25,17},{2,26},{10... | collective-permute-start | bytes 1179656 | tf_op jit(solution)/shard_map/ppermute | solution.py:35
  117.5 12.6 %copy-start.3 = (bf16[4,128,384]{2,1,0:T(8,128)(2,1)}, bf16[4,128,384]{2,1,0:T(8,128)(2,1)S(1)}, u32[]{:S(2)}) copy-start(bf16[4,128,384]{2,1,0:T(8,128)(2,1)S(1)} %collective-permute-done.6.refs_1_) | copy-start | bytes 1179652
  117.5 12.6 %copy-start.4 = (bf16[4,128,384]{2,1,0:T(8,128)(2,1)}, bf16[4,128,384]{2,1,0:T(8,128)(2,1)S(1)}, u32[]{:S(2)}) copy-start(bf16[4,128,384]{2,1,0:T(8,128)(2,1)S(1)} %collective-permute-done.7.refs_2_) | copy-start | bytes 1179652
  117.5 12.5 %copy-start.5 = (bf16[4,128,384]{2,1,0:T(8,128)(2,1)}, bf16[4,128,384]{2,1,0:T(8,128)(2,1)S(1)}, u32[]{:S(2)}) copy-start(bf16[4,128,384]{2,1,0:T(8,128)(2,1)S(1)} %collective-permute-done.8.refs_3_) | copy-start | bytes 1179652
  132.7 23.9 %all-to-all-start.1 = ((bf16[16,128,128]{2,1,0:T(8,128)(2,1)}), bf16[16,128,128]{2,1,0:T(8,128)(2,1)S(1)}, u32[]{:S(2)}, u32[]{:S(2)}) async-start(bf16[16,128,128]{2,1,0:T(8,128)(2,1)} %bitcast.23), calls=%async_computation.1 | async-start | bytes 1048576 | tf_op jit(solution)/shard_map/all_to_all | solution.py:30
  156.6 25.7 %copy-start.13 = (bf16[3,128,128]{2,1,0:T(8,128)(2,1)S(1)}, bf16[3,128,128]{2,1,0:T(8,128)(2,1)}, u32[]{:S(2)}) copy-start(bf16[3,128,128]{2,1,0:T(8,128)(2,1)} %get-tuple-element.60) | copy-start | bytes 294916
  156.6 13.9 %collective-permute-start.10 = (bf16[4,128,384]{2,1,0:T(8,128)(2,1)}, bf16[4,128,384]{2,1,0:T(8,128)(2,1)S(1)}, u32[]{:S(2)}, u32[]{:S(2)}) collective-permute-start(bf16[4,128,384]{2,1,0:T(8,128)(2,1)} %get-tuple-element.58), channel_id=1, source_target_pairs={{0,16},{8,24},{16,0},{24,8},{1,17},{9,25},{17,1},{25,9},{2,18},{10... | collective-permute-start | bytes 1179656 | tf_op jit(solution)/shard_map/ppermute | solution.py:35
  160.1 15.6 %collective-permute-start.11 = (bf16[4,128,384]{2,1,0:T(8,128)(2,1)}, bf16[4,128,384]{2,1,0:T(8,128)(2,1)S(1)}, u32[]{:S(2)}, u32[]{:S(2)}) collective-permute-start(bf16[4,128,384]{2,1,0:T(8,128)(2,1)} %get-tuple-element.59), channel_id=1, source_target_pairs={{0,24},{8,0},{16,8},{24,16},{1,25},{9,1},{17,9},{25,17},{2,26},{10... | collective-permute-start | bytes 1179656 | tf_op jit(solution)/shard_map/ppermute | solution.py:35
  161.3 14.4 %collective-permute-start.9 = (bf16[4,128,384]{2,1,0:T(8,128)(2,1)}, bf16[4,128,384]{2,1,0:T(8,128)(2,1)S(1)}, u32[]{:S(2)}, u32[]{:S(2)}) collective-permute-start(bf16[4,128,384]{2,1,0:T(8,128)(2,1)} %get-tuple-element.57), channel_id=1, source_target_pairs={{0,8},{8,16},{16,24},{24,0},{1,9},{9,17},{17,25},{25,1},{2,10},{10... | collective-permute-start | bytes 1179656 | tf_op jit(solution)/shard_map/ppermute | solution.py:35
  176.9 16.4 %collective-permute-start.12 = (bf16[128,384]{1,0:T(8,128)(2,1)S(1)}, bf16[128,384]{1,0:T(8,128)(2,1)S(1)}, u32[]{:S(2)}, u32[]{:S(2)}) collective-permute-start(bf16[128,384]{1,0:T(8,128)(2,1)S(1)} %get-tuple-element.80), channel_id=1, source_target_pairs={{0,32},{32,64},{64,96},{96,0},{1,33},{33,65},{65,97},{97,1},{2,34}... | collective-permute-start | bytes 294920 | tf_op jit(solution)/shard_map/ppermute | solution.py:35
  178.5 14.8 %collective-permute-start.13 = (bf16[128,384]{1,0:T(8,128)(2,1)S(1)}, bf16[128,384]{1,0:T(8,128)(2,1)S(1)}, u32[]{:S(2)}, u32[]{:S(2)}) collective-permute-start(bf16[128,384]{1,0:T(8,128)(2,1)S(1)} %get-tuple-element.82), channel_id=1, source_target_pairs={{0,64},{32,96},{64,0},{96,32},{1,65},{33,97},{65,1},{97,33},{2,66}... | collective-permute-start | bytes 294920 | tf_op jit(solution)/shard_map/ppermute | solution.py:35
  180.9 12.5 %collective-permute-start.14 = (bf16[128,384]{1,0:T(8,128)(2,1)S(1)}, bf16[128,384]{1,0:T(8,128)(2,1)S(1)}, u32[]{:S(2)}, u32[]{:S(2)}) collective-permute-start(bf16[128,384]{1,0:T(8,128)(2,1)S(1)} %get-tuple-element.81), channel_id=1, source_target_pairs={{0,96},{32,0},{64,32},{96,64},{1,97},{33,1},{65,33},{97,65},{2,98}... | collective-permute-start | bytes 294920 | tf_op jit(solution)/shard_map/ppermute | solution.py:35
  183.0 18.6 %all-to-all-start.2 = ((bf16[16,3,8,128]{3,2,1,0:T(8,128)(2,1)}), bf16[16,3,8,128]{3,2,1,0:T(8,128)(2,1)S(1)}, u32[]{:S(2)}, u32[]{:S(2)}) async-start(bf16[16,3,8,128]{3,2,1,0:T(8,128)(2,1)} %copy_bitcast_fusion), calls=%async_computation.2 | async-start | bytes 196608 | tf_op jit(solution)/shard_map/all_to_all | solution.py:30
  201.6 6.0 %collective-permute-start.15 = (bf16[128,384]{1,0:T(8,128)(2,1)S(1)}, bf16[128,384]{1,0:T(8,128)(2,1)S(1)}, u32[]{:S(2)}, u32[]{:S(2)}) collective-permute-start(bf16[128,384]{1,0:T(8,128)(2,1)S(1)} %fusion.25), channel_id=1, source_target_pairs={{0,8},{8,16},{16,24},{24,0},{1,9},{9,17},{17,25},{25,1},{2,10},{10... | collective-permute-start | bytes 294920 | tf_op jit(solution)/shard_map/ppermute | solution.py:35
  203.0 7.5 %collective-permute-start.16 = (bf16[128,384]{1,0:T(8,128)(2,1)S(1)}, bf16[128,384]{1,0:T(8,128)(2,1)S(1)}, u32[]{:S(2)}, u32[]{:S(2)}) collective-permute-start(bf16[128,384]{1,0:T(8,128)(2,1)S(1)} %fusion.25), channel_id=1, source_target_pairs={{0,16},{8,24},{16,0},{24,8},{1,17},{9,25},{17,1},{25,9},{2,18},{10... | collective-permute-start | bytes 294920 | tf_op jit(solution)/shard_map/ppermute | solution.py:35
  205.7 4.9 %collective-permute-start.17 = (bf16[128,384]{1,0:T(8,128)(2,1)S(1)}, bf16[128,384]{1,0:T(8,128)(2,1)S(1)}, u32[]{:S(2)}, u32[]{:S(2)}) collective-permute-start(bf16[128,384]{1,0:T(8,128)(2,1)S(1)} %fusion.25), channel_id=1, source_target_pairs={{0,24},{8,0},{16,8},{24,16},{1,25},{9,1},{17,9},{25,17},{2,26},{10... | collective-permute-start | bytes 294920 | tf_op jit(solution)/shard_map/ppermute | solution.py:35
  213.3 5.4 %collective-permute-start.18 = (bf16[2,4,12,384]{3,2,1,0:T(8,128)(2,1)S(1)}, bf16[2,4,12,384]{3,2,1,0:T(8,128)(2,1)S(1)}, u32[]{:S(2)}, u32[]{:S(2)}) collective-permute-start(bf16[2,4,12,384]{3,2,1,0:T(8,128)(2,1)S(1)} %get-tuple-element.69), channel_id=1, source_target_pairs={{0,1},{1,0},{2,3},{3,2},{4,5},{5,4},{6,7},{7,6},{8,9},{9,8},{10,11... | collective-permute-start | bytes 221192 | tf_op jit(solution)/shard_map/ppermute | solution.py:68
  213.3 6.9 %collective-permute-start.19 = (bf16[2,4,12,384]{3,2,1,0:T(8,128)(2,1)S(1)}, bf16[2,4,12,384]{3,2,1,0:T(8,128)(2,1)S(1)}, u32[]{:S(2)}, u32[]{:S(2)}) collective-permute-start(bf16[2,4,12,384]{3,2,1,0:T(8,128)(2,1)S(1)} %get-tuple-element.75), channel_id=1, source_target_pairs={{0,2},{1,3},{2,4},{3,5},{4,6},{5,7},{6,0},{7,1},{8,10},{9,11},{10,... | collective-permute-start | bytes 221192 | tf_op jit(solution)/shard_map/ppermute | solution.py:68
  215.2 9.2 %collective-permute-start.20 = (bf16[2,4,12,384]{3,2,1,0:T(8,128)(2,1)}, bf16[2,4,12,384]{3,2,1,0:T(8,128)(2,1)}, u32[]{:S(2)}, u32[]{:S(2)}) collective-permute-start(bf16[2,4,12,384]{3,2,1,0:T(8,128)(2,1)} %get-tuple-element.74), channel_id=1, source_target_pairs={{0,3},{1,2},{2,5},{3,4},{4,7},{5,6},{6,1},{7,0},{8,11},{9,10},{10,... | collective-permute-start | bytes 221192 | tf_op jit(solution)/shard_map/ppermute | solution.py:68
  215.6 8.8 %collective-permute-start.21 = (bf16[2,4,12,384]{3,2,1,0:T(8,128)(2,1)}, bf16[2,4,12,384]{3,2,1,0:T(8,128)(2,1)}, u32[]{:S(2)}, u32[]{:S(2)}) collective-permute-start(bf16[2,4,12,384]{3,2,1,0:T(8,128)(2,1)} %get-tuple-element.73), channel_id=1, source_target_pairs={{0,4},{1,5},{2,6},{3,7},{4,0},{5,1},{6,2},{7,3},{8,12},{9,13},{10,... | collective-permute-start | bytes 221192 | tf_op jit(solution)/shard_map/ppermute | solution.py:68
  217.2 7.1 %collective-permute-start.22 = (bf16[2,4,12,384]{3,2,1,0:T(8,128)(2,1)S(1)}, bf16[2,4,12,384]{3,2,1,0:T(8,128)(2,1)}, u32[]{:S(2)}, u32[]{:S(2)}) collective-permute-start(bf16[2,4,12,384]{3,2,1,0:T(8,128)(2,1)S(1)} %get-tuple-element.72), channel_id=1, source_target_pairs={{0,5},{1,4},{2,7},{3,6},{4,1},{5,0},{6,3},{7,2},{8,13},{9,12},{10,... | collective-permute-start | bytes 221192 | tf_op jit(solution)/shard_map/ppermute | solution.py:68
  218.7 7.9 %collective-permute-start.23 = (bf16[2,4,12,384]{3,2,1,0:T(8,128)(2,1)S(1)}, bf16[2,4,12,384]{3,2,1,0:T(8,128)(2,1)}, u32[]{:S(2)}, u32[]{:S(2)}) collective-permute-start(bf16[2,4,12,384]{3,2,1,0:T(8,128)(2,1)S(1)} %get-tuple-element.71), channel_id=1, source_target_pairs={{0,6},{1,7},{2,0},{3,1},{4,2},{5,3},{6,4},{7,5},{8,14},{9,15},{10,... | collective-permute-start | bytes 221192 | tf_op jit(solution)/shard_map/ppermute | solution.py:68
  220.2 8.5 %collective-permute-start.24 = (bf16[2,4,12,384]{3,2,1,0:T(8,128)(2,1)S(1)}, bf16[2,4,12,384]{3,2,1,0:T(8,128)(2,1)}, u32[]{:S(2)}, u32[]{:S(2)}) collective-permute-start(bf16[2,4,12,384]{3,2,1,0:T(8,128)(2,1)S(1)} %get-tuple-element.70), channel_id=1, source_target_pairs={{0,7},{1,6},{2,1},{3,0},{4,3},{5,2},{6,5},{7,4},{8,15},{9,14},{10,... | collective-permute-start | bytes 221192 | tf_op jit(solution)/shard_map/ppermute | solution.py:68
  220.4 24.5 %copy-start.12 = (bf16[16,3,8,128]{3,2,1,0:T(8,128)(2,1)S(1)}, bf16[16,3,8,128]{3,2,1,0:T(8,128)(2,1)}, u32[]{:S(2)}) copy-start(bf16[16,3,8,128]{3,2,1,0:T(8,128)(2,1)} %copy-done.11) | copy-start | bytes 294916
  229.9 10.3 %collective-permute-start.25 = (bf16[12,384]{1,0:T(8,128)(2,1)S(1)}, bf16[12,384]{1,0:T(8,128)(2,1)S(1)}, u32[]{:S(2)}, u32[]{:S(2)}) collective-permute-start(bf16[12,384]{1,0:T(8,128)(2,1)S(1)} %get-tuple-element.83), channel_id=1, source_target_pairs={{0,32},{32,64},{64,96},{96,0},{128,160},{160,192},{192,224},{224,1... | collective-permute-start | bytes 27656 | tf_op jit(solution)/shard_map/ppermute | solution.py:68
  231.5 9.2 %collective-permute-start.26 = (bf16[12,384]{1,0:T(8,128)(2,1)S(1)}, bf16[12,384]{1,0:T(8,128)(2,1)S(1)}, u32[]{:S(2)}, u32[]{:S(2)}) collective-permute-start(bf16[12,384]{1,0:T(8,128)(2,1)S(1)} %get-tuple-element.89), channel_id=1, source_target_pairs={{0,64},{32,96},{64,0},{96,32},{128,192},{160,224},{192,128},{224,1... | collective-permute-start | bytes 27656 | tf_op jit(solution)/shard_map/ppermute | solution.py:68
  232.9 12.6 %collective-permute-start.27 = (bf16[12,384]{1,0:T(8,128)(2,1)S(1)}, bf16[12,384]{1,0:T(8,128)(2,1)S(1)}, u32[]{:S(2)}, u32[]{:S(2)}) collective-permute-start(bf16[12,384]{1,0:T(8,128)(2,1)S(1)} %get-tuple-element.88), channel_id=1, source_target_pairs={{0,96},{32,0},{64,32},{96,64},{128,224},{160,128},{192,160},{224,1... | collective-permute-start | bytes 27656 | tf_op jit(solution)/shard_map/ppermute | solution.py:68
  235.4 10.1 %collective-permute-start.28 = (bf16[12,384]{1,0:T(8,128)(2,1)S(1)}, bf16[12,384]{1,0:T(8,128)(2,1)S(1)}, u32[]{:S(2)}, u32[]{:S(2)}) collective-permute-start(bf16[12,384]{1,0:T(8,128)(2,1)S(1)} %get-tuple-element.87), channel_id=1, source_target_pairs={{0,128},{32,160},{64,192},{96,224},{128,0},{160,32},{192,64},{224,... | collective-permute-start | bytes 27656 | tf_op jit(solution)/shard_map/ppermute | solution.py:68
  235.9 9.6 %collective-permute-start.29 = (bf16[12,384]{1,0:T(8,128)(2,1)S(1)}, bf16[12,384]{1,0:T(8,128)(2,1)S(1)}, u32[]{:S(2)}, u32[]{:S(2)}) collective-permute-start(bf16[12,384]{1,0:T(8,128)(2,1)S(1)} %get-tuple-element.86), channel_id=1, source_target_pairs={{0,160},{32,192},{64,224},{96,128},{128,32},{160,64},{192,96},{224... | collective-permute-start | bytes 27656 | tf_op jit(solution)/shard_map/ppermute | solution.py:68
  240.2 5.8 %collective-permute-start.30 = (bf16[12,384]{1,0:T(8,128)(2,1)S(1)}, bf16[12,384]{1,0:T(8,128)(2,1)S(1)}, u32[]{:S(2)}, u32[]{:S(2)}) collective-permute-start(bf16[12,384]{1,0:T(8,128)(2,1)S(1)} %get-tuple-element.85), channel_id=1, source_target_pairs={{0,192},{32,224},{64,128},{96,160},{128,64},{160,96},{192,0},{224,... | collective-permute-start | bytes 27656 | tf_op jit(solution)/shard_map/ppermute | solution.py:68
  240.7 6.7 %collective-permute-start.31 = (bf16[12,384]{1,0:T(8,128)(2,1)S(1)}, bf16[12,384]{1,0:T(8,128)(2,1)S(1)}, u32[]{:S(2)}, u32[]{:S(2)}) collective-permute-start(bf16[12,384]{1,0:T(8,128)(2,1)S(1)} %get-tuple-element.84), channel_id=1, source_target_pairs={{0,224},{32,128},{64,160},{96,192},{128,96},{160,0},{192,32},{224,... | collective-permute-start | bytes 27656 | tf_op jit(solution)/shard_map/ppermute | solution.py:68
  (6 other events, 27.9 us)

commit v4 on v3

--- a/solution.py
+++ b/solution.py
@@ -54,20 +54,10 @@
     ]
 
 
-def summed_over_pair(value, slow, fast):
-    n_slow, n_fast = lax.axis_size(slow), lax.axis_size(fast)
-    total = None
-    for ds, across in enumerate(parts_ahead(value, slow, 0)):
-        for df, part in enumerate(parts_ahead(across, fast, 0)):
-            if ds or df:
-                pairs = [
-                    (i * n_fast + j, (i + ds) % n_slow * n_fast + (j + df) % n_fast)
-                    for i in range(n_slow)
-                    for j in range(n_fast)
-                ]
-                part = lax.ppermute(part.astype(BF), (slow, fast), pairs)
-            total = part.astype(F32) if total is None else total + part.astype(F32)
-    return total
+def reduced(value, axes):
+    for axis in axes:
+        value = summed_parts(parts_ahead(value, axis, 0), axis)
+    return value
 
 
 def pack_kernel(q_ref, k_ref, v_ref, out_ref):
@@ -92,35 +82,51 @@
     )(q, k, v)
 
 
-def softmax_rows(query, key):
-    scores = dot(query, key, NT)
+def with_ones(ref, values):
+    ref[:, :HDIM] = values
+    ref[:, HDIM:] = jnp.ones_like(values)
+
+
+def attended_rows(scores, value_ref):
     highest = jnp.max(scores, axis=-1, keepdims=True)
-    raised = jnp.exp2((scores - highest) * SCALE2)
-    total = jnp.sum(raised, axis=-1, keepdims=True)
-    return raised.astype(BF), highest, total
-
-
-def teacher_kernel(scale_ref, heads_ref, target_ref, keys_ref):
+    raised = jnp.exp2((scores - highest) * SCALE2).astype(BF)
+    both = dot(raised, value_ref[...])
+    total = both[:, HDIM:]
+    return both[:, :HDIM] / total, highest, total
+
+
+def teacher_kernel(scale_ref, heads_ref, target_ref, query_ref, key_ref, value_ref, scores_ref):
     blocks, rows = heads_ref.shape[1], heads_ref.shape[3]
     tokens = blocks * rows
     scale = scale_ref[0]
     for one in range(2):
-        for part in range(3):
-            for block in range(blocks):
-                keys_ref[one, part, block * rows : (block + 1) * rows] = heads_ref[one, block, part]
-    step_rows = 256
+        for block in range(blocks):
+            where = slice(block * rows, (block + 1) * rows)
+            query_ref[one, where] = heads_ref[one, block, 0]
+            key_ref[one, :, where] = jnp.transpose(heads_ref[one, block, 1])
+            with_ones(value_ref.at[one, where], heads_ref[one, block, 2])
+    step_rows = scores_ref.shape[1]
+    steps = tokens // step_rows
+
+    def rows_of(step):
+        return pl.ds(pl.multiple_of(step * step_rows, step_rows), step_rows)
+
+    def put_scores(step, one):
+        scores_ref[one] = dot(query_ref[one, rows_of(step)], key_ref[one])
+
+    def rounded(one):
+        return attended_rows(scores_ref[one], value_ref.at[one])[0].astype(BF).astype(F32)
 
     def one_block(step, carry):
-        here = pl.ds(pl.multiple_of(step * step_rows, step_rows), step_rows)
-        outs = []
-        for one in range(2):
-            raised, _, total = softmax_rows(keys_ref[one, 0, here], keys_ref[one, 1])
-            attended = dot(raised, keys_ref[one, 2]) / total
-            outs.append(attended.astype(BF).astype(F32))
-        target_ref[here] = outs[1] + scale * (outs[0] - outs[1])
+        put_scores(step, 1)
+        conditional = rounded(0)
+        put_scores(jnp.minimum(step + 1, steps - 1), 0)
+        unconditional = rounded(1)
+        target_ref[rows_of(step)] = unconditional + scale * (conditional - unconditional)
         return carry
 
-    lax.fori_loop(0, tokens // step_rows, one_block, 0)
+    put_scores(0, 0)
+    lax.fori_loop(0, steps, one_block, 0)
 
 
 def teacher(scale, heads):
@@ -131,20 +137,25 @@
         in_specs=[pl.BlockSpec(memory_space=pltpu.SMEM), vmem],
         out_specs=vmem,
         out_shape=jax.ShapeDtypeStruct((tokens, HDIM), F32),
-        scratch_shapes=[pltpu.VMEM((2, 3, tokens, HDIM), BF)],
+        scratch_shapes=[
+            pltpu.VMEM((2, tokens, HDIM), BF),
+            pltpu.VMEM((2, HDIM, tokens), BF),
+            pltpu.VMEM((2, tokens, 2 * HDIM), BF),
+            pltpu.VMEM((2, 256, tokens), F32),
+        ],
         cost_estimate=pl.CostEstimate(
             flops=8 * tokens * tokens * HDIM,
             transcendentals=2 * tokens * tokens,
             bytes_accessed=4 * MIB,
         ),
-        compiler_params=pltpu.CompilerParams(vmem_limit_bytes=48 * MIB),
+        compiler_params=pltpu.CompilerParams(vmem_limit_bytes=24 * MIB),
         name="teacher_forward",
     )(scale, heads)
 
 
 def student_kernel(n_fast, place_ref, inv_ref, heads_ref, target_ref, up_ref, *refs):
     low_refs = refs[:n_fast]
-    out_ref, upstream_ref, student_ref, stats_ref = refs[n_fast:]
+    out_ref, upstream_ref, student_ref, stats_ref, key_ref, value_ref, scores_ref = refs[n_fast:]
     rows = heads_ref.shape[3]
     tokens = out_ref.shape[0]
     n_slow = low_refs[0].shape[0]
@@ -154,33 +165,52 @@
     for part in range(3):
         up = up_ref[part]
         for fast in range(n_fast):
+            low = low_refs[fast][:, :, part * RANK : (part + 1) * RANK]
+            adapted = dot(low.reshape(n_slow * rows, RANK), up)
             for slow in range(n_slow):
                 block = lax.rem(here_slow - slow + n_slow, n_slow) * n_fast + lax.rem(
                     here_fast - fast + n_fast, n_fast
                 )
-                columns = slice(part * RANK, (part + 1) * RANK)
-                adapted = dot(low_refs[fast][slow, :, columns], up)
                 frozen = heads_ref[0, block, part].astype(F32)
                 where = pl.ds(pl.multiple_of(block * rows, rows), rows)
-                student_ref[part, where] = (frozen + adapted).astype(BF)
-    step_rows = 256
-
-    def one_block(step, carry):
-        here = pl.ds(pl.multiple_of(step * step_rows, step_rows), step_rows)
-        raised, highest, total = softmax_rows(student_ref[0, here], student_ref[1])
-        attended = dot(raised, student_ref[2]) / total
+                student_ref[part, where] = (
+                    frozen + adapted[slow * rows : (slow + 1) * rows]
+                ).astype(BF)
+    for block in range(n_slow * n_fast):
+        where = slice(block * rows, (block + 1) * rows)
+        key_ref[:, where] = jnp.transpose(student_ref[1, where])
+        with_ones(value_ref.at[where], student_ref[2, where])
+    step_rows = scores_ref.shape[1]
+    steps = tokens // step_rows
+
+    def rows_of(step):
+        return pl.ds(pl.multiple_of(step * step_rows, step_rows), step_rows)
+
+    def put_scores(step, slot):
+        scores_ref[slot] = dot(student_ref[0, rows_of(step)], key_ref[...])
+
+    def finish(step, slot):
+        here = rows_of(step)
+        attended, highest, total = attended_rows(scores_ref[slot], value_ref)
         rounded = attended.astype(BF)
         out_ref[here] = rounded
         upstream = ((rounded.astype(F32) - target_ref[here]) * inverse).astype(BF)
         upstream_ref[here] = upstream
         level = highest * SCALE2 + jnp.log2(total)
         center = jnp.sum(attended * upstream.astype(F32), axis=-1, keepdims=True)
-        stats_ref[0:1, here] = jnp.transpose(jnp.broadcast_to(level, (step_rows, HDIM)))[0:1]
+        stats_ref[0:1, here] = jnp.transpose(level)[0:1]
         stats_ref[1:2, here] = jnp.transpose(jnp.broadcast_to(center, (step_rows, HDIM)))[0:1]
+
+    def two_blocks(pair, carry):
+        put_scores(2 * pair + 1, 1)
+        finish(2 * pair, 0)
+        put_scores(jnp.minimum(2 * pair + 2, steps - 1), 0)
+        finish(2 * pair + 1, 1)
         return carry
 
     stats_ref[...] = jnp.zeros_like(stats_ref)
-    lax.fori_loop(0, tokens // step_rows, one_block, 0)
+    put_scores(0, 0)
+    lax.fori_loop(0, steps // 2, two_blocks, 0)
 
 
 def student_forward(place, inverse, heads, target, up, low):
@@ -200,12 +230,17 @@
             jax.ShapeDtypeStruct((3, tokens, HDIM), BF),
             jax.ShapeDtypeStruct((8, tokens), F32),
         ],
+        scratch_shapes=[
+            pltpu.VMEM((HDIM, tokens), BF),
+            pltpu.VMEM((tokens, 2 * HDIM), BF),
+            pltpu.VMEM((2, 256, tokens), F32),
+        ],
         cost_estimate=pl.CostEstimate(
             flops=4 * tokens * tokens * HDIM,
             transcendentals=tokens * tokens,
             bytes_accessed=6 * MIB,
         ),
-        compiler_params=pltpu.CompilerParams(vmem_limit_bytes=48 * MIB),
+        compiler_params=pltpu.CompilerParams(vmem_limit_bytes=24 * MIB),
         name="student_forward",
     )(place, inverse, heads, target, up, *low)
 
@@ -214,27 +249,27 @@
     n_fast, place_ref, student_ref, upstream_ref, stats_ref, up_ref, *refs
 ):
     low_refs, back_refs = refs[:n_fast], refs[n_fast : 2 * n_fast]
-    grad_up_ref, dq_ref, dk_ref, dv_ref = refs[2 * n_fast :]
+    grad_up_ref, dq_ref, dk_ref, dv_ref, flat_ref = refs[2 * n_fast :]
     tokens = student_ref.shape[1]
     n_slow, rows, _ = low_refs[0].shape
     here_slow, here_fast = place_ref[0], place_ref[1]
-    step_rows = 256
+    step_rows = 512
     dk_ref[...] = jnp.zeros_like(dk_ref)
     dv_ref[...] = jnp.zeros_like(dv_ref)
+    flat_ref[...] = jnp.transpose(student_ref[1])
 
     def one_block(step, carry):
         here = pl.ds(pl.multiple_of(step * step_rows, step_rows), step_rows)
         query = student_ref[0, here]
         upstream = upstream_ref[here]
-        key = student_ref[1]
         level = stats_ref[0:1, here]
         center = stats_ref[1:2, here]
-        prob = jnp.exp2(dot(key, query, NT) * SCALE2 - level)
+        prob = jnp.exp2(dot(student_ref[1], query, NT) * SCALE2 - level)
         dv_ref[...] += dot(prob.astype(BF), upstream)
         dprob = dot(student_ref[2], upstream, NT)
         dscore = (prob * (dprob - center)).astype(BF)
         dk_ref[...] += dot(dscore, query)
-        dq_ref[here] = dot(dscore, key, TN)
+        dq_ref[here] = jnp.transpose(dot(flat_ref[...], dscore))
         return carry
 
     lax.fori_loop(0, tokens // step_rows, one_block, 0)
@@ -254,7 +289,7 @@
                 back_refs[fast][slow, :, columns] = dot(grad.astype(BF), up, NT).astype(BF)
                 grad = ref[pl.ds(pl.multiple_of(behind * rows, rows), rows)] * factor
                 total += dot(low_refs[fast][slow, :, columns], grad.astype(BF), TN)
-        grad_up_ref[part] = total.astype(BF)
+        grad_up_ref[:, part * HDIM : (part + 1) * HDIM] = total.astype(BF)
 
 
 def backward(place, student, upstream, stats, up, low):
@@ -266,15 +301,15 @@
         out_specs=[vmem] * (n_fast + 1),
         out_shape=[jax.ShapeDtypeStruct(low[0].shape, BF)] * n_fast
         + [
-            jax.ShapeDtypeStruct((3, RANK, HDIM), BF),
+            jax.ShapeDtypeStruct((RANK, 3 * HDIM), BF),
         ],
-        scratch_shapes=[pltpu.VMEM((tokens, HDIM), F32)] * 3,
+        scratch_shapes=[pltpu.VMEM((tokens, HDIM), F32)] * 3 + [pltpu.VMEM((HDIM, tokens), BF)],
         cost_estimate=pl.CostEstimate(
             flops=10 * tokens * tokens * HDIM,
             transcendentals=tokens * tokens,
             bytes_accessed=6 * MIB,
         ),
-        compiler_params=pltpu.CompilerParams(vmem_limit_bytes=56 * MIB),
+        compiler_params=pltpu.CompilerParams(vmem_limit_bytes=40 * MIB),
         name="attention_backward",
     )(place, student, upstream, stats, up, *low)
 
@@ -334,21 +369,20 @@
     tokens_out, up_partial, *back = lax.optimization_barrier((tokens_out, up_partial, *back))
     student_out = jnp.moveaxis(tokens_out, 0, 1).reshape(rows, -1)
 
-    owners = n_cfg * n_x * n_core
-    up_blocks = jnp.moveaxis(up_partial.reshape(3, owners, RANK // owners, HDIM), 1, 0)
-    grad_up = exchange(up_blocks, ("cfg", "x", "core"))
-
     back = summed_parts(back, "y").astype(BF)
     back = summed_parts([back[d] for d in range(n_slow)], "z")
     low_grad = (back.reshape(rows, 3, RANK) * modulation).astype(BF).reshape(rows, 3 * RANK)
-    low_grad, grad_up = lax.optimization_barrier((low_grad, grad_up))
-    grad_up = grad_up.astype(F32).sum(axis=0)
     low_grads = jnp.concatenate(from_each(low_grad, "y"))
     down = dot(jnp.concatenate(columns), low_grads, TN).astype(BF)
-    down = down.reshape(n_cfg, n_slow, n_x, n_core, -1, 3 * RANK).transpose(2, 3, 0, 1, 4, 5)
-    down = summed_over_pair(down, "x", "core")
-    down = summed_over_pair(down, "cfg", "z")
-    grad_down = jnp.moveaxis(down.reshape(-1, 3, RANK), 1, 0)
+    down = down.reshape(n_cfg, n_slow, n_x, n_core, -1, 3 * RANK).transpose(3, 2, 0, 1, 4, 5)
+    down_rows, up_rows = down.shape[-2], RANK // (n_cfg * n_x * n_core)
+    down = down.reshape(n_core, n_x, n_cfg, n_slow * down_rows, 3 * RANK)
+    up_partial = up_partial.reshape(n_cfg, n_x, n_core, up_rows, 3 * HDIM).transpose(2, 1, 0, 3, 4)
+    both = reduced(jnp.concatenate([down, up_partial], axis=3), ("core", "x", "cfg"))
+    down, grad_up = both[: n_slow * down_rows], both[n_slow * down_rows :]
+    grad_up = jnp.moveaxis(grad_up.reshape(up_rows, 3, HDIM), 1, 0)
+    down = reduced(down.reshape(n_slow, down_rows, 3 * RANK), ("z",))
+    grad_down = jnp.moveaxis(down.reshape(down_rows, 3, RANK), 1, 0)
     return student_out[None, None], grad_down, grad_up
 
 

time: 249 us -> 226 us (0.908)
  starting transfers between devices: 83.1 us -> 64.4 us
  Pallas kernels: 50.3 us -> 40.1 us
  local copies, waits for them, and re-layouts: 12.8 us -> 19.8 us
    ppermute x14 -> x0, starting transfers between devices: 20.7 us -> none  [summed_over_pair(): part = lax.ppermute(part.astype(BF), (slow, fast), pairs)]
    ppermute x18 -> x26, waiting for transfers between devices: 72 us -> 91.1 us  [shifted(): lax.ppermute(value, axis, [(i, (i + distance) % size) for i in range(size)])]
    ppermute x18 -> x26, starting transfers between devices: 34.2 us -> 44.9 us  [shifted(): lax.ppermute(value, axis, [(i, (i + distance) % size) for i in range(size)])]
    ppermute x14 -> x0, waiting for transfers between devices: 10.2 us -> none  [summed_over_pair(): part = lax.ppermute(part.astype(BF), (slow, fast), pairs)]
    all_to_all x3 -> x2, starting transfers between devices: 28.2 us -> 19.5 us  [exchange(): return lax.all_to_all(value, axes, split_axis=0, concat_axis=0, tiled=True)]
    all_to_all x3 -> x2, waiting for transfers between devices: 8.19 us -> 0.01 us  [exchange(): return lax.all_to_all(value, axes, split_axis=0, concat_axis=0, tiled=True)]
    unnamed x41 -> x36, local copies, waits for them, and re-layouts: 8.09 us -> 13.8 us
    pallas_call x1, Pallas kernels: 17.8 us -> 13.3 us  [backward(): pl.pallas_call(functools.partial(backward_kernel, n_fast), in_specs=[pl.B...]
  transfers between devices with their start and end apart: 35 -> 28, of which waited for: 13 -> 15; matrix products, arithmetic and copies ran while one was open for 5% -> 6% of each run, Pallas kernels for 14% -> 12%
where the time goes in v4:
time: 226 us; the launch traced here: 225 us
  waiting for transfers between devices  91.1 us (40%)
  starting transfers between devices  64.4 us (28%)
  Pallas kernels  40.1 us (18%)
  local copies, waits for them, and re-layouts  19.8 us (9%)
  matrix products  4.13 us (2%)
  other arithmetic  3.13 us (1%)
  between operations  2.38 us (1%)
    ppermute x26, waiting for transfers between devices, shifted(): lax.ppermute(value, axis, [(i, (i + distance) % size) for i in range(size)])  91.1 us
    ppermute x26, starting transfers between devices, shifted(): lax.ppermute(value, axis, [(i, (i + distance) % size) for i in range(size)])  44.9 us
    all_to_all x2, starting transfers between devices, exchange(): return lax.all_to_all(value, axes, split_axis=0, concat_axis=0, tiled=True)  19.5 us
    unnamed x36, local copies, waits for them, and re-layouts  13.8 us
    pallas_call x1, Pallas kernels, teacher(): pl.pallas_call(teacher_kernel, in_specs=[pl.BlockSpec(memory_space=pltpu....  13.7 us
    pallas_call x1, Pallas kernels, backward(): pl.pallas_call(functools.partial(backward_kernel, n_fast), in_specs=[pl.B...  13.3 us
    pallas_call x1, Pallas kernels, student_forward(): pl.pallas_call(functools.partial(student_kernel, len(low)), grid=(1,), in...  9.64 us
  transfers between devices with their start and end apart: 28, of which 15 were waited for; matrix products, arithmetic and copies ran while one was open for 6% of the time, Pallas kernels for 12%

profile of v4, /device:TPU:6, one launch (start us, length us, event | category | flops | bytes accessed | tf_op | source)
XLA Modules:
  0.0 225.1 jit_solution(3584665667004894413)
XLA Ops:
  0.6 3.4 %pack_heads.1 = bf16[32,3,128,128]{3,2,1,0:T(8,128)(2,1)} custom-call(bf16[2,128,2048]{2,1,0:T(8,128)(2,1)} %bitcast.93, bf16[2,128,2048]{2,1,0:T(8,128)(2,1)} %bitcast.94, bf16[2,128,2048]{2,1,0:T(8,128)(2,1)} %bitcast.95), custom_call_target="tpu_custom_call" | custom-call | bytes 6291456 | tf_op jit(solution)/shard_map/pack_heads/pallas_call | solution.py:74
  4.1 11.7 %all-to-all-start = ((bf16[32,3,128,128]{3,2,1,0:T(8,128)(2,1)}), bf16[32,3,128,128]{3,2,1,0:T(8,128)(2,1)}, u32[]{:S(2)}, u32[]{:S(2)}) async-start(bf16[32,3,128,128]{3,2,1,0:T(8,128)(2,1)} %pack_heads.1), calls=%async_computation | async-start | bytes 6291456 | tf_op jit(solution)/shard_map/all_to_all | solution.py:30
  17.8 4.4 %copy.26 = bf16[3,3072,128]{1,2,0:T(8,128)(2,1)} copy(bf16[3,3072,128]{2,1,0:T(8,128)(2,1)} %param.12) | data formatting | bytes 4718592 | tf_op args[4]
  22.2 2.4 %fusion.7 = f32[128,384]{0,1:S(1)} fusion(bf16[3072,384]{0,1:T(8,128)(2,1)} %bitcast.88, bf16[1,1,128,3072]{3,2,1,0:T(8,128)(2,1)S(1)} %copy-done.10), kind=kOutput, calls=%fused_computation.8 | convolution fusion | flops 301989888 | bytes 3342336
  25.5 1.7 collective-permute-start
  27.2 2.4 %collective-permute-start.1 = (bf16[128,384]{1,0:T(8,128)(2,1)}, bf16[128,384]{1,0:T(8,128)(2,1)}, u32[]{:S(2)}, u32[]{:S(2)}) collective-permute-start(bf16[128,384]{1,0:T(8,128)(2,1)} %copy.27), channel_id=1, source_target_pairs={{0,64},{32,96},{64,0},{96,32},{1,65},{33,97},{65,1},{97,33},{2,66}... | collective-permute-start | bytes 294920 | tf_op jit(solution)/shard_map/ppermute | solution.py:35
  29.6 1.5 collective-permute-start.2
  32.3 1.5 collective-permute-start.3
  33.8 2.7 %collective-permute-start.4 = (bf16[128,768]{0,1:T(8,128)(2,1)}, bf16[128,768]{0,1:T(8,128)(2,1)S(1)}, u32[]{:S(2)}, u32[]{:S(2)}) collective-permute-start(bf16[128,768]{0,1:T(8,128)(2,1)} %bitcast.21), channel_id=1, source_target_pairs={{0,16},{8,24},{16,0},{24,8},{1,17},{9,25},{17,1},{25,9},{2,18},{10... | collective-permute-start | bytes 589832 | tf_op jit(solution)/shard_map/ppermute | solution.py:35
  36.6 52.9 %collective-permute-done = bf16[128,384]{1,0:T(8,128)(2,1)S(1)} collective-permute-done((bf16[128,384]{1,0:T(8,128)(2,1)}, bf16[128,384]{1,0:T(8,128)(2,1)S(1)}, u32[]{:S(2)}, u32[]{:S(2)}) %collective-permute-start) | collective-permute-done | bytes 98336 | tf_op jit(solution)/shard_map/ppermute | solution.py:35
  89.5 2.7 %collective-permute-start.5 = (bf16[128,768]{0,1:T(8,128)(2,1)S(1)}, bf16[128,768]{0,1:T(8,128)(2,1)S(1)}, u32[]{:S(2)}, u32[]{:S(2)}) collective-permute-start(bf16[128,768]{0,1:T(8,128)(2,1)S(1)} %bitcast.102), channel_id=1, source_target_pairs={{0,24},{8,0},{16,8},{24,16},{1,25},{9,1},{17,9},{25,17},{2,26},{10... | collective-permute-start | bytes 589832 | tf_op jit(solution)/shard_map/ppermute | solution.py:35
  92.3 1.4 collective-permute-done.1
  93.7 1.0 pad_maximum_fusion.refs_0_
  96.1 1.3 collective-permute-start.6
  97.3 3.9 %collective-permute-start.7 = (bf16[4,128,384]{2,1,0:T(8,128)(2,1)S(1)}, bf16[4,128,384]{2,1,0:T(8,128)(2,1)S(1)}, u32[]{:S(2)}, u32[]{:S(2)}) collective-permute-start(bf16[4,128,384]{2,1,0:T(8,128)(2,1)S(1)} %pad_maximum_fusion.refs_0_), channel_id=1, source_target_pairs={{0,16},{8,24},{16,0},{24,8},{1,17},{9,25},{17,1},{25,9},{2,18},{10... | collective-permute-start | bytes 1179656 | tf_op jit(solution)/shard_map/ppermute | solution.py:35
  101.5 13.7 %teacher_forward.1.target_ref = f32[2048,128]{1,0:T(8,128)S(1)} custom-call(f32[1]{0:T(128)} %bitcast.9.scale_ref, bf16[2,16,3,128,128]{4,3,2,1,0:T(8,128)(2,1)} %bitcast.3.heads_ref), custom_call_target="tpu_custom_call" | custom-call | flops 4294967296 | bytes 4194304 | tf_op jit(solution)/shard_map/teacher_forward/pallas_call | solution.py:135
  115.2 9.6 %student_forward.1 = (bf16[2048,128]{1,0:T(8,128)(2,1)}, bf16[2048,128]{1,0:T(8,128)(2,1)S(1)}, bf16[3,2048,128]{2,1,0:T(8,128)(2,1)S(1)}, f32[8,2048]{1,0:T(8,128)S(1)}) custom-call(s32[2]{0:T(128)S(1)} %pad_add_fusion.place_ref, f32[1]{0:T(128)} %constant.172.clone.1.inv_ref, bf16[2,16,3,128,128]{4,3,2,1,0:T(8,128)(2,1)} %bitcast.3.heads_ref, ...), custom_call_target="tpu_custom_call" | custom-call | flops 2147483648 | bytes 6291456 | tf_op jit(solution)/shard_map/student_forward/pallas_call | solution.py:221
  124.9 1.2 copy-done.6
  126.8 7.8 %all-to-all-start.1 = ((bf16[16,128,128]{2,1,0:T(8,128)(2,1)}), bf16[16,128,128]{2,1,0:T(8,128)(2,1)}, u32[]{:S(2)}, u32[]{:S(2)}) async-start(bf16[16,128,128]{2,1,0:T(8,128)(2,1)} %bitcast.23), calls=%async_computation.1 | async-start | bytes 1048576 | tf_op jit(solution)/shard_map/all_to_all | solution.py:30
  135.7 1.4 copy-done.7
  137.1 1.0 copy-done.9
  138.1 13.3 %attention_backward.1 = (bf16[4,128,384]{2,1,0:T(8,128)(2,1)S(1)}, bf16[4,128,384]{2,1,0:T(8,128)(2,1)S(1)}, bf16[4,128,384]{2,1,0:T(8,128)(2,1)S(1)}, bf16[4,12...) custom-call(s32[2]{0:T(128)S(1)} %pad_add_fusion.place_ref, bf16[3,2048,128]{2,1,0:T(8,128)(2,1)S(1)} %copy-done.7, ...), custom_call_target="tpu_custom_call" | custom-call | flops 5368709120 | bytes 6291456 | tf_op jit(solution)/shard_map/attention_backward/pallas_call | solution.py:298
  153.7 3.4 %collective-permute-start.10 = (bf16[4,128,384]{2,1,0:T(8,128)(2,1)}, bf16[4,128,384]{2,1,0:T(8,128)(2,1)S(1)}, u32[]{:S(2)}, u32[]{:S(2)}) collective-permute-start(bf16[4,128,384]{2,1,0:T(8,128)(2,1)} %copy-done.5), channel_id=1, source_target_pairs={{0,16},{8,24},{16,0},{24,8},{1,17},{9,25},{17,1},{25,9},{2,18},{10... | collective-permute-start | bytes 1179656 | tf_op jit(solution)/shard_map/ppermute | solution.py:35
  157.1 1.2 collective-permute-start.11
  159.1 8.4 %collective-permute-done.10 = bf16[4,128,384]{2,1,0:T(8,128)(2,1)S(1)} collective-permute-done((bf16[4,128,384]{2,1,0:T(8,128)(2,1)}, bf16[4,128,384]{2,1,0:T(8,128)(2,1)S(1)}, u32[]{:S(2)}, u32[]{:S(2)}) %collective-permute-start.10) | collective-permute-done | bytes 393248 | tf_op jit(solution)/shard_map/ppermute | solution.py:35
  167.5 6.5 %collective-permute-done.11 = bf16[4,128,384]{2,1,0:T(8,128)(2,1)S(1)} collective-permute-done((bf16[4,128,384]{2,1,0:T(8,128)(2,1)}, bf16[4,128,384]{2,1,0:T(8,128)(2,1)S(1)}, u32[]{:S(2)}, u32[]{:S(2)}) %collective-permute-start.11) | collective-permute-done | bytes 393248 | tf_op jit(solution)/shard_map/ppermute | solution.py:35
  174.3 1.8 collective-permute-start.12
  176.1 2.4 %collective-permute-start.13 = (bf16[128,384]{1,0:T(8,128)(2,1)S(1)}, bf16[128,384]{1,0:T(8,128)(2,1)S(1)}, u32[]{:S(2)}, u32[]{:S(2)}) collective-permute-start(bf16[128,384]{1,0:T(8,128)(2,1)S(1)} %get-tuple-element.74), channel_id=1, source_target_pairs={{0,64},{32,96},{64,0},{96,32},{1,65},{33,97},{65,1},{97,33},{2,66}... | collective-permute-start | bytes 294920 | tf_op jit(solution)/shard_map/ppermute | solution.py:35
  178.5 1.5 collective-permute-start.14
  179.9 2.0 collective-permute-done.12
  181.9 3.4 %collective-permute-done.13 = bf16[128,384]{1,0:T(8,128)(2,1)S(1)} collective-permute-done((bf16[128,384]{1,0:T(8,128)(2,1)S(1)}, bf16[128,384]{1,0:T(8,128)(2,1)S(1)}, u32[]{:S(2)}, u32[]{:S(2)}) %collective-permute-start.13) | collective-permute-done | bytes 98336 | tf_op jit(solution)/shard_map/ppermute | solution.py:35
  185.4 1.7 collective-permute-start.15
  187.0 2.7 %collective-permute-start.16 = (bf16[128,384]{1,0:T(8,128)(2,1)S(1)}, bf16[128,384]{1,0:T(8,128)(2,1)S(1)}, u32[]{:S(2)}, u32[]{:S(2)}) collective-permute-start(bf16[128,384]{1,0:T(8,128)(2,1)S(1)} %fusion.22), channel_id=1, source_target_pairs={{0,16},{8,24},{16,0},{24,8},{1,17},{9,25},{17,1},{25,9},{2,18},{10... | collective-permute-start | bytes 294920 | tf_op jit(solution)/shard_map/ppermute | solution.py:35
  189.7 1.5 collective-permute-start.17
  191.3 3.1 %collective-permute-done.16 = bf16[128,384]{1,0:T(8,128)(2,1)S(1)} collective-permute-done((bf16[128,384]{1,0:T(8,128)(2,1)S(1)}, bf16[128,384]{1,0:T(8,128)(2,1)S(1)}, u32[]{:S(2)}, u32[]{:S(2)}) %collective-permute-start.16) | collective-permute-done | bytes 98336 | tf_op jit(solution)/shard_map/ppermute | solution.py:35
  194.4 1.7 convolution_convert_fusion
  197.5 1.6 collective-permute-done.18
  200.3 2.4 %collective-permute-start.20 = (bf16[2,56,384]{2,0,1:T(2,128)(2,1)S(1)}, bf16[2,56,384]{2,0,1:T(2,128)(2,1)S(1)}, u32[]{:S(2)}, u32[]{:S(2)}) collective-permute-start(bf16[2,56,384]{2,0,1:T(2,128)(2,1)S(1)} %get-tuple-element.71), channel_id=1, source_target_pairs={{0,4},{2,6},{4,0},{6,2},{1,5},{3,7},{5,1},{7,3},{8,12},{10,14},{12... | collective-permute-start | bytes 258056 | tf_op jit(solution)/shard_map/ppermute | solution.py:35
  202.7 1.4 copy.32
  204.1 1.0 broadcast_in_dim_reshape.3
  205.2 1.3 collective-permute-done.20
  206.5 1.9 collective-permute-done.21
  208.7 2.0 collective-permute-start.22
  210.7 6.0 %collective-permute-done.22 = bf16[56,384]{1,0:T(8,128)(2,1)S(1)} collective-permute-done((bf16[56,384]{1,0:T(8,128)(2,1)S(1)}, bf16[56,384]{1,0:T(8,128)(2,1)S(1)}, u32[]{:S(2)}, u32[]{:S(2)}) %collective-permute-start.22) | collective-permute-done | bytes 43040 | tf_op jit(solution)/shard_map/ppermute | solution.py:35
  216.8 2.7 %collective-permute-start.23 = (bf16[12,384]{1,0:T(8,128)(2,1)S(1)}, bf16[12,384]{1,0:T(8,128)(2,1)S(1)}, u32[]{:S(2)}, u32[]{:S(2)}) collective-permute-start(bf16[12,384]{1,0:T(8,128)(2,1)S(1)} %get-tuple-element.75), channel_id=1, source_target_pairs={{0,32},{32,64},{64,96},{96,0},{1,33},{33,65},{65,97},{97,1},{2,34}... | collective-permute-start | bytes 27656 | tf_op jit(solution)/shard_map/ppermute | solution.py:35
  219.5 1.2 collective-permute-start.24
  220.7 1.2 collective-permute-start.25
  222.6 1.5 collective-permute-done.24
  (81 shorter events, 14.4 us)
Async XLA Ops:
  0.6 36.0 %copy-start = (bf16[3,128,2048]{2,1,0:T(8,128)(2,1)S(1)}, bf16[3,128,2048]{2,1,0:T(8,128)(2,1)}, u32[]{:S(2)}) copy-start(bf16[3,128,2048]{2,1,0:T(8,128)(2,1)} %param.13) | copy-start | bytes 4718596
  4.1 11.8 %copy-start.12 = (s32[2,1]{0,1:T(1,128)S(1)}, s32[2,1]{0,1:T(1,128)}, u32[]{:S(2)}) copy-start(s32[2,1]{0,1:T(1,128)} %param.15) | copy-start | bytes 28
  4.1 11.8 %copy-start.13 = (s32[2,1]{0,1:T(1,128)S(1)}, s32[2,1]{0,1:T(1,128)}, u32[]{:S(2)}) copy-start(s32[2,1]{0,1:T(1,128)} %param.14) | copy-start | bytes 28
  4.1 91.3 %all-to-all-start = ((bf16[32,3,128,128]{3,2,1,0:T(8,128)(2,1)}), bf16[32,3,128,128]{3,2,1,0:T(8,128)(2,1)}, u32[]{:S(2)}, u32[]{:S(2)}) async-start(bf16[32,3,128,128]{3,2,1,0:T(8,128)(2,1)} %pack_heads.1), calls=%async_computation | async-start | bytes 6291456 | tf_op jit(solution)/shard_map/all_to_all | solution.py:30
  17.7 4.5 %copy-start.10 = (bf16[1,1,128,3072]{3,2,1,0:T(8,128)(2,1)S(1)}, bf16[1,1,128,3072]{3,2,1,0:T(8,128)(2,1)}, u32[]{:S(2)}) copy-start(bf16[1,1,128,3072]{3,2,1,0:T(8,128)(2,1)} %param.11) | copy-start | bytes 2359300
  25.5 64.0 %collective-permute-start = (bf16[128,384]{1,0:T(8,128)(2,1)}, bf16[128,384]{1,0:T(8,128)(2,1)S(1)}, u32[]{:S(2)}, u32[]{:S(2)}) collective-permute-start(bf16[128,384]{1,0:T(8,128)(2,1)} %copy.27), channel_id=1, source_target_pairs={{0,32},{32,64},{64,96},{96,0},{1,33},{33,65},{65,97},{97,1},{2,34}... | collective-permute-start | bytes 294920 | tf_op jit(solution)/shard_map/ppermute | solution.py:35
  27.2 66.4 %collective-permute-start.1 = (bf16[128,384]{1,0:T(8,128)(2,1)}, bf16[128,384]{1,0:T(8,128)(2,1)}, u32[]{:S(2)}, u32[]{:S(2)}) collective-permute-start(bf16[128,384]{1,0:T(8,128)(2,1)} %copy.27), channel_id=1, source_target_pairs={{0,64},{32,96},{64,0},{96,32},{1,65},{33,97},{65,1},{97,33},{2,66}... | collective-permute-start | bytes 294920 | tf_op jit(solution)/shard_map/ppermute | solution.py:35
  29.6 64.0 %collective-permute-start.2 = (bf16[128,384]{1,0:T(8,128)(2,1)}, bf16[128,384]{1,0:T(8,128)(2,1)}, u32[]{:S(2)}, u32[]{:S(2)}) collective-permute-start(bf16[128,384]{1,0:T(8,128)(2,1)} %copy.27), channel_id=1, source_target_pairs={{0,96},{32,0},{64,32},{96,64},{1,97},{33,1},{65,33},{97,65},{2,98}... | collective-permute-start | bytes 294920 | tf_op jit(solution)/shard_map/ppermute | solution.py:35
  32.3 62.3 %collective-permute-start.3 = (bf16[128,768]{0,1:T(8,128)(2,1)}, bf16[128,768]{0,1:T(8,128)(2,1)}, u32[]{:S(2)}, u32[]{:S(2)}) collective-permute-start(bf16[128,768]{0,1:T(8,128)(2,1)} %bitcast.20), channel_id=1, source_target_pairs={{0,8},{8,16},{16,24},{24,0},{1,9},{9,17},{17,25},{25,1},{2,10},{10... | collective-permute-start | bytes 589832 | tf_op jit(solution)/shard_map/ppermute | solution.py:35
  33.8 60.9 %collective-permute-start.4 = (bf16[128,768]{0,1:T(8,128)(2,1)}, bf16[128,768]{0,1:T(8,128)(2,1)S(1)}, u32[]{:S(2)}, u32[]{:S(2)}) collective-permute-start(bf16[128,768]{0,1:T(8,128)(2,1)} %bitcast.21), channel_id=1, source_target_pairs={{0,16},{8,24},{16,0},{24,8},{1,17},{9,25},{17,1},{25,9},{2,18},{10... | collective-permute-start | bytes 589832 | tf_op jit(solution)/shard_map/ppermute | solution.py:35
  89.5 5.9 %collective-permute-start.5 = (bf16[128,768]{0,1:T(8,128)(2,1)S(1)}, bf16[128,768]{0,1:T(8,128)(2,1)S(1)}, u32[]{:S(2)}, u32[]{:S(2)}) collective-permute-start(bf16[128,768]{0,1:T(8,128)(2,1)S(1)} %bitcast.102), channel_id=1, source_target_pairs={{0,24},{8,0},{16,8},{24,16},{1,25},{9,1},{17,9},{25,17},{2,26},{10... | collective-permute-start | bytes 589832 | tf_op jit(solution)/shard_map/ppermute | solution.py:35
  94.7 0.7 copy-start.14
  95.4 0.7 copy-start.15
  96.1 19.1 %collective-permute-start.6 = (bf16[4,128,384]{2,1,0:T(8,128)(2,1)S(1)}, bf16[4,128,384]{2,1,0:T(8,128)(2,1)S(1)}, u32[]{:S(2)}, u32[]{:S(2)}) collective-permute-start(bf16[4,128,384]{2,1,0:T(8,128)(2,1)S(1)} %pad_maximum_fusion.refs_0_), channel_id=1, source_target_pairs={{0,8},{8,16},{16,24},{24,0},{1,9},{9,17},{17,25},{25,1},{2,10},{10... | collective-permute-start | bytes 1179656 | tf_op jit(solution)/shard_map/ppermute | solution.py:35
  97.3 17.9 %collective-permute-start.7 = (bf16[4,128,384]{2,1,0:T(8,128)(2,1)S(1)}, bf16[4,128,384]{2,1,0:T(8,128)(2,1)S(1)}, u32[]{:S(2)}, u32[]{:S(2)}) collective-permute-start(bf16[4,128,384]{2,1,0:T(8,128)(2,1)S(1)} %pad_maximum_fusion.refs_0_), channel_id=1, source_target_pairs={{0,16},{8,24},{16,0},{24,8},{1,17},{9,25},{17,1},{25,9},{2,18},{10... | collective-permute-start | bytes 1179656 | tf_op jit(solution)/shard_map/ppermute | solution.py:35
  101.2 14.0 %collective-permute-start.8 = (bf16[4,128,384]{2,1,0:T(8,128)(2,1)S(1)}, bf16[4,128,384]{2,1,0:T(8,128)(2,1)S(1)}, u32[]{:S(2)}, u32[]{:S(2)}) collective-permute-start(bf16[4,128,384]{2,1,0:T(8,128)(2,1)S(1)} %pad_maximum_fusion.refs_0_), channel_id=1, source_target_pairs={{0,24},{8,0},{16,8},{24,16},{1,25},{9,1},{17,9},{25,17},{2,26},{10... | collective-permute-start | bytes 1179656 | tf_op jit(solution)/shard_map/ppermute | solution.py:35
  115.2 9.6 %copy-start.2 = (bf16[4,128,384]{2,1,0:T(8,128)(2,1)}, bf16[4,128,384]{2,1,0:T(8,128)(2,1)S(1)}, u32[]{:S(2)}) copy-start(bf16[4,128,384]{2,1,0:T(8,128)(2,1)S(1)} %collective-permute-done.8.refs_3_) | copy-start | bytes 1179652
  124.9 1.2 copy-start.6
  126.0 0.8 copy-start.8
  126.8 26.9 %all-to-all-start.1 = ((bf16[16,128,128]{2,1,0:T(8,128)(2,1)}), bf16[16,128,128]{2,1,0:T(8,128)(2,1)}, u32[]{:S(2)}, u32[]{:S(2)}) async-start(bf16[16,128,128]{2,1,0:T(8,128)(2,1)} %bitcast.23), calls=%async_computation.1 | async-start | bytes 1048576 | tf_op jit(solution)/shard_map/all_to_all | solution.py:30
  134.7 1.0 copy-start.3
  135.7 1.4 copy-start.7
  137.1 1.0 copy-start.9
  151.4 0.8 copy-start.1
  152.2 0.8 copy-start.4
  153.0 0.7 copy-start.5
  153.7 40.7 %copy-start.11 = (bf16[128,8,1,96]{0,3,2,1:T(8,128)(2,1)S(1)}, bf16[128,8,1,96]{0,3,2,1:T(8,128)(2,1)}, u32[]{:S(2)}) copy-start(bf16[128,8,1,96]{0,3,2,1:T(8,128)(2,1)} %get-tuple-element.68) | copy-start | bytes 589828
  153.7 13.8 %collective-permute-start.10 = (bf16[4,128,384]{2,1,0:T(8,128)(2,1)}, bf16[4,128,384]{2,1,0:T(8,128)(2,1)S(1)}, u32[]{:S(2)}, u32[]{:S(2)}) collective-permute-start(bf16[4,128,384]{2,1,0:T(8,128)(2,1)} %copy-done.5), channel_id=1, source_target_pairs={{0,16},{8,24},{16,0},{24,8},{1,17},{9,25},{17,1},{25,9},{2,18},{10... | collective-permute-start | bytes 1179656 | tf_op jit(solution)/shard_map/ppermute | solution.py:35
  157.1 17.0 %collective-permute-start.11 = (bf16[4,128,384]{2,1,0:T(8,128)(2,1)}, bf16[4,128,384]{2,1,0:T(8,128)(2,1)S(1)}, u32[]{:S(2)}, u32[]{:S(2)}) collective-permute-start(bf16[4,128,384]{2,1,0:T(8,128)(2,1)} %copy-done.4), channel_id=1, source_target_pairs={{0,24},{8,0},{16,8},{24,16},{1,25},{9,1},{17,9},{25,17},{2,26},{10... | collective-permute-start | bytes 1179656 | tf_op jit(solution)/shard_map/ppermute | solution.py:35
  158.3 15.8 %collective-permute-start.9 = (bf16[4,128,384]{2,1,0:T(8,128)(2,1)}, bf16[4,128,384]{2,1,0:T(8,128)(2,1)S(1)}, u32[]{:S(2)}, u32[]{:S(2)}) collective-permute-start(bf16[4,128,384]{2,1,0:T(8,128)(2,1)} %copy-done.1), channel_id=1, source_target_pairs={{0,8},{8,16},{16,24},{24,0},{1,9},{9,17},{17,25},{25,1},{2,10},{10... | collective-permute-start | bytes 1179656 | tf_op jit(solution)/shard_map/ppermute | solution.py:35
  174.3 7.6 %collective-permute-start.12 = (bf16[128,384]{1,0:T(8,128)(2,1)S(1)}, bf16[128,384]{1,0:T(8,128)(2,1)S(1)}, u32[]{:S(2)}, u32[]{:S(2)}) collective-permute-start(bf16[128,384]{1,0:T(8,128)(2,1)S(1)} %get-tuple-element.72), channel_id=1, source_target_pairs={{0,32},{32,64},{64,96},{96,0},{1,33},{33,65},{65,97},{97,1},{2,34}... | collective-permute-start | bytes 294920 | tf_op jit(solution)/shard_map/ppermute | solution.py:35
  176.1 9.2 %collective-permute-start.13 = (bf16[128,384]{1,0:T(8,128)(2,1)S(1)}, bf16[128,384]{1,0:T(8,128)(2,1)S(1)}, u32[]{:S(2)}, u32[]{:S(2)}) collective-permute-start(bf16[128,384]{1,0:T(8,128)(2,1)S(1)} %get-tuple-element.74), channel_id=1, source_target_pairs={{0,64},{32,96},{64,0},{96,32},{1,65},{33,97},{65,1},{97,33},{2,66}... | collective-permute-start | bytes 294920 | tf_op jit(solution)/shard_map/ppermute | solution.py:35
  178.5 6.9 %collective-permute-start.14 = (bf16[128,384]{1,0:T(8,128)(2,1)S(1)}, bf16[128,384]{1,0:T(8,128)(2,1)S(1)}, u32[]{:S(2)}, u32[]{:S(2)}) collective-permute-start(bf16[128,384]{1,0:T(8,128)(2,1)S(1)} %get-tuple-element.73), channel_id=1, source_target_pairs={{0,96},{32,0},{64,32},{96,64},{1,97},{33,1},{65,33},{97,65},{2,98}... | collective-permute-start | bytes 294920 | tf_op jit(solution)/shard_map/ppermute | solution.py:35
  185.4 5.9 %collective-permute-start.15 = (bf16[128,384]{1,0:T(8,128)(2,1)S(1)}, bf16[128,384]{1,0:T(8,128)(2,1)S(1)}, u32[]{:S(2)}, u32[]{:S(2)}) collective-permute-start(bf16[128,384]{1,0:T(8,128)(2,1)S(1)} %fusion.22), channel_id=1, source_target_pairs={{0,8},{8,16},{16,24},{24,0},{1,9},{9,17},{17,25},{25,1},{2,10},{10... | collective-permute-start | bytes 294920 | tf_op jit(solution)/shard_map/ppermute | solution.py:35
  187.0 7.4 %collective-permute-start.16 = (bf16[128,384]{1,0:T(8,128)(2,1)S(1)}, bf16[128,384]{1,0:T(8,128)(2,1)S(1)}, u32[]{:S(2)}, u32[]{:S(2)}) collective-permute-start(bf16[128,384]{1,0:T(8,128)(2,1)S(1)} %fusion.22), channel_id=1, source_target_pairs={{0,16},{8,24},{16,0},{24,8},{1,17},{9,25},{17,1},{25,9},{2,18},{10... | collective-permute-start | bytes 294920 | tf_op jit(solution)/shard_map/ppermute | solution.py:35
  189.7 4.7 %collective-permute-start.17 = (bf16[128,384]{1,0:T(8,128)(2,1)S(1)}, bf16[128,384]{1,0:T(8,128)(2,1)S(1)}, u32[]{:S(2)}, u32[]{:S(2)}) collective-permute-start(bf16[128,384]{1,0:T(8,128)(2,1)S(1)} %fusion.22), channel_id=1, source_target_pairs={{0,24},{8,0},{16,8},{24,16},{1,25},{9,1},{17,9},{25,17},{2,26},{10... | collective-permute-start | bytes 294920 | tf_op jit(solution)/shard_map/ppermute | solution.py:35
  197.3 1.7 collective-permute-start.18
  199.7 5.5 %collective-permute-start.19 = (bf16[2,56,384]{2,0,1:T(2,128)(2,1)S(1)}, bf16[2,56,384]{2,0,1:T(2,128)(2,1)S(1)}, u32[]{:S(2)}, u32[]{:S(2)}) collective-permute-start(bf16[2,56,384]{2,0,1:T(2,128)(2,1)S(1)} %get-tuple-element.69), channel_id=1, source_target_pairs={{0,2},{2,4},{4,6},{6,0},{1,3},{3,5},{5,7},{7,1},{8,10},{10,12},{12... | collective-permute-start | bytes 258056 | tf_op jit(solution)/shard_map/ppermute | solution.py:35
  200.3 6.2 %collective-permute-start.20 = (bf16[2,56,384]{2,0,1:T(2,128)(2,1)S(1)}, bf16[2,56,384]{2,0,1:T(2,128)(2,1)S(1)}, u32[]{:S(2)}, u32[]{:S(2)}) collective-permute-start(bf16[2,56,384]{2,0,1:T(2,128)(2,1)S(1)} %get-tuple-element.71), channel_id=1, source_target_pairs={{0,4},{2,6},{4,0},{6,2},{1,5},{3,7},{5,1},{7,3},{8,12},{10,14},{12... | collective-permute-start | bytes 258056 | tf_op jit(solution)/shard_map/ppermute | solution.py:35
  202.7 5.7 %collective-permute-start.21 = (bf16[2,56,384]{2,0,1:T(2,128)(2,1)S(1)}, bf16[2,56,384]{2,0,1:T(2,128)(2,1)S(1)}, u32[]{:S(2)}, u32[]{:S(2)}) collective-permute-start(bf16[2,56,384]{2,0,1:T(2,128)(2,1)S(1)} %get-tuple-element.70), channel_id=1, source_target_pairs={{0,6},{2,0},{4,2},{6,4},{1,7},{3,1},{5,3},{7,5},{8,14},{10,8},{12,... | collective-permute-start | bytes 258056 | tf_op jit(solution)/shard_map/ppermute | solution.py:35
  208.7 8.0 %collective-permute-start.22 = (bf16[56,384]{1,0:T(8,128)(2,1)S(1)}, bf16[56,384]{1,0:T(8,128)(2,1)S(1)}, u32[]{:S(2)}, u32[]{:S(2)}) collective-permute-start(bf16[56,384]{1,0:T(8,128)(2,1)S(1)} %bitcast.105), channel_id=1, source_target_pairs={{0,128},{128,0},{1,129},{129,1},{2,130},{130,2},{3,131},{131,3},{4... | collective-permute-start | bytes 129032 | tf_op jit(solution)/shard_map/ppermute | solution.py:35
  216.8 5.8 %collective-permute-start.23 = (bf16[12,384]{1,0:T(8,128)(2,1)S(1)}, bf16[12,384]{1,0:T(8,128)(2,1)S(1)}, u32[]{:S(2)}, u32[]{:S(2)}) collective-permute-start(bf16[12,384]{1,0:T(8,128)(2,1)S(1)} %get-tuple-element.75), channel_id=1, source_target_pairs={{0,32},{32,64},{64,96},{96,0},{1,33},{33,65},{65,97},{97,1},{2,34}... | collective-permute-start | bytes 27656 | tf_op jit(solution)/shard_map/ppermute | solution.py:35
  219.5 4.6 %collective-permute-start.24 = (bf16[12,384]{1,0:T(8,128)(2,1)S(1)}, bf16[12,384]{1,0:T(8,128)(2,1)S(1)}, u32[]{:S(2)}, u32[]{:S(2)}) collective-permute-start(bf16[12,384]{1,0:T(8,128)(2,1)S(1)} %get-tuple-element.77), channel_id=1, source_target_pairs={{0,64},{32,96},{64,0},{96,32},{1,65},{33,97},{65,1},{97,33},{2,66}... | collective-permute-start | bytes 27656 | tf_op jit(solution)/shard_map/ppermute | solution.py:35
  220.7 3.7 %collective-permute-start.25 = (bf16[12,384]{1,0:T(8,128)(2,1)S(1)}, bf16[12,384]{1,0:T(8,128)(2,1)S(1)}, u32[]{:S(2)}, u32[]{:S(2)}) collective-permute-start(bf16[12,384]{1,0:T(8,128)(2,1)S(1)} %get-tuple-element.76), channel_id=1, source_target_pairs={{0,96},{32,0},{64,32},{96,64},{1,97},{33,1},{65,33},{97,65},{2,98}... | collective-permute-start | bytes 27656 | tf_op jit(solution)/shard_map/ppermute | solution.py:35

commit v5 on v4

--- a/solution.py
+++ b/solution.py
@@ -60,6 +60,23 @@
     return value
 
 
+def whole(shape):
+    return pl.BlockSpec(shape, lambda i: (0,) * len(shape))
+
+
+HBM = pl.BlockSpec(memory_space=pltpu.HBM)
+
+
+def kept(arrays):
+    return [pltpu.with_memory_space_constraint(array, pltpu.HBM) for array in arrays]
+
+
+def started(source, target, semaphore):
+    copy = pltpu.make_async_copy(source, target, semaphore)
+    copy.start()
+    return copy
+
+
 def pack_kernel(q_ref, k_ref, v_ref, out_ref):
     heads = out_ref.shape[0]
     for part, ref in enumerate((q_ref, k_ref, v_ref)):
@@ -70,12 +87,13 @@
 def packed_by_head(q, k, v):
     halves, rows, columns = q.shape
     heads = columns // HDIM
-    spec = pl.BlockSpec((1, rows, columns), lambda i: (i, 0, 0))
+    step_rows = rows // 4
+    spec = pl.BlockSpec((1, step_rows, columns), lambda i, j: (i, j, 0))
     return pl.pallas_call(
         pack_kernel,
-        grid=(halves,),
+        grid=(halves, rows // step_rows),
         in_specs=[spec] * 3,
-        out_specs=pl.BlockSpec((heads, 3, rows, HDIM), lambda i: (i, 0, 0, 0)),
+        out_specs=pl.BlockSpec((heads, 3, step_rows, HDIM), lambda i, j: (i, 0, j, 0)),
         out_shape=jax.ShapeDtypeStruct((halves * heads, 3, rows, HDIM), q.dtype),
         cost_estimate=pl.CostEstimate(flops=0, transcendentals=0, bytes_accessed=12 * q.size),
         name="pack_heads",
@@ -131,11 +149,11 @@
 
 def teacher(scale, heads):
     tokens = heads.shape[1] * heads.shape[3]
-    vmem = pl.BlockSpec(memory_space=pltpu.VMEM)
     return pl.pallas_call(
         teacher_kernel,
-        in_specs=[pl.BlockSpec(memory_space=pltpu.SMEM), vmem],
-        out_specs=vmem,
+        grid=(1,),
+        in_specs=[pl.BlockSpec(memory_space=pltpu.SMEM), whole(heads.shape)],
+        out_specs=whole((tokens, HDIM)),
         out_shape=jax.ShapeDtypeStruct((tokens, HDIM), F32),
         scratch_shapes=[
             pltpu.VMEM((2, tokens, HDIM), BF),
@@ -148,14 +166,16 @@
             transcendentals=2 * tokens * tokens,
             bytes_accessed=4 * MIB,
         ),
-        compiler_params=pltpu.CompilerParams(vmem_limit_bytes=24 * MIB),
+        compiler_params=pltpu.CompilerParams(vmem_limit_bytes=48 * MIB),
         name="teacher_forward",
     )(scale, heads)
 
 
 def student_kernel(n_fast, place_ref, inv_ref, heads_ref, target_ref, up_ref, *refs):
     low_refs = refs[:n_fast]
-    out_ref, upstream_ref, student_ref, stats_ref, key_ref, value_ref, scores_ref = refs[n_fast:]
+    outs, locals_ = refs[n_fast : n_fast + 4], refs[n_fast + 4 : n_fast + 8]
+    out_ref, upstream_ref, student_ref, stats_ref = locals_
+    key_ref, value_ref, scores_ref, sems = refs[n_fast + 8 :]
     rows = heads_ref.shape[3]
     tokens = out_ref.shape[0]
     n_slow = low_refs[0].shape[0]
@@ -176,6 +196,7 @@
                 student_ref[part, where] = (
                     frozen + adapted[slow * rows : (slow + 1) * rows]
                 ).astype(BF)
+    copies = [started(student_ref, outs[2], sems.at[2])]
     for block in range(n_slow * n_fast):
         where = slice(block * rows, (block + 1) * rows)
         key_ref[:, where] = jnp.transpose(student_ref[1, where])
@@ -211,48 +232,57 @@
     stats_ref[...] = jnp.zeros_like(stats_ref)
     put_scores(0, 0)
     lax.fori_loop(0, steps // 2, two_blocks, 0)
+    copies += [started(locals_[i], outs[i], sems.at[i]) for i in (0, 1, 3)]
+    for copy in copies:
+        copy.wait()
 
 
 def student_forward(place, inverse, heads, target, up, low):
     tokens = target.shape[0]
     one_pass = (1, *heads.shape[1:])
-    vmem = pl.BlockSpec(memory_space=pltpu.VMEM)
     smem = pl.BlockSpec(memory_space=pltpu.SMEM)
+    outs = [
+        jax.ShapeDtypeStruct((tokens, HDIM), BF),
+        jax.ShapeDtypeStruct((tokens, HDIM), BF),
+        jax.ShapeDtypeStruct((3, tokens, HDIM), BF),
+        jax.ShapeDtypeStruct((8, tokens), F32),
+    ]
     return pl.pallas_call(
         functools.partial(student_kernel, len(low)),
         grid=(1,),
-        in_specs=[smem, smem, pl.BlockSpec(one_pass, lambda i: (0, 0, 0, 0, 0))]
-        + [vmem] * (2 + len(low)),
-        out_specs=[vmem] * 4,
-        out_shape=[
-            jax.ShapeDtypeStruct((tokens, HDIM), BF),
-            jax.ShapeDtypeStruct((tokens, HDIM), BF),
-            jax.ShapeDtypeStruct((3, tokens, HDIM), BF),
-            jax.ShapeDtypeStruct((8, tokens), F32),
-        ],
-        scratch_shapes=[
+        in_specs=[smem, smem, whole(one_pass)]
+        + [whole(operand.shape) for operand in (target, up, *low)],
+        out_specs=[HBM] * len(outs),
+        out_shape=[pltpu.HBM(out.shape, out.dtype) for out in outs],
+        scratch_shapes=[pltpu.VMEM(out.shape, out.dtype) for out in outs]
+        + [
             pltpu.VMEM((HDIM, tokens), BF),
             pltpu.VMEM((tokens, 2 * HDIM), BF),
             pltpu.VMEM((2, 256, tokens), F32),
+            pltpu.SemaphoreType.DMA((len(outs),)),
         ],
         cost_estimate=pl.CostEstimate(
             flops=4 * tokens * tokens * HDIM,
             transcendentals=tokens * tokens,
             bytes_accessed=6 * MIB,
         ),
-        compiler_params=pltpu.CompilerParams(vmem_limit_bytes=24 * MIB),
+        compiler_params=pltpu.CompilerParams(vmem_limit_bytes=48 * MIB),
         name="student_forward",
     )(place, inverse, heads, target, up, *low)
 
 
-def backward_kernel(
-    n_fast, place_ref, student_ref, upstream_ref, stats_ref, up_ref, *refs
-):
-    low_refs, back_refs = refs[:n_fast], refs[n_fast : 2 * n_fast]
-    grad_up_ref, dq_ref, dk_ref, dv_ref, flat_ref = refs[2 * n_fast :]
+def backward_kernel(n_fast, place_ref, up_ref, *refs):
+    n_in = n_fast + 3
+    sources, outs, refs = refs[:n_in], refs[n_in : n_in + n_fast + 1], refs[n_in + n_fast + 1 :]
+    student_ref, upstream_ref, stats_ref, low_ref, back_ref, grad_up_ref = refs[:6]
+    dq_ref, dk_ref, dv_ref, flat_ref, in_sems, out_sems = refs[6:]
+    _, n_slow, rows, _ = low_ref.shape
     tokens = student_ref.shape[1]
-    n_slow, rows, _ = low_refs[0].shape
     here_slow, here_fast = place_ref[0], place_ref[1]
+    targets = [student_ref, upstream_ref, stats_ref] + [low_ref.at[d] for d in range(n_fast)]
+    loads = [started(sources[i], targets[i], in_sems.at[i]) for i in range(n_in)]
+    for load in loads[:3]:
+        load.wait()
     step_rows = 512
     dk_ref[...] = jnp.zeros_like(dk_ref)
     dv_ref[...] = jnp.zeros_like(dv_ref)
@@ -273,45 +303,66 @@
         return carry
 
     lax.fori_loop(0, tokens // step_rows, one_block, 0)
-    for part, (ref, factor) in enumerate(((dq_ref, FACTOR), (dk_ref, FACTOR), (dv_ref, 1.0))):
-        up = up_ref[part]
+    for load in loads[3:]:
+        load.wait()
+
+    def grads(ref, factor, slow, fast):
+        block = lax.rem(here_slow + slow, n_slow) * n_fast + lax.rem(here_fast + fast, n_fast)
+        grad = ref[pl.ds(pl.multiple_of(block * rows, rows), rows)] * factor
+        return grad.astype(BF)
+
+    parts = ((dq_ref, FACTOR), (dk_ref, FACTOR), (dv_ref, 1.0))
+    stores = []
+    for fast in (*range(1, n_fast), 0):
+        for part, (ref, factor) in enumerate(parts):
+            columns = slice(part * RANK, (part + 1) * RANK)
+            for slow in range(n_slow):
+                grad = grads(ref, factor, slow, fast)
+                back_ref[fast, slow, :, columns] = dot(grad, up_ref[part], NT).astype(BF)
+        stores.append(started(back_ref.at[fast], outs[fast], out_sems.at[fast]))
+    for part, (ref, factor) in enumerate(parts):
+        columns = slice(part * RANK, (part + 1) * RANK)
         total = jnp.zeros((RANK, HDIM), F32)
-        columns = slice(part * RANK, (part + 1) * RANK)
         for fast in range(n_fast):
             for slow in range(n_slow):
-                ahead = lax.rem(here_slow + slow, n_slow) * n_fast + lax.rem(
-                    here_fast + fast, n_fast
-                )
-                behind = lax.rem(here_slow - slow + n_slow, n_slow) * n_fast + lax.rem(
-                    here_fast - fast + n_fast, n_fast
-                )
-                grad = ref[pl.ds(pl.multiple_of(ahead * rows, rows), rows)] * factor
-                back_refs[fast][slow, :, columns] = dot(grad.astype(BF), up, NT).astype(BF)
-                grad = ref[pl.ds(pl.multiple_of(behind * rows, rows), rows)] * factor
-                total += dot(low_refs[fast][slow, :, columns], grad.astype(BF), TN)
+                grad = grads(ref, factor, n_slow - slow, n_fast - fast)
+                total += dot(low_ref[fast, slow, :, columns], grad, TN)
         grad_up_ref[:, part * HDIM : (part + 1) * HDIM] = total.astype(BF)
+    stores.append(started(grad_up_ref, outs[n_fast], out_sems.at[n_fast]))
+    for store in stores:
+        store.wait()
 
 
 def backward(place, student, upstream, stats, up, low):
     tokens, n_fast = student.shape[1], len(low)
-    vmem = pl.BlockSpec(memory_space=pltpu.VMEM)
+    outs = [jax.ShapeDtypeStruct(low[0].shape, BF)] * n_fast
+    outs.append(jax.ShapeDtypeStruct((RANK, 3 * HDIM), BF))
     return pl.pallas_call(
         functools.partial(backward_kernel, n_fast),
-        in_specs=[pl.BlockSpec(memory_space=pltpu.SMEM)] + [vmem] * (4 + n_fast),
-        out_specs=[vmem] * (n_fast + 1),
-        out_shape=[jax.ShapeDtypeStruct(low[0].shape, BF)] * n_fast
-        + [
-            jax.ShapeDtypeStruct((RANK, 3 * HDIM), BF),
+        grid=(1,),
+        in_specs=[pl.BlockSpec(memory_space=pltpu.SMEM), whole(up.shape)] + [HBM] * (n_fast + 3),
+        out_specs=[HBM] * len(outs),
+        out_shape=[pltpu.HBM(out.shape, out.dtype) for out in outs],
+        scratch_shapes=[
+            pltpu.VMEM(student.shape, BF),
+            pltpu.VMEM(upstream.shape, BF),
+            pltpu.VMEM(stats.shape, F32),
+            pltpu.VMEM((n_fast, *low[0].shape), BF),
+            pltpu.VMEM((n_fast, *low[0].shape), BF),
+            pltpu.VMEM((RANK, 3 * HDIM), BF),
+            *[pltpu.VMEM((tokens, HDIM), F32)] * 3,
+            pltpu.VMEM((HDIM, tokens), BF),
+            pltpu.SemaphoreType.DMA((n_fast + 3,)),
+            pltpu.SemaphoreType.DMA((n_fast + 1,)),
         ],
-        scratch_shapes=[pltpu.VMEM((tokens, HDIM), F32)] * 3 + [pltpu.VMEM((HDIM, tokens), BF)],
         cost_estimate=pl.CostEstimate(
             flops=10 * tokens * tokens * HDIM,
             transcendentals=tokens * tokens,
             bytes_accessed=6 * MIB,
         ),
-        compiler_params=pltpu.CompilerParams(vmem_limit_bytes=40 * MIB),
+        compiler_params=pltpu.CompilerParams(vmem_limit_bytes=48 * MIB),
         name="attention_backward",
-    )(place, student, upstream, stats, up, *low)
+    )(place, up, *kept((student, upstream, stats, *low)))
 
 
 def body(
@@ -350,14 +401,15 @@
     part_cols = width // (groups * n_fast)
     spread = parts_ahead(features.reshape(rows, groups, n_fast, part_cols), "y", 2)
     spread = [part.reshape(rows, groups * part_cols) for part in spread]
-    columns = [spread[0]] + [shifted(spread[d], "y", d) for d in range(1, n_fast)]
+    columns = [spread[0]] + [shifted(spread[d], "y", d) for d in range(1, n_fast - 1)]
+    spread = spread[-1]
 
     place = jnp.stack([lax.axis_index("z"), lax.axis_index("y")]).astype(jnp.int32)
     up = lax.dynamic_slice_in_dim(adapter_up_weight, seq_index * HDIM, HDIM, 2)
     inverse = jnp.full((1,), 1.0 / math.sqrt(total_rows), F32)
 
-    heads, low_slow, up, place, *columns = lax.optimization_barrier(
-        (heads, low_slow, up, place, *columns)
+    heads, low_slow, up, place, spread, *columns = lax.optimization_barrier(
+        (heads, low_slow, up, place, spread, *columns)
     )
     low_all = from_each(low_slow, "y")
     target = teacher(scale, heads)
@@ -366,7 +418,10 @@
     tokens_out = exchange(out.reshape(n_slow * n_fast, rows, HDIM), ("z", "y"))
 
     *back, up_partial = backward(place, student, upstream, stats, up, low_all)
-    tokens_out, up_partial, *back = lax.optimization_barrier((tokens_out, up_partial, *back))
+    tokens_out, up_partial, spread, *back = lax.optimization_barrier(
+        (tokens_out, up_partial, spread, *back)
+    )
+    columns.append(shifted(spread, "y", n_fast - 1))
     student_out = jnp.moveaxis(tokens_out, 0, 1).reshape(rows, -1)
 
     back = summed_parts(back, "y").astype(BF)

time: 226 us -> 229 us (1.013)
  local copies, waits for them, and re-layouts: 19.8 us -> 11.7 us
  Pallas kernels: 40.1 us -> 46.1 us
  other arithmetic: 3.13 us -> 6.88 us
    unnamed x36 -> x30, local copies, waits for them, and re-layouts: 13.8 us -> 5.48 us
    pallas_call x3, Pallas kernels: 30.5 us -> 36 us  [the longest x1 15.6 us: backward(): pl.pallas_call(functools.partial(backward_kernel, n_fast), grid=(1,), in_...]
  transfers between devices with their start and end apart: 28 -> 28, of which waited for: 15 -> 14; matrix products, arithmetic and copies ran while one was open for 6% -> 6% of each run, Pallas kernels for 12% -> 13%
where the time goes in v5:
time: 229 us; the launch traced here: 228 us
  waiting for transfers between devices  90.5 us (40%)
  starting transfers between devices  66 us (29%)
  Pallas kernels  46.1 us (20%)
  local copies, waits for them, and re-layouts  11.7 us (5%)
  other arithmetic  6.88 us (3%)
  matrix products  4.12 us (2%)
  between operations  2.46 us (1%)
    ppermute x26, waiting for transfers between devices, shifted(): lax.ppermute(value, axis, [(i, (i + distance) % size) for i in range(size)])  90.5 us
    ppermute x26, starting transfers between devices, shifted(): lax.ppermute(value, axis, [(i, (i + distance) % size) for i in range(size)])  46.2 us
    all_to_all x2, starting transfers between devices, exchange(): return lax.all_to_all(value, axes, split_axis=0, concat_axis=0, tiled=True)  19.8 us
    pallas_call x1, Pallas kernels, backward(): pl.pallas_call(functools.partial(backward_kernel, n_fast), grid=(1,), in_...  15.6 us
    pallas_call x1, Pallas kernels, teacher(): pl.pallas_call(teacher_kernel, grid=(1,), in_specs=[pl.BlockSpec(memory_s...  13.7 us
    pallas_call x1, Pallas kernels, student_forward(): pl.pallas_call(functools.partial(student_kernel, len(low)), grid=(1,), in...  10.1 us
    pallas_call x1, Pallas kernels, packed_by_head(): pl.pallas_call(pack_kernel, grid=(halves, rows // step_rows), in_specs=[s...  6.63 us
    unnamed x30, local copies, waits for them, and re-layouts  5.48 us
  transfers between devices with their start and end apart: 28, of which 14 were waited for; matrix products, arithmetic and copies ran while one was open for 6% of the time, Pallas kernels for 13%

profile of v5, /device:TPU:6, one launch (start us, length us, event | category | flops | bytes accessed | tf_op | source)
XLA Modules:
  0.0 227.8 jit_solution(811129976778603526)
XLA Ops:
  0.6 6.6 %pack_heads.1 = bf16[32,3,128,128]{3,2,1,0:T(8,128)(2,1)} custom-call(bf16[2,128,2048]{2,1,0:T(8,128)(2,1)} %bitcast.93, bf16[2,128,2048]{2,1,0:T(8,128)(2,1)} %bitcast.94, bf16[2,128,2048]{2,1,0:T(8,128)(2,1)} %bitcast.95), custom_call_target="tpu_custom_call" | custom-call | bytes 6291456 | tf_op jit(solution)/shard_map/pack_heads/pallas_call | solution.py:92
  7.3 11.7 %all-to-all-start = ((bf16[32,3,128,128]{3,2,1,0:T(8,128)(2,1)}), bf16[32,3,128,128]{3,2,1,0:T(8,128)(2,1)}, u32[]{:S(2)}, u32[]{:S(2)}) async-start(bf16[32,3,128,128]{3,2,1,0:T(8,128)(2,1)} %pack_heads.1), calls=%async_computation | async-start | bytes 6291456 | tf_op jit(solution)/shard_map/all_to_all | solution.py:30
  20.9 4.4 %copy.26 = bf16[3,3072,128]{1,2,0:T(8,128)(2,1)} copy(bf16[3,3072,128]{2,1,0:T(8,128)(2,1)} %param.12) | data formatting | bytes 4718592 | tf_op args[4]
  25.4 2.4 %fusion.7 = f32[128,384]{0,1:S(1)} fusion(bf16[3072,384]{0,1:T(8,128)(2,1)} %bitcast.87, bf16[1,1,128,3072]{3,2,1,0:T(8,128)(2,1)S(1)} %copy-done.5), kind=kOutput, calls=%fused_computation.8 | convolution fusion | flops 301989888 | bytes 3342336
  28.7 1.7 collective-permute-start
  30.4 2.4 %collective-permute-start.1 = (bf16[128,384]{1,0:T(8,128)(2,1)}, bf16[128,384]{1,0:T(8,128)(2,1)}, u32[]{:S(2)}, u32[]{:S(2)}) collective-permute-start(bf16[128,384]{1,0:T(8,128)(2,1)} %copy.27), channel_id=1, source_target_pairs={{0,64},{32,96},{64,0},{96,32},{1,65},{33,97},{65,1},{97,33},{2,66}... | collective-permute-start | bytes 294920 | tf_op jit(solution)/shard_map/ppermute | solution.py:35
  32.8 1.5 collective-permute-start.2
  35.5 1.5 collective-permute-start.3
  36.9 2.7 %collective-permute-start.4 = (bf16[128,768]{0,1:T(8,128)(2,1)S(1)}, bf16[128,768]{0,1:T(8,128)(2,1)S(1)}, u32[]{:S(2)}, u32[]{:S(2)}) collective-permute-start(bf16[128,768]{0,1:T(8,128)(2,1)S(1)} %bitcast.104), channel_id=1, source_target_pairs={{0,16},{8,24},{16,0},{24,8},{1,17},{9,25},{17,1},{25,9},{2,18},{10... | collective-permute-start | bytes 589832 | tf_op jit(solution)/shard_map/ppermute | solution.py:35
  39.9 52.8 %collective-permute-done = bf16[128,384]{1,0:T(8,128)(2,1)S(1)} collective-permute-done((bf16[128,384]{1,0:T(8,128)(2,1)}, bf16[128,384]{1,0:T(8,128)(2,1)S(1)}, u32[]{:S(2)}, u32[]{:S(2)}) %collective-permute-start) | collective-permute-done | bytes 98336 | tf_op jit(solution)/shard_map/ppermute | solution.py:35
  92.7 4.1 %collective-permute-done.1 = bf16[128,384]{1,0:T(8,128)(2,1)} collective-permute-done((bf16[128,384]{1,0:T(8,128)(2,1)}, bf16[128,384]{1,0:T(8,128)(2,1)}, u32[]{:S(2)}, u32[]{:S(2)}) %collective-permute-start.1) | collective-permute-done | bytes 98336 | tf_op jit(solution)/shard_map/ppermute | solution.py:35
  96.8 1.0 pad_maximum_fusion.refs_0_.refs_3_
  97.9 1.5 collective-permute-start.5
  99.4 2.6 %collective-permute-start.6 = (bf16[4,128,384]{2,1,0:T(8,128)(2,1)S(1)}, bf16[4,128,384]{2,1,0:T(8,128)(2,1)S(1)}, u32[]{:S(2)}, u32[]{:S(2)}) collective-permute-start(bf16[4,128,384]{2,1,0:T(8,128)(2,1)S(1)} %pad_maximum_fusion.refs_0_.refs_3_), channel_id=1, source_target_pairs={{0,16},{8,24},{16,0},{24,8},{1,17},{9,25},{17,1},{25,9},{2,18},{10... | collective-permute-start | bytes 1179656 | tf_op jit(solution)/shard_map/ppermute | solution.py:35
  102.0 1.5 collective-permute-start.7
  103.5 13.7 %teacher_forward.1.target_ref = f32[2048,128]{1,0:T(8,128)S(1)} custom-call(f32[1]{0:T(128)} %bitcast.9.scale_ref, bf16[2,16,3,128,128]{4,3,2,1,0:T(8,128)(2,1)} %bitcast.3.heads_ref), custom_call_target="tpu_custom_call" | custom-call | flops 4294967296 | bytes 4194304 | tf_op jit(solution)/shard_map/teacher_forward/pallas_call | solution.py:152
  117.3 10.1 %student_forward.1 = (bf16[2048,128]{1,0:T(8,128)(2,1)}, bf16[2048,128]{1,0:T(8,128)(2,1)}, bf16[3,2048,128]{2,1,0:T(8,128)(2,1)}, f32[8,2048]{1,0:T(8,128)}) custom-call(s32[2]{0:T(128)S(1)} %pad_add_fusion.place_ref, f32[1]{0:T(128)} %constant.172.clone.1.inv_ref, bf16[2,16,3,128,128]{4,3,2,1,0:T(8,128)(2,1)} %bitcast.3.heads_ref, ...), custom_call_target="tpu_custom_call" | custom-call | flops 2147483648 | bytes 6291456 | tf_op jit(solution)/shard_map/student_forward/pallas_call | solution.py:250
  127.4 8.0 %all-to-all-start.1 = ((bf16[16,128,128]{2,1,0:T(8,128)(2,1)}), bf16[16,128,128]{2,1,0:T(8,128)(2,1)S(1)}, u32[]{:S(2)}, u32[]{:S(2)}) async-start(bf16[16,128,128]{2,1,0:T(8,128)(2,1)} %bitcast.101), calls=%async_computation.1 | async-start | bytes 1048576 | tf_op jit(solution)/shard_map/all_to_all | solution.py:30
  135.5 15.6 %attention_backward.1 = (bf16[4,128,384]{2,1,0:T(8,128)(2,1)}, bf16[4,128,384]{2,1,0:T(8,128)(2,1)}, bf16[4,128,384]{2,1,0:T(8,128)(2,1)}, bf16[4,128,384]{2,1,0:T(8,128)(2,1)}, bf16[128,384]{1,0:T(8,128)(2,1)}) custom-call(s32[2]{0:T(128)S(1)} %pad_add_fusion.place_ref, bf16[3,128,128]{2,1,0:T(8,128)(2,1)S(1)} %constant_dynamic-slice_fusion.5.up_ref, ...), custom_call_target="tpu_custom_call" | custom-call | flops 5368709120 | bytes 6291456 | tf_op jit(solution)/shard_map/attention_backward/pallas_call | solution.py:340
  151.2 3.5 %collective-permute-start.10 = (bf16[4,128,384]{2,1,0:T(8,128)(2,1)}, bf16[4,128,384]{2,1,0:T(8,128)(2,1)S(1)}, u32[]{:S(2)}, u32[]{:S(2)}) collective-permute-start(bf16[4,128,384]{2,1,0:T(8,128)(2,1)} %get-tuple-element.58), channel_id=1, source_target_pairs={{0,16},{8,24},{16,0},{24,8},{1,17},{9,25},{17,1},{25,9},{2,18},{10... | collective-permute-start | bytes 1179656 | tf_op jit(solution)/shard_map/ppermute | solution.py:35
  154.7 1.2 collective-permute-start.11
  156.7 8.4 %collective-permute-done.10 = bf16[4,128,384]{2,1,0:T(8,128)(2,1)S(1)} collective-permute-done((bf16[4,128,384]{2,1,0:T(8,128)(2,1)}, bf16[4,128,384]{2,1,0:T(8,128)(2,1)S(1)}, u32[]{:S(2)}, u32[]{:S(2)}) %collective-permute-start.10) | collective-permute-done | bytes 393248 | tf_op jit(solution)/shard_map/ppermute | solution.py:35
  165.1 6.7 %collective-permute-done.11 = bf16[4,128,384]{2,1,0:T(8,128)(2,1)S(1)} collective-permute-done((bf16[4,128,384]{2,1,0:T(8,128)(2,1)}, bf16[4,128,384]{2,1,0:T(8,128)(2,1)S(1)}, u32[]{:S(2)}, u32[]{:S(2)}) %collective-permute-start.11) | collective-permute-done | bytes 393248 | tf_op jit(solution)/shard_map/ppermute | solution.py:35
  171.8 1.2 add_convert_fusion
  173.0 1.8 collective-permute-start.12
  174.8 2.4 %collective-permute-start.13 = (bf16[128,384]{1,0:T(8,128)(2,1)S(1)}, bf16[128,384]{1,0:T(8,128)(2,1)S(1)}, u32[]{:S(2)}, u32[]{:S(2)}) collective-permute-start(bf16[128,384]{1,0:T(8,128)(2,1)S(1)} %get-tuple-element.76), channel_id=1, source_target_pairs={{0,64},{32,96},{64,0},{96,32},{1,65},{33,97},{65,1},{97,33},{2,66}... | collective-permute-start | bytes 294920 | tf_op jit(solution)/shard_map/ppermute | solution.py:35
  177.1 1.5 collective-permute-start.14
  178.6 2.6 %collective-permute-start.8 = (bf16[128,768]{0,1:T(8,128)(2,1)S(1)}, bf16[128,768]{0,1:T(8,128)(2,1)}, u32[]{:S(2)}, u32[]{:S(2)}) collective-permute-start(bf16[128,768]{0,1:T(8,128)(2,1)S(1)} %bitcast.103), channel_id=1, source_target_pairs={{0,24},{8,0},{16,8},{24,16},{1,25},{9,1},{17,9},{25,17},{2,26},{10... | collective-permute-start | bytes 589832 | tf_op jit(solution)/shard_map/ppermute | solution.py:35
  181.2 2.7 %collective-permute-done.13 = bf16[128,384]{1,0:T(8,128)(2,1)S(1)} collective-permute-done((bf16[128,384]{1,0:T(8,128)(2,1)S(1)}, bf16[128,384]{1,0:T(8,128)(2,1)S(1)}, u32[]{:S(2)}, u32[]{:S(2)}) %collective-permute-start.13) | collective-permute-done | bytes 98336 | tf_op jit(solution)/shard_map/ppermute | solution.py:35
  184.0 1.7 collective-permute-start.15
  185.7 2.7 %collective-permute-start.16 = (bf16[128,384]{1,0:T(8,128)(2,1)S(1)}, bf16[128,384]{1,0:T(8,128)(2,1)S(1)}, u32[]{:S(2)}, u32[]{:S(2)}) collective-permute-start(bf16[128,384]{1,0:T(8,128)(2,1)S(1)} %fusion.22), channel_id=1, source_target_pairs={{0,16},{8,24},{16,0},{24,8},{1,17},{9,25},{17,1},{25,9},{2,18},{10... | collective-permute-start | bytes 294920 | tf_op jit(solution)/shard_map/ppermute | solution.py:35
  188.4 1.5 collective-permute-start.17
  190.6 2.6 %collective-permute-done.16 = bf16[128,384]{1,0:T(8,128)(2,1)S(1)} collective-permute-done((bf16[128,384]{1,0:T(8,128)(2,1)S(1)}, bf16[128,384]{1,0:T(8,128)(2,1)S(1)}, u32[]{:S(2)}, u32[]{:S(2)}) %collective-permute-start.16) | collective-permute-done | bytes 98336 | tf_op jit(solution)/shard_map/ppermute | solution.py:35
  193.2 1.7 convolution_convert_fusion
  195.6 1.3 fusion.18
  197.1 1.7 collective-permute-done.18
  198.8 1.4 convert_add_fusion
  201.5 2.4 %collective-permute-start.20 = (bf16[2,56,384]{2,0,1:T(2,128)(2,1)}, bf16[2,56,384]{2,0,1:T(2,128)(2,1)}, u32[]{:S(2)}, u32[]{:S(2)}) collective-permute-start(bf16[2,56,384]{2,0,1:T(2,128)(2,1)} %get-tuple-element.73), channel_id=1, source_target_pairs={{0,4},{2,6},{4,0},{6,2},{1,5},{3,7},{5,1},{7,3},{8,12},{10,14},{12... | collective-permute-start | bytes 258056 | tf_op jit(solution)/shard_map/ppermute | solution.py:35
  204.3 1.0 broadcast_in_dim_reshape.3
  205.3 1.4 collective-permute-done.19
  206.7 1.5 collective-permute-done.20
  208.3 1.5 collective-permute-done.21
  209.7 1.1 fusion.24
  211.0 3.8 %collective-permute-start.22 = (bf16[56,384]{1,0:T(8,128)(2,1)S(1)}, bf16[56,384]{1,0:T(8,128)(2,1)S(1)}, u32[]{:S(2)}, u32[]{:S(2)}) collective-permute-start(bf16[56,384]{1,0:T(8,128)(2,1)S(1)} %bitcast.108), channel_id=1, source_target_pairs={{0,128},{128,0},{1,129},{129,1},{2,130},{130,2},{3,131},{131,3},{4... | collective-permute-start | bytes 129032 | tf_op jit(solution)/shard_map/ppermute | solution.py:35
  214.8 4.6 %collective-permute-done.22 = bf16[56,384]{1,0:T(8,128)(2,1)S(1)} collective-permute-done((bf16[56,384]{1,0:T(8,128)(2,1)S(1)}, bf16[56,384]{1,0:T(8,128)(2,1)S(1)}, u32[]{:S(2)}, u32[]{:S(2)}) %collective-permute-start.22) | collective-permute-done | bytes 43040 | tf_op jit(solution)/shard_map/ppermute | solution.py:35
  219.5 2.2 collective-permute-start.23
  221.7 1.7 collective-permute-start.24
  225.1 1.2 collective-permute-done.24
  (75 shorter events, 10.5 us)
Async XLA Ops:
  0.6 39.1 %copy-start = (bf16[3,128,2048]{2,1,0:T(8,128)(2,1)S(1)}, bf16[3,128,2048]{2,1,0:T(8,128)(2,1)}, u32[]{:S(2)}) copy-start(bf16[3,128,2048]{2,1,0:T(8,128)(2,1)} %param.13) | copy-start | bytes 4718596
  7.3 11.8 %copy-start.9 = (s32[2,1]{0,1:T(1,128)S(1)}, s32[2,1]{0,1:T(1,128)}, u32[]{:S(2)}) copy-start(s32[2,1]{0,1:T(1,128)} %param.15) | copy-start | bytes 28
  7.3 11.8 %copy-start.10 = (s32[2,1]{0,1:T(1,128)S(1)}, s32[2,1]{0,1:T(1,128)}, u32[]{:S(2)}) copy-start(s32[2,1]{0,1:T(1,128)} %param.14) | copy-start | bytes 28
  7.3 90.6 %all-to-all-start = ((bf16[32,3,128,128]{3,2,1,0:T(8,128)(2,1)}), bf16[32,3,128,128]{3,2,1,0:T(8,128)(2,1)}, u32[]{:S(2)}, u32[]{:S(2)}) async-start(bf16[32,3,128,128]{3,2,1,0:T(8,128)(2,1)} %pack_heads.1), calls=%async_computation | async-start | bytes 6291456 | tf_op jit(solution)/shard_map/all_to_all | solution.py:30
  20.9 4.5 %copy-start.5 = (bf16[1,1,128,3072]{3,2,1,0:T(8,128)(2,1)S(1)}, bf16[1,1,128,3072]{3,2,1,0:T(8,128)(2,1)}, u32[]{:S(2)}) copy-start(bf16[1,1,128,3072]{3,2,1,0:T(8,128)(2,1)} %param.11) | copy-start | bytes 2359300
  28.7 64.0 %collective-permute-start = (bf16[128,384]{1,0:T(8,128)(2,1)}, bf16[128,384]{1,0:T(8,128)(2,1)S(1)}, u32[]{:S(2)}, u32[]{:S(2)}) collective-permute-start(bf16[128,384]{1,0:T(8,128)(2,1)} %copy.27), channel_id=1, source_target_pairs={{0,32},{32,64},{64,96},{96,0},{1,33},{33,65},{65,97},{97,1},{2,34}... | collective-permute-start | bytes 294920 | tf_op jit(solution)/shard_map/ppermute | solution.py:35
  30.4 66.4 %collective-permute-start.1 = (bf16[128,384]{1,0:T(8,128)(2,1)}, bf16[128,384]{1,0:T(8,128)(2,1)}, u32[]{:S(2)}, u32[]{:S(2)}) collective-permute-start(bf16[128,384]{1,0:T(8,128)(2,1)} %copy.27), channel_id=1, source_target_pairs={{0,64},{32,96},{64,0},{96,32},{1,65},{33,97},{65,1},{97,33},{2,66}... | collective-permute-start | bytes 294920 | tf_op jit(solution)/shard_map/ppermute | solution.py:35
  32.8 64.0 %collective-permute-start.2 = (bf16[128,384]{1,0:T(8,128)(2,1)}, bf16[128,384]{1,0:T(8,128)(2,1)}, u32[]{:S(2)}, u32[]{:S(2)}) collective-permute-start(bf16[128,384]{1,0:T(8,128)(2,1)} %copy.27), channel_id=1, source_target_pairs={{0,96},{32,0},{64,32},{96,64},{1,97},{33,1},{65,33},{97,65},{2,98}... | collective-permute-start | bytes 294920 | tf_op jit(solution)/shard_map/ppermute | solution.py:35
  35.5 62.4 %collective-permute-start.3 = (bf16[128,768]{0,1:T(8,128)(2,1)}, bf16[128,768]{0,1:T(8,128)(2,1)S(1)}, u32[]{:S(2)}, u32[]{:S(2)}) collective-permute-start(bf16[128,768]{0,1:T(8,128)(2,1)} %bitcast.21), channel_id=1, source_target_pairs={{0,8},{8,16},{16,24},{24,0},{1,9},{9,17},{17,25},{25,1},{2,10},{10... | collective-permute-start | bytes 589832 | tf_op jit(solution)/shard_map/ppermute | solution.py:35
  36.9 60.9 %collective-permute-start.4 = (bf16[128,768]{0,1:T(8,128)(2,1)S(1)}, bf16[128,768]{0,1:T(8,128)(2,1)S(1)}, u32[]{:S(2)}, u32[]{:S(2)}) collective-permute-start(bf16[128,768]{0,1:T(8,128)(2,1)S(1)} %bitcast.104), channel_id=1, source_target_pairs={{0,16},{8,24},{16,0},{24,8},{1,17},{9,25},{17,1},{25,9},{2,18},{10... | collective-permute-start | bytes 589832 | tf_op jit(solution)/shard_map/ppermute | solution.py:35
  97.9 19.5 %copy-start.1 = (bf16[4,128,384]{2,1,0:T(8,128)(2,1)}, bf16[4,128,384]{2,1,0:T(8,128)(2,1)S(1)}, u32[]{:S(2)}) copy-start(bf16[4,128,384]{2,1,0:T(8,128)(2,1)S(1)} %pad_maximum_fusion.refs_0_.refs_3_) | copy-start | bytes 1179652
  97.9 19.4 %copy-start.11 = (bf16[128,768]{0,1:T(8,128)(2,1)}, bf16[128,768]{0,1:T(8,128)(2,1)S(1)}, u32[]{:S(2)}) copy-start(bf16[128,768]{0,1:T(8,128)(2,1)S(1)} %collective-permute-done.3) | copy-start | bytes 589828
  97.9 19.4 %copy-start.12 = (bf16[128,768]{0,1:T(8,128)(2,1)}, bf16[128,768]{0,1:T(8,128)(2,1)S(1)}, u32[]{:S(2)}) copy-start(bf16[128,768]{0,1:T(8,128)(2,1)S(1)} %collective-permute-done.4) | copy-start | bytes 589828
  97.9 19.3 %collective-permute-start.5 = (bf16[4,128,384]{2,1,0:T(8,128)(2,1)S(1)}, bf16[4,128,384]{2,1,0:T(8,128)(2,1)S(1)}, u32[]{:S(2)}, u32[]{:S(2)}) collective-permute-start(bf16[4,128,384]{2,1,0:T(8,128)(2,1)S(1)} %pad_maximum_fusion.refs_0_.refs_3_), channel_id=1, source_target_pairs={{0,8},{8,16},{16,24},{24,0},{1,9},{9,17},{17,25},{25,1},{2,10},{10... | collective-permute-start | bytes 1179656 | tf_op jit(solution)/shard_map/ppermute | solution.py:35
  99.4 17.9 %collective-permute-start.6 = (bf16[4,128,384]{2,1,0:T(8,128)(2,1)S(1)}, bf16[4,128,384]{2,1,0:T(8,128)(2,1)S(1)}, u32[]{:S(2)}, u32[]{:S(2)}) collective-permute-start(bf16[4,128,384]{2,1,0:T(8,128)(2,1)S(1)} %pad_maximum_fusion.refs_0_.refs_3_), channel_id=1, source_target_pairs={{0,16},{8,24},{16,0},{24,8},{1,17},{9,25},{17,1},{25,9},{2,18},{10... | collective-permute-start | bytes 1179656 | tf_op jit(solution)/shard_map/ppermute | solution.py:35
  102.0 15.3 %collective-permute-start.7 = (bf16[4,128,384]{2,1,0:T(8,128)(2,1)S(1)}, bf16[4,128,384]{2,1,0:T(8,128)(2,1)S(1)}, u32[]{:S(2)}, u32[]{:S(2)}) collective-permute-start(bf16[4,128,384]{2,1,0:T(8,128)(2,1)S(1)} %pad_maximum_fusion.refs_0_.refs_3_), channel_id=1, source_target_pairs={{0,24},{8,0},{16,8},{24,16},{1,25},{9,1},{17,9},{25,17},{2,26},{10... | collective-permute-start | bytes 1179656 | tf_op jit(solution)/shard_map/ppermute | solution.py:35
  117.3 10.2 %copy-start.2 = (bf16[4,128,384]{2,1,0:T(8,128)(2,1)}, bf16[4,128,384]{2,1,0:T(8,128)(2,1)S(1)}, u32[]{:S(2)}) copy-start(bf16[4,128,384]{2,1,0:T(8,128)(2,1)S(1)} %collective-permute-done.5.refs_1_.refs_4_) | copy-start | bytes 1179652
  117.3 10.2 %copy-start.3 = (bf16[4,128,384]{2,1,0:T(8,128)(2,1)}, bf16[4,128,384]{2,1,0:T(8,128)(2,1)S(1)}, u32[]{:S(2)}) copy-start(bf16[4,128,384]{2,1,0:T(8,128)(2,1)S(1)} %collective-permute-done.6.refs_2_.refs_5_) | copy-start | bytes 1179652
  117.3 10.1 %copy-start.4 = (bf16[4,128,384]{2,1,0:T(8,128)(2,1)}, bf16[4,128,384]{2,1,0:T(8,128)(2,1)S(1)}, u32[]{:S(2)}) copy-start(bf16[4,128,384]{2,1,0:T(8,128)(2,1)S(1)} %collective-permute-done.7.refs_3_.refs_6_) | copy-start | bytes 1179652
  127.4 23.7 %all-to-all-start.1 = ((bf16[16,128,128]{2,1,0:T(8,128)(2,1)}), bf16[16,128,128]{2,1,0:T(8,128)(2,1)S(1)}, u32[]{:S(2)}, u32[]{:S(2)}) async-start(bf16[16,128,128]{2,1,0:T(8,128)(2,1)} %bitcast.101), calls=%async_computation.1 | async-start | bytes 1048576 | tf_op jit(solution)/shard_map/all_to_all | solution.py:30
  151.1 27.5 %copy-start.7 = (bf16[128,8,1,96]{0,3,2,1:T(8,128)(2,1)S(1)}, bf16[128,8,1,96]{0,3,2,1:T(8,128)(2,1)}, u32[]{:S(2)}) copy-start(bf16[128,8,1,96]{0,3,2,1:T(8,128)(2,1)} %get-tuple-element.70) | copy-start | bytes 589828
  151.1 38.7 %copy-start.8 = (bf16[128,384]{1,0:T(8,128)(2,1)S(1)}, bf16[128,384]{1,0:T(8,128)(2,1)}, u32[]{:S(2)}) copy-start(bf16[128,384]{1,0:T(8,128)(2,1)} %get-tuple-element.60) | copy-start | bytes 294916
  151.2 42.0 %copy-start.6 = (bf16[128,8,1,96]{0,3,2,1:T(8,128)(2,1)S(1)}, bf16[128,8,1,96]{0,3,2,1:T(8,128)(2,1)}, u32[]{:S(2)}) copy-start(bf16[128,8,1,96]{0,3,2,1:T(8,128)(2,1)} %get-tuple-element.69) | copy-start | bytes 589828
  151.2 13.9 %collective-permute-start.10 = (bf16[4,128,384]{2,1,0:T(8,128)(2,1)}, bf16[4,128,384]{2,1,0:T(8,128)(2,1)S(1)}, u32[]{:S(2)}, u32[]{:S(2)}) collective-permute-start(bf16[4,128,384]{2,1,0:T(8,128)(2,1)} %get-tuple-element.58), channel_id=1, source_target_pairs={{0,16},{8,24},{16,0},{24,8},{1,17},{9,25},{17,1},{25,9},{2,18},{10... | collective-permute-start | bytes 1179656 | tf_op jit(solution)/shard_map/ppermute | solution.py:35
  154.7 17.1 %collective-permute-start.11 = (bf16[4,128,384]{2,1,0:T(8,128)(2,1)}, bf16[4,128,384]{2,1,0:T(8,128)(2,1)S(1)}, u32[]{:S(2)}, u32[]{:S(2)}) collective-permute-start(bf16[4,128,384]{2,1,0:T(8,128)(2,1)} %get-tuple-element.59), channel_id=1, source_target_pairs={{0,24},{8,0},{16,8},{24,16},{1,25},{9,1},{17,9},{25,17},{2,26},{10... | collective-permute-start | bytes 1179656 | tf_op jit(solution)/shard_map/ppermute | solution.py:35
  155.8 15.9 %collective-permute-start.9 = (bf16[4,128,384]{2,1,0:T(8,128)(2,1)}, bf16[4,128,384]{2,1,0:T(8,128)(2,1)S(1)}, u32[]{:S(2)}, u32[]{:S(2)}) collective-permute-start(bf16[4,128,384]{2,1,0:T(8,128)(2,1)} %get-tuple-element.57), channel_id=1, source_target_pairs={{0,8},{8,16},{16,24},{24,0},{1,9},{9,17},{17,25},{25,1},{2,10},{10... | collective-permute-start | bytes 1179656 | tf_op jit(solution)/shard_map/ppermute | solution.py:35
  173.0 8.2 %collective-permute-start.12 = (bf16[128,384]{1,0:T(8,128)(2,1)S(1)}, bf16[128,384]{1,0:T(8,128)(2,1)S(1)}, u32[]{:S(2)}, u32[]{:S(2)}) collective-permute-start(bf16[128,384]{1,0:T(8,128)(2,1)S(1)} %get-tuple-element.74), channel_id=1, source_target_pairs={{0,32},{32,64},{64,96},{96,0},{1,33},{33,65},{65,97},{97,1},{2,34}... | collective-permute-start | bytes 294920 | tf_op jit(solution)/shard_map/ppermute | solution.py:35
  174.8 9.2 %collective-permute-start.13 = (bf16[128,384]{1,0:T(8,128)(2,1)S(1)}, bf16[128,384]{1,0:T(8,128)(2,1)S(1)}, u32[]{:S(2)}, u32[]{:S(2)}) collective-permute-start(bf16[128,384]{1,0:T(8,128)(2,1)S(1)} %get-tuple-element.76), channel_id=1, source_target_pairs={{0,64},{32,96},{64,0},{96,32},{1,65},{33,97},{65,1},{97,33},{2,66}... | collective-permute-start | bytes 294920 | tf_op jit(solution)/shard_map/ppermute | solution.py:35
  177.1 6.8 %collective-permute-start.14 = (bf16[128,384]{1,0:T(8,128)(2,1)S(1)}, bf16[128,384]{1,0:T(8,128)(2,1)S(1)}, u32[]{:S(2)}, u32[]{:S(2)}) collective-permute-start(bf16[128,384]{1,0:T(8,128)(2,1)S(1)} %get-tuple-element.75), channel_id=1, source_target_pairs={{0,96},{32,0},{64,32},{96,64},{1,97},{33,1},{65,33},{97,65},{2,98}... | collective-permute-start | bytes 294920 | tf_op jit(solution)/shard_map/ppermute | solution.py:35
  178.6 12.0 %collective-permute-start.8 = (bf16[128,768]{0,1:T(8,128)(2,1)S(1)}, bf16[128,768]{0,1:T(8,128)(2,1)}, u32[]{:S(2)}, u32[]{:S(2)}) collective-permute-start(bf16[128,768]{0,1:T(8,128)(2,1)S(1)} %bitcast.103), channel_id=1, source_target_pairs={{0,24},{8,0},{16,8},{24,16},{1,25},{9,1},{17,9},{25,17},{2,26},{10... | collective-permute-start | bytes 589832 | tf_op jit(solution)/shard_map/ppermute | solution.py:35
  184.0 6.6 %collective-permute-start.15 = (bf16[128,384]{1,0:T(8,128)(2,1)S(1)}, bf16[128,384]{1,0:T(8,128)(2,1)S(1)}, u32[]{:S(2)}, u32[]{:S(2)}) collective-permute-start(bf16[128,384]{1,0:T(8,128)(2,1)S(1)} %fusion.22), channel_id=1, source_target_pairs={{0,8},{8,16},{16,24},{24,0},{1,9},{9,17},{17,25},{25,1},{2,10},{10... | collective-permute-start | bytes 294920 | tf_op jit(solution)/shard_map/ppermute | solution.py:35
  185.7 7.5 %collective-permute-start.16 = (bf16[128,384]{1,0:T(8,128)(2,1)S(1)}, bf16[128,384]{1,0:T(8,128)(2,1)S(1)}, u32[]{:S(2)}, u32[]{:S(2)}) collective-permute-start(bf16[128,384]{1,0:T(8,128)(2,1)S(1)} %fusion.22), channel_id=1, source_target_pairs={{0,16},{8,24},{16,0},{24,8},{1,17},{9,25},{17,1},{25,9},{2,18},{10... | collective-permute-start | bytes 294920 | tf_op jit(solution)/shard_map/ppermute | solution.py:35
  188.4 4.8 %collective-permute-start.17 = (bf16[128,384]{1,0:T(8,128)(2,1)S(1)}, bf16[128,384]{1,0:T(8,128)(2,1)S(1)}, u32[]{:S(2)}, u32[]{:S(2)}) collective-permute-start(bf16[128,384]{1,0:T(8,128)(2,1)S(1)} %fusion.22), channel_id=1, source_target_pairs={{0,24},{8,0},{16,8},{24,16},{1,25},{9,1},{17,9},{25,17},{2,26},{10... | collective-permute-start | bytes 294920 | tf_op jit(solution)/shard_map/ppermute | solution.py:35
  196.9 1.9 collective-permute-start.18
  201.1 5.7 %collective-permute-start.19 = (bf16[2,56,384]{2,0,1:T(2,128)(2,1)}, bf16[2,56,384]{2,0,1:T(2,128)(2,1)}, u32[]{:S(2)}, u32[]{:S(2)}) collective-permute-start(bf16[2,56,384]{2,0,1:T(2,128)(2,1)} %get-tuple-element.71), channel_id=1, source_target_pairs={{0,2},{2,4},{4,6},{6,0},{1,3},{3,5},{5,7},{7,1},{8,10},{10,12},{12... | collective-permute-start | bytes 258056 | tf_op jit(solution)/shard_map/ppermute | solution.py:35
  201.5 6.7 %collective-permute-start.20 = (bf16[2,56,384]{2,0,1:T(2,128)(2,1)}, bf16[2,56,384]{2,0,1:T(2,128)(2,1)}, u32[]{:S(2)}, u32[]{:S(2)}) collective-permute-start(bf16[2,56,384]{2,0,1:T(2,128)(2,1)} %get-tuple-element.73), channel_id=1, source_target_pairs={{0,4},{2,6},{4,0},{6,2},{1,5},{3,7},{5,1},{7,3},{8,12},{10,14},{12... | collective-permute-start | bytes 258056 | tf_op jit(solution)/shard_map/ppermute | solution.py:35
  203.9 5.8 %collective-permute-start.21 = (bf16[2,56,384]{2,0,1:T(2,128)(2,1)S(1)}, bf16[2,56,384]{2,0,1:T(2,128)(2,1)}, u32[]{:S(2)}, u32[]{:S(2)}) collective-permute-start(bf16[2,56,384]{2,0,1:T(2,128)(2,1)S(1)} %get-tuple-element.72), channel_id=1, source_target_pairs={{0,6},{2,0},{4,2},{6,4},{1,7},{3,1},{5,3},{7,5},{8,14},{10,8},{12,... | collective-permute-start | bytes 258056 | tf_op jit(solution)/shard_map/ppermute | solution.py:35
  211.0 8.5 %collective-permute-start.22 = (bf16[56,384]{1,0:T(8,128)(2,1)S(1)}, bf16[56,384]{1,0:T(8,128)(2,1)S(1)}, u32[]{:S(2)}, u32[]{:S(2)}) collective-permute-start(bf16[56,384]{1,0:T(8,128)(2,1)S(1)} %bitcast.108), channel_id=1, source_target_pairs={{0,128},{128,0},{1,129},{129,1},{2,130},{130,2},{3,131},{131,3},{4... | collective-permute-start | bytes 129032 | tf_op jit(solution)/shard_map/ppermute | solution.py:35
  219.5 5.6 %collective-permute-start.23 = (bf16[12,384]{1,0:T(8,128)(2,1)S(1)}, bf16[12,384]{1,0:T(8,128)(2,1)S(1)}, u32[]{:S(2)}, u32[]{:S(2)}) collective-permute-start(bf16[12,384]{1,0:T(8,128)(2,1)S(1)} %get-tuple-element.77), channel_id=1, source_target_pairs={{0,32},{32,64},{64,96},{96,0},{1,33},{33,65},{65,97},{97,1},{2,34}... | collective-permute-start | bytes 27656 | tf_op jit(solution)/shard_map/ppermute | solution.py:35
  221.7 4.6 %collective-permute-start.24 = (bf16[12,384]{1,0:T(8,128)(2,1)S(1)}, bf16[12,384]{1,0:T(8,128)(2,1)S(1)}, u32[]{:S(2)}, u32[]{:S(2)}) collective-permute-start(bf16[12,384]{1,0:T(8,128)(2,1)S(1)} %get-tuple-element.79), channel_id=1, source_target_pairs={{0,64},{32,96},{64,0},{96,32},{1,65},{33,97},{65,1},{97,33},{2,66}... | collective-permute-start | bytes 27656 | tf_op jit(solution)/shard_map/ppermute | solution.py:35
  223.4 3.7 %collective-permute-start.25 = (bf16[12,384]{1,0:T(8,128)(2,1)S(1)}, bf16[12,384]{1,0:T(8,128)(2,1)S(1)}, u32[]{:S(2)}, u32[]{:S(2)}) collective-permute-start(bf16[12,384]{1,0:T(8,128)(2,1)S(1)} %get-tuple-element.78), channel_id=1, source_target_pairs={{0,96},{32,0},{64,32},{96,64},{1,97},{33,1},{65,33},{97,65},{2,98}... | collective-permute-start | bytes 27656 | tf_op jit(solution)/shard_map/ppermute | solution.py:35

commit v6 on v5

--- a/solution.py
+++ b/solution.py
@@ -87,13 +87,12 @@
 def packed_by_head(q, k, v):
     halves, rows, columns = q.shape
     heads = columns // HDIM
-    step_rows = rows // 4
-    spec = pl.BlockSpec((1, step_rows, columns), lambda i, j: (i, j, 0))
+    spec = pl.BlockSpec((1, rows, columns), lambda i: (i, 0, 0))
     return pl.pallas_call(
         pack_kernel,
-        grid=(halves, rows // step_rows),
+        grid=(halves,),
         in_specs=[spec] * 3,
-        out_specs=pl.BlockSpec((heads, 3, step_rows, HDIM), lambda i, j: (i, 0, j, 0)),
+        out_specs=pl.BlockSpec((heads, 3, rows, HDIM), lambda i: (i, 0, 0, 0)),
         out_shape=jax.ShapeDtypeStruct((halves * heads, 3, rows, HDIM), q.dtype),
         cost_estimate=pl.CostEstimate(flops=0, transcendentals=0, bytes_accessed=12 * q.size),
         name="pack_heads",
@@ -273,8 +272,8 @@
 
 def backward_kernel(n_fast, place_ref, up_ref, *refs):
     n_in = n_fast + 3
-    sources, outs, refs = refs[:n_in], refs[n_in : n_in + n_fast + 1], refs[n_in + n_fast + 1 :]
-    student_ref, upstream_ref, stats_ref, low_ref, back_ref, grad_up_ref = refs[:6]
+    sources, outs, refs = refs[:n_in], refs[n_in : n_in + n_fast], refs[n_in + n_fast :]
+    grad_up_ref, student_ref, upstream_ref, stats_ref, low_ref, back_ref = refs[:6]
     dq_ref, dk_ref, dv_ref, flat_ref, in_sems, out_sems = refs[6:]
     _, n_slow, rows, _ = low_ref.shape
     tokens = student_ref.shape[1]
@@ -328,32 +327,29 @@
                 grad = grads(ref, factor, n_slow - slow, n_fast - fast)
                 total += dot(low_ref[fast, slow, :, columns], grad, TN)
         grad_up_ref[:, part * HDIM : (part + 1) * HDIM] = total.astype(BF)
-    stores.append(started(grad_up_ref, outs[n_fast], out_sems.at[n_fast]))
     for store in stores:
         store.wait()
 
 
 def backward(place, student, upstream, stats, up, low):
     tokens, n_fast = student.shape[1], len(low)
-    outs = [jax.ShapeDtypeStruct(low[0].shape, BF)] * n_fast
-    outs.append(jax.ShapeDtypeStruct((RANK, 3 * HDIM), BF))
+    up_shape = (RANK, 3 * HDIM)
     return pl.pallas_call(
         functools.partial(backward_kernel, n_fast),
         grid=(1,),
         in_specs=[pl.BlockSpec(memory_space=pltpu.SMEM), whole(up.shape)] + [HBM] * (n_fast + 3),
-        out_specs=[HBM] * len(outs),
-        out_shape=[pltpu.HBM(out.shape, out.dtype) for out in outs],
+        out_specs=[HBM] * n_fast + [whole(up_shape)],
+        out_shape=[pltpu.HBM(low[0].shape, BF)] * n_fast + [jax.ShapeDtypeStruct(up_shape, BF)],
         scratch_shapes=[
             pltpu.VMEM(student.shape, BF),
             pltpu.VMEM(upstream.shape, BF),
             pltpu.VMEM(stats.shape, F32),
             pltpu.VMEM((n_fast, *low[0].shape), BF),
             pltpu.VMEM((n_fast, *low[0].shape), BF),
-            pltpu.VMEM((RANK, 3 * HDIM), BF),
             *[pltpu.VMEM((tokens, HDIM), F32)] * 3,
             pltpu.VMEM((HDIM, tokens), BF),
             pltpu.SemaphoreType.DMA((n_fast + 3,)),
-            pltpu.SemaphoreType.DMA((n_fast + 1,)),
+            pltpu.SemaphoreType.DMA((n_fast,)),
         ],
         cost_estimate=pl.CostEstimate(
             flops=10 * tokens * tokens * HDIM,
@@ -384,21 +380,25 @@
     tokens = rows * n_slow * n_fast
     total_rows = n_cfg * n_x * n_core * tokens
 
-    packed = packed_by_head(teacher_query[0, :, 0], teacher_key[0, :, 0], teacher_value[0, :, 0])
-    heads = exchange(packed, ("cfg", "z", "y"))
-    heads = heads.reshape(n_cfg, n_slow * n_fast, 3, rows, HDIM)
-
     scale = 1.0 + 0.5 * lax.dynamic_slice(guidance_index[:, 0], (cfg_index,), (1,)).astype(F32)
     time = (lax.dynamic_slice(timestep_index[:, 0], (cfg_index,), (1,)).astype(F32) + 0.5) / TSTEPS
     rank_index = jnp.arange(1, RANK + 1).astype(F32)
     modulation = 1.0 + 0.5 * jnp.cos(math.pi * rank_index * time + 0.25 * rank_index * scale)
 
-    low = jnp.einsum("cl,elj->cej", features, adapter_down_weight, preferred_element_type=F32)
-    low = (low * modulation).astype(BF).reshape(rows, 3 * RANK)
-    low_slow = jnp.stack(from_each(low, "z"))
+    low = [
+        (dot(features, adapter_down_weight[part]) * modulation).astype(BF) for part in range(3)
+    ]
+    low = jnp.concatenate(low, axis=1)
+    packed = packed_by_head(teacher_query[0, :, 0], teacher_key[0, :, 0], teacher_value[0, :, 0])
+    low_parts = from_each(low, "z")
+    packed, *low_parts = lax.optimization_barrier((packed, *low_parts))
+    heads = exchange(packed, ("cfg", "z", "y"))
+    heads = heads.reshape(n_cfg, n_slow * n_fast, 3, rows, HDIM)
+    low_all = from_each(jnp.stack(low_parts), "y")
 
     groups = n_cfg * n_slow
     part_cols = width // (groups * n_fast)
+    features, low_all[0] = lax.optimization_barrier((features, low_all[0]))
     spread = parts_ahead(features.reshape(rows, groups, n_fast, part_cols), "y", 2)
     spread = [part.reshape(rows, groups * part_cols) for part in spread]
     columns = [spread[0]] + [shifted(spread[d], "y", d) for d in range(1, n_fast - 1)]
@@ -408,10 +408,9 @@
     up = lax.dynamic_slice_in_dim(adapter_up_weight, seq_index * HDIM, HDIM, 2)
     inverse = jnp.full((1,), 1.0 / math.sqrt(total_rows), F32)
 
-    heads, low_slow, up, place, spread, *columns = lax.optimization_barrier(
-        (heads, low_slow, up, place, spread, *columns)
+    heads, up, place, spread, *columns = lax.optimization_barrier(
+        (heads, up, place, spread, *columns)
     )
-    low_all = from_each(low_slow, "y")
     target = teacher(scale, heads)
     target, *low_all = lax.optimization_barrier((target, *low_all))
     out, upstream, student, stats = student_forward(place, inverse, heads, target, up, low_all)

time: 229 us -> 226 us (0.987)
  waiting for transfers between devices: 90.5 us -> 97.5 us
  local copies, waits for them, and re-layouts: 11.7 us -> 7.1 us
  starting transfers between devices: 66 us -> 61.9 us
  Pallas kernels: 46.1 us -> 42.6 us
    all_to_all x2, waiting for transfers between devices: 0.01 us -> 43.6 us  [exchange(): return lax.all_to_all(value, axes, split_axis=0, concat_axis=0, tiled=True)]
    ppermute x26, waiting for transfers between devices: 90.5 us -> 53.8 us  [shifted(): lax.ppermute(value, axis, [(i, (i + distance) % size) for i in range(size)])]
    dot_general x1 -> x4, matrix products: 1.68 us -> 6.4 us  [dot(): return lax.dot_general(a, b, dims, preferred_element_type=F32)]
    unnamed x30 -> x25, local copies, waits for them, and re-layouts: 5.48 us -> 1.67 us
    pallas_call x1, Pallas kernels: 6.63 us -> 3.27 us  [packed_by_head(): pl.pallas_call(pack_kernel, grid=(halves,), in_specs=[spec] * 3, out_spec...]
    all_to_all x2, starting transfers between devices: 19.8 us -> 16.9 us  [exchange(): return lax.all_to_all(value, axes, split_axis=0, concat_axis=0, tiled=True)]
    unnamed x1 -> x0, matrix products: 2.44 us -> none
  transfers between devices with their start and end apart: 28 -> 28, of which waited for: 14 -> 15; matrix products, arithmetic and copies ran while one was open for 6% -> 2% of each run, Pallas kernels for 13% -> 14%
where the time goes in v6:
time: 226 us
  waiting for transfers between devices  97.5 us (43%)
  starting transfers between devices  61.9 us (27%)
  Pallas kernels  42.6 us (19%)
  other arithmetic  7.73 us (3%)
  local copies, waits for them, and re-layouts  7.1 us (3%)
  matrix products  6.4 us (3%)
  between operations  2.42 us (1%)
    ppermute x26, waiting for transfers between devices, shifted(): lax.ppermute(value, axis, [(i, (i + distance) % size) for i in range(size)])  53.8 us
    ppermute x26, starting transfers between devices, shifted(): lax.ppermute(value, axis, [(i, (i + distance) % size) for i in range(size)])  45.1 us
    all_to_all x2, waiting for transfers between devices, exchange(): return lax.all_to_all(value, axes, split_axis=0, concat_axis=0, tiled=True)  43.6 us
    all_to_all x2, starting transfers between devices, exchange(): return lax.all_to_all(value, axes, split_axis=0, concat_axis=0, tiled=True)  16.9 us
    pallas_call x1, Pallas kernels, backward(): pl.pallas_call(functools.partial(backward_kernel, n_fast), grid=(1,), in_...  15.5 us
    pallas_call x1, Pallas kernels, teacher(): pl.pallas_call(teacher_kernel, grid=(1,), in_specs=[pl.BlockSpec(memory_s...  13.7 us
    pallas_call x1, Pallas kernels, student_forward(): pl.pallas_call(functools.partial(student_kernel, len(low)), grid=(1,), in...  10.1 us
    dot_general x4, matrix products, dot(): return lax.dot_general(a, b, dims, preferred_element_type=F32)  6.4 us
  transfers between devices with their start and end apart: 28, of which 15 were waited for; matrix products, arithmetic and copies ran while one was open for 2% of the time, Pallas kernels for 14%

profile of v6, /device:TPU:6, one launch (start us, length us, event | category | flops | bytes accessed | tf_op | source)
XLA Modules:
  0.0 225.6 jit_solution(3227899339956926194)
XLA Ops:
  0.7 1.4 fusion.46
  3.4 1.7 fusion
  5.2 1.5 fusion.1
  6.7 1.5 fusion.2
  8.2 2.0 collective-permute-start
  10.2 3.3 %collective-permute-start.1 = (bf16[128,384]{1,0:T(8,128)(2,1)S(1)}, bf16[128,384]{1,0:T(8,128)(2,1)S(1)}, u32[]{:S(2)}, u32[]{:S(2)}) collective-permute-start(bf16[128,384]{1,0:T(8,128)(2,1)S(1)} %pad_maximum_fusion.1), channel_id=1, source_target_pairs={{0,64},{32,96},{64,0},{96,32},{1,65},{33,97},{65,1},{97,33},{2,66}... | collective-permute-start | bytes 294920 | tf_op jit(solution)/shard_map/ppermute | solution.py:35
  14.5 3.3 %pack_heads.1 = bf16[32,3,128,128]{3,2,1,0:T(8,128)(2,1)} custom-call(bf16[2,128,2048]{2,1,0:T(8,128)(2,1)} %bitcast.103, bf16[2,128,2048]{2,1,0:T(8,128)(2,1)} %bitcast.104, bf16[2,128,2048]{2,1,0:T(8,128)(2,1)} %bitcast.105), custom_call_target="tpu_custom_call" | custom-call | bytes 6291456 | tf_op jit(solution)/shard_map/pack_heads/pallas_call | solution.py:91
  17.7 2.3 %collective-permute-done.1 = bf16[128,384]{1,0:T(8,128)(2,1)S(1)} collective-permute-done((bf16[128,384]{1,0:T(8,128)(2,1)S(1)}, bf16[128,384]{1,0:T(8,128)(2,1)S(1)}, u32[]{:S(2)}, u32[]{:S(2)}) %collective-permute-start.1) | collective-permute-done | bytes 98336 | tf_op jit(solution)/shard_map/ppermute | solution.py:35
  20.7 11.4 %all-to-all-start = ((bf16[32,3,128,128]{3,2,1,0:T(8,128)(2,1)}), bf16[32,3,128,128]{3,2,1,0:T(8,128)(2,1)}, u32[]{:S(2)}, u32[]{:S(2)}) async-start(bf16[32,3,128,128]{3,2,1,0:T(8,128)(2,1)} %pack_heads.1), calls=%async_computation | async-start | bytes 6291456 | tf_op jit(solution)/shard_map/all_to_all | solution.py:30
  32.6 1.1 pad_maximum_fusion.refs_0_.refs_3_
  34.5 1.7 collective-permute-start.3
  36.2 2.7 %collective-permute-start.4 = (bf16[128,768]{0,1:T(8,128)(2,1)S(1)}, bf16[128,768]{0,1:T(8,128)(2,1)}, u32[]{:S(2)}, u32[]{:S(2)}) collective-permute-start(bf16[128,768]{0,1:T(8,128)(2,1)S(1)} %bitcast.111), channel_id=1, source_target_pairs={{0,16},{8,24},{16,0},{24,8},{1,17},{9,25},{17,1},{25,9},{2,18},{10... | collective-permute-start | bytes 589832 | tf_op jit(solution)/shard_map/ppermute | solution.py:35
  39.1 2.9 %collective-permute-start.6 = (bf16[4,128,384]{2,1,0:T(8,128)(2,1)S(1)}, bf16[4,128,384]{2,1,0:T(8,128)(2,1)S(1)}, u32[]{:S(2)}, u32[]{:S(2)}) collective-permute-start(bf16[4,128,384]{2,1,0:T(8,128)(2,1)S(1)} %pad_maximum_fusion.refs_0_.refs_3_), channel_id=1, source_target_pairs={{0,16},{8,24},{16,0},{24,8},{1,17},{9,25},{17,1},{25,9},{2,18},{10... | collective-permute-start | bytes 1179656 | tf_op jit(solution)/shard_map/ppermute | solution.py:35
  42.6 4.4 %collective-permute-done.3 = bf16[128,768]{0,1:T(8,128)(2,1)S(1)} collective-permute-done((bf16[128,768]{0,1:T(8,128)(2,1)S(1)}, bf16[128,768]{0,1:T(8,128)(2,1)S(1)}, u32[]{:S(2)}, u32[]{:S(2)}) %collective-permute-start.3) | collective-permute-done | bytes 196640 | tf_op jit(solution)/shard_map/ppermute | solution.py:35
  47.0 13.8 %collective-permute-done.4 = bf16[128,768]{0,1:T(8,128)(2,1)} collective-permute-done((bf16[128,768]{0,1:T(8,128)(2,1)S(1)}, bf16[128,768]{0,1:T(8,128)(2,1)}, u32[]{:S(2)}, u32[]{:S(2)}) %collective-permute-start.4) | collective-permute-done | bytes 196640 | tf_op jit(solution)/shard_map/ppermute | solution.py:35
  60.8 43.6 %all-to-all-done = bf16[32,3,128,128]{3,2,1,0:T(8,128)(2,1)} async-done(((bf16[32,3,128,128]{3,2,1,0:T(8,128)(2,1)}), bf16[32,3,128,128]{3,2,1,0:T(8,128)(2,1)}, u32[]{:S(2)}, u32[]{:S(2)}) %all-to-all-start) | async-done | bytes 3145760 | tf_op jit(solution)/shard_map/all_to_all | solution.py:30
  104.4 13.7 %teacher_forward.1.target_ref = f32[2048,128]{1,0:T(8,128)S(1)} custom-call(f32[1]{0:T(128)} %bitcast.6.scale_ref, bf16[2,16,3,128,128]{4,3,2,1,0:T(8,128)(2,1)} %bitcast.10.heads_ref), custom_call_target="tpu_custom_call" | custom-call | flops 4294967296 | bytes 4194304 | tf_op jit(solution)/shard_map/teacher_forward/pallas_call | solution.py:151
  118.2 10.1 %student_forward.1 = (bf16[2048,128]{1,0:T(8,128)(2,1)}, bf16[2048,128]{1,0:T(8,128)(2,1)}, bf16[3,2048,128]{2,1,0:T(8,128)(2,1)}, f32[8,2048]{1,0:T(8,128)}) custom-call(s32[2]{0:T(128)S(1)} %pad_add_fusion.place_ref, f32[1]{0:T(128)} %constant.172.clone.1.inv_ref, bf16[2,16,3,128,128]{4,3,2,1,0:T(8,128)(2,1)} %bitcast.10.heads_ref, ...), custom_call_target="tpu_custom_call" | custom-call | flops 2147483648 | bytes 6291456 | tf_op jit(solution)/shard_map/student_forward/pallas_call | solution.py:249
  128.3 5.5 %all-to-all-start.1 = ((bf16[16,128,128]{2,1,0:T(8,128)(2,1)}), bf16[16,128,128]{2,1,0:T(8,128)(2,1)S(1)}, u32[]{:S(2)}, u32[]{:S(2)}) async-start(bf16[16,128,128]{2,1,0:T(8,128)(2,1)} %bitcast.108), calls=%async_computation.1 | async-start | bytes 1048576 | tf_op jit(solution)/shard_map/all_to_all | solution.py:30
  133.9 15.5 %attention_backward.1 = (bf16[4,128,384]{2,1,0:T(8,128)(2,1)}, bf16[4,128,384]{2,1,0:T(8,128)(2,1)}, bf16[4,128,384]{2,1,0:T(8,128)(2,1)}, bf16[4,128,384]{2,1,0:T(8,128)(2,1)}, bf16[128,384]{1,0:T(8,128)(2,1)S(1)}) custom-call(s32[2]{0:T(128)S(1)} %pad_add_fusion.place_ref, bf16[3,128,128]{2,1,0:T(8,128)(2,1)S(1)} %constant_dynamic-slice_fusion.5.up_ref, ...), custom_call_target="tpu_custom_call" | custom-call | flops 5368709120 | bytes 6291456 | tf_op jit(solution)/shard_map/attention_backward/pallas_call | solution.py:337
  149.4 3.5 %collective-permute-start.10 = (bf16[4,128,384]{2,1,0:T(8,128)(2,1)}, bf16[4,128,384]{2,1,0:T(8,128)(2,1)S(1)}, u32[]{:S(2)}, u32[]{:S(2)}) collective-permute-start(bf16[4,128,384]{2,1,0:T(8,128)(2,1)} %get-tuple-element.70), channel_id=1, source_target_pairs={{0,16},{8,24},{16,0},{24,8},{1,17},{9,25},{17,1},{25,9},{2,18},{10... | collective-permute-start | bytes 1179656 | tf_op jit(solution)/shard_map/ppermute | solution.py:35
  152.9 1.2 collective-permute-start.11
  154.9 8.4 %collective-permute-done.10 = bf16[4,128,384]{2,1,0:T(8,128)(2,1)S(1)} collective-permute-done((bf16[4,128,384]{2,1,0:T(8,128)(2,1)}, bf16[4,128,384]{2,1,0:T(8,128)(2,1)S(1)}, u32[]{:S(2)}, u32[]{:S(2)}) %collective-permute-start.10) | collective-permute-done | bytes 393248 | tf_op jit(solution)/shard_map/ppermute | solution.py:35
  163.3 6.6 %collective-permute-done.11 = bf16[4,128,384]{2,1,0:T(8,128)(2,1)S(1)} collective-permute-done((bf16[4,128,384]{2,1,0:T(8,128)(2,1)}, bf16[4,128,384]{2,1,0:T(8,128)(2,1)S(1)}, u32[]{:S(2)}, u32[]{:S(2)}) %collective-permute-start.11) | collective-permute-done | bytes 393248 | tf_op jit(solution)/shard_map/ppermute | solution.py:35
  169.9 1.2 add_convert_fusion
  171.1 1.8 collective-permute-start.12
  172.9 2.4 %collective-permute-start.13 = (bf16[128,384]{1,0:T(8,128)(2,1)S(1)}, bf16[128,384]{1,0:T(8,128)(2,1)S(1)}, u32[]{:S(2)}, u32[]{:S(2)}) collective-permute-start(bf16[128,384]{1,0:T(8,128)(2,1)S(1)} %get-tuple-element.88), channel_id=1, source_target_pairs={{0,64},{32,96},{64,0},{96,32},{1,65},{33,97},{65,1},{97,33},{2,66}... | collective-permute-start | bytes 294920 | tf_op jit(solution)/shard_map/ppermute | solution.py:35
  175.3 1.5 collective-permute-start.14
  176.7 2.6 %collective-permute-start.8 = (bf16[128,768]{0,1:T(8,128)(2,1)}, bf16[128,768]{0,1:T(8,128)(2,1)S(1)}, u32[]{:S(2)}, u32[]{:S(2)}) collective-permute-start(bf16[128,768]{0,1:T(8,128)(2,1)} %bitcast.18), channel_id=1, source_target_pairs={{0,24},{8,0},{16,8},{24,16},{1,25},{9,1},{17,9},{25,17},{2,26},{10... | collective-permute-start | bytes 589832 | tf_op jit(solution)/shard_map/ppermute | solution.py:35
  179.4 2.7 %collective-permute-done.13 = bf16[128,384]{1,0:T(8,128)(2,1)S(1)} collective-permute-done((bf16[128,384]{1,0:T(8,128)(2,1)S(1)}, bf16[128,384]{1,0:T(8,128)(2,1)S(1)}, u32[]{:S(2)}, u32[]{:S(2)}) %collective-permute-start.13) | collective-permute-done | bytes 98336 | tf_op jit(solution)/shard_map/ppermute | solution.py:35
  182.2 1.7 collective-permute-start.15
  183.9 2.7 %collective-permute-start.16 = (bf16[128,384]{1,0:T(8,128)(2,1)S(1)}, bf16[128,384]{1,0:T(8,128)(2,1)S(1)}, u32[]{:S(2)}, u32[]{:S(2)}) collective-permute-start(bf16[128,384]{1,0:T(8,128)(2,1)S(1)} %fusion.32), channel_id=1, source_target_pairs={{0,16},{8,24},{16,0},{24,8},{1,17},{9,25},{17,1},{25,9},{2,18},{10... | collective-permute-start | bytes 294920 | tf_op jit(solution)/shard_map/ppermute | solution.py:35
  186.5 1.5 collective-permute-start.17
  188.7 2.5 %collective-permute-done.16 = bf16[128,384]{1,0:T(8,128)(2,1)S(1)} collective-permute-done((bf16[128,384]{1,0:T(8,128)(2,1)S(1)}, bf16[128,384]{1,0:T(8,128)(2,1)S(1)}, u32[]{:S(2)}, u32[]{:S(2)}) %collective-permute-start.16) | collective-permute-done | bytes 98336 | tf_op jit(solution)/shard_map/ppermute | solution.py:35
  191.2 1.7 convolution_convert_fusion
  193.7 1.3 fusion.28
  195.1 1.7 collective-permute-done.18
  196.8 1.4 convert_add_fusion
  199.6 2.4 %collective-permute-start.20 = (bf16[2,56,384]{2,0,1:T(2,128)(2,1)}, bf16[2,56,384]{2,0,1:T(2,128)(2,1)}, u32[]{:S(2)}, u32[]{:S(2)}) collective-permute-start(bf16[2,56,384]{2,0,1:T(2,128)(2,1)} %get-tuple-element.85), channel_id=1, source_target_pairs={{0,4},{2,6},{4,0},{6,2},{1,5},{3,7},{5,1},{7,3},{8,12},{10,14},{12... | collective-permute-start | bytes 258056 | tf_op jit(solution)/shard_map/ppermute | solution.py:35
  203.4 1.4 collective-permute-done.19
  204.8 1.5 collective-permute-done.20
  206.3 1.5 collective-permute-done.21
  207.8 1.1 fusion.34
  209.0 3.1 %collective-permute-start.22 = (bf16[56,384]{1,0:T(8,128)(2,1)S(1)}, bf16[56,384]{1,0:T(8,128)(2,1)S(1)}, u32[]{:S(2)}, u32[]{:S(2)}) collective-permute-start(bf16[56,384]{1,0:T(8,128)(2,1)S(1)} %bitcast.117), channel_id=1, source_target_pairs={{0,128},{128,0},{1,129},{129,1},{2,130},{130,2},{3,131},{131,3},{4... | collective-permute-start | bytes 129032 | tf_op jit(solution)/shard_map/ppermute | solution.py:35
  212.3 4.9 %collective-permute-done.22 = bf16[56,384]{1,0:T(8,128)(2,1)S(1)} collective-permute-done((bf16[56,384]{1,0:T(8,128)(2,1)S(1)}, bf16[56,384]{1,0:T(8,128)(2,1)S(1)}, u32[]{:S(2)}, u32[]{:S(2)}) %collective-permute-start.22) | collective-permute-done | bytes 43040 | tf_op jit(solution)/shard_map/ppermute | solution.py:35
  217.2 2.6 %collective-permute-start.23 = (bf16[12,384]{1,0:T(8,128)(2,1)S(1)}, bf16[12,384]{1,0:T(8,128)(2,1)S(1)}, u32[]{:S(2)}, u32[]{:S(2)}) collective-permute-start(bf16[12,384]{1,0:T(8,128)(2,1)S(1)} %get-tuple-element.89), channel_id=1, source_target_pairs={{0,32},{32,64},{64,96},{96,0},{1,33},{33,65},{65,97},{97,1},{2,34}... | collective-permute-start | bytes 27656 | tf_op jit(solution)/shard_map/ppermute | solution.py:35
  219.9 1.4 collective-permute-start.24
  222.9 1.5 collective-permute-done.24
  (70 shorter events, 12.0 us)
Async XLA Ops:
  0.6 38.4 %copy-start = (bf16[3,128,2048]{2,1,0:T(8,128)(2,1)S(1)}, bf16[3,128,2048]{2,1,0:T(8,128)(2,1)}, u32[]{:S(2)}) copy-start(bf16[3,128,2048]{2,1,0:T(8,128)(2,1)} %param.13) | copy-start | bytes 4718596
  0.6 4.5 %copy-start.5 = (bf16[1,1,128,3072]{3,2,1,0:T(8,128)(2,1)S(1)}, bf16[1,1,128,3072]{3,2,1,0:T(8,128)(2,1)}, u32[]{:S(2)}) copy-start(bf16[1,1,128,3072]{3,2,1,0:T(8,128)(2,1)} %param.11) | copy-start | bytes 2359300
  8.2 11.9 %copy-start.6 = (bf16[128,384]{1,0:T(8,128)(2,1)}, bf16[128,384]{1,0:T(8,128)(2,1)S(1)}, u32[]{:S(2)}) copy-start(bf16[128,384]{1,0:T(8,128)(2,1)S(1)} %pad_maximum_fusion.1) | copy-start | bytes 294916
  8.2 9.5 %collective-permute-start = (bf16[128,384]{1,0:T(8,128)(2,1)S(1)}, bf16[128,384]{1,0:T(8,128)(2,1)S(1)}, u32[]{:S(2)}, u32[]{:S(2)}) collective-permute-start(bf16[128,384]{1,0:T(8,128)(2,1)S(1)} %pad_maximum_fusion.1), channel_id=1, source_target_pairs={{0,32},{32,64},{64,96},{96,0},{1,33},{33,65},{65,97},{97,1},{2,34}... | collective-permute-start | bytes 294920 | tf_op jit(solution)/shard_map/ppermute | solution.py:35
  10.2 9.9 %collective-permute-start.1 = (bf16[128,384]{1,0:T(8,128)(2,1)S(1)}, bf16[128,384]{1,0:T(8,128)(2,1)S(1)}, u32[]{:S(2)}, u32[]{:S(2)}) collective-permute-start(bf16[128,384]{1,0:T(8,128)(2,1)S(1)} %pad_maximum_fusion.1), channel_id=1, source_target_pairs={{0,64},{32,96},{64,0},{96,32},{1,65},{33,97},{65,1},{97,33},{2,66}... | collective-permute-start | bytes 294920 | tf_op jit(solution)/shard_map/ppermute | solution.py:35
  13.5 6.6 %collective-permute-start.2 = (bf16[128,384]{1,0:T(8,128)(2,1)S(1)}, bf16[128,384]{1,0:T(8,128)(2,1)S(1)}, u32[]{:S(2)}, u32[]{:S(2)}) collective-permute-start(bf16[128,384]{1,0:T(8,128)(2,1)S(1)} %pad_maximum_fusion.1), channel_id=1, source_target_pairs={{0,96},{32,0},{64,32},{96,64},{1,97},{33,1},{65,33},{97,65},{2,98}... | collective-permute-start | bytes 294920 | tf_op jit(solution)/shard_map/ppermute | solution.py:35
  17.7 2.4 %copy-start.7 = (bf16[128,384]{1,0:T(8,128)(2,1)}, bf16[128,384]{1,0:T(8,128)(2,1)S(1)}, u32[]{:S(2)}) copy-start(bf16[128,384]{1,0:T(8,128)(2,1)S(1)} %collective-permute-done) | copy-start | bytes 294916
  20.0 0.6 copy-start.8
  20.1 0.6 copy-start.9
  20.7 83.7 %all-to-all-start = ((bf16[32,3,128,128]{3,2,1,0:T(8,128)(2,1)}), bf16[32,3,128,128]{3,2,1,0:T(8,128)(2,1)}, u32[]{:S(2)}, u32[]{:S(2)}) async-start(bf16[32,3,128,128]{3,2,1,0:T(8,128)(2,1)} %pack_heads.1), calls=%async_computation | async-start | bytes 6291456 | tf_op jit(solution)/shard_map/all_to_all | solution.py:30
  33.7 84.6 %copy-start.1 = (bf16[4,128,384]{2,1,0:T(8,128)(2,1)}, bf16[4,128,384]{2,1,0:T(8,128)(2,1)S(1)}, u32[]{:S(2)}) copy-start(bf16[4,128,384]{2,1,0:T(8,128)(2,1)S(1)} %pad_maximum_fusion.refs_0_.refs_3_) | copy-start | bytes 1179652
  34.5 12.5 %collective-permute-start.3 = (bf16[128,768]{0,1:T(8,128)(2,1)S(1)}, bf16[128,768]{0,1:T(8,128)(2,1)S(1)}, u32[]{:S(2)}, u32[]{:S(2)}) collective-permute-start(bf16[128,768]{0,1:T(8,128)(2,1)S(1)} %bitcast.112), channel_id=1, source_target_pairs={{0,8},{8,16},{16,24},{24,0},{1,9},{9,17},{17,25},{25,1},{2,10},{10... | collective-permute-start | bytes 589832 | tf_op jit(solution)/shard_map/ppermute | solution.py:35
  36.2 24.6 %collective-permute-start.4 = (bf16[128,768]{0,1:T(8,128)(2,1)S(1)}, bf16[128,768]{0,1:T(8,128)(2,1)}, u32[]{:S(2)}, u32[]{:S(2)}) collective-permute-start(bf16[128,768]{0,1:T(8,128)(2,1)S(1)} %bitcast.111), channel_id=1, source_target_pairs={{0,16},{8,24},{16,0},{24,8},{1,17},{9,25},{17,1},{25,9},{2,18},{10... | collective-permute-start | bytes 589832 | tf_op jit(solution)/shard_map/ppermute | solution.py:35
  39.0 79.1 %collective-permute-start.5 = (bf16[4,128,384]{2,1,0:T(8,128)(2,1)S(1)}, bf16[4,128,384]{2,1,0:T(8,128)(2,1)S(1)}, u32[]{:S(2)}, u32[]{:S(2)}) collective-permute-start(bf16[4,128,384]{2,1,0:T(8,128)(2,1)S(1)} %pad_maximum_fusion.refs_0_.refs_3_), channel_id=1, source_target_pairs={{0,8},{8,16},{16,24},{24,0},{1,9},{9,17},{17,25},{25,1},{2,10},{10... | collective-permute-start | bytes 1179656 | tf_op jit(solution)/shard_map/ppermute | solution.py:35
  39.1 79.1 %collective-permute-start.6 = (bf16[4,128,384]{2,1,0:T(8,128)(2,1)S(1)}, bf16[4,128,384]{2,1,0:T(8,128)(2,1)S(1)}, u32[]{:S(2)}, u32[]{:S(2)}) collective-permute-start(bf16[4,128,384]{2,1,0:T(8,128)(2,1)S(1)} %pad_maximum_fusion.refs_0_.refs_3_), channel_id=1, source_target_pairs={{0,16},{8,24},{16,0},{24,8},{1,17},{9,25},{17,1},{25,9},{2,18},{10... | collective-permute-start | bytes 1179656 | tf_op jit(solution)/shard_map/ppermute | solution.py:35
  42.0 76.2 %collective-permute-start.7 = (bf16[4,128,384]{2,1,0:T(8,128)(2,1)S(1)}, bf16[4,128,384]{2,1,0:T(8,128)(2,1)S(1)}, u32[]{:S(2)}, u32[]{:S(2)}) collective-permute-start(bf16[4,128,384]{2,1,0:T(8,128)(2,1)S(1)} %pad_maximum_fusion.refs_0_.refs_3_), channel_id=1, source_target_pairs={{0,24},{8,0},{16,8},{24,16},{1,25},{9,1},{17,9},{25,17},{2,26},{10... | collective-permute-start | bytes 1179656 | tf_op jit(solution)/shard_map/ppermute | solution.py:35
  47.0 71.1 %copy-start.10 = (bf16[128,768]{0,1:T(8,128)(2,1)}, bf16[128,768]{0,1:T(8,128)(2,1)S(1)}, u32[]{:S(2)}) copy-start(bf16[128,768]{0,1:T(8,128)(2,1)S(1)} %collective-permute-done.3) | copy-start | bytes 589828
  118.2 10.2 %copy-start.2 = (bf16[4,128,384]{2,1,0:T(8,128)(2,1)}, bf16[4,128,384]{2,1,0:T(8,128)(2,1)S(1)}, u32[]{:S(2)}) copy-start(bf16[4,128,384]{2,1,0:T(8,128)(2,1)S(1)} %collective-permute-done.5.refs_1_.refs_4_) | copy-start | bytes 1179652
  118.2 10.1 %copy-start.3 = (bf16[4,128,384]{2,1,0:T(8,128)(2,1)}, bf16[4,128,384]{2,1,0:T(8,128)(2,1)S(1)}, u32[]{:S(2)}) copy-start(bf16[4,128,384]{2,1,0:T(8,128)(2,1)S(1)} %collective-permute-done.6.refs_2_.refs_5_) | copy-start | bytes 1179652
  118.2 10.1 %copy-start.4 = (bf16[4,128,384]{2,1,0:T(8,128)(2,1)}, bf16[4,128,384]{2,1,0:T(8,128)(2,1)S(1)}, u32[]{:S(2)}) copy-start(bf16[4,128,384]{2,1,0:T(8,128)(2,1)S(1)} %collective-permute-done.7.refs_3_.refs_6_) | copy-start | bytes 1179652
  128.3 21.0 %all-to-all-start.1 = ((bf16[16,128,128]{2,1,0:T(8,128)(2,1)}), bf16[16,128,128]{2,1,0:T(8,128)(2,1)S(1)}, u32[]{:S(2)}, u32[]{:S(2)}) async-start(bf16[16,128,128]{2,1,0:T(8,128)(2,1)} %bitcast.108), calls=%async_computation.1 | async-start | bytes 1048576 | tf_op jit(solution)/shard_map/all_to_all | solution.py:30
  149.4 13.9 %collective-permute-start.10 = (bf16[4,128,384]{2,1,0:T(8,128)(2,1)}, bf16[4,128,384]{2,1,0:T(8,128)(2,1)S(1)}, u32[]{:S(2)}, u32[]{:S(2)}) collective-permute-start(bf16[4,128,384]{2,1,0:T(8,128)(2,1)} %get-tuple-element.70), channel_id=1, source_target_pairs={{0,16},{8,24},{16,0},{24,8},{1,17},{9,25},{17,1},{25,9},{2,18},{10... | collective-permute-start | bytes 1179656 | tf_op jit(solution)/shard_map/ppermute | solution.py:35
  152.9 17.0 %collective-permute-start.11 = (bf16[4,128,384]{2,1,0:T(8,128)(2,1)}, bf16[4,128,384]{2,1,0:T(8,128)(2,1)S(1)}, u32[]{:S(2)}, u32[]{:S(2)}) collective-permute-start(bf16[4,128,384]{2,1,0:T(8,128)(2,1)} %get-tuple-element.71), channel_id=1, source_target_pairs={{0,24},{8,0},{16,8},{24,16},{1,25},{9,1},{17,9},{25,17},{2,26},{10... | collective-permute-start | bytes 1179656 | tf_op jit(solution)/shard_map/ppermute | solution.py:35
  154.0 15.9 %collective-permute-start.9 = (bf16[4,128,384]{2,1,0:T(8,128)(2,1)}, bf16[4,128,384]{2,1,0:T(8,128)(2,1)S(1)}, u32[]{:S(2)}, u32[]{:S(2)}) collective-permute-start(bf16[4,128,384]{2,1,0:T(8,128)(2,1)} %get-tuple-element.69), channel_id=1, source_target_pairs={{0,8},{8,16},{16,24},{24,0},{1,9},{9,17},{17,25},{25,1},{2,10},{10... | collective-permute-start | bytes 1179656 | tf_op jit(solution)/shard_map/ppermute | solution.py:35
  171.1 8.2 %collective-permute-start.12 = (bf16[128,384]{1,0:T(8,128)(2,1)S(1)}, bf16[128,384]{1,0:T(8,128)(2,1)S(1)}, u32[]{:S(2)}, u32[]{:S(2)}) collective-permute-start(bf16[128,384]{1,0:T(8,128)(2,1)S(1)} %get-tuple-element.86), channel_id=1, source_target_pairs={{0,32},{32,64},{64,96},{96,0},{1,33},{33,65},{65,97},{97,1},{2,34}... | collective-permute-start | bytes 294920 | tf_op jit(solution)/shard_map/ppermute | solution.py:35
  172.9 9.2 %collective-permute-start.13 = (bf16[128,384]{1,0:T(8,128)(2,1)S(1)}, bf16[128,384]{1,0:T(8,128)(2,1)S(1)}, u32[]{:S(2)}, u32[]{:S(2)}) collective-permute-start(bf16[128,384]{1,0:T(8,128)(2,1)S(1)} %get-tuple-element.88), channel_id=1, source_target_pairs={{0,64},{32,96},{64,0},{96,32},{1,65},{33,97},{65,1},{97,33},{2,66}... | collective-permute-start | bytes 294920 | tf_op jit(solution)/shard_map/ppermute | solution.py:35
  175.3 6.8 %collective-permute-start.14 = (bf16[128,384]{1,0:T(8,128)(2,1)S(1)}, bf16[128,384]{1,0:T(8,128)(2,1)S(1)}, u32[]{:S(2)}, u32[]{:S(2)}) collective-permute-start(bf16[128,384]{1,0:T(8,128)(2,1)S(1)} %get-tuple-element.87), channel_id=1, source_target_pairs={{0,96},{32,0},{64,32},{96,64},{1,97},{33,1},{65,33},{97,65},{2,98}... | collective-permute-start | bytes 294920 | tf_op jit(solution)/shard_map/ppermute | solution.py:35
  176.7 12.0 %collective-permute-start.8 = (bf16[128,768]{0,1:T(8,128)(2,1)}, bf16[128,768]{0,1:T(8,128)(2,1)S(1)}, u32[]{:S(2)}, u32[]{:S(2)}) collective-permute-start(bf16[128,768]{0,1:T(8,128)(2,1)} %bitcast.18), channel_id=1, source_target_pairs={{0,24},{8,0},{16,8},{24,16},{1,25},{9,1},{17,9},{25,17},{2,26},{10... | collective-permute-start | bytes 589832 | tf_op jit(solution)/shard_map/ppermute | solution.py:35
  182.2 6.6 %collective-permute-start.15 = (bf16[128,384]{1,0:T(8,128)(2,1)S(1)}, bf16[128,384]{1,0:T(8,128)(2,1)S(1)}, u32[]{:S(2)}, u32[]{:S(2)}) collective-permute-start(bf16[128,384]{1,0:T(8,128)(2,1)S(1)} %fusion.32), channel_id=1, source_target_pairs={{0,8},{8,16},{16,24},{24,0},{1,9},{9,17},{17,25},{25,1},{2,10},{10... | collective-permute-start | bytes 294920 | tf_op jit(solution)/shard_map/ppermute | solution.py:35
  183.9 7.4 %collective-permute-start.16 = (bf16[128,384]{1,0:T(8,128)(2,1)S(1)}, bf16[128,384]{1,0:T(8,128)(2,1)S(1)}, u32[]{:S(2)}, u32[]{:S(2)}) collective-permute-start(bf16[128,384]{1,0:T(8,128)(2,1)S(1)} %fusion.32), channel_id=1, source_target_pairs={{0,16},{8,24},{16,0},{24,8},{1,17},{9,25},{17,1},{25,9},{2,18},{10... | collective-permute-start | bytes 294920 | tf_op jit(solution)/shard_map/ppermute | solution.py:35
  186.5 4.7 %collective-permute-start.17 = (bf16[128,384]{1,0:T(8,128)(2,1)S(1)}, bf16[128,384]{1,0:T(8,128)(2,1)S(1)}, u32[]{:S(2)}, u32[]{:S(2)}) collective-permute-start(bf16[128,384]{1,0:T(8,128)(2,1)S(1)} %fusion.32), channel_id=1, source_target_pairs={{0,24},{8,0},{16,8},{24,16},{1,25},{9,1},{17,9},{25,17},{2,26},{10... | collective-permute-start | bytes 294920 | tf_op jit(solution)/shard_map/ppermute | solution.py:35
  194.9 1.9 collective-permute-start.18
  199.1 5.7 %collective-permute-start.19 = (bf16[2,56,384]{2,0,1:T(2,128)(2,1)}, bf16[2,56,384]{2,0,1:T(2,128)(2,1)}, u32[]{:S(2)}, u32[]{:S(2)}) collective-permute-start(bf16[2,56,384]{2,0,1:T(2,128)(2,1)} %get-tuple-element.83), channel_id=1, source_target_pairs={{0,2},{2,4},{4,6},{6,0},{1,3},{3,5},{5,7},{7,1},{8,10},{10,12},{12... | collective-permute-start | bytes 258056 | tf_op jit(solution)/shard_map/ppermute | solution.py:35
  199.6 6.7 %collective-permute-start.20 = (bf16[2,56,384]{2,0,1:T(2,128)(2,1)}, bf16[2,56,384]{2,0,1:T(2,128)(2,1)}, u32[]{:S(2)}, u32[]{:S(2)}) collective-permute-start(bf16[2,56,384]{2,0,1:T(2,128)(2,1)} %get-tuple-element.85), channel_id=1, source_target_pairs={{0,4},{2,6},{4,0},{6,2},{1,5},{3,7},{5,1},{7,3},{8,12},{10,14},{12... | collective-permute-start | bytes 258056 | tf_op jit(solution)/shard_map/ppermute | solution.py:35
  202.0 5.8 %collective-permute-start.21 = (bf16[2,56,384]{2,0,1:T(2,128)(2,1)S(1)}, bf16[2,56,384]{2,0,1:T(2,128)(2,1)}, u32[]{:S(2)}, u32[]{:S(2)}) collective-permute-start(bf16[2,56,384]{2,0,1:T(2,128)(2,1)S(1)} %get-tuple-element.84), channel_id=1, source_target_pairs={{0,6},{2,0},{4,2},{6,4},{1,7},{3,1},{5,3},{7,5},{8,14},{10,8},{12,... | collective-permute-start | bytes 258056 | tf_op jit(solution)/shard_map/ppermute | solution.py:35
  209.0 8.1 %collective-permute-start.22 = (bf16[56,384]{1,0:T(8,128)(2,1)S(1)}, bf16[56,384]{1,0:T(8,128)(2,1)S(1)}, u32[]{:S(2)}, u32[]{:S(2)}) collective-permute-start(bf16[56,384]{1,0:T(8,128)(2,1)S(1)} %bitcast.117), channel_id=1, source_target_pairs={{0,128},{128,0},{1,129},{129,1},{2,130},{130,2},{3,131},{131,3},{4... | collective-permute-start | bytes 129032 | tf_op jit(solution)/shard_map/ppermute | solution.py:35
  217.2 5.7 %collective-permute-start.23 = (bf16[12,384]{1,0:T(8,128)(2,1)S(1)}, bf16[12,384]{1,0:T(8,128)(2,1)S(1)}, u32[]{:S(2)}, u32[]{:S(2)}) collective-permute-start(bf16[12,384]{1,0:T(8,128)(2,1)S(1)} %get-tuple-element.89), channel_id=1, source_target_pairs={{0,32},{32,64},{64,96},{96,0},{1,33},{33,65},{65,97},{97,1},{2,34}... | collective-permute-start | bytes 27656 | tf_op jit(solution)/shard_map/ppermute | solution.py:35
  219.9 4.6 %collective-permute-start.24 = (bf16[12,384]{1,0:T(8,128)(2,1)S(1)}, bf16[12,384]{1,0:T(8,128)(2,1)S(1)}, u32[]{:S(2)}, u32[]{:S(2)}) collective-permute-start(bf16[12,384]{1,0:T(8,128)(2,1)S(1)} %get-tuple-element.91), channel_id=1, source_target_pairs={{0,64},{32,96},{64,0},{96,32},{1,65},{33,97},{65,1},{97,33},{2,66}... | collective-permute-start | bytes 27656 | tf_op jit(solution)/shard_map/ppermute | solution.py:35
  221.3 3.7 %collective-permute-start.25 = (bf16[12,384]{1,0:T(8,128)(2,1)S(1)}, bf16[12,384]{1,0:T(8,128)(2,1)S(1)}, u32[]{:S(2)}, u32[]{:S(2)}) collective-permute-start(bf16[12,384]{1,0:T(8,128)(2,1)S(1)} %get-tuple-element.90), channel_id=1, source_target_pairs={{0,96},{32,0},{64,32},{96,64},{1,97},{33,1},{65,33},{97,65},{2,98}... | collective-permute-start | bytes 27656 | tf_op jit(solution)/shard_map/ppermute | solution.py:35

commit v7 on v6

--- a/solution.py
+++ b/solution.py
@@ -380,6 +380,10 @@
     tokens = rows * n_slow * n_fast
     total_rows = n_cfg * n_x * n_core * tokens
 
+    packed = packed_by_head(teacher_query[0, :, 0], teacher_key[0, :, 0], teacher_value[0, :, 0])
+    heads = exchange(packed, ("cfg", "z", "y"))
+    heads = heads.reshape(n_cfg, n_slow * n_fast, 3, rows, HDIM)
+
     scale = 1.0 + 0.5 * lax.dynamic_slice(guidance_index[:, 0], (cfg_index,), (1,)).astype(F32)
     time = (lax.dynamic_slice(timestep_index[:, 0], (cfg_index,), (1,)).astype(F32) + 0.5) / TSTEPS
     rank_index = jnp.arange(1, RANK + 1).astype(F32)
@@ -389,16 +393,10 @@
         (dot(features, adapter_down_weight[part]) * modulation).astype(BF) for part in range(3)
     ]
     low = jnp.concatenate(low, axis=1)
-    packed = packed_by_head(teacher_query[0, :, 0], teacher_key[0, :, 0], teacher_value[0, :, 0])
-    low_parts = from_each(low, "z")
-    packed, *low_parts = lax.optimization_barrier((packed, *low_parts))
-    heads = exchange(packed, ("cfg", "z", "y"))
-    heads = heads.reshape(n_cfg, n_slow * n_fast, 3, rows, HDIM)
-    low_all = from_each(jnp.stack(low_parts), "y")
+    low_slow = jnp.stack(from_each(low, "z"))
 
     groups = n_cfg * n_slow
     part_cols = width // (groups * n_fast)
-    features, low_all[0] = lax.optimization_barrier((features, low_all[0]))
     spread = parts_ahead(features.reshape(rows, groups, n_fast, part_cols), "y", 2)
     spread = [part.reshape(rows, groups * part_cols) for part in spread]
     columns = [spread[0]] + [shifted(spread[d], "y", d) for d in range(1, n_fast - 1)]
@@ -408,22 +406,24 @@
     up = lax.dynamic_slice_in_dim(adapter_up_weight, seq_index * HDIM, HDIM, 2)
     inverse = jnp.full((1,), 1.0 / math.sqrt(total_rows), F32)
 
-    heads, up, place, spread, *columns = lax.optimization_barrier(
-        (heads, up, place, spread, *columns)
+    heads, low_slow, up, place, spread, *columns = lax.optimization_barrier(
+        (heads, low_slow, up, place, spread, *columns)
     )
+    low_all = from_each(low_slow, "y")
     target = teacher(scale, heads)
     target, *low_all = lax.optimization_barrier((target, *low_all))
     out, upstream, student, stats = student_forward(place, inverse, heads, target, up, low_all)
     tokens_out = exchange(out.reshape(n_slow * n_fast, rows, HDIM), ("z", "y"))
 
     *back, up_partial = backward(place, student, upstream, stats, up, low_all)
-    tokens_out, up_partial, spread, *back = lax.optimization_barrier(
-        (tokens_out, up_partial, spread, *back)
-    )
+    tokens_out, up_partial, *back = lax.optimization_barrier((tokens_out, up_partial, *back))
+    student_out = jnp.moveaxis(tokens_out, 0, 1).reshape(rows, -1)
+
+    arrived = [shifted(back[d], "y", d) for d in range(1, n_fast)]
+    arrived[0], spread = lax.optimization_barrier((arrived[0], spread))
     columns.append(shifted(spread, "y", n_fast - 1))
-    student_out = jnp.moveaxis(tokens_out, 0, 1).reshape(rows, -1)
-
-    back = summed_parts(back, "y").astype(BF)
+    back = sum((part.astype(F32) for part in arrived), back[0].astype(F32)).astype(BF)
+    back, student_out = lax.optimization_barrier((back, student_out))
     back = summed_parts([back[d] for d in range(n_slow)], "z")
     low_grad = (back.reshape(rows, 3, RANK) * modulation).astype(BF).reshape(rows, 3 * RANK)
     low_grads = jnp.concatenate(from_each(low_grad, "y"))

time: 226 us -> 218 us (0.965)
  other arithmetic: 7.73 us -> 3.75 us
  local copies, waits for them, and re-layouts: 7.1 us -> 3.85 us
  waiting for transfers between devices: 97.5 us -> 95.1 us
    all_to_all x2, waiting for transfers between devices: 43.6 us -> 0.01 us  [exchange(): return lax.all_to_all(value, axes, split_axis=0, concat_axis=0, tiled=True)]
    ppermute x26, waiting for transfers between devices: 53.8 us -> 95.1 us  [shifted(): lax.ppermute(value, axis, [(i, (i + distance) % size) for i in range(size)])]
    all_to_all x2, starting transfers between devices: 16.9 us -> 19.8 us  [exchange(): return lax.all_to_all(value, axes, split_axis=0, concat_axis=0, tiled=True)]
  transfers between devices with their start and end apart: 28 -> 28, of which waited for: 15 -> 17; matrix products, arithmetic and copies ran while one was open for 2% -> 4% of each run, Pallas kernels for 14% -> 13%
where the time goes in v7:
time: 218 us; the launch traced here: 217 us
  waiting for transfers between devices  95.1 us (44%)
  starting transfers between devices  63.4 us (29%)
  Pallas kernels  42.7 us (20%)
  matrix products  6.06 us (3%)
  local copies, waits for them, and re-layouts  3.85 us (2%)
  other arithmetic  3.75 us (2%)
  between operations  2.4 us (1%)
    ppermute x26, waiting for transfers between devices, shifted(): lax.ppermute(value, axis, [(i, (i + distance) % size) for i in range(size)])  95.1 us
    ppermute x26, starting transfers between devices, shifted(): lax.ppermute(value, axis, [(i, (i + distance) % size) for i in range(size)])  43.6 us
    all_to_all x2, starting transfers between devices, exchange(): return lax.all_to_all(value, axes, split_axis=0, concat_axis=0, tiled=True)  19.8 us
    pallas_call x1, Pallas kernels, backward(): pl.pallas_call(functools.partial(backward_kernel, n_fast), grid=(1,), in_...  15.4 us
    pallas_call x1, Pallas kernels, teacher(): pl.pallas_call(teacher_kernel, grid=(1,), in_specs=[pl.BlockSpec(memory_s...  13.7 us
    pallas_call x1, Pallas kernels, student_forward(): pl.pallas_call(functools.partial(student_kernel, len(low)), grid=(1,), in...  10.1 us
    dot_general x4, matrix products, dot(): return lax.dot_general(a, b, dims, preferred_element_type=F32)  6.06 us
  transfers between devices with their start and end apart: 28, of which 17 were waited for; matrix products, arithmetic and copies ran while one was open for 4% of the time, Pallas kernels for 13%

profile of v7, /device:TPU:6, one launch (start us, length us, event | category | flops | bytes accessed | tf_op | source)
XLA Modules:
  0.0 217.2 jit_solution(17485992334141510014)
XLA Ops:
  0.6 3.4 %pack_heads.1 = bf16[32,3,128,128]{3,2,1,0:T(8,128)(2,1)} custom-call(bf16[2,128,2048]{2,1,0:T(8,128)(2,1)} %bitcast.104, bf16[2,128,2048]{2,1,0:T(8,128)(2,1)} %bitcast.105, bf16[2,128,2048]{2,1,0:T(8,128)(2,1)} %bitcast.106), custom_call_target="tpu_custom_call" | custom-call | bytes 6291456 | tf_op jit(solution)/shard_map/pack_heads/pallas_call | solution.py:91
  4.1 11.7 %all-to-all-start = ((bf16[32,3,128,128]{3,2,1,0:T(8,128)(2,1)}), bf16[32,3,128,128]{3,2,1,0:T(8,128)(2,1)}, u32[]{:S(2)}, u32[]{:S(2)}) async-start(bf16[32,3,128,128]{3,2,1,0:T(8,128)(2,1)} %pack_heads.1), calls=%async_computation | async-start | bytes 6291456 | tf_op jit(solution)/shard_map/all_to_all | solution.py:30
  17.8 1.5 fusion
  19.3 1.5 fusion.1
  20.8 1.5 fusion.2
  23.0 1.7 collective-permute-start
  24.7 2.4 %collective-permute-start.1 = (bf16[128,384]{1,0:T(8,128)(2,1)}, bf16[128,384]{1,0:T(8,128)(2,1)S(1)}, u32[]{:S(2)}, u32[]{:S(2)}) collective-permute-start(bf16[128,384]{1,0:T(8,128)(2,1)} %get-tuple-element.87), channel_id=1, source_target_pairs={{0,64},{32,96},{64,0},{96,32},{1,65},{33,97},{65,1},{97,33},{2,66}... | collective-permute-start | bytes 294920 | tf_op jit(solution)/shard_map/ppermute | solution.py:35
  27.1 1.5 collective-permute-start.2
  29.0 1.5 collective-permute-start.3
  30.5 2.7 %collective-permute-start.4 = (bf16[128,768]{0,1:T(8,128)(2,1)S(1)}, bf16[128,768]{0,1:T(8,128)(2,1)}, u32[]{:S(2)}, u32[]{:S(2)}) collective-permute-start(bf16[128,768]{0,1:T(8,128)(2,1)S(1)} %bitcast.113), channel_id=1, source_target_pairs={{0,16},{8,24},{16,0},{24,8},{1,17},{9,25},{17,1},{25,9},{2,18},{10... | collective-permute-start | bytes 589832 | tf_op jit(solution)/shard_map/ppermute | solution.py:35
  33.3 56.2 %collective-permute-done = bf16[128,384]{1,0:T(8,128)(2,1)S(1)} collective-permute-done((bf16[128,384]{1,0:T(8,128)(2,1)}, bf16[128,384]{1,0:T(8,128)(2,1)S(1)}, u32[]{:S(2)}, u32[]{:S(2)}) %collective-permute-start) | collective-permute-done | bytes 98336 | tf_op jit(solution)/shard_map/ppermute | solution.py:35
  89.5 4.0 %collective-permute-done.1 = bf16[128,384]{1,0:T(8,128)(2,1)S(1)} collective-permute-done((bf16[128,384]{1,0:T(8,128)(2,1)}, bf16[128,384]{1,0:T(8,128)(2,1)S(1)}, u32[]{:S(2)}, u32[]{:S(2)}) %collective-permute-start.1) | collective-permute-done | bytes 98336 | tf_op jit(solution)/shard_map/ppermute | solution.py:35
  93.7 1.5 collective-permute-start.5
  95.2 2.9 %collective-permute-start.6 = (bf16[4,128,384]{2,1,0:T(8,128)(2,1)S(1)}, bf16[4,128,384]{2,1,0:T(8,128)(2,1)S(1)}, u32[]{:S(2)}, u32[]{:S(2)}) collective-permute-start(bf16[4,128,384]{2,1,0:T(8,128)(2,1)S(1)} %pad_maximum_fusion.refs_0_.refs_3_), channel_id=1, source_target_pairs={{0,16},{8,24},{16,0},{24,8},{1,17},{9,25},{17,1},{25,9},{2,18},{10... | collective-permute-start | bytes 1179656 | tf_op jit(solution)/shard_map/ppermute | solution.py:35
  98.0 1.2 collective-permute-start.7
  99.3 13.7 %teacher_forward.1.target_ref = f32[2048,128]{1,0:T(8,128)S(1)} custom-call(f32[1]{0:T(128)} %bitcast.7.scale_ref, bf16[2,16,3,128,128]{4,3,2,1,0:T(8,128)(2,1)} %bitcast.3.heads_ref), custom_call_target="tpu_custom_call" | custom-call | flops 4294967296 | bytes 4194304 | tf_op jit(solution)/shard_map/teacher_forward/pallas_call | solution.py:151
  113.1 10.1 %student_forward.1 = (bf16[2048,128]{1,0:T(8,128)(2,1)}, bf16[2048,128]{1,0:T(8,128)(2,1)}, bf16[3,2048,128]{2,1,0:T(8,128)(2,1)}, f32[8,2048]{1,0:T(8,128)}) custom-call(s32[2]{0:T(128)S(1)} %pad_add_fusion.place_ref, f32[1]{0:T(128)} %constant.172.clone.1.inv_ref, bf16[2,16,3,128,128]{4,3,2,1,0:T(8,128)(2,1)} %bitcast.3.heads_ref, ...), custom_call_target="tpu_custom_call" | custom-call | flops 2147483648 | bytes 6291456 | tf_op jit(solution)/shard_map/student_forward/pallas_call | solution.py:249
  123.2 8.1 %all-to-all-start.1 = ((bf16[16,128,128]{2,1,0:T(8,128)(2,1)}), bf16[16,128,128]{2,1,0:T(8,128)(2,1)S(1)}, u32[]{:S(2)}, u32[]{:S(2)}) async-start(bf16[16,128,128]{2,1,0:T(8,128)(2,1)} %bitcast.110), calls=%async_computation.1 | async-start | bytes 1048576 | tf_op jit(solution)/shard_map/all_to_all | solution.py:30
  131.2 15.4 %attention_backward.1 = (bf16[4,128,384]{2,1,0:T(8,128)(2,1)}, bf16[4,128,384]{2,1,0:T(8,128)(2,1)}, bf16[4,128,384]{2,1,0:T(8,128)(2,1)}, bf16[4,128,384]{2,1,0:T(8,128)(2,1)}, bf16[128,384]{1,0:T(8,128)(2,1)S(1)}) custom-call(s32[2]{0:T(128)S(1)} %pad_add_fusion.place_ref, bf16[3,128,128]{2,1,0:T(8,128)(2,1)S(1)} %constant_dynamic-slice_fusion.5.up_ref, ...), custom_call_target="tpu_custom_call" | custom-call | flops 5368709120 | bytes 6291456 | tf_op jit(solution)/shard_map/attention_backward/pallas_call | solution.py:337
  146.7 2.0 collective-permute-start.8
  148.7 1.3 collective-permute-start.10
  150.0 2.2 %collective-permute-start.9 = (bf16[4,128,384]{2,1,0:T(8,128)(2,1)}, bf16[4,128,384]{2,1,0:T(8,128)(2,1)S(1)}, u32[]{:S(2)}, u32[]{:S(2)}) collective-permute-start(bf16[4,128,384]{2,1,0:T(8,128)(2,1)} %get-tuple-element.57), channel_id=1, source_target_pairs={{0,16},{8,24},{16,0},{24,8},{1,17},{9,25},{17,1},{25,9},{2,18},{10... | collective-permute-start | bytes 1179656 | tf_op jit(solution)/shard_map/ppermute | solution.py:35
  152.2 0.9 copy_bitcast_fusion
  153.1 6.4 %collective-permute-done.8 = bf16[4,128,384]{2,1,0:T(8,128)(2,1)S(1)} collective-permute-done((bf16[4,128,384]{2,1,0:T(8,128)(2,1)}, bf16[4,128,384]{2,1,0:T(8,128)(2,1)S(1)}, u32[]{:S(2)}, u32[]{:S(2)}) %collective-permute-start.8) | collective-permute-done | bytes 393248 | tf_op jit(solution)/shard_map/ppermute | solution.py:35
  159.4 1.5 collective-permute-done.10
  161.0 6.9 %collective-permute-done.9 = bf16[4,128,384]{2,1,0:T(8,128)(2,1)S(1)} collective-permute-done((bf16[4,128,384]{2,1,0:T(8,128)(2,1)}, bf16[4,128,384]{2,1,0:T(8,128)(2,1)S(1)}, u32[]{:S(2)}, u32[]{:S(2)}) %collective-permute-start.9) | collective-permute-done | bytes 393248 | tf_op jit(solution)/shard_map/ppermute | solution.py:35
  167.8 1.2 add_convert_fusion
  169.1 1.8 collective-permute-start.12
  170.8 2.4 %collective-permute-start.13 = (bf16[128,384]{1,0:T(8,128)(2,1)S(1)}, bf16[128,384]{1,0:T(8,128)(2,1)S(1)}, u32[]{:S(2)}, u32[]{:S(2)}) collective-permute-start(bf16[128,384]{1,0:T(8,128)(2,1)S(1)} %get-tuple-element.82), channel_id=1, source_target_pairs={{0,64},{32,96},{64,0},{96,32},{1,65},{33,97},{65,1},{97,33},{2,66}... | collective-permute-start | bytes 294920 | tf_op jit(solution)/shard_map/ppermute | solution.py:35
  173.2 1.5 collective-permute-start.14
  174.7 2.1 collective-permute-start.11
  176.7 2.3 %collective-permute-done.13 = bf16[128,384]{1,0:T(8,128)(2,1)S(1)} collective-permute-done((bf16[128,384]{1,0:T(8,128)(2,1)S(1)}, bf16[128,384]{1,0:T(8,128)(2,1)S(1)}, u32[]{:S(2)}, u32[]{:S(2)}) %collective-permute-start.13) | collective-permute-done | bytes 98336 | tf_op jit(solution)/shard_map/ppermute | solution.py:35
  179.1 0.9 collective-permute-start.15
  180.0 2.2 %collective-permute-start.16 = (bf16[128,384]{1,0:T(8,128)(2,1)S(1)}, bf16[128,384]{1,0:T(8,128)(2,1)S(1)}, u32[]{:S(2)}, u32[]{:S(2)}) collective-permute-start(bf16[128,384]{1,0:T(8,128)(2,1)S(1)} %fusion.32), channel_id=1, source_target_pairs={{0,16},{8,24},{16,0},{24,8},{1,17},{9,25},{17,1},{25,9},{2,18},{10... | collective-permute-start | bytes 294920 | tf_op jit(solution)/shard_map/ppermute | solution.py:35
  182.9 2.1 collective-permute-done.15
  185.0 1.2 collective-permute-done.16
  186.9 1.6 convolution_convert_fusion
  189.9 1.6 collective-permute-done.18
  192.7 2.4 %collective-permute-start.20 = (bf16[2,56,384]{2,0,1:T(2,128)(2,1)S(1)}, bf16[2,56,384]{2,0,1:T(2,128)(2,1)S(1)}, u32[]{:S(2)}, u32[]{:S(2)}) collective-permute-start(bf16[2,56,384]{2,0,1:T(2,128)(2,1)S(1)} %get-tuple-element.79), channel_id=1, source_target_pairs={{0,4},{2,6},{4,0},{6,2},{1,5},{3,7},{5,1},{7,3},{8,12},{10,14},{12... | collective-permute-start | bytes 258056 | tf_op jit(solution)/shard_map/ppermute | solution.py:35
  195.1 2.5 %collective-permute-done.19 = bf16[2,56,384]{2,0,1:T(2,128)(2,1)S(1)} collective-permute-done((bf16[2,56,384]{2,0,1:T(2,128)(2,1)S(1)}, bf16[2,56,384]{2,0,1:T(2,128)(2,1)S(1)}, u32[]{:S(2)}, u32[]{:S(2)}) %collective-permute-start.19) | collective-permute-done | bytes 86048 | tf_op jit(solution)/shard_map/ppermute | solution.py:35
  197.6 1.3 collective-permute-done.20
  198.8 1.9 collective-permute-done.21
  201.1 4.1 %collective-permute-start.22 = (bf16[56,384]{1,0:T(8,128)(2,1)S(1)}, bf16[56,384]{1,0:T(8,128)(2,1)S(1)}, u32[]{:S(2)}, u32[]{:S(2)}) collective-permute-start(bf16[56,384]{1,0:T(8,128)(2,1)S(1)} %bitcast.119), channel_id=1, source_target_pairs={{0,128},{128,0},{1,129},{129,1},{2,130},{130,2},{3,131},{131,3},{4... | collective-permute-start | bytes 129032 | tf_op jit(solution)/shard_map/ppermute | solution.py:35
  205.2 3.9 %collective-permute-done.22 = bf16[56,384]{1,0:T(8,128)(2,1)S(1)} collective-permute-done((bf16[56,384]{1,0:T(8,128)(2,1)S(1)}, bf16[56,384]{1,0:T(8,128)(2,1)S(1)}, u32[]{:S(2)}, u32[]{:S(2)}) %collective-permute-start.22) | collective-permute-done | bytes 43040 | tf_op jit(solution)/shard_map/ppermute | solution.py:35
  209.1 1.7 collective-permute-start.23
  210.9 2.0 collective-permute-start.24
  214.7 0.8 collective-permute-done.24
  215.5 1.1 collective-permute-done.25
  (63 shorter events, 8.8 us)
Async XLA Ops:
  0.6 32.6 %copy-start = (bf16[3,128,2048]{2,1,0:T(8,128)(2,1)S(1)}, bf16[3,128,2048]{2,1,0:T(8,128)(2,1)}, u32[]{:S(2)}) copy-start(bf16[3,128,2048]{2,1,0:T(8,128)(2,1)} %param.13) | copy-start | bytes 4718596
  4.1 11.8 %copy-start.6 = (s32[2,1]{0,1:T(1,128)S(1)}, s32[2,1]{0,1:T(1,128)}, u32[]{:S(2)}) copy-start(s32[2,1]{0,1:T(1,128)} %param.15) | copy-start | bytes 28
  4.1 11.8 %copy-start.7 = (s32[2,1]{0,1:T(1,128)S(1)}, s32[2,1]{0,1:T(1,128)}, u32[]{:S(2)}) copy-start(s32[2,1]{0,1:T(1,128)} %param.14) | copy-start | bytes 28
  4.1 13.7 %copy-start.5 = (bf16[1,1,128,3072]{3,2,1,0:T(8,128)(2,1)S(1)}, bf16[1,1,128,3072]{3,2,1,0:T(8,128)(2,1)}, u32[]{:S(2)}) copy-start(bf16[1,1,128,3072]{3,2,1,0:T(8,128)(2,1)} %param.11) | copy-start | bytes 2359300
  4.1 89.6 %all-to-all-start = ((bf16[32,3,128,128]{3,2,1,0:T(8,128)(2,1)}), bf16[32,3,128,128]{3,2,1,0:T(8,128)(2,1)}, u32[]{:S(2)}, u32[]{:S(2)}) async-start(bf16[32,3,128,128]{3,2,1,0:T(8,128)(2,1)} %pack_heads.1), calls=%async_computation | async-start | bytes 6291456 | tf_op jit(solution)/shard_map/all_to_all | solution.py:30
  23.0 66.6 %collective-permute-start = (bf16[128,384]{1,0:T(8,128)(2,1)}, bf16[128,384]{1,0:T(8,128)(2,1)S(1)}, u32[]{:S(2)}, u32[]{:S(2)}) collective-permute-start(bf16[128,384]{1,0:T(8,128)(2,1)} %get-tuple-element.87), channel_id=1, source_target_pairs={{0,32},{32,64},{64,96},{96,0},{1,33},{33,65},{65,97},{97,1},{2,34}... | collective-permute-start | bytes 294920 | tf_op jit(solution)/shard_map/ppermute | solution.py:35
  24.7 68.9 %collective-permute-start.1 = (bf16[128,384]{1,0:T(8,128)(2,1)}, bf16[128,384]{1,0:T(8,128)(2,1)S(1)}, u32[]{:S(2)}, u32[]{:S(2)}) collective-permute-start(bf16[128,384]{1,0:T(8,128)(2,1)} %get-tuple-element.87), channel_id=1, source_target_pairs={{0,64},{32,96},{64,0},{96,32},{1,65},{33,97},{65,1},{97,33},{2,66}... | collective-permute-start | bytes 294920 | tf_op jit(solution)/shard_map/ppermute | solution.py:35
  27.1 66.5 %collective-permute-start.2 = (bf16[128,384]{1,0:T(8,128)(2,1)}, bf16[128,384]{1,0:T(8,128)(2,1)S(1)}, u32[]{:S(2)}, u32[]{:S(2)}) collective-permute-start(bf16[128,384]{1,0:T(8,128)(2,1)} %get-tuple-element.87), channel_id=1, source_target_pairs={{0,96},{32,0},{64,32},{96,64},{1,97},{33,1},{65,33},{97,65},{2,98}... | collective-permute-start | bytes 294920 | tf_op jit(solution)/shard_map/ppermute | solution.py:35
  29.0 64.7 %collective-permute-start.3 = (bf16[128,768]{0,1:T(8,128)(2,1)S(1)}, bf16[128,768]{0,1:T(8,128)(2,1)}, u32[]{:S(2)}, u32[]{:S(2)}) collective-permute-start(bf16[128,768]{0,1:T(8,128)(2,1)S(1)} %bitcast.114), channel_id=1, source_target_pairs={{0,8},{8,16},{16,24},{24,0},{1,9},{9,17},{17,25},{25,1},{2,10},{10... | collective-permute-start | bytes 589832 | tf_op jit(solution)/shard_map/ppermute | solution.py:35
  30.5 63.1 %collective-permute-start.4 = (bf16[128,768]{0,1:T(8,128)(2,1)S(1)}, bf16[128,768]{0,1:T(8,128)(2,1)}, u32[]{:S(2)}, u32[]{:S(2)}) collective-permute-start(bf16[128,768]{0,1:T(8,128)(2,1)S(1)} %bitcast.113), channel_id=1, source_target_pairs={{0,16},{8,24},{16,0},{24,8},{1,17},{9,25},{17,1},{25,9},{2,18},{10... | collective-permute-start | bytes 589832 | tf_op jit(solution)/shard_map/ppermute | solution.py:35
  93.6 19.4 %copy-start.1 = (bf16[4,128,384]{2,1,0:T(8,128)(2,1)}, bf16[4,128,384]{2,1,0:T(8,128)(2,1)S(1)}, u32[]{:S(2)}) copy-start(bf16[4,128,384]{2,1,0:T(8,128)(2,1)S(1)} %pad_maximum_fusion.refs_0_.refs_3_) | copy-start | bytes 1179652
  93.7 19.3 %collective-permute-start.5 = (bf16[4,128,384]{2,1,0:T(8,128)(2,1)S(1)}, bf16[4,128,384]{2,1,0:T(8,128)(2,1)S(1)}, u32[]{:S(2)}, u32[]{:S(2)}) collective-permute-start(bf16[4,128,384]{2,1,0:T(8,128)(2,1)S(1)} %pad_maximum_fusion.refs_0_.refs_3_), channel_id=1, source_target_pairs={{0,8},{8,16},{16,24},{24,0},{1,9},{9,17},{17,25},{25,1},{2,10},{10... | collective-permute-start | bytes 1179656 | tf_op jit(solution)/shard_map/ppermute | solution.py:35
  95.2 17.9 %collective-permute-start.6 = (bf16[4,128,384]{2,1,0:T(8,128)(2,1)S(1)}, bf16[4,128,384]{2,1,0:T(8,128)(2,1)S(1)}, u32[]{:S(2)}, u32[]{:S(2)}) collective-permute-start(bf16[4,128,384]{2,1,0:T(8,128)(2,1)S(1)} %pad_maximum_fusion.refs_0_.refs_3_), channel_id=1, source_target_pairs={{0,16},{8,24},{16,0},{24,8},{1,17},{9,25},{17,1},{25,9},{2,18},{10... | collective-permute-start | bytes 1179656 | tf_op jit(solution)/shard_map/ppermute | solution.py:35
  98.0 15.0 %collective-permute-start.7 = (bf16[4,128,384]{2,1,0:T(8,128)(2,1)S(1)}, bf16[4,128,384]{2,1,0:T(8,128)(2,1)S(1)}, u32[]{:S(2)}, u32[]{:S(2)}) collective-permute-start(bf16[4,128,384]{2,1,0:T(8,128)(2,1)S(1)} %pad_maximum_fusion.refs_0_.refs_3_), channel_id=1, source_target_pairs={{0,24},{8,0},{16,8},{24,16},{1,25},{9,1},{17,9},{25,17},{2,26},{10... | collective-permute-start | bytes 1179656 | tf_op jit(solution)/shard_map/ppermute | solution.py:35
  113.0 10.1 %copy-start.2 = (bf16[4,128,384]{2,1,0:T(8,128)(2,1)}, bf16[4,128,384]{2,1,0:T(8,128)(2,1)S(1)}, u32[]{:S(2)}) copy-start(bf16[4,128,384]{2,1,0:T(8,128)(2,1)S(1)} %collective-permute-done.5.refs_1_.refs_4_) | copy-start | bytes 1179652
  113.0 10.1 %copy-start.3 = (bf16[4,128,384]{2,1,0:T(8,128)(2,1)}, bf16[4,128,384]{2,1,0:T(8,128)(2,1)S(1)}, u32[]{:S(2)}) copy-start(bf16[4,128,384]{2,1,0:T(8,128)(2,1)S(1)} %collective-permute-done.6.refs_2_.refs_5_) | copy-start | bytes 1179652
  113.1 10.1 %copy-start.4 = (bf16[4,128,384]{2,1,0:T(8,128)(2,1)}, bf16[4,128,384]{2,1,0:T(8,128)(2,1)S(1)}, u32[]{:S(2)}) copy-start(bf16[4,128,384]{2,1,0:T(8,128)(2,1)S(1)} %collective-permute-done.7.refs_3_.refs_6_) | copy-start | bytes 1179652
  123.2 23.5 %all-to-all-start.1 = ((bf16[16,128,128]{2,1,0:T(8,128)(2,1)}), bf16[16,128,128]{2,1,0:T(8,128)(2,1)S(1)}, u32[]{:S(2)}, u32[]{:S(2)}) async-start(bf16[16,128,128]{2,1,0:T(8,128)(2,1)} %bitcast.110), calls=%async_computation.1 | async-start | bytes 1048576 | tf_op jit(solution)/shard_map/all_to_all | solution.py:30
  146.7 12.8 %collective-permute-start.8 = (bf16[4,128,384]{2,1,0:T(8,128)(2,1)}, bf16[4,128,384]{2,1,0:T(8,128)(2,1)S(1)}, u32[]{:S(2)}, u32[]{:S(2)}) collective-permute-start(bf16[4,128,384]{2,1,0:T(8,128)(2,1)} %get-tuple-element.54), channel_id=1, source_target_pairs={{0,8},{8,16},{16,24},{24,0},{1,9},{9,17},{17,25},{25,1},{2,10},{10... | collective-permute-start | bytes 1179656 | tf_op jit(solution)/shard_map/ppermute | solution.py:35
  148.7 12.3 %collective-permute-start.10 = (bf16[4,128,384]{2,1,0:T(8,128)(2,1)}, bf16[4,128,384]{2,1,0:T(8,128)(2,1)S(1)}, u32[]{:S(2)}, u32[]{:S(2)}) collective-permute-start(bf16[4,128,384]{2,1,0:T(8,128)(2,1)} %get-tuple-element.58), channel_id=1, source_target_pairs={{0,24},{8,0},{16,8},{24,16},{1,25},{9,1},{17,9},{25,17},{2,26},{10... | collective-permute-start | bytes 1179656 | tf_op jit(solution)/shard_map/ppermute | solution.py:35
  150.0 17.8 %collective-permute-start.9 = (bf16[4,128,384]{2,1,0:T(8,128)(2,1)}, bf16[4,128,384]{2,1,0:T(8,128)(2,1)S(1)}, u32[]{:S(2)}, u32[]{:S(2)}) collective-permute-start(bf16[4,128,384]{2,1,0:T(8,128)(2,1)} %get-tuple-element.57), channel_id=1, source_target_pairs={{0,16},{8,24},{16,0},{24,8},{1,17},{9,25},{17,1},{25,9},{2,18},{10... | collective-permute-start | bytes 1179656 | tf_op jit(solution)/shard_map/ppermute | solution.py:35
  169.1 7.7 %collective-permute-start.12 = (bf16[128,384]{1,0:T(8,128)(2,1)S(1)}, bf16[128,384]{1,0:T(8,128)(2,1)S(1)}, u32[]{:S(2)}, u32[]{:S(2)}) collective-permute-start(bf16[128,384]{1,0:T(8,128)(2,1)S(1)} %get-tuple-element.80), channel_id=1, source_target_pairs={{0,32},{32,64},{64,96},{96,0},{1,33},{33,65},{65,97},{97,1},{2,34}... | collective-permute-start | bytes 294920 | tf_op jit(solution)/shard_map/ppermute | solution.py:35
  170.8 8.2 %collective-permute-start.13 = (bf16[128,384]{1,0:T(8,128)(2,1)S(1)}, bf16[128,384]{1,0:T(8,128)(2,1)S(1)}, u32[]{:S(2)}, u32[]{:S(2)}) collective-permute-start(bf16[128,384]{1,0:T(8,128)(2,1)S(1)} %get-tuple-element.82), channel_id=1, source_target_pairs={{0,64},{32,96},{64,0},{96,32},{1,65},{33,97},{65,1},{97,33},{2,66}... | collective-permute-start | bytes 294920 | tf_op jit(solution)/shard_map/ppermute | solution.py:35
  173.2 5.8 %collective-permute-start.14 = (bf16[128,384]{1,0:T(8,128)(2,1)S(1)}, bf16[128,384]{1,0:T(8,128)(2,1)S(1)}, u32[]{:S(2)}, u32[]{:S(2)}) collective-permute-start(bf16[128,384]{1,0:T(8,128)(2,1)S(1)} %get-tuple-element.81), channel_id=1, source_target_pairs={{0,96},{32,0},{64,32},{96,64},{1,97},{33,1},{65,33},{97,65},{2,98}... | collective-permute-start | bytes 294920 | tf_op jit(solution)/shard_map/ppermute | solution.py:35
  174.7 12.3 %collective-permute-start.11 = (bf16[128,768]{0,1:T(8,128)(2,1)S(1)}, bf16[128,768]{0,1:T(8,128)(2,1)S(1)}, u32[]{:S(2)}, u32[]{:S(2)}) collective-permute-start(bf16[128,768]{0,1:T(8,128)(2,1)S(1)} %bitcast.112), channel_id=1, source_target_pairs={{0,24},{8,0},{16,8},{24,16},{1,25},{9,1},{17,9},{25,17},{2,26},{10... | collective-permute-start | bytes 589832 | tf_op jit(solution)/shard_map/ppermute | solution.py:35
  179.1 5.9 %collective-permute-start.15 = (bf16[128,384]{1,0:T(8,128)(2,1)S(1)}, bf16[128,384]{1,0:T(8,128)(2,1)S(1)}, u32[]{:S(2)}, u32[]{:S(2)}) collective-permute-start(bf16[128,384]{1,0:T(8,128)(2,1)S(1)} %fusion.32), channel_id=1, source_target_pairs={{0,8},{8,16},{16,24},{24,0},{1,9},{9,17},{17,25},{25,1},{2,10},{10... | collective-permute-start | bytes 294920 | tf_op jit(solution)/shard_map/ppermute | solution.py:35
  180.0 6.1 %collective-permute-start.16 = (bf16[128,384]{1,0:T(8,128)(2,1)S(1)}, bf16[128,384]{1,0:T(8,128)(2,1)S(1)}, u32[]{:S(2)}, u32[]{:S(2)}) collective-permute-start(bf16[128,384]{1,0:T(8,128)(2,1)S(1)} %fusion.32), channel_id=1, source_target_pairs={{0,16},{8,24},{16,0},{24,8},{1,17},{9,25},{17,1},{25,9},{2,18},{10... | collective-permute-start | bytes 294920 | tf_op jit(solution)/shard_map/ppermute | solution.py:35
  182.3 4.7 %collective-permute-start.17 = (bf16[128,384]{1,0:T(8,128)(2,1)S(1)}, bf16[128,384]{1,0:T(8,128)(2,1)S(1)}, u32[]{:S(2)}, u32[]{:S(2)}) collective-permute-start(bf16[128,384]{1,0:T(8,128)(2,1)S(1)} %fusion.32), channel_id=1, source_target_pairs={{0,24},{8,0},{16,8},{24,16},{1,25},{9,1},{17,9},{25,17},{2,26},{10... | collective-permute-start | bytes 294920 | tf_op jit(solution)/shard_map/ppermute | solution.py:35
  189.7 1.7 collective-permute-start.18
  192.1 5.5 %collective-permute-start.19 = (bf16[2,56,384]{2,0,1:T(2,128)(2,1)S(1)}, bf16[2,56,384]{2,0,1:T(2,128)(2,1)S(1)}, u32[]{:S(2)}, u32[]{:S(2)}) collective-permute-start(bf16[2,56,384]{2,0,1:T(2,128)(2,1)S(1)} %get-tuple-element.77), channel_id=1, source_target_pairs={{0,2},{2,4},{4,6},{6,0},{1,3},{3,5},{5,7},{7,1},{8,10},{10,12},{12... | collective-permute-start | bytes 258056 | tf_op jit(solution)/shard_map/ppermute | solution.py:35
  192.7 6.2 %collective-permute-start.20 = (bf16[2,56,384]{2,0,1:T(2,128)(2,1)S(1)}, bf16[2,56,384]{2,0,1:T(2,128)(2,1)S(1)}, u32[]{:S(2)}, u32[]{:S(2)}) collective-permute-start(bf16[2,56,384]{2,0,1:T(2,128)(2,1)S(1)} %get-tuple-element.79), channel_id=1, source_target_pairs={{0,4},{2,6},{4,0},{6,2},{1,5},{3,7},{5,1},{7,3},{8,12},{10,14},{12... | collective-permute-start | bytes 258056 | tf_op jit(solution)/shard_map/ppermute | solution.py:35
  195.1 5.7 %collective-permute-start.21 = (bf16[2,56,384]{2,0,1:T(2,128)(2,1)S(1)}, bf16[2,56,384]{2,0,1:T(2,128)(2,1)S(1)}, u32[]{:S(2)}, u32[]{:S(2)}) collective-permute-start(bf16[2,56,384]{2,0,1:T(2,128)(2,1)S(1)} %get-tuple-element.78), channel_id=1, source_target_pairs={{0,6},{2,0},{4,2},{6,4},{1,7},{3,1},{5,3},{7,5},{8,14},{10,8},{12,... | collective-permute-start | bytes 258056 | tf_op jit(solution)/shard_map/ppermute | solution.py:35
  201.1 8.0 %collective-permute-start.22 = (bf16[56,384]{1,0:T(8,128)(2,1)S(1)}, bf16[56,384]{1,0:T(8,128)(2,1)S(1)}, u32[]{:S(2)}, u32[]{:S(2)}) collective-permute-start(bf16[56,384]{1,0:T(8,128)(2,1)S(1)} %bitcast.119), channel_id=1, source_target_pairs={{0,128},{128,0},{1,129},{129,1},{2,130},{130,2},{3,131},{131,3},{4... | collective-permute-start | bytes 129032 | tf_op jit(solution)/shard_map/ppermute | solution.py:35
  209.1 5.6 %collective-permute-start.23 = (bf16[12,384]{1,0:T(8,128)(2,1)S(1)}, bf16[12,384]{1,0:T(8,128)(2,1)S(1)}, u32[]{:S(2)}, u32[]{:S(2)}) collective-permute-start(bf16[12,384]{1,0:T(8,128)(2,1)S(1)} %get-tuple-element.83), channel_id=1, source_target_pairs={{0,32},{32,64},{64,96},{96,0},{1,33},{33,65},{65,97},{97,1},{2,34}... | collective-permute-start | bytes 27656 | tf_op jit(solution)/shard_map/ppermute | solution.py:35
  210.9 4.6 %collective-permute-start.24 = (bf16[12,384]{1,0:T(8,128)(2,1)S(1)}, bf16[12,384]{1,0:T(8,128)(2,1)S(1)}, u32[]{:S(2)}, u32[]{:S(2)}) collective-permute-start(bf16[12,384]{1,0:T(8,128)(2,1)S(1)} %get-tuple-element.85), channel_id=1, source_target_pairs={{0,64},{32,96},{64,0},{96,32},{1,65},{33,97},{65,1},{97,33},{2,66}... | collective-permute-start | bytes 27656 | tf_op jit(solution)/shard_map/ppermute | solution.py:35
  212.9 3.7 %collective-permute-start.25 = (bf16[12,384]{1,0:T(8,128)(2,1)S(1)}, bf16[12,384]{1,0:T(8,128)(2,1)S(1)}, u32[]{:S(2)}, u32[]{:S(2)}) collective-permute-start(bf16[12,384]{1,0:T(8,128)(2,1)S(1)} %get-tuple-element.84), channel_id=1, source_target_pairs={{0,96},{32,0},{64,32},{96,64},{1,97},{33,1},{65,33},{97,65},{2,98}... | collective-permute-start | bytes 27656 | tf_op jit(solution)/shard_map/ppermute | solution.py:35

commit v8 on v7

--- a/solution.py
+++ b/solution.py
@@ -112,65 +112,62 @@
     return both[:, :HDIM] / total, highest, total
 
 
-def teacher_kernel(scale_ref, heads_ref, target_ref, query_ref, key_ref, value_ref, scores_ref):
+def teacher_kernel(heads_ref, out_ref, query_ref, key_ref, value_ref, scores_ref):
     blocks, rows = heads_ref.shape[1], heads_ref.shape[3]
-    tokens = blocks * rows
-    scale = scale_ref[0]
-    for one in range(2):
-        for block in range(blocks):
-            where = slice(block * rows, (block + 1) * rows)
-            query_ref[one, where] = heads_ref[one, block, 0]
-            key_ref[one, :, where] = jnp.transpose(heads_ref[one, block, 1])
-            with_ones(value_ref.at[one, where], heads_ref[one, block, 2])
+    for block in range(blocks):
+        where = slice(block * rows, (block + 1) * rows)
+        query_ref[where] = heads_ref[0, block, 0]
+        key_ref[:, where] = jnp.transpose(heads_ref[0, block, 1])
+        with_ones(value_ref.at[where], heads_ref[0, block, 2])
     step_rows = scores_ref.shape[1]
-    steps = tokens // step_rows
+    steps = blocks * rows // step_rows
 
     def rows_of(step):
         return pl.ds(pl.multiple_of(step * step_rows, step_rows), step_rows)
 
-    def put_scores(step, one):
-        scores_ref[one] = dot(query_ref[one, rows_of(step)], key_ref[one])
-
-    def rounded(one):
-        return attended_rows(scores_ref[one], value_ref.at[one])[0].astype(BF).astype(F32)
-
-    def one_block(step, carry):
-        put_scores(step, 1)
-        conditional = rounded(0)
-        put_scores(jnp.minimum(step + 1, steps - 1), 0)
-        unconditional = rounded(1)
-        target_ref[rows_of(step)] = unconditional + scale * (conditional - unconditional)
+    def put_scores(step, slot):
+        scores_ref[slot] = dot(query_ref[rows_of(step)], key_ref[...])
+
+    def finish(step, slot):
+        out_ref[rows_of(step)] = attended_rows(scores_ref[slot], value_ref)[0].astype(BF)
+
+    def two_blocks(pair, carry):
+        put_scores(2 * pair + 1, 1)
+        finish(2 * pair, 0)
+        put_scores(jnp.minimum(2 * pair + 2, steps - 1), 0)
+        finish(2 * pair + 1, 1)
         return carry
 
     put_scores(0, 0)
-    lax.fori_loop(0, steps, one_block, 0)
-
-
-def teacher(scale, heads):
+    lax.fori_loop(0, steps // 2, two_blocks, 0)
+
+
+def teacher(heads, one):
     tokens = heads.shape[1] * heads.shape[3]
     return pl.pallas_call(
         teacher_kernel,
         grid=(1,),
-        in_specs=[pl.BlockSpec(memory_space=pltpu.SMEM), whole(heads.shape)],
+        in_specs=[pl.BlockSpec((1, *heads.shape[1:]), lambda i: (one, 0, 0, 0, 0))],
         out_specs=whole((tokens, HDIM)),
-        out_shape=jax.ShapeDtypeStruct((tokens, HDIM), F32),
+        out_shape=jax.ShapeDtypeStruct((tokens, HDIM), BF),
         scratch_shapes=[
-            pltpu.VMEM((2, tokens, HDIM), BF),
-            pltpu.VMEM((2, HDIM, tokens), BF),
-            pltpu.VMEM((2, tokens, 2 * HDIM), BF),
+            pltpu.VMEM((tokens, HDIM), BF),
+            pltpu.VMEM((HDIM, tokens), BF),
+            pltpu.VMEM((tokens, 2 * HDIM), BF),
             pltpu.VMEM((2, 256, tokens), F32),
         ],
         cost_estimate=pl.CostEstimate(
-            flops=8 * tokens * tokens * HDIM,
-            transcendentals=2 * tokens * tokens,
-            bytes_accessed=4 * MIB,
+            flops=4 * tokens * tokens * HDIM,
+            transcendentals=tokens * tokens,
+            bytes_accessed=2 * MIB,
         ),
         compiler_params=pltpu.CompilerParams(vmem_limit_bytes=48 * MIB),
         name="teacher_forward",
-    )(scale, heads)
-
-
-def student_kernel(n_fast, place_ref, inv_ref, heads_ref, target_ref, up_ref, *refs):
+    )(heads)
+
+
+def student_kernel(n_fast, place_ref, scale_ref, inv_ref, heads_ref, *refs):
+    cond_ref, uncond_ref, up_ref, *refs = refs
     low_refs = refs[:n_fast]
     outs, locals_ = refs[n_fast : n_fast + 4], refs[n_fast + 4 : n_fast + 8]
     out_ref, upstream_ref, student_ref, stats_ref = locals_
@@ -179,7 +176,7 @@
     tokens = out_ref.shape[0]
     n_slow = low_refs[0].shape[0]
     here_slow, here_fast = place_ref[0], place_ref[1]
-    inverse = inv_ref[0]
+    scale, inverse = scale_ref[0], inv_ref[0]
 
     for part in range(3):
         up = up_ref[part]
@@ -214,7 +211,9 @@
         attended, highest, total = attended_rows(scores_ref[slot], value_ref)
         rounded = attended.astype(BF)
         out_ref[here] = rounded
-        upstream = ((rounded.astype(F32) - target_ref[here]) * inverse).astype(BF)
+        unconditional = uncond_ref[here].astype(F32)
+        target = unconditional + scale * (cond_ref[here].astype(F32) - unconditional)
+        upstream = ((rounded.astype(F32) - target) * inverse).astype(BF)
         upstream_ref[here] = upstream
         level = highest * SCALE2 + jnp.log2(total)
         center = jnp.sum(attended * upstream.astype(F32), axis=-1, keepdims=True)
@@ -236,8 +235,8 @@
         copy.wait()
 
 
-def student_forward(place, inverse, heads, target, up, low):
-    tokens = target.shape[0]
+def student_forward(place, scale, inverse, heads, teachers, up, low):
+    tokens = teachers[0].shape[0]
     one_pass = (1, *heads.shape[1:])
     smem = pl.BlockSpec(memory_space=pltpu.SMEM)
     outs = [
@@ -249,8 +248,8 @@
     return pl.pallas_call(
         functools.partial(student_kernel, len(low)),
         grid=(1,),
-        in_specs=[smem, smem, whole(one_pass)]
-        + [whole(operand.shape) for operand in (target, up, *low)],
+        in_specs=[smem, smem, smem, whole(one_pass)]
+        + [whole(operand.shape) for operand in (*teachers, up, *low)],
         out_specs=[HBM] * len(outs),
         out_shape=[pltpu.HBM(out.shape, out.dtype) for out in outs],
         scratch_shapes=[pltpu.VMEM(out.shape, out.dtype) for out in outs]
@@ -267,7 +266,7 @@
         ),
         compiler_params=pltpu.CompilerParams(vmem_limit_bytes=48 * MIB),
         name="student_forward",
-    )(place, inverse, heads, target, up, *low)
+    )(place, scale, inverse, heads, *teachers, up, *low)
 
 
 def backward_kernel(n_fast, place_ref, up_ref, *refs):
@@ -393,26 +392,27 @@
         (dot(features, adapter_down_weight[part]) * modulation).astype(BF) for part in range(3)
     ]
     low = jnp.concatenate(low, axis=1)
-    low_slow = jnp.stack(from_each(low, "z"))
-
     groups = n_cfg * n_slow
     part_cols = width // (groups * n_fast)
     spread = parts_ahead(features.reshape(rows, groups, n_fast, part_cols), "y", 2)
     spread = [part.reshape(rows, groups * part_cols) for part in spread]
-    columns = [spread[0]] + [shifted(spread[d], "y", d) for d in range(1, n_fast - 1)]
-    spread = spread[-1]
+    columns = [spread[0]] + [shifted(spread[d], "y", d) for d in range(1, n_fast)]
 
     place = jnp.stack([lax.axis_index("z"), lax.axis_index("y")]).astype(jnp.int32)
     up = lax.dynamic_slice_in_dim(adapter_up_weight, seq_index * HDIM, HDIM, 2)
     inverse = jnp.full((1,), 1.0 / math.sqrt(total_rows), F32)
 
-    heads, low_slow, up, place, spread, *columns = lax.optimization_barrier(
-        (heads, low_slow, up, place, spread, *columns)
+    heads, low, up, place, *columns = lax.optimization_barrier((heads, low, up, place, *columns))
+    low_slow = from_each(low, "z")
+    conditional = teacher(heads, 0)
+    conditional, heads, *low_slow = lax.optimization_barrier((conditional, heads, *low_slow))
+    low_all = from_each(jnp.stack(low_slow), "y")
+    unconditional = teacher(heads, 1)
+    unconditional, *low_all = lax.optimization_barrier((unconditional, *low_all))
+    teachers = (conditional, unconditional)
+    out, upstream, student, stats = student_forward(
+        place, scale.reshape(1), inverse, heads, teachers, up, low_all
     )
-    low_all = from_each(low_slow, "y")
-    target = teacher(scale, heads)
-    target, *low_all = lax.optimization_barrier((target, *low_all))
-    out, upstream, student, stats = student_forward(place, inverse, heads, target, up, low_all)
     tokens_out = exchange(out.reshape(n_slow * n_fast, rows, HDIM), ("z", "y"))
 
     *back, up_partial = backward(place, student, upstream, stats, up, low_all)
@@ -420,8 +420,6 @@
     student_out = jnp.moveaxis(tokens_out, 0, 1).reshape(rows, -1)
 
     arrived = [shifted(back[d], "y", d) for d in range(1, n_fast)]
-    arrived[0], spread = lax.optimization_barrier((arrived[0], spread))
-    columns.append(shifted(spread, "y", n_fast - 1))
     back = sum((part.astype(F32) for part in arrived), back[0].astype(F32)).astype(BF)
     back, student_out = lax.optimization_barrier((back, student_out))
     back = summed_parts([back[d] for d in range(n_slow)], "z")

time: 218 us -> 224 us (1.028)
  waiting for transfers between devices: 95.1 us -> 103 us
  starting transfers between devices: 63.4 us -> 60.4 us
    all_to_all x2, waiting for transfers between devices: 0.01 us -> 44.4 us  [exchange(): return lax.all_to_all(value, axes, split_axis=0, concat_axis=0, tiled=True)]
    ppermute x26, waiting for transfers between devices: 95.1 us -> 58.5 us  [shifted(): lax.ppermute(value, axis, [(i, (i + distance) % size) for i in range(size)])]
    all_to_all x2, starting transfers between devices: 19.8 us -> 16.3 us  [exchange(): return lax.all_to_all(value, axes, split_axis=0, concat_axis=0, tiled=True)]
    pallas_call x1 -> x2, Pallas kernels: 13.7 us -> 15.1 us  [teacher(): pl.pallas_call(teacher_kernel, grid=(1,), in_specs=[pl.BlockSpec((1, *hea...]
  transfers between devices with their start and end apart: 28 -> 28, of which waited for: 17 -> 18; matrix products, arithmetic and copies ran while one was open for 4% -> 4% of each run, Pallas kernels for 13% -> 14%
where the time goes in v8:
time: 224 us
  waiting for transfers between devices  103 us (46%)
  starting transfers between devices  60.4 us (27%)
  Pallas kernels  44 us (20%)
  matrix products  5.98 us (3%)
  local copies, waits for them, and re-layouts  4.65 us (2%)
  other arithmetic  3.18 us (1%)
  between operations  2.49 us (1%)
    ppermute x26, waiting for transfers between devices, shifted(): lax.ppermute(value, axis, [(i, (i + distance) % size) for i in range(size)])  58.5 us
    all_to_all x2, waiting for transfers between devices, exchange(): return lax.all_to_all(value, axes, split_axis=0, concat_axis=0, tiled=True)  44.4 us
    ppermute x26, starting transfers between devices, shifted(): lax.ppermute(value, axis, [(i, (i + distance) % size) for i in range(size)])  44.1 us
    all_to_all x2, starting transfers between devices, exchange(): return lax.all_to_all(value, axes, split_axis=0, concat_axis=0, tiled=True)  16.3 us
    pallas_call x1, Pallas kernels, backward(): pl.pallas_call(functools.partial(backward_kernel, n_fast), grid=(1,), in_...  15.4 us
    pallas_call x2, Pallas kernels, teacher(): pl.pallas_call(teacher_kernel, grid=(1,), in_specs=[pl.BlockSpec((1, *hea...  15.1 us
    pallas_call x1, Pallas kernels, student_forward(): pl.pallas_call(functools.partial(student_kernel, len(low)), grid=(1,), in...  10 us
    dot_general x4, matrix products, dot(): return lax.dot_general(a, b, dims, preferred_element_type=F32)  5.98 us
  transfers between devices with their start and end apart: 28, of which 18 were waited for; matrix products, arithmetic and copies ran while one was open for 4% of the time, Pallas kernels for 14%

profile of v8, /device:TPU:6, one launch (start us, length us, event | category | flops | bytes accessed | tf_op | source)
XLA Modules:
  0.0 223.7 jit_solution(16581706453950964607)
XLA Ops:
  0.6 3.4 %pack_heads.1 = bf16[32,3,128,128]{3,2,1,0:T(8,128)(2,1)} custom-call(bf16[2,128,2048]{2,1,0:T(8,128)(2,1)} %bitcast.103, bf16[2,128,2048]{2,1,0:T(8,128)(2,1)} %bitcast.104, bf16[2,128,2048]{2,1,0:T(8,128)(2,1)} %bitcast.105), custom_call_target="tpu_custom_call" | custom-call | bytes 6291456 | tf_op jit(solution)/shard_map/pack_heads/pallas_call | solution.py:91
  4.1 11.7 %all-to-all-start = ((bf16[32,3,128,128]{3,2,1,0:T(8,128)(2,1)}), bf16[32,3,128,128]{3,2,1,0:T(8,128)(2,1)}, u32[]{:S(2)}, u32[]{:S(2)}) async-start(bf16[32,3,128,128]{3,2,1,0:T(8,128)(2,1)} %pack_heads.1), calls=%async_computation | async-start | bytes 6291456 | tf_op jit(solution)/shard_map/all_to_all | solution.py:30
  17.1 1.7 collective-permute-start
  18.9 2.7 %collective-permute-start.1 = (bf16[128,768]{0,1:T(8,128)(2,1)}, bf16[128,768]{0,1:T(8,128)(2,1)S(1)}, u32[]{:S(2)}, u32[]{:S(2)}) collective-permute-start(bf16[128,768]{0,1:T(8,128)(2,1)} %bitcast.16), channel_id=1, source_target_pairs={{0,16},{8,24},{16,0},{24,8},{1,17},{9,25},{17,1},{25,9},{2,18},{10... | collective-permute-start | bytes 589832 | tf_op jit(solution)/shard_map/ppermute | solution.py:35
  21.5 1.5 collective-permute-start.2
  25.1 1.5 fusion
  26.6 1.5 fusion.1
  28.1 1.5 fusion.2
  29.7 1.1 collective-permute-done
  30.7 12.1 %collective-permute-done.1 = bf16[128,768]{0,1:T(8,128)(2,1)S(1)} collective-permute-done((bf16[128,768]{0,1:T(8,128)(2,1)}, bf16[128,768]{0,1:T(8,128)(2,1)S(1)}, u32[]{:S(2)}, u32[]{:S(2)}) %collective-permute-start.1) | collective-permute-done | bytes 196640 | tf_op jit(solution)/shard_map/ppermute | solution.py:35
  43.8 44.3 %all-to-all-done = bf16[32,3,128,128]{3,2,1,0:T(8,128)(2,1)} async-done(((bf16[32,3,128,128]{3,2,1,0:T(8,128)(2,1)}), bf16[32,3,128,128]{3,2,1,0:T(8,128)(2,1)}, u32[]{:S(2)}, u32[]{:S(2)}) %all-to-all-start) | async-done | bytes 3145760 | tf_op jit(solution)/shard_map/all_to_all | solution.py:30
  88.1 1.7 collective-permute-start.3
  89.8 1.5 collective-permute-start.4
  91.2 2.9 %collective-permute-start.5 = (bf16[128,384]{1,0:T(8,128)(2,1)S(1)}, bf16[128,384]{1,0:T(8,128)(2,1)S(1)}, u32[]{:S(2)}, u32[]{:S(2)}) collective-permute-start(bf16[128,384]{1,0:T(8,128)(2,1)S(1)} %pad_maximum_fusion.1), channel_id=1, source_target_pairs={{0,96},{32,0},{64,32},{96,64},{1,97},{33,1},{65,33},{97,65},{2,98}... | collective-permute-start | bytes 294920 | tf_op jit(solution)/shard_map/ppermute | solution.py:35
  94.2 7.5 %teacher_forward.2.refs_0_ = bf16[2048,128]{1,0:T(8,128)(2,1)S(1)} custom-call(bf16[2,16,3,128,128]{4,3,2,1,0:T(8,128)(2,1)} %bitcast.3.heads_ref), custom_call_target="tpu_custom_call" | custom-call | flops 2147483648 | bytes 2097152 | tf_op jit(solution)/shard_map/teacher_forward/pallas_call | solution.py:147
  101.9 2.7 %collective-permute-start.7 = (bf16[4,128,384]{2,1,0:T(8,128)(2,1)S(1)}, bf16[4,128,384]{2,1,0:T(8,128)(2,1)S(1)}, u32[]{:S(2)}, u32[]{:S(2)}) collective-permute-start(bf16[4,128,384]{2,1,0:T(8,128)(2,1)S(1)} %pad_maximum_fusion.refs_3_), channel_id=1, source_target_pairs={{0,16},{8,24},{16,0},{24,8},{1,17},{9,25},{17,1},{25,9},{2,18},{10... | collective-permute-start | bytes 1179656 | tf_op jit(solution)/shard_map/ppermute | solution.py:35
  104.6 1.5 collective-permute-start.8
  106.1 7.5 %teacher_forward.3.refs_1_ = bf16[2048,128]{1,0:T(8,128)(2,1)S(1)} custom-call(bf16[2,16,3,128,128]{4,3,2,1,0:T(8,128)(2,1)} %bitcast.3.heads_ref), custom_call_target="tpu_custom_call" | custom-call | flops 2147483648 | bytes 2097152 | tf_op jit(solution)/shard_map/teacher_forward/pallas_call | solution.py:147
  113.7 6.9 %collective-permute-done.7.refs_5_ = bf16[4,128,384]{2,1,0:T(8,128)(2,1)S(1)} collective-permute-done((bf16[4,128,384]{2,1,0:T(8,128)(2,1)S(1)}, bf16[4,128,384]{2,1,0:T(8,128)(2,1)S(1)}, u32[]{:S(2)}, u32[]{:S(2)}) %collective-permute-start.7) | collective-permute-done | bytes 393248 | tf_op jit(solution)/shard_map/ppermute | solution.py:35
  120.6 10.0 %student_forward.1 = (bf16[2048,128]{1,0:T(8,128)(2,1)}, bf16[2048,128]{1,0:T(8,128)(2,1)}, bf16[3,2048,128]{2,1,0:T(8,128)(2,1)}, f32[8,2048]{1,0:T(8,128)}) custom-call(s32[2]{0:T(128)S(1)} %pad_add_fusion.place_ref, f32[1]{0:T(128)} %bitcast.7.scale_ref, f32[1]{0:T(128)} %constant.172.clone.1.inv_ref, bf16[2,16,3,128,128]{4,3,2,1,0:T(8,128)(2,1)} %bitcast.3.heads_ref, ...), custom_call_target="tpu_custom_call" | custom-call | flops 2147483648 | bytes 6291456 | tf_op jit(solution)/shard_map/student_forward/pallas_call | solution.py:248
  130.6 4.6 %all-to-all-start.1 = ((bf16[16,128,128]{2,1,0:T(8,128)(2,1)}), bf16[16,128,128]{2,1,0:T(8,128)(2,1)S(1)}, u32[]{:S(2)}, u32[]{:S(2)}) async-start(bf16[16,128,128]{2,1,0:T(8,128)(2,1)} %bitcast.109), calls=%async_computation.1 | async-start | bytes 1048576 | tf_op jit(solution)/shard_map/all_to_all | solution.py:30
  135.2 15.4 %attention_backward.1 = (bf16[4,128,384]{2,1,0:T(8,128)(2,1)}, bf16[4,128,384]{2,1,0:T(8,128)(2,1)}, bf16[4,128,384]{2,1,0:T(8,128)(2,1)}, bf16[4,128,384]{2,1,0:T(8,128)(2,1)}, bf16[128,384]{1,0:T(8,128)(2,1)S(1)}) custom-call(s32[2]{0:T(128)S(1)} %pad_add_fusion.place_ref, bf16[3,128,128]{2,1,0:T(8,128)(2,1)S(1)} %constant_dynamic-slice_fusion.5.refs_2_.up_ref, ...), custom_call_target="tpu_custom_call" | custom-call | flops 5368709120 | bytes 6291456 | tf_op jit(solution)/shard_map/attention_backward/pallas_call | solution.py:336
  150.8 3.4 %collective-permute-start.10 = (bf16[4,128,384]{2,1,0:T(8,128)(2,1)}, bf16[4,128,384]{2,1,0:T(8,128)(2,1)S(1)}, u32[]{:S(2)}, u32[]{:S(2)}) collective-permute-start(bf16[4,128,384]{2,1,0:T(8,128)(2,1)} %get-tuple-element.65), channel_id=1, source_target_pairs={{0,16},{8,24},{16,0},{24,8},{1,17},{9,25},{17,1},{25,9},{2,18},{10... | collective-permute-start | bytes 1179656 | tf_op jit(solution)/shard_map/ppermute | solution.py:35
  154.2 1.2 collective-permute-start.11
  157.1 7.5 %collective-permute-done.10 = bf16[4,128,384]{2,1,0:T(8,128)(2,1)S(1)} collective-permute-done((bf16[4,128,384]{2,1,0:T(8,128)(2,1)}, bf16[4,128,384]{2,1,0:T(8,128)(2,1)S(1)}, u32[]{:S(2)}, u32[]{:S(2)}) %collective-permute-start.10) | collective-permute-done | bytes 393248 | tf_op jit(solution)/shard_map/ppermute | solution.py:35
  164.6 7.3 %collective-permute-done.11 = bf16[4,128,384]{2,1,0:T(8,128)(2,1)S(1)} collective-permute-done((bf16[4,128,384]{2,1,0:T(8,128)(2,1)}, bf16[4,128,384]{2,1,0:T(8,128)(2,1)S(1)}, u32[]{:S(2)}, u32[]{:S(2)}) %collective-permute-start.11) | collective-permute-done | bytes 393248 | tf_op jit(solution)/shard_map/ppermute | solution.py:35
  171.9 1.2 add_convert_fusion
  173.1 1.8 collective-permute-start.12
  174.9 2.4 %collective-permute-start.13 = (bf16[128,384]{1,0:T(8,128)(2,1)S(1)}, bf16[128,384]{1,0:T(8,128)(2,1)S(1)}, u32[]{:S(2)}, u32[]{:S(2)}) collective-permute-start(bf16[128,384]{1,0:T(8,128)(2,1)S(1)} %get-tuple-element.90), channel_id=1, source_target_pairs={{0,64},{32,96},{64,0},{96,32},{1,65},{33,97},{65,1},{97,33},{2,66}... | collective-permute-start | bytes 294920 | tf_op jit(solution)/shard_map/ppermute | solution.py:35
  177.2 1.5 collective-permute-start.14
  178.7 2.0 collective-permute-done.12
  180.7 3.4 %collective-permute-done.13 = bf16[128,384]{1,0:T(8,128)(2,1)S(1)} collective-permute-done((bf16[128,384]{1,0:T(8,128)(2,1)S(1)}, bf16[128,384]{1,0:T(8,128)(2,1)S(1)}, u32[]{:S(2)}, u32[]{:S(2)}) %collective-permute-start.13) | collective-permute-done | bytes 98336 | tf_op jit(solution)/shard_map/ppermute | solution.py:35
  184.1 1.7 collective-permute-start.15
  185.8 2.7 %collective-permute-start.16 = (bf16[128,384]{1,0:T(8,128)(2,1)S(1)}, bf16[128,384]{1,0:T(8,128)(2,1)S(1)}, u32[]{:S(2)}, u32[]{:S(2)}) collective-permute-start(bf16[128,384]{1,0:T(8,128)(2,1)S(1)} %fusion.32), channel_id=1, source_target_pairs={{0,16},{8,24},{16,0},{24,8},{1,17},{9,25},{17,1},{25,9},{2,18},{10... | collective-permute-start | bytes 294920 | tf_op jit(solution)/shard_map/ppermute | solution.py:35
  188.5 1.5 collective-permute-start.17
  190.1 3.1 %collective-permute-done.16 = bf16[128,384]{1,0:T(8,128)(2,1)S(1)} collective-permute-done((bf16[128,384]{1,0:T(8,128)(2,1)S(1)}, bf16[128,384]{1,0:T(8,128)(2,1)S(1)}, u32[]{:S(2)}, u32[]{:S(2)}) %collective-permute-start.16) | collective-permute-done | bytes 98336 | tf_op jit(solution)/shard_map/ppermute | solution.py:35
  193.2 1.5 convolution_convert_fusion
  196.1 1.6 collective-permute-done.18
  198.9 2.4 %collective-permute-start.20 = (bf16[2,56,384]{2,0,1:T(2,128)(2,1)S(1)}, bf16[2,56,384]{2,0,1:T(2,128)(2,1)S(1)}, u32[]{:S(2)}, u32[]{:S(2)}) collective-permute-start(bf16[2,56,384]{2,0,1:T(2,128)(2,1)S(1)} %get-tuple-element.87), channel_id=1, source_target_pairs={{0,4},{2,6},{4,0},{6,2},{1,5},{3,7},{5,1},{7,3},{8,12},{10,14},{12... | collective-permute-start | bytes 258056 | tf_op jit(solution)/shard_map/ppermute | solution.py:35
  201.3 2.5 %collective-permute-done.19 = bf16[2,56,384]{2,0,1:T(2,128)(2,1)S(1)} collective-permute-done((bf16[2,56,384]{2,0,1:T(2,128)(2,1)S(1)}, bf16[2,56,384]{2,0,1:T(2,128)(2,1)S(1)}, u32[]{:S(2)}, u32[]{:S(2)}) %collective-permute-start.19) | collective-permute-done | bytes 86048 | tf_op jit(solution)/shard_map/ppermute | solution.py:35
  203.8 1.3 collective-permute-done.20
  205.1 1.9 collective-permute-done.21
  207.3 2.8 %collective-permute-start.22 = (bf16[56,384]{1,0:T(8,128)(2,1)S(1)}, bf16[56,384]{1,0:T(8,128)(2,1)S(1)}, u32[]{:S(2)}, u32[]{:S(2)}) collective-permute-start(bf16[56,384]{1,0:T(8,128)(2,1)S(1)} %bitcast.117), channel_id=1, source_target_pairs={{0,128},{128,0},{1,129},{129,1},{2,130},{130,2},{3,131},{131,3},{4... | collective-permute-start | bytes 129032 | tf_op jit(solution)/shard_map/ppermute | solution.py:35
  210.2 5.1 %collective-permute-done.22 = bf16[56,384]{1,0:T(8,128)(2,1)S(1)} collective-permute-done((bf16[56,384]{1,0:T(8,128)(2,1)S(1)}, bf16[56,384]{1,0:T(8,128)(2,1)S(1)}, u32[]{:S(2)}, u32[]{:S(2)}) %collective-permute-start.22) | collective-permute-done | bytes 43040 | tf_op jit(solution)/shard_map/ppermute | solution.py:35
  215.4 2.7 %collective-permute-start.23 = (bf16[12,384]{1,0:T(8,128)(2,1)S(1)}, bf16[12,384]{1,0:T(8,128)(2,1)S(1)}, u32[]{:S(2)}, u32[]{:S(2)}) collective-permute-start(bf16[12,384]{1,0:T(8,128)(2,1)S(1)} %get-tuple-element.91), channel_id=1, source_target_pairs={{0,32},{32,64},{64,96},{96,0},{1,33},{33,65},{65,97},{97,1},{2,34}... | collective-permute-start | bytes 27656 | tf_op jit(solution)/shard_map/ppermute | solution.py:35
  218.1 1.2 collective-permute-start.24
  219.3 1.2 collective-permute-start.25
  221.2 1.5 collective-permute-done.24
  (72 shorter events, 9.7 us)
Async XLA Ops:
  0.6 24.4 %copy-start = (bf16[3,128,2048]{2,1,0:T(8,128)(2,1)S(1)}, bf16[3,128,2048]{2,1,0:T(8,128)(2,1)}, u32[]{:S(2)}) copy-start(bf16[3,128,2048]{2,1,0:T(8,128)(2,1)} %param.13) | copy-start | bytes 4718596
  4.1 11.8 %copy-start.5 = (bf16[1,1,128,3072]{3,2,1,0:T(8,128)(2,1)S(1)}, bf16[1,1,128,3072]{3,2,1,0:T(8,128)(2,1)}, u32[]{:S(2)}) copy-start(bf16[1,1,128,3072]{3,2,1,0:T(8,128)(2,1)} %param.11) | copy-start | bytes 2359300
  4.1 84.0 %all-to-all-start = ((bf16[32,3,128,128]{3,2,1,0:T(8,128)(2,1)}), bf16[32,3,128,128]{3,2,1,0:T(8,128)(2,1)}, u32[]{:S(2)}, u32[]{:S(2)}) async-start(bf16[32,3,128,128]{3,2,1,0:T(8,128)(2,1)} %pack_heads.1), calls=%async_computation | async-start | bytes 6291456 | tf_op jit(solution)/shard_map/all_to_all | solution.py:30
  15.9 7.1 %copy-start.6 = (s32[2,1]{0,1:T(1,128)S(1)}, s32[2,1]{0,1:T(1,128)}, u32[]{:S(2)}) copy-start(s32[2,1]{0,1:T(1,128)} %param.15) | copy-start | bytes 28
  15.9 7.1 %copy-start.7 = (s32[2,1]{0,1:T(1,128)S(1)}, s32[2,1]{0,1:T(1,128)}, u32[]{:S(2)}) copy-start(s32[2,1]{0,1:T(1,128)} %param.14) | copy-start | bytes 28
  17.1 13.6 %collective-permute-start = (bf16[128,768]{0,1:T(8,128)(2,1)}, bf16[128,768]{0,1:T(8,128)(2,1)S(1)}, u32[]{:S(2)}, u32[]{:S(2)}) collective-permute-start(bf16[128,768]{0,1:T(8,128)(2,1)} %bitcast.15), channel_id=1, source_target_pairs={{0,8},{8,16},{16,24},{24,0},{1,9},{9,17},{17,25},{25,1},{2,10},{10... | collective-permute-start | bytes 589832 | tf_op jit(solution)/shard_map/ppermute | solution.py:35
  18.9 24.0 %collective-permute-start.1 = (bf16[128,768]{0,1:T(8,128)(2,1)}, bf16[128,768]{0,1:T(8,128)(2,1)S(1)}, u32[]{:S(2)}, u32[]{:S(2)}) collective-permute-start(bf16[128,768]{0,1:T(8,128)(2,1)} %bitcast.16), channel_id=1, source_target_pairs={{0,16},{8,24},{16,0},{24,8},{1,17},{9,25},{17,1},{25,9},{2,18},{10... | collective-permute-start | bytes 589832 | tf_op jit(solution)/shard_map/ppermute | solution.py:35
  21.5 22.3 %collective-permute-start.2 = (bf16[128,768]{0,1:T(8,128)(2,1)S(1)}, bf16[128,768]{0,1:T(8,128)(2,1)}, u32[]{:S(2)}, u32[]{:S(2)}) collective-permute-start(bf16[128,768]{0,1:T(8,128)(2,1)S(1)} %bitcast.112), channel_id=1, source_target_pairs={{0,24},{8,0},{16,8},{24,16},{1,25},{9,1},{17,9},{25,17},{2,26},{10... | collective-permute-start | bytes 589832 | tf_op jit(solution)/shard_map/ppermute | solution.py:35
  30.7 57.4 %copy-start.8 = (bf16[128,768]{0,1:T(8,128)(2,1)}, bf16[128,768]{0,1:T(8,128)(2,1)S(1)}, u32[]{:S(2)}) copy-start(bf16[128,768]{0,1:T(8,128)(2,1)S(1)} %collective-permute-done) | copy-start | bytes 589828
  42.9 58.9 %copy-start.10 = (bf16[128,768]{0,1:T(8,128)(2,1)}, bf16[128,768]{0,1:T(8,128)(2,1)S(1)}, u32[]{:S(2)}) copy-start(bf16[128,768]{0,1:T(8,128)(2,1)S(1)} %collective-permute-done.1) | copy-start | bytes 589828
  88.1 13.6 %collective-permute-start.3 = (bf16[128,384]{1,0:T(8,128)(2,1)S(1)}, bf16[128,384]{1,0:T(8,128)(2,1)S(1)}, u32[]{:S(2)}, u32[]{:S(2)}) collective-permute-start(bf16[128,384]{1,0:T(8,128)(2,1)S(1)} %pad_maximum_fusion.1), channel_id=1, source_target_pairs={{0,32},{32,64},{64,96},{96,0},{1,33},{33,65},{65,97},{97,1},{2,34}... | collective-permute-start | bytes 294920 | tf_op jit(solution)/shard_map/ppermute | solution.py:35
  89.8 12.0 %collective-permute-start.4 = (bf16[128,384]{1,0:T(8,128)(2,1)S(1)}, bf16[128,384]{1,0:T(8,128)(2,1)S(1)}, u32[]{:S(2)}, u32[]{:S(2)}) collective-permute-start(bf16[128,384]{1,0:T(8,128)(2,1)S(1)} %pad_maximum_fusion.1), channel_id=1, source_target_pairs={{0,64},{32,96},{64,0},{96,32},{1,65},{33,97},{65,1},{97,33},{2,66}... | collective-permute-start | bytes 294920 | tf_op jit(solution)/shard_map/ppermute | solution.py:35
  91.2 10.5 %collective-permute-start.5 = (bf16[128,384]{1,0:T(8,128)(2,1)S(1)}, bf16[128,384]{1,0:T(8,128)(2,1)S(1)}, u32[]{:S(2)}, u32[]{:S(2)}) collective-permute-start(bf16[128,384]{1,0:T(8,128)(2,1)S(1)} %pad_maximum_fusion.1), channel_id=1, source_target_pairs={{0,96},{32,0},{64,32},{96,64},{1,97},{33,1},{65,33},{97,65},{2,98}... | collective-permute-start | bytes 294920 | tf_op jit(solution)/shard_map/ppermute | solution.py:35
  101.8 18.7 %copy-start.1 = (bf16[4,128,384]{2,1,0:T(8,128)(2,1)}, bf16[4,128,384]{2,1,0:T(8,128)(2,1)S(1)}, u32[]{:S(2)}) copy-start(bf16[4,128,384]{2,1,0:T(8,128)(2,1)S(1)} %pad_maximum_fusion.refs_3_) | copy-start | bytes 1179652
  101.8 11.8 %collective-permute-start.6 = (bf16[4,128,384]{2,1,0:T(8,128)(2,1)S(1)}, bf16[4,128,384]{2,1,0:T(8,128)(2,1)S(1)}, u32[]{:S(2)}, u32[]{:S(2)}) collective-permute-start(bf16[4,128,384]{2,1,0:T(8,128)(2,1)S(1)} %pad_maximum_fusion.refs_3_), channel_id=1, source_target_pairs={{0,8},{8,16},{16,24},{24,0},{1,9},{9,17},{17,25},{25,1},{2,10},{10... | collective-permute-start | bytes 1179656 | tf_op jit(solution)/shard_map/ppermute | solution.py:35
  101.9 18.6 %collective-permute-start.7 = (bf16[4,128,384]{2,1,0:T(8,128)(2,1)S(1)}, bf16[4,128,384]{2,1,0:T(8,128)(2,1)S(1)}, u32[]{:S(2)}, u32[]{:S(2)}) collective-permute-start(bf16[4,128,384]{2,1,0:T(8,128)(2,1)S(1)} %pad_maximum_fusion.refs_3_), channel_id=1, source_target_pairs={{0,16},{8,24},{16,0},{24,8},{1,17},{9,25},{17,1},{25,9},{2,18},{10... | collective-permute-start | bytes 1179656 | tf_op jit(solution)/shard_map/ppermute | solution.py:35
  104.6 15.9 %collective-permute-start.8 = (bf16[4,128,384]{2,1,0:T(8,128)(2,1)S(1)}, bf16[4,128,384]{2,1,0:T(8,128)(2,1)S(1)}, u32[]{:S(2)}, u32[]{:S(2)}) collective-permute-start(bf16[4,128,384]{2,1,0:T(8,128)(2,1)S(1)} %pad_maximum_fusion.refs_3_), channel_id=1, source_target_pairs={{0,24},{8,0},{16,8},{24,16},{1,25},{9,1},{17,9},{25,17},{2,26},{10... | collective-permute-start | bytes 1179656 | tf_op jit(solution)/shard_map/ppermute | solution.py:35
  113.7 16.9 %copy-start.2 = (bf16[4,128,384]{2,1,0:T(8,128)(2,1)}, bf16[4,128,384]{2,1,0:T(8,128)(2,1)S(1)}, u32[]{:S(2)}) copy-start(bf16[4,128,384]{2,1,0:T(8,128)(2,1)S(1)} %collective-permute-done.6.refs_4_) | copy-start | bytes 1179652
  120.5 10.0 %copy-start.3 = (bf16[4,128,384]{2,1,0:T(8,128)(2,1)}, bf16[4,128,384]{2,1,0:T(8,128)(2,1)S(1)}, u32[]{:S(2)}) copy-start(bf16[4,128,384]{2,1,0:T(8,128)(2,1)S(1)} %collective-permute-done.7.refs_5_) | copy-start | bytes 1179652
  120.6 10.0 %copy-start.4 = (bf16[4,128,384]{2,1,0:T(8,128)(2,1)}, bf16[4,128,384]{2,1,0:T(8,128)(2,1)S(1)}, u32[]{:S(2)}) copy-start(bf16[4,128,384]{2,1,0:T(8,128)(2,1)S(1)} %collective-permute-done.8.refs_6_) | copy-start | bytes 1179652
  130.6 20.2 %all-to-all-start.1 = ((bf16[16,128,128]{2,1,0:T(8,128)(2,1)}), bf16[16,128,128]{2,1,0:T(8,128)(2,1)S(1)}, u32[]{:S(2)}, u32[]{:S(2)}) async-start(bf16[16,128,128]{2,1,0:T(8,128)(2,1)} %bitcast.109), calls=%async_computation.1 | async-start | bytes 1048576 | tf_op jit(solution)/shard_map/all_to_all | solution.py:30
  150.8 13.8 %collective-permute-start.10 = (bf16[4,128,384]{2,1,0:T(8,128)(2,1)}, bf16[4,128,384]{2,1,0:T(8,128)(2,1)S(1)}, u32[]{:S(2)}, u32[]{:S(2)}) collective-permute-start(bf16[4,128,384]{2,1,0:T(8,128)(2,1)} %get-tuple-element.65), channel_id=1, source_target_pairs={{0,16},{8,24},{16,0},{24,8},{1,17},{9,25},{17,1},{25,9},{2,18},{10... | collective-permute-start | bytes 1179656 | tf_op jit(solution)/shard_map/ppermute | solution.py:35
  154.2 17.7 %collective-permute-start.11 = (bf16[4,128,384]{2,1,0:T(8,128)(2,1)}, bf16[4,128,384]{2,1,0:T(8,128)(2,1)S(1)}, u32[]{:S(2)}, u32[]{:S(2)}) collective-permute-start(bf16[4,128,384]{2,1,0:T(8,128)(2,1)} %get-tuple-element.66), channel_id=1, source_target_pairs={{0,24},{8,0},{16,8},{24,16},{1,25},{9,1},{17,9},{25,17},{2,26},{10... | collective-permute-start | bytes 1179656 | tf_op jit(solution)/shard_map/ppermute | solution.py:35
  155.4 16.5 %collective-permute-start.9 = (bf16[4,128,384]{2,1,0:T(8,128)(2,1)}, bf16[4,128,384]{2,1,0:T(8,128)(2,1)S(1)}, u32[]{:S(2)}, u32[]{:S(2)}) collective-permute-start(bf16[4,128,384]{2,1,0:T(8,128)(2,1)} %get-tuple-element.64), channel_id=1, source_target_pairs={{0,8},{8,16},{16,24},{24,0},{1,9},{9,17},{17,25},{25,1},{2,10},{10... | collective-permute-start | bytes 1179656 | tf_op jit(solution)/shard_map/ppermute | solution.py:35
  157.1 36.1 %copy-start.9 = (bf16[128,768]{0,1:T(8,128)(2,1)S(1)}, bf16[128,768]{0,1:T(8,128)(2,1)}, u32[]{:S(2)}) copy-start(bf16[128,768]{0,1:T(8,128)(2,1)} %copy-done.8) | copy-start | bytes 589828
  157.1 36.1 %copy-start.11 = (bf16[128,768]{0,1:T(8,128)(2,1)S(1)}, bf16[128,768]{0,1:T(8,128)(2,1)}, u32[]{:S(2)}) copy-start(bf16[128,768]{0,1:T(8,128)(2,1)} %copy-done.10) | copy-start | bytes 589828
  173.1 7.6 %collective-permute-start.12 = (bf16[128,384]{1,0:T(8,128)(2,1)S(1)}, bf16[128,384]{1,0:T(8,128)(2,1)S(1)}, u32[]{:S(2)}, u32[]{:S(2)}) collective-permute-start(bf16[128,384]{1,0:T(8,128)(2,1)S(1)} %get-tuple-element.88), channel_id=1, source_target_pairs={{0,32},{32,64},{64,96},{96,0},{1,33},{33,65},{65,97},{97,1},{2,34}... | collective-permute-start | bytes 294920 | tf_op jit(solution)/shard_map/ppermute | solution.py:35
  174.9 9.2 %collective-permute-start.13 = (bf16[128,384]{1,0:T(8,128)(2,1)S(1)}, bf16[128,384]{1,0:T(8,128)(2,1)S(1)}, u32[]{:S(2)}, u32[]{:S(2)}) collective-permute-start(bf16[128,384]{1,0:T(8,128)(2,1)S(1)} %get-tuple-element.90), channel_id=1, source_target_pairs={{0,64},{32,96},{64,0},{96,32},{1,65},{33,97},{65,1},{97,33},{2,66}... | collective-permute-start | bytes 294920 | tf_op jit(solution)/shard_map/ppermute | solution.py:35
  177.2 6.8 %collective-permute-start.14 = (bf16[128,384]{1,0:T(8,128)(2,1)S(1)}, bf16[128,384]{1,0:T(8,128)(2,1)S(1)}, u32[]{:S(2)}, u32[]{:S(2)}) collective-permute-start(bf16[128,384]{1,0:T(8,128)(2,1)S(1)} %get-tuple-element.89), channel_id=1, source_target_pairs={{0,96},{32,0},{64,32},{96,64},{1,97},{33,1},{65,33},{97,65},{2,98}... | collective-permute-start | bytes 294920 | tf_op jit(solution)/shard_map/ppermute | solution.py:35
  184.1 5.9 %collective-permute-start.15 = (bf16[128,384]{1,0:T(8,128)(2,1)S(1)}, bf16[128,384]{1,0:T(8,128)(2,1)S(1)}, u32[]{:S(2)}, u32[]{:S(2)}) collective-permute-start(bf16[128,384]{1,0:T(8,128)(2,1)S(1)} %fusion.32), channel_id=1, source_target_pairs={{0,8},{8,16},{16,24},{24,0},{1,9},{9,17},{17,25},{25,1},{2,10},{10... | collective-permute-start | bytes 294920 | tf_op jit(solution)/shard_map/ppermute | solution.py:35
  185.8 7.4 %collective-permute-start.16 = (bf16[128,384]{1,0:T(8,128)(2,1)S(1)}, bf16[128,384]{1,0:T(8,128)(2,1)S(1)}, u32[]{:S(2)}, u32[]{:S(2)}) collective-permute-start(bf16[128,384]{1,0:T(8,128)(2,1)S(1)} %fusion.32), channel_id=1, source_target_pairs={{0,16},{8,24},{16,0},{24,8},{1,17},{9,25},{17,1},{25,9},{2,18},{10... | collective-permute-start | bytes 294920 | tf_op jit(solution)/shard_map/ppermute | solution.py:35
  188.5 4.7 %collective-permute-start.17 = (bf16[128,384]{1,0:T(8,128)(2,1)S(1)}, bf16[128,384]{1,0:T(8,128)(2,1)S(1)}, u32[]{:S(2)}, u32[]{:S(2)}) collective-permute-start(bf16[128,384]{1,0:T(8,128)(2,1)S(1)} %fusion.32), channel_id=1, source_target_pairs={{0,24},{8,0},{16,8},{24,16},{1,25},{9,1},{17,9},{25,17},{2,26},{10... | collective-permute-start | bytes 294920 | tf_op jit(solution)/shard_map/ppermute | solution.py:35
  195.9 1.7 collective-permute-start.18
  198.3 5.5 %collective-permute-start.19 = (bf16[2,56,384]{2,0,1:T(2,128)(2,1)S(1)}, bf16[2,56,384]{2,0,1:T(2,128)(2,1)S(1)}, u32[]{:S(2)}, u32[]{:S(2)}) collective-permute-start(bf16[2,56,384]{2,0,1:T(2,128)(2,1)S(1)} %get-tuple-element.85), channel_id=1, source_target_pairs={{0,2},{2,4},{4,6},{6,0},{1,3},{3,5},{5,7},{7,1},{8,10},{10,12},{12... | collective-permute-start | bytes 258056 | tf_op jit(solution)/shard_map/ppermute | solution.py:35
  198.9 6.2 %collective-permute-start.20 = (bf16[2,56,384]{2,0,1:T(2,128)(2,1)S(1)}, bf16[2,56,384]{2,0,1:T(2,128)(2,1)S(1)}, u32[]{:S(2)}, u32[]{:S(2)}) collective-permute-start(bf16[2,56,384]{2,0,1:T(2,128)(2,1)S(1)} %get-tuple-element.87), channel_id=1, source_target_pairs={{0,4},{2,6},{4,0},{6,2},{1,5},{3,7},{5,1},{7,3},{8,12},{10,14},{12... | collective-permute-start | bytes 258056 | tf_op jit(solution)/shard_map/ppermute | solution.py:35
  201.3 5.7 %collective-permute-start.21 = (bf16[2,56,384]{2,0,1:T(2,128)(2,1)S(1)}, bf16[2,56,384]{2,0,1:T(2,128)(2,1)S(1)}, u32[]{:S(2)}, u32[]{:S(2)}) collective-permute-start(bf16[2,56,384]{2,0,1:T(2,128)(2,1)S(1)} %get-tuple-element.86), channel_id=1, source_target_pairs={{0,6},{2,0},{4,2},{6,4},{1,7},{3,1},{5,3},{7,5},{8,14},{10,8},{12,... | collective-permute-start | bytes 258056 | tf_op jit(solution)/shard_map/ppermute | solution.py:35
  207.3 8.0 %collective-permute-start.22 = (bf16[56,384]{1,0:T(8,128)(2,1)S(1)}, bf16[56,384]{1,0:T(8,128)(2,1)S(1)}, u32[]{:S(2)}, u32[]{:S(2)}) collective-permute-start(bf16[56,384]{1,0:T(8,128)(2,1)S(1)} %bitcast.117), channel_id=1, source_target_pairs={{0,128},{128,0},{1,129},{129,1},{2,130},{130,2},{3,131},{131,3},{4... | collective-permute-start | bytes 129032 | tf_op jit(solution)/shard_map/ppermute | solution.py:35
  215.4 5.8 %collective-permute-start.23 = (bf16[12,384]{1,0:T(8,128)(2,1)S(1)}, bf16[12,384]{1,0:T(8,128)(2,1)S(1)}, u32[]{:S(2)}, u32[]{:S(2)}) collective-permute-start(bf16[12,384]{1,0:T(8,128)(2,1)S(1)} %get-tuple-element.91), channel_id=1, source_target_pairs={{0,32},{32,64},{64,96},{96,0},{1,33},{33,65},{65,97},{97,1},{2,34}... | collective-permute-start | bytes 27656 | tf_op jit(solution)/shard_map/ppermute | solution.py:35
  218.1 4.6 %collective-permute-start.24 = (bf16[12,384]{1,0:T(8,128)(2,1)S(1)}, bf16[12,384]{1,0:T(8,128)(2,1)S(1)}, u32[]{:S(2)}, u32[]{:S(2)}) collective-permute-start(bf16[12,384]{1,0:T(8,128)(2,1)S(1)} %get-tuple-element.93), channel_id=1, source_target_pairs={{0,64},{32,96},{64,0},{96,32},{1,65},{33,97},{65,1},{97,33},{2,66}... | collective-permute-start | bytes 27656 | tf_op jit(solution)/shard_map/ppermute | solution.py:35
  219.3 3.7 %collective-permute-start.25 = (bf16[12,384]{1,0:T(8,128)(2,1)S(1)}, bf16[12,384]{1,0:T(8,128)(2,1)S(1)}, u32[]{:S(2)}, u32[]{:S(2)}) collective-permute-start(bf16[12,384]{1,0:T(8,128)(2,1)S(1)} %get-tuple-element.92), channel_id=1, source_target_pairs={{0,96},{32,0},{64,32},{96,64},{1,97},{33,1},{65,33},{97,65},{2,98}... | collective-permute-start | bytes 27656 | tf_op jit(solution)/shard_map/ppermute | solution.py:35
